TPU v7x, 32 devices: a whole 2x2x4 slice. The times are simulated.
32 devices in a mesh: fsdp: 8 (over z, y), seq: 4 (over x, core).
Axes of the slice: x: 2, y: 2, z: 4, core: 2. Of those that a mesh axis runs over, the one named last changes fastest.
Arguments:
- tokens: bfloat16 [64, 320, 1024], P('fsdp', 'seq'), may hold values from -6 to 6
- lengths: int32 [64], P('fsdp'), may hold values from 200 to 320, as said below
- attn_gain: bfloat16 [1024], P('fsdp'), may hold values from 0.5 to 1.5
- attn_shift: bfloat16 [1024], P('fsdp'), may hold values from -4 to 4
- attn_weight: bfloat16 [1024, 3072], P('fsdp'), may hold values from -0.1875 to 0.1875
- attn_bias: bfloat16 [2048], P('fsdp'), may hold values from -4 to 4
- out_weight: bfloat16 [1024, 1024], P('fsdp'), may hold values from -0.75 to 0.75
- out_bias: bfloat16 [1024], P('fsdp'), may hold values from -4 to 4
- mlp_gain: bfloat16 [1024], P('fsdp'), may hold values from 0.5 to 1.5
- mlp_shift: bfloat16 [1024], P('fsdp'), may hold values from -4 to 4
- up_weight: bfloat16 [1024, 4096], P('fsdp'), may hold values from -0.1875 to 0.1875
- up_bias: bfloat16 [4096], P('fsdp'), may hold values from -4 to 4
- down_weight: bfloat16 [4096, 1024], P('fsdp'), may hold values from -0.09375 to 0.09375
- down_bias: bfloat16 [1024], P('fsdp'), may hold values from -4 to 4
- cotangent: bfloat16 [64, 320, 1024], P('fsdp', 'seq'), may hold values from -6 to 6
Outputs:
- layer_out: bfloat16 [64, 320, 1024], P('fsdp', 'seq')
- input_grad: bfloat16 [64, 320, 1024], P('fsdp', 'seq')
- attn_gain_grad: float32 [1024], P('fsdp')
- attn_shift_grad: float32 [1024], P('fsdp')
- attn_weight_grad: float32 [1024, 3072], P('fsdp')
- attn_bias_grad: float32 [2048], P('fsdp')
- out_weight_grad: float32 [1024, 1024], P('fsdp')
- out_bias_grad: float32 [1024], P('fsdp')
- mlp_gain_grad: float32 [1024], P('fsdp')
- mlp_shift_grad: float32 [1024], P('fsdp')
- up_weight_grad: float32 [1024, 4096], P('fsdp')
- up_bias_grad: float32 [4096], P('fsdp')
- down_weight_grad: float32 [4096, 1024], P('fsdp')
- down_bias_grad: float32 [1024], P('fsdp')
Inputs may be any that keep to these rules, and one draw needn't show every extreme that they name: `lengths`: valid slots come first in each image; among the 8 images of each index of fsdp one has exactly 320 valid slots; some image has 200.
All inputs are finite; a program needn't handle non-finite values.
Results may differ from a plain program's by a relative error of at most 0.015.
Values may be sent and summed in bfloat16 or wider, within the bound.
No kernel may reach another device: no remote copies, remote signals or barrier semaphores. Data moves between devices by JAX's collectives and lax.ppermute only.
A program may use at most 192 MiB of HBM per device.

v0:
```python
import functools

import jax
import jax.numpy as jnp
from jax import lax
from jax.experimental import pallas as pl
from jax.experimental.pallas import tpu as pltpu
from jax.sharding import Mesh
from jax.sharding import PartitionSpec as P

HEAD_DIM = 64
LANES = 128
GROUPS = 2
TILES = 2
EPSILON = 1e-06
BF16 = jnp.bfloat16
F32 = jnp.float32
FSDP, SEQ = ("z", "y"), ("x", "c")


def cost(microseconds, nbytes=0):
    return pl.CostEstimate(flops=int(microseconds * 1.1e9), bytes_accessed=nbytes, transcendentals=0)


def norm_back(grad_norm, gain, normal, inv_std):
    scaled = grad_norm * gain
    return inv_std * (
        scaled
        - jnp.mean(scaled, axis=-1, keepdims=True)
        - normal * jnp.mean(scaled * normal, axis=-1, keepdims=True)
    )


def contract(a, b, ca, cb):
    return lax.dot_general(a, b, (((ca,), (cb,)), ((), ())), preferred_element_type=F32)


def lanes_of(shape):
    lane = lax.broadcasted_iota(jnp.int32, shape, 1)
    return lane // HEAD_DIM, lane % HEAD_DIM


def spread_over(places, place, columns, rest=0.0):
    out = jnp.full(place.shape, rest, F32)
    for i in places:
        out = jnp.where(place == i, columns[i], out)
    return out


def parts_of(value, count):
    parts = []
    for _ in range(count):
        parts.append(value.astype(BF16).astype(F32))
        value = value - parts[-1]
    return parts


SCALE = HEAD_DIM ** (-0.5)


def attend_kernel(bias_ref, q_ref, k_ref, v_ref, out_ref, lse_ref):
    bias = bias_ref[0]
    for tile in range(q_ref.shape[2] // LANES):
        at = slice(tile * LANES, (tile + 1) * LANES)
        q, k, v = (ref[0, :, at].astype(F32) for ref in (q_ref, k_ref, v_ref))
        head_of, place = lanes_of(q.shape)
        context, lse = jnp.zeros(q.shape, F32), jnp.zeros(q.shape, F32)
        for head in range(LANES // HEAD_DIM):
            own = head_of == head
            left = jnp.where(own, q * SCALE, spread_over((0,), place, (1.0,))).astype(BF16)
            right = jnp.where(own, k, spread_over((0,), place, (bias,))).astype(BF16)
            scores = contract(left, right, 1, 1)
            top = jnp.max(scores, axis=-1, keepdims=True)
            exps = jnp.exp(scores - top).astype(BF16)
            both = contract(exps, jnp.where(own, v, 1.0).astype(BF16), 1, 0)
            other = (1 - head) * HEAD_DIM
            total = both[:, other : other + 1]
            context = jnp.where(own, both * (1.0 / total), context)
            lse = jnp.where(own, lse, top + jnp.log(total))
        out_ref[0, :, at] = context.astype(BF16)
        lse_ref[0, :, at] = lse


def attend_back_kernel(bias_ref, q_ref, k_ref, v_ref, lse_ref, context_ref, g_ref, out_ref):
    bias = bias_ref[0]
    tiles = q_ref.shape[2] // LANES
    width = out_ref.shape[2] // 3
    for tile in range(tiles):
        at = slice(tile * LANES, (tile + 1) * LANES)
        q_low, k_low, g_low = q_ref[0, :, at], k_ref[0, :, at], g_ref[0, :, at]
        q, k, v, g, context = (ref[0, :, at].astype(F32) for ref in (q_ref, k_ref, v_ref, g_ref, context_ref))
        head_of, place = lanes_of(q.shape)
        dq, dk, dv = (jnp.zeros(q.shape, F32) for _ in range(3))
        lse_parts = [-part for part in parts_of(lse_ref[0, :, at], 3)] + [1.0]
        product = g * context
        for head in range(LANES // HEAD_DIM):
            own = head_of == head
            left = jnp.where(own, q * SCALE, spread_over(range(4), place, lse_parts)).astype(BF16)
            right = jnp.where(own, k, spread_over(range(4), place, (1.0, 1.0, 1.0, bias))).astype(BF16)
            probs = jnp.exp(contract(left, right, 1, 1))
            inner = jnp.sum(jnp.where(own, product, 0.0), axis=-1, keepdims=True)
            inner_parts = [-part for part in parts_of(inner, 2)]
            left = jnp.where(own, g, spread_over(range(2), place, inner_parts)).astype(BF16)
            right = jnp.where(own, v, spread_over(range(2), place, (1.0, 1.0))).astype(BF16)
            grad_scores = (probs * contract(left, right, 1, 1)).astype(BF16)
            dq = jnp.where(own, contract(grad_scores, k_low, 1, 0), dq)
            dk = jnp.where(own, contract(grad_scores, q_low, 0, 0), dk)
            dv = jnp.where(own, contract(probs.astype(BF16), g_low, 0, 0), dv)
        for block, value in enumerate((dq * SCALE, dk * SCALE, dv)):
            start = block * width + (pl.program_id(1) * tiles + tile) * LANES
            out_ref[0, :, pl.ds(pl.multiple_of(start, LANES), LANES)] = value.astype(BF16)


def attention(key_bias, joint, saved=(), group=0):
    images, slots, width = joint.shape[0], joint.shape[1], joint.shape[2] // 3
    lanes = TILES * LANES
    in_group = width // lanes // GROUPS
    back = len(saved) > 0
    pairs = in_group if back else in_group * GROUPS
    block = (1, slots, lanes)

    def spec(part):
        def index(i, h):
            h = h + group * in_group
            return i, 0, (h // in_group * 3 + part) * in_group + h % in_group

        return pl.BlockSpec(block, index)

    plain = pl.BlockSpec(block, lambda i, h: (i, 0, h + group * in_group))
    bias = pl.BlockSpec((1, slots, 1), lambda i, h: (i, 0, 0))
    whole = pl.BlockSpec((1, slots, 3 * pairs * lanes), lambda i, h: (i, 0, 0))
    shape = lambda columns, kind: jax.ShapeDtypeStruct((images, slots, columns), kind)
    return pl.pallas_call(
        attend_back_kernel if back else attend_kernel,
        grid=(images, pairs),
        in_specs=[bias] + [spec(part) for part in range(3)] + [plain] * len(saved),
        out_specs=whole if back else [plain, plain],
        out_shape=shape(3 * pairs * lanes, BF16) if back else [shape(width, BF16), shape(width, F32)],
        cost_estimate=cost((1.3 if back else 0.8) * images * pairs * TILES),
    )(key_bias, joint, joint, joint, *saved)


STEP = 512


def stats(values):
    center = values - jnp.mean(values, axis=-1, keepdims=True)
    inv_std = lax.rsqrt(jnp.mean(center * center, axis=-1, keepdims=True) + EPSILON)
    return center * inv_std, inv_std


def column_sums(values):
    return jnp.sum(values, axis=0, keepdims=True)


def block_spec(shape, index=lambda j: 0, at=1):
    def position(j, place):
        value = index(j, place) if index.__code__.co_argcount == 2 else index(j)
        return (0, value) if at else (value, 0)

    return pl.BlockSpec(shape, position)


def whole_spec(array):
    return block_spec(array.shape)


def columns_spec(rows, index=lambda j: j):
    return block_spec((rows, STEP), index)


class Weight:
    def __init__(self, arrays, by_rows=False, base=0, blocks=None):
        self.arrays, self.by_rows, self.base, self.blocks = tuple(arrays), by_rows, base, blocks

    def specs(self):
        return [pl.BlockSpec(memory_space=pl.ANY)] * len(self.arrays)

    def copies(self, refs, place_ref, j, block, buf, sem):
        copy = lambda source, target: pltpu.make_async_copy(source, target, sem)
        if len(refs) == 1:
            at = pl.ds(pl.multiple_of(block * STEP, STEP), STEP)
            return [(None, [copy(refs[0].at[at] if self.by_rows else refs[0].at[:, at], buf)])]
        y, x, c = place_ref[0], place_ref[1], place_ref[2]
        depth, rows = refs[0].shape[0], refs[0].shape[1]

        def piece(owner, i, z):
            five = refs[5 * owner : 5 * owner + 5]
            if i < 3:
                return five[i].at[z]
            return five[3].at[z] if z < depth // 2 else five[4].at[z - depth // 2]

        found = []
        if not self.by_rows:
            half = self.blocks // 2
            lanes = pl.ds(pl.multiple_of(self.base + block % half * STEP, LANES), STEP)
            for owner in range(2):
                some = []
                for i in range(4):
                    for z in range(depth):
                        row = (2 * z + (y ^ (i // 2))) * 2 * rows + (x ^ (i % 2)) * rows
                        target = buf.at[pl.ds(pl.multiple_of(row, rows), rows)]
                        some.append(copy(piece(owner, i, z).at[:, lanes], target))
                found.append(((block // half == c) == (owner == 0), some))
            return found
        width = buf.shape[1]
        segments = refs[0].shape[2] // width
        for z in range(depth):
            for far in range(2):
                some = []
                for owner in range(2):
                    for i in range(2):
                        for k in range(segments):
                            row = ((c ^ owner) * 2 + (x ^ i)) * segments * rows + k * rows
                            source = piece(owner, 2 * far + i, z).at[:, pl.ds(k * width, width)]
                            some.append(copy(source, buf.at[pl.ds(pl.multiple_of(row, rows), rows)]))
                found.append((j == 2 * z + far, some))
        return found

    def start(self, *where):
        for condition, some in self.copies(*where):
            go = lambda some=some: [one.start() for one in some] and None
            go() if condition is None else pl.when(condition)(go)

    def wait(self, *where):
        for condition, some in self.copies(*where):
            go = lambda some=some: [one.wait() for one in some] and None
            go() if condition is None else pl.when(condition)(go)


def shard_block(j, place):
    return j // 2 * 2 + (place[0] ^ (j % 2))


def stream(weight, refs, place_ref, block, buf, sems):
    j = pl.program_id(0)

    def where(step):
        slot = step % 2
        return refs, place_ref, step, block(step), buf.at[slot], sems.at[slot]

    @pl.when(j == 0)
    def _():
        weight.start(*where(j))

    @pl.when(j + 1 < pl.num_programs(0))
    def _():
        weight.start(*where(j + 1))

    weight.wait(*where(j))
    return buf[j % 2]


def split_refs(refs, weights):
    groups = []
    for weight in weights:
        groups.append(refs[: len(weight.arrays)])
        refs = refs[len(weight.arrays) :]
    return groups, refs


def stepped(kernel, steps, place, weights, in_specs, operands, out_specs, out_shape, scratch, microseconds):
    specs = [spec for weight in weights for spec in weight.specs()]
    arrays = [v for weight in weights for v in weight.arrays]
    return pl.pallas_call(
        functools.partial(kernel, weights),
        grid_spec=pltpu.PrefetchScalarGridSpec(
            num_scalar_prefetch=1,
            grid=(steps,),
            in_specs=specs + in_specs,
            out_specs=out_specs,
            scratch_shapes=scratch,
        ),
        out_shape=out_shape,
        compiler_params=pltpu.CompilerParams(vmem_limit_bytes=56 << 20),
        cost_estimate=cost(microseconds),
    )(place, *arrays, *operands)


def streamed(rows, columns):
    return [pltpu.VMEM((2, rows, columns), BF16), pltpu.SemaphoreType.DMA((2,))]


def project_kernel(weights, place_ref, *refs):
    (weight_refs,), refs = split_refs(refs, weights)
    tokens_ref, gain_ref, shift_ref, bias_ref, normed_ref, joint_ref, buf, sems = refs
    j = pl.program_id(0)

    @pl.when(j == 0)
    def _():
        normal, _ = stats(tokens_ref[...].astype(F32))
        normed_ref[...] = (normal * gain_ref[...] + shift_ref[...]).astype(BF16)

    weight = stream(weights[0], weight_refs, place_ref, lambda step: step, buf, sems)
    bias = jnp.where(j % 3 == 1, 0.0, bias_ref[...])
    joint_ref[...] = (contract(normed_ref[...], weight, 1, 0) + bias).astype(BF16)


def project(place, tokens, gain, shift, weight, bias_qv):
    rows, width = tokens.shape
    assert width // GROUPS == STEP
    return stepped(
        project_kernel,
        3 * width // STEP,
        place,
        [weight],
        [whole_spec(tokens), whole_spec(gain), whole_spec(shift)]
        + [columns_spec(1, lambda j: j // 3 + jnp.where(j % 3 == 2, GROUPS, 0))],
        (tokens, gain, shift, bias_qv),
        [whole_spec(tokens), columns_spec(rows)],
        [jax.ShapeDtypeStruct((rows, width), BF16), jax.ShapeDtypeStruct((rows, 3 * width), BF16)],
        streamed(width, STEP),
        11,
    )


def out_blocks(weight, refs, place_ref, buf, sem):
    for block in range(buf.shape[0]):
        yield weight, (refs, place_ref, 0, block, buf.at[block], sem)


def expand_kernel(weights, place_ref, *refs):
    (up_refs, out_w_refs), refs = split_refs(refs, weights)
    tokens_ref, context_ref, bias_out_ref, gain_ref, shift_ref, bias_ref, *refs = refs
    middle_ref, normed_ref, hidden_ref, slope_ref, buf, sems, out_buf, out_sem = refs

    @pl.when(pl.program_id(0) == 0)
    def _():
        blocks = list(out_blocks(weights[1], out_w_refs, place_ref, out_buf, out_sem))
        for weight, where in blocks:
            weight.start(*where)
        for weight, where in blocks:
            weight.wait(*where)
        context = context_ref[...]
        branch = jnp.concatenate([contract(context, out_buf[b], 1, 0) for b in range(out_buf.shape[0])], axis=1)
        middle = tokens_ref[...].astype(F32) + (branch + bias_out_ref[...])
        middle_ref[...] = middle
        normal, _ = stats(middle)
        normed_ref[...] = (normal * gain_ref[...] + shift_ref[...]).astype(BF16)

    weight = stream(weights[0], up_refs, place_ref, lambda step: step, buf, sems)
    pre = contract(normed_ref[...], weight, 1, 0) + bias_ref[...]
    cumul = 0.5 * (1.0 + lax.erf(pre * 0.7071067811865476))
    hidden_ref[...] = (pre * cumul).astype(BF16)
    slope = cumul + pre * (jnp.exp(-0.5 * pre * pre) * 0.3989422804014327)
    slope_ref[...] = slope.astype(BF16)


def expand(place, tokens, context, out_weight, bias_out, gain, shift, up, bias_up):
    rows, width = tokens.shape
    hidden = bias_up.shape[1]
    return stepped(
        expand_kernel,
        hidden // STEP,
        place,
        [up, out_weight],
        [whole_spec(v) for v in (tokens, context, bias_out, gain, shift)] + [columns_spec(1)],
        (tokens, context, bias_out, gain, shift, bias_up),
        [whole_spec(tokens)] * 2 + [columns_spec(rows)] * 2,
        [jax.ShapeDtypeStruct((rows, width), F32), jax.ShapeDtypeStruct((rows, width), BF16)]
        + [jax.ShapeDtypeStruct((rows, hidden), BF16)] * 2,
        streamed(width, STEP) + [pltpu.VMEM((width // STEP, width, STEP), BF16), pltpu.SemaphoreType.DMA],
        20,
    )


def accumulate(total_ref, part, first=None):
    j = pl.program_id(0)

    @pl.when(j == 0)
    def _():
        total_ref[...] = part if first is None else first() + part

    @pl.when(j > 0)
    def _():
        total_ref[...] += part


def finish_kernel(weights, place_ref, *refs):
    (down_refs,), refs = split_refs(refs, weights)
    hidden_ref, middle_ref, bias_ref, valid_ref, result_ref, total_ref, buf, sems = refs
    block = lambda step: shard_block(step, place_ref)
    weight = stream(weights[0], down_refs, place_ref, block, buf, sems)
    part = contract(hidden_ref[...], weight, 1, 0)
    accumulate(total_ref, part, lambda: middle_ref[...] + bias_ref[...])

    @pl.when(pl.program_id(0) == pl.num_programs(0) - 1)
    def _():
        result_ref[...] = jnp.where(valid_ref[...] > 0.5, total_ref[...], 0.0).astype(BF16)


def finish(place, hidden, down, middle, bias_down, valid):
    rows, width = middle.shape
    return stepped(
        finish_kernel,
        hidden.shape[1] // STEP,
        place,
        [down],
        [columns_spec(rows, shard_block)] + [whole_spec(v) for v in (middle, bias_down, valid)],
        (hidden, middle, bias_down, valid),
        whole_spec(middle),
        jax.ShapeDtypeStruct((rows, width), BF16),
        [pltpu.VMEM((rows, width), F32)] + streamed(STEP, width),
        11,
    )


def back_kernel(weights, place_ref, *refs):
    (down_refs, up_refs, out_w_refs), refs = split_refs(refs, weights)
    grad_ref, slope_ref, middle_ref, gain_ref, *refs = refs
    pre_ref, bias_up_ref, grad_middle_ref, branch_ref, context_ref, sums_ref, total_ref, *refs = refs
    down_buf, down_sems, up_buf, up_sems, out_buf, out_sem = refs
    j = pl.program_id(0)
    blocks = lambda: out_blocks(weights[2], out_w_refs, place_ref, out_buf, out_sem)

    @pl.when(j == 0)
    def _():
        for weight, where in blocks():
            weight.start(*where)

    block = lambda step: shard_block(step, place_ref)
    down = stream(weights[0], down_refs, place_ref, block, down_buf, down_sems)
    up = stream(weights[1], up_refs, place_ref, block, up_buf, up_sems)
    pre = (contract(grad_ref[...], down, 1, 1) * slope_ref[...].astype(F32)).astype(BF16)
    pre_ref[...] = pre
    bias_up_ref[...] = column_sums(pre.astype(F32))
    accumulate(total_ref, contract(pre, up, 1, 1))

    @pl.when(j == pl.num_programs(0) - 1)
    def _():
        for weight, where in blocks():
            weight.wait(*where)
        normal, inv_std = stats(middle_ref[...])
        total = total_ref[...]
        grad_middle = grad_ref[...].astype(F32) + norm_back(total, gain_ref[...], normal, inv_std)
        grad_middle_ref[...] = grad_middle
        branch = grad_middle.astype(BF16)
        branch_ref[...] = branch
        context_ref[...] = sum(
            contract(branch[:, b * STEP : (b + 1) * STEP], out_buf[b], 1, 1) for b in range(out_buf.shape[0])
        ).astype(BF16)
        sums_ref[0:1] = column_sums(total * normal)
        sums_ref[1:2] = column_sums(total)
        sums_ref[2:3] = column_sums(branch.astype(F32))


def back(place, grad_out, down, slope, up, middle, gain, out_weight):
    rows, width = middle.shape
    hidden = slope.shape[1]
    return stepped(
        back_kernel,
        hidden // STEP,
        place,
        [down, up, out_weight],
        [whole_spec(grad_out), columns_spec(rows, shard_block), whole_spec(middle), whole_spec(gain)],
        (grad_out, slope, middle, gain),
        [columns_spec(rows, shard_block), columns_spec(1, shard_block)]
        + [whole_spec(middle)] * 3
        + [block_spec((8, width))],
        [
            jax.ShapeDtypeStruct((rows, hidden), BF16),
            jax.ShapeDtypeStruct((1, hidden), F32),
            jax.ShapeDtypeStruct((rows, width), F32),
            jax.ShapeDtypeStruct((rows, width), BF16),
            jax.ShapeDtypeStruct((rows, width), BF16),
            jax.ShapeDtypeStruct((8, width), F32),
        ],
        [pltpu.VMEM((rows, width), F32)]
        + streamed(STEP, width)
        + streamed(width, STEP)
        + [pltpu.VMEM((width // STEP, width, STEP), BF16), pltpu.SemaphoreType.DMA],
        23,
    )


def input_kernel(weights, place_ref, *refs):
    (weight_refs,), refs = split_refs(refs, weights)
    joint_0_ref, joint_1_ref, tokens_ref, gain_ref, grad_middle_ref, *refs = refs
    input_ref, bias_ref, sums_ref, total_ref, buf, sems = refs
    j = pl.program_id(0)
    first = jnp.broadcast_to(j < 3, joint_0_ref.shape)
    joint = jnp.where(first, joint_0_ref[...], joint_1_ref[...])
    bias_ref[...] = column_sums(joint.astype(F32))
    weight = stream(weights[0], weight_refs, place_ref, lambda step: step, buf, sems)
    accumulate(total_ref, contract(joint, weight, 1, 1))

    @pl.when(j == pl.num_programs(0) - 1)
    def _():
        normal, inv_std = stats(tokens_ref[...].astype(F32))
        total = total_ref[...]
        grad = grad_middle_ref[...] + norm_back(total, gain_ref[...], normal, inv_std)
        input_ref[...] = grad.astype(BF16)
        sums_ref[0:1] = column_sums(total * normal)
        sums_ref[1:2] = column_sums(total)


def back_input(place, joint_0, joint_1, weight, tokens, gain, grad_middle):
    rows, width = tokens.shape
    return stepped(
        input_kernel,
        3 * width // STEP,
        place,
        [weight],
        [columns_spec(rows, lambda j: jnp.minimum(j, 2)), columns_spec(rows, lambda j: jnp.maximum(j - 3, 0))]
        + [whole_spec(v) for v in (tokens, gain, grad_middle)],
        (joint_0, joint_1, tokens, gain, grad_middle),
        [whole_spec(tokens), columns_spec(1), block_spec((8, width))],
        [
            jax.ShapeDtypeStruct((rows, width), BF16),
            jax.ShapeDtypeStruct((1, 3 * width), F32),
            jax.ShapeDtypeStruct((8, width), F32),
        ],
        [pltpu.VMEM((rows, width), F32)] + streamed(width, STEP),
        14,
    )


def grouped(value):
    width = value.shape[-1] // 3
    part = width // GROUPS
    return jnp.concatenate(
        [value[..., t * width + g * part :][..., :part] for g in range(GROUPS) for t in range(3)], axis=-1
    )


def ungrouped(values):
    part = values[0].shape[-1] // 3
    return jnp.concatenate(
        [v[..., t * part : (t + 1) * part] for t in range(3) for v in values], axis=-1
    )


def swap(value, axis):
    return lax.ppermute(value, axis, [(0, 1), (1, 0)])


def send(value, axis, step):
    return lax.ppermute(value, axis, [(i, i ^ step) for i in range(lax.axis_size(axis))])


def pick(blocks, index):
    return lax.dynamic_index_in_dim(blocks, index, 0, keepdims=False)


def tie(*values):
    return lax.optimization_barrier(values)


def after(value, *others):
    return lax.optimization_barrier((value,) + others)[0]


def my_place():
    return jnp.stack([lax.axis_index(n) for n in ("y", "x", "c")]).astype(jnp.int32)


class Split:
    def __init__(self, shard, by_rows=False, columns=None):
        self.shard_rows, self.columns = shard[0], columns or shard[1]
        self.by_rows = by_rows
        self.rows = self.shard_rows // 4 if by_rows else self.shard_rows // 2
        self.wide = self.columns if by_rows else self.columns // 2

def exchange(blocks, axis):
    return lax.all_to_all(blocks, axis, split_axis=0, concat_axis=0, tiled=True)


def pieces_kernel(depth, rows, place_ref, qkv_ref, out_ref, up_ref, down_ref, *refs):
    *vector_refs, first_ref, second_ref, third_ref = refs
    x, c = place_ref[1], place_ref[2]
    at = pl.ds(pl.multiple_of(x * rows, rows), rows)

    def put(ref, lane, value):
        for z in range(depth):
            ref[z, : value.shape[0], lane : lane + value.shape[1]] = value
        return lane + value.shape[1]

    def columns(ref, start, count):
        return ref[at, pl.ds(pl.multiple_of(start, LANES), count)]

    width = out_ref.shape[1]
    part = width // 2
    lane = 0
    for t in range(3):
        lane = put(first_ref, lane, columns(qkv_ref, t * width + c * part, part))
    lane = put(first_ref, lane, columns(out_ref, c * part, part))
    packed = jnp.concatenate([ref[...] for ref in vector_refs], axis=0)
    padding = jnp.zeros((rows - packed.shape[0], LANES), packed.dtype)
    put(first_ref, lane, jnp.concatenate([packed, padding], axis=0))
    half = up_ref.shape[1] // 2
    put(second_ref, 0, columns(up_ref, c * half, half))
    blocks = down_ref.shape[0] // 4 // rows
    lane = 0
    for block in range(blocks):
        start = ((2 * c + x) * blocks + block) * rows
        lane = put(third_ref, lane, down_ref[pl.ds(pl.multiple_of(start, rows), rows), :])


def pieces(qkv, out, up, down, vectors):
    depth, rows = lax.axis_size("z"), qkv.shape[0] // 2
    vectors = [v.reshape(-1, LANES) for v in vectors]
    width = out.shape[1]
    wide = (2 * width + LANES, up.shape[1] // 2, down.shape[0] // 4 // rows * width)
    vmem = pl.BlockSpec(memory_space=pltpu.VMEM)
    return pl.pallas_call(
        functools.partial(pieces_kernel, depth, rows),
        in_specs=[pl.BlockSpec(memory_space=pltpu.SMEM)] + [vmem] * (4 + len(vectors)),
        out_specs=[vmem] * 3,
        out_shape=[jax.ShapeDtypeStruct((depth, rows, n), BF16) for n in wide],
        cost_estimate=cost(3),
    )(my_place(), qkv, out, up, down, *vectors)


def corner(from_x, from_y):
    half = from_x.shape[0] // 2
    return swap(from_x[:half], "y"), swap(from_y[half:], "x")


def core_swap(*pieces):
    return tuple(swap(v, "c") for v in pieces)


def my_place():
    return jnp.stack([lax.axis_index(n) for n in ("y", "x", "c")]).astype(jnp.int32)


def part_refs(x, near, far, rows, refs, at):
    own_ref, to_x_ref, to_y_ref, corner_ref = refs
    low, high = near[:rows], near[rows:]
    own_ref[at] = jnp.where(x == 0, low, high)
    to_x_ref[at] = jnp.where(x == 0, high, low)
    low, high = far[:rows], far[rows:]
    to_y_ref[at] = jnp.where(x == 0, low, high)
    corner_ref[at] = jnp.where(x == 0, high, low)


def grad_columns_kernel(ends, cut, place_ref, *refs):
    y, x = place_ref[0], place_ref[1]
    out_refs, turned_ref = refs[-5:-1], refs[-1]
    j = pl.program_id(0)

    def one(first, a_ref, a_sib_ref, g_ref, g_sib_ref):
        @pl.when(j == first)
        def _():
            turned_ref[0] = a_ref[...].T
            turned_ref[1] = a_sib_ref[...].T

        total = contract(turned_ref[0], g_ref[...], 1, 0) + contract(turned_ref[1], g_sib_ref[...], 1, 0)
        total = total.reshape(-1, 2, cut.shard_rows, total.shape[1])
        for z in range(total.shape[0]):
            near = jnp.where(y == 0, total[z, 0], total[z, 1]).astype(BF16)
            far = jnp.where(y == 0, total[z, 1], total[z, 0]).astype(BF16)
            part_refs(x, near, far, cut.rows, out_refs, z)

    if len(ends) == 1:
        one(0, *refs[:4])
        return
    for i, end in enumerate(ends):
        first = 0 if i == 0 else ends[i - 1]
        pl.when((j >= first) & (j < end))(functools.partial(one, first, *refs[4 * i : 4 * i + 4]))


def grad_rows_kernel(cut, place_ref, a0_ref, a1_ref, a0_sib_ref, a1_sib_ref, g_ref, g_sib_ref, *out_refs):
    y, x = place_ref[0], place_ref[1]
    by_y = [
        contract(ref[...], g_ref[...], 0, 0)
        + contract(sib_ref[...], g_sib_ref[...], 0, 0)
        for ref, sib_ref in ((a0_ref, a0_sib_ref), (a1_ref, a1_sib_ref))
    ]
    near = jnp.where(y == 0, by_y[0], by_y[1]).astype(BF16)
    far = jnp.where(y == 0, by_y[1], by_y[0]).astype(BF16)
    part_refs(x, near, far, cut.rows, out_refs, 0)


def grad_parts(jobs, cut, depth, step=512):
    tokens = jobs[0][0].shape[0]
    specs, operands, ends = [], [], []
    if cut.by_rows:
        ((a, a_sib, g, g_sib, _, _),) = jobs
        half = 2 * cut.rows
        every = pl.BlockSpec((tokens, cut.wide), lambda j, place: (0, 0))
        specs = [
            pl.BlockSpec((tokens, half), lambda j, place: (0, 4 * j + place[2])),
            pl.BlockSpec((tokens, half), lambda j, place: (0, 4 * j + 2 + place[2])),
            pl.BlockSpec((tokens, half), lambda j, place: (0, 4 * j + place[2])),
            pl.BlockSpec((tokens, half), lambda j, place: (0, 4 * j + 2 + place[2])),
            every,
            every,
        ]
        operands, kernel, grid, wide = [a, a, a_sib, a_sib, g, g_sib], functools.partial(grad_rows_kernel, cut), depth, cut.wide
        out_spec = lambda n: pl.BlockSpec((1, n, wide), lambda j, place: (j, 0, 0))
    else:
        grid = 0
        for a, a_sib, g, g_sib, start, steps in jobs:
            in_half = g.shape[1] // 2 // step
            every = pl.BlockSpec((tokens, a.shape[1]), lambda j, place: (0, 0))
            at = lambda j, first=grid, steps=steps: jnp.clip(j - first, 0, steps - 1)
            specs += [
                every,
                every,
            ] + [
                pl.BlockSpec(
                    (tokens, step), lambda j, place, at=at, n=in_half, s=start: (0, place[2] * n + s + at(j))
                )
            ] * 2
            operands += [a, a_sib, g, g_sib]
            grid += steps
            ends.append(grid)
        kernel, wide = functools.partial(grad_columns_kernel, ends, cut), grid * step
        out_spec = lambda n: pl.BlockSpec((depth, n, step), lambda j, place: (0, 0, j))
    total = 8 * depth * cut.rows * wide
    return pl.pallas_call(
        kernel,
        grid_spec=pltpu.PrefetchScalarGridSpec(
            num_scalar_prefetch=1,
            grid=(grid,),
            in_specs=specs,
            out_specs=[out_spec(cut.rows)] * 4,
            scratch_shapes=[] if cut.by_rows else [pltpu.VMEM((2, jobs[0][0].shape[1], tokens), BF16)],
        ),
        out_shape=[jax.ShapeDtypeStruct((depth, cut.rows, wide), BF16)] * 4,
        compiler_params=pltpu.CompilerParams(vmem_limit_bytes=52 << 20),
        cost_estimate=cost(total * 2.2e-6),
    )(my_place(), *operands)


def add(one, other):
    return (one.astype(F32) + other.astype(F32)).astype(BF16)


def grad_z(parts, from_x, from_y):
    return exchange(sum(v.astype(F32) for v in (parts[0], from_x, from_y)).astype(BF16), "z")


def grad_x(blocks):
    mine = jnp.sum(blocks.astype(F32), axis=0).astype(BF16)
    return mine, swap(mine, "x")


def grad_core(mine, from_x):
    return mine, from_x, swap(mine, "c"), swap(from_x, "c")


def shard_kernel(plan, place_ref, *refs):
    x, c = place_ref[1], place_ref[2]
    parts, out_refs = refs[: -len(plan)], refs[-len(plan) :]
    for (by_rows, sources), out_ref in zip(plan, out_refs):
        column = 0
        for core in range(2):
            for number, start, count, at in sources:
                four = parts[4 * number : 4 * number + 4]
                rows = four[0].shape[0]
                for half in range(2):
                    both = [
                        jnp.where(c == core, four[i][:, start : start + count], four[2 + i][:, start : start + count])
                        for i in range(2)
                    ]
                    value = jnp.where(x == half, both[0], both[1]).astype(F32)
                    if by_rows:
                        row = (2 * core + half) * rows
                        out_ref[row : row + rows, :] = value
                    else:
                        out_ref[half * rows : (half + 1) * rows, at[core] : at[core] + count] = value


def shards_of(gradients, plan):
    parts = [v for gradient in gradients for v in gradient]
    vmem = pl.BlockSpec(memory_space=pltpu.VMEM)
    return pl.pallas_call(
        functools.partial(shard_kernel, [(by_rows, sources) for by_rows, _, sources in plan]),
        in_specs=[pl.BlockSpec(memory_space=pltpu.SMEM)] + [vmem] * len(parts),
        out_specs=[vmem] * len(plan),
        out_shape=[jax.ShapeDtypeStruct(shape, F32) for _, shape, _ in plan],
        cost_estimate=cost(2),
    )(my_place(), *parts)


def pack_kernel(sums_a_ref, joint_ref, sums_b_ref, up_ref, down_ref, out_ref):
    shards = out_ref.shape[0]
    width = down_ref.shape[1]
    part = width // GROUPS

    def put(at, count, source):
        for i in range(shards):
            out_ref[i : i + 1, at : at + count] = source(i, count)
        return at + count

    def plain(ref, row):
        return lambda i, n: ref[row : row + 1, i * n : (i + 1) * n]

    def query_value(i, n):
        value, at = divmod(i * n, width)
        group, at = divmod(at, part)
        start = (3 * group + 2 * value) * part + at
        return joint_ref[0:1, start : start + n]

    n = width // shards
    at = put(0, n, plain(sums_a_ref, 0))
    at = put(at, n, plain(sums_a_ref, 1))
    at = put(at, 2 * n, query_value)
    at = put(at, n, plain(sums_b_ref, 2))
    at = put(at, n, plain(sums_b_ref, 0))
    at = put(at, n, plain(sums_b_ref, 1))
    at = put(at, up_ref.shape[1] // shards, plain(up_ref, 0))
    put(at, n, plain(down_ref, 0))


def pack(shards, sums_a, joint_sums, sums_b, up_sums, down_sums):
    vmem = pl.BlockSpec(memory_space=pltpu.VMEM)
    columns = (9 - 1) * down_sums.shape[1] + up_sums.shape[1]
    return pl.pallas_call(
        pack_kernel,
        in_specs=[vmem] * 5,
        out_specs=vmem,
        out_shape=jax.ShapeDtypeStruct((shards, columns // shards), F32),
        cost_estimate=cost(1),
    )(sums_a, joint_sums, sums_b, up_sums, down_sums)


def in_order(index, mine, theirs, axis):
    first, second = jnp.where(index == 0, mine, theirs), jnp.where(index == 0, theirs, mine)
    return jnp.concatenate([first, second], axis=axis)


def order_vectors(own_y, other_y):
    y = lax.axis_index("y")
    rows = [jnp.where(y == 0, own_y, other_y), jnp.where(y == 0, other_y, own_y)]
    return jnp.stack(rows, axis=1).reshape(2 * own_y.shape[0], -1)


def over_pairs(packed):
    y = lax.axis_index("y")
    packed = packed + swap(packed, "c")
    packed = packed + swap(packed, "x")
    packed = packed.reshape(lax.axis_size("z"), 2, -1)
    row = lambda yy: lax.dynamic_index_in_dim(packed, yy, 1, keepdims=False)
    return row(y) + swap(row(1 - y), "y")


def over_line(packed):
    z = lax.axis_index("z")
    return pick(packed, z) + sum(send(pick(packed, z ^ k), "z", k) for k in range(1, lax.axis_size("z")))


def scatter_plain(a, g):
    grad = lax.psum_scatter(contract(a, g, 0, 0).astype(BF16), FSDP, scatter_dimension=0, tiled=True)
    return lax.psum(grad, SEQ).astype(F32)


def shards(
    tokens,
    lengths,
    attn_gain,
    attn_shift,
    attn_weight,
    attn_bias,
    out_weight,
    out_bias,
    mlp_gain,
    mlp_shift,
    up_weight,
    up_bias,
    down_weight,
    down_bias,
    cotangent,
):
    width = tokens.shape[2]
    members = lax.axis_size(SEQ)
    staged = lax.axis_size("z") <= 8 and attn_weight.shape[0] % 128 == 0
    images = tokens.shape[0] // members
    slots = tokens.shape[1] * members
    rows = images * slots

    small = (attn_gain, attn_shift, attn_bias, out_bias, mlp_gain, mlp_shift, up_bias, down_bias)
    sizes = [v.shape[0] for v in small]
    cuts = [sum(sizes[:i]) for i in range(len(sizes))]
    packed = jnp.concatenate(small)

    few = tokens.shape[1]
    here = lax.axis_index(SEQ)
    lens = lax.dynamic_slice_in_dim(lengths, here * images, images, 0)
    slot = jnp.arange(slots, dtype=jnp.int32)
    slot = (slot // few ^ here) * few + slot % few
    valid = slot[None, :] < lens[:, None]
    key_bias = jnp.where(valid, 0.0, -1000000000.0)[:, :, None]
    valid = valid.reshape(rows, 1)

    def by_image(value):
        value = value.reshape(members, images, few, width)
        return [send(pick(value, here ^ k), SEQ, k) if k else pick(value, here) for k in range(members)]

    def by_slot(value):
        value = value.reshape(images, members, few, width)
        return [send(value[:, k], SEQ, k) if k else value[:, 0] for k in range(members)]

    def in_images(blocks):
        return jnp.stack(blocks, axis=1).reshape(rows, width)

    def in_slots(blocks):
        blocks = jnp.stack(blocks)
        return jnp.concatenate([pick(blocks, here ^ k) for k in range(members)], axis=0)

    def unpack(vectors):
        vectors = vectors.astype(F32)
        return [vectors[:, c : c + n].reshape(1, -1) for c, n in zip(cuts, sizes)]

    if staged:
        cut_qkv, cut_out, cut_up = (Split(w.shape) for w in (attn_weight, out_weight, up_weight))
        cut_down = Split(down_weight.shape, by_rows=True)
        cut_group = Split(attn_weight.shape, columns=3 * width // GROUPS)
        place = my_place()
        first, second, third = pieces(attn_weight, out_weight, up_weight, down_weight, small)
        tokens, cot, z1, second, third = tie(
            by_image(tokens), by_image(cotangent), exchange(first, "z"), second, third
        )
        tokens, cot = in_images(tokens), in_images(cot)
        x1, y1 = swap(z1, "x"), swap(z1, "y")
        z2 = exchange(second, "z")
        x1, y1, z1, third = tie(x1, y1, z1, third)
        vec_z, vec_y = (v[:, : sum(sizes) // LANES, -LANES:].reshape(v.shape[0], -1) for v in (z1, y1))
        vectors = unpack(order_vectors(vec_z, vec_y))
        d1, c1, z2, vectors, third = tie(corner(x1, y1), core_swap(z1, x1, y1), z2, vectors, third)
        gain_a, shift_a, bias_qv, bias_out, gain_b, shift_b, bias_up, bias_down = vectors
        arrays = (z1, x1, y1, *d1, *c1, *core_swap(*d1))
        qkv_full = Weight(arrays, blocks=3 * width // STEP)
        out_full = Weight(arrays, base=cut_qkv.wide, blocks=width // STEP)
        x2, y2, z3 = swap(z2, "x"), swap(z2, "y"), exchange(third, "z")
        normed_a, joint = project(place, tokens, gain_a, shift_a, qkv_full, bias_qv)
        joint, x2, y2, z2, normed_a = tie(joint, x2, y2, z2, normed_a)
        joint = joint.reshape(images, slots, 3 * width)
        d2, c2 = corner(x2, y2), core_swap(z2, x2, y2)
        context, lse = attention(key_bias, joint)
        context, d2, c2, z3 = tie(context.reshape(rows, width), d2, c2, z3)
        x3, y3 = swap(z3, "x"), swap(z3, "y")
        up_full = Weight((z2, x2, y2, *d2, *c2, *core_swap(*d2)), blocks=cut_up.columns // STEP)
        middle, normed_b, hidden, slope = expand(
            place, tokens, context, out_full, bias_out, gain_b, shift_b, up_full, bias_up
        )
        hidden, slope, x3, y3, z3, normed_sib = tie(hidden, slope, x3, y3, z3, swap(normed_a, "c"))
    else:
        vectors = unpack(lax.all_gather(packed, FSDP, axis=0))
        gain_a, shift_a, bias_qv, bias_out, gain_b, shift_b, bias_up, bias_down = vectors
        place = jnp.zeros((3,), jnp.int32)
        qkv_full, out_full, up_full, down_full = (
            Weight([lax.all_gather(w, FSDP, axis=0, tiled=True)], by_rows=w is down_weight)
            for w in (grouped(attn_weight), out_weight, up_weight, down_weight)
        )
        tokens = in_images(by_image(tokens))
        cot = in_images(by_image(cotangent))
        normed_a, joint = project(place, tokens, gain_a, shift_a, qkv_full, bias_qv)
        joint = joint.reshape(images, slots, 3 * width)
        context, lse = attention(key_bias, joint)
        context = context.reshape(rows, width)
        middle, normed_b, hidden, slope = expand(
            place, tokens, context, out_full, bias_out, gain_b, shift_b, up_full, bias_up
        )

    grad_out = jnp.where(valid, cot, jnp.zeros_like(cot))
    g_bias_down = jnp.sum(grad_out.astype(F32), axis=0, keepdims=True)
    valid_wide = valid.astype(F32)

    def back_attention(grad_context, group):
        saved = (lse, context.reshape(images, slots, width), grad_context)
        grad = attention(key_bias, joint, saved, group)
        return grad.reshape(rows, 3 * width // GROUPS)

    shard_count = lax.axis_size(FSDP)
    depth = lax.axis_size("z")
    if staged:
        d3, c3 = corner(x3, y3), core_swap(z3, x3, y3)
        down_parts = grad_parts([(hidden, swap(hidden, "c"), grad_out, swap(grad_out, "c"), 0, 0)], cut_down, depth)
        down_parts, slope, d3, c3, hidden = tie(down_parts, slope, d3, c3, hidden)
        down_full = Weight((z3, x3, y3, *d3, *c3, *core_swap(*d3)), by_rows=True)
        down_e = swap(down_parts[3], "y")
        grad_pre, bias_up_sums, grad_middle, grad_branch, grad_context, sums_b = back(
            place, grad_out, down_full, slope, up_full, middle, gain_b, out_full
        )
        grad_pre, down_e, grad_context, grad_branch, context_sib, normed_sib_b = tie(
            grad_pre, down_e, grad_context, grad_branch, swap(context, "c"), swap(normed_b, "c")
        )
        grad_context = grad_context.reshape(images, slots, width)
        pre_sib, branch_sib = swap(grad_pre, "c"), swap(grad_branch, "c")
        down_x, down_y = swap(add(down_parts[1], down_e), "x"), swap(down_parts[2], "y")
        joint_0 = back_attention(grad_context, 0)
        joint_0, grad_context, pre_sib, branch_sib = tie(joint_0, grad_context, pre_sib, branch_sib)
        half = cut_up.wide // STEP // 2
        up_job = (normed_b, normed_sib_b, grad_pre, pre_sib)
        a_parts = grad_parts([up_job + (0, half)], cut_up, depth)
        joint_0_sib = swap(joint_0, "c")
        a_parts, grad_context = tie(a_parts, grad_context)
        a_e = swap(a_parts[3], "y")
        out_job = (context, context_sib, grad_branch, branch_sib, 0, cut_out.wide // STEP)
        b_parts = grad_parts([up_job + (half, half), out_job], cut_up, depth)
        b_parts, grad_context, a_e, down_x, down_y = tie(b_parts, grad_context, a_e, down_x, down_y)
        a_x, a_y = swap(add(a_parts[1], a_e), "x"), swap(a_parts[2], "y")
        b_e = swap(b_parts[3], "y")
        down_b = grad_z(down_parts, down_x, down_y)
        qkv_job = lambda joint, sib: [(normed_a, normed_sib, joint, sib, 0, 1)]
        parts_0 = grad_parts(qkv_job(joint_0, joint_0_sib), cut_group, depth, cut_group.wide)
        parts_0, grad_context = tie(parts_0, grad_context)
        e_0 = swap(parts_0[3], "x")
        joint_1 = back_attention(grad_context, 1)
        joint_1, e_0, a_x, a_y, b_e, down_b, hidden = tie(joint_1, e_0, a_x, a_y, b_e, down_b, hidden)
        b_x, b_y = swap(add(b_parts[1], b_e), "x"), swap(b_parts[2], "y")
        a_z = grad_z(a_parts, a_x, a_y)
        x_0, y_0 = swap(parts_0[1], "x"), swap(add(parts_0[2], e_0), "y")
        parts_1 = grad_parts(qkv_job(joint_1, swap(joint_1, "c")), cut_group, depth, cut_group.wide)
        parts_1, joint_1 = tie(parts_1, joint_1)
        e_1 = swap(parts_1[3], "y")
        input_grad, joint_sums, sums_a = back_input(place, joint_0, joint_1, qkv_full, tokens, gain_a, grad_middle)
        input_grad, e_1, x_0, y_0, b_x, b_y, a_z, hidden = tie(input_grad, e_1, x_0, y_0, b_x, b_y, a_z, hidden)
        x_1, y_1 = swap(add(parts_1[1], e_1), "x"), swap(parts_1[2], "y")
        b_z = grad_z(b_parts, b_x, b_y)
        result = finish(place, hidden, down_full, middle, bias_down, valid_wide)
    else:
        grad_pre, bias_up_sums, grad_middle, grad_branch, grad_context, sums_b = back(
            place,
            grad_out, down_full, slope, up_full, middle, gain_b, out_full
        )
        grad_context = grad_context.reshape(images, slots, width)
        joint_0, joint_1 = (back_attention(grad_context, g) for g in range(GROUPS))
        input_grad, joint_sums, sums_a = back_input(place, joint_0, joint_1, qkv_full, tokens, gain_a, grad_middle)
        grad_joint = jnp.concatenate([joint_0, joint_1], axis=1)
        layer_out = by_slot(finish(place, hidden, down_full, middle, bias_down, valid_wide))

    if staged:
        packed = pack(shard_count, sums_a, joint_sums, sums_b, bias_up_sums, g_bias_down)
    else:
        group = 3 * width // GROUPS
        joint_sums = ungrouped([joint_sums[:, g * group : (g + 1) * group] for g in range(GROUPS)])
        g_bias_qv = jnp.concatenate([joint_sums[:, :width], joint_sums[:, 2 * width :]], axis=1)
        small_grads = (sums_a[0], sums_a[1], g_bias_qv, sums_b[2], sums_b[0], sums_b[1], bias_up_sums, g_bias_down)
        packed = jnp.concatenate([v.reshape(shard_count, -1) for v in small_grads], axis=1)
    if staged:
        x_1, y_1, b_z, result, input_grad, packed, a_g, down_g = tie(
            x_1, y_1, b_z, result, by_slot(input_grad), packed, grad_x(a_z), grad_x(down_b)
        )
        qkv_b = grad_z(
            tuple(jnp.concatenate([p, q], axis=2) for p, q in zip(parts_0[:1], parts_1[:1])),
            jnp.concatenate([x_0, x_1], axis=2),
            jnp.concatenate([y_0, y_1], axis=2),
        )
        qkv_b, a_g, b_g, down_g, layer_out, packed = tie(
            qkv_b, grad_core(*a_g), grad_core(*grad_x(b_z)), grad_core(*down_g), by_slot(result), over_pairs(packed)
        )
        packed = over_line(packed)
        half, n_out, n_qkv = cut_up.wide // 2, cut_out.wide, cut_group.wide
        up_plan = [(0, 0, half, (0, 2 * half)), (1, 0, half, (half, 3 * half))]
        g_up, g_out, g_down = shards_of(
            (a_g, b_g, down_g),
            [
                (False, up_weight.shape, up_plan),
                (False, out_weight.shape, [(1, half, n_out, (0, n_out))]),
                (True, down_weight.shape, [(2, 0, width, None)]),
            ],
        )
        part = width // GROUPS
        qkv_plan = []
        for g in range(GROUPS):
            for low in range(0, n_qkv, LANES):
                places = [divmod(c * n_qkv + low, part) for c in range(2)]
                places = [t * width + g * part + at for t, at in places]
                qkv_plan.append((0, g * n_qkv + low, LANES, places))
        (g_qkv,) = shards_of([grad_core(*grad_x(qkv_b))], [(False, attn_weight.shape, qkv_plan)])
    else:
        input_grad = by_slot(input_grad)
        packed = lax.psum_scatter(packed, FSDP, scatter_dimension=0)
        packed = lax.psum(packed, SEQ)
        g_qkv, g_out, g_up, g_down = (
            scatter_plain(a, g)
            for a, g in ((normed_a, grad_joint), (context, grad_branch), (normed_b, grad_pre), (hidden, grad_out))
        )
        g_qkv = ungrouped([g_qkv[:, : 3 * width // GROUPS], g_qkv[:, 3 * width // GROUPS :]])
    layer_out, input_grad = in_slots(layer_out), in_slots(input_grad)
    (g_gain_a, g_shift_a, g_bias_qv, g_bias_out, g_gain_b, g_shift_b, g_bias_up, g_bias_down) = (
        packed[c : c + n] for c, n in zip(cuts, sizes)
    )
    return (
        layer_out,
        input_grad,
        g_gain_a,
        g_shift_a,
        g_qkv,
        g_bias_qv,
        g_out,
        g_bias_out,
        g_gain_b,
        g_shift_b,
        g_up,
        g_bias_up,
        g_down,
        g_bias_down,
    )


def solution(mesh):
    shard_count, members = mesh.devices.shape
    fine = Mesh(mesh.devices.reshape(shard_count // 2, 2, members // 2, 2), FSDP + SEQ)
    rows, vector, matrix = P(FSDP, SEQ, None), P(FSDP), P(FSDP, None)
    weights = (vector, vector, matrix, vector, matrix, vector, vector, vector, matrix, vector, matrix, vector)
    return jax.shard_map(
        shards,
        mesh=fine,
        in_specs=(rows, vector) + weights + (rows,),
        out_specs=(rows, rows) + weights,
        check_vma=False,
    )
```

profile of v0, /device:TPU:0, one launch (start us, length us, event | category | flops | bytes accessed | tf_op | source)
XLA Modules:
  0.0 440.2 jit_solution(3316771122858441677)
XLA Ops:
  1.3 3.7 shard_map.254
  5.0 6.4 %all-to-all-start = ((bf16[4,64,2176]{2,1,0:T(8,128)(2,1)}), bf16[4,64,2176]{2,1,0:T(8,128)(2,1)S(1)}, u32[]{:S(2)}, u32[]{:S(2)}) async-start(bf16[4,64,2176]{2,1,0:T(8,128)(2,1)} %get-tuple-element.195), calls=%async_computation | async-start | bytes 2228224 | tf_op jit(solution)/shard_map/all_to_all | solution.py:565
  11.6 1.6 collective-permute-start.4
  14.0 1.5 collective-permute-start.1
  15.6 6.7 %collective-permute-done.4 = bf16[2,80,1024]{2,1,0:T(8,128)(2,1)S(1)} collective-permute-done((bf16[2,80,1024]{2,1,0:T(8,128)(2,1)S(1)}, bf16[2,80,1024]{2,1,0:T(8,128)(2,1)S(1)}, u32[]{:S(2)}, u32[]{:S(2)}) %collective-permute-start.4) | collective-permute-done | bytes 327712 | tf_op jit(solution)/shard_map/ppermute | solution.py:538
  22.2 6.1 %collective-permute-done.5 = bf16[2,80,1024]{2,1,0:T(8,128)(2,1)S(1)} collective-permute-done((bf16[2,80,1024]{2,1,0:T(8,128)(2,1)S(1)}, bf16[2,80,1024]{2,1,0:T(8,128)(2,1)S(1)}, u32[]{:S(2)}, u32[]{:S(2)}) %collective-permute-start.5) | collective-permute-done | bytes 327712 | tf_op jit(solution)/shard_map/ppermute | solution.py:538
  28.3 7.9 %collective-permute-done.1 = bf16[2,80,1024]{2,1,0:T(8,128)(2,1)S(1)} collective-permute-done((bf16[2,80,1024]{2,1,0:T(8,128)(2,1)S(1)}, bf16[2,80,1024]{2,1,0:T(8,128)(2,1)S(1)}, u32[]{:S(2)}, u32[]{:S(2)}) %collective-permute-start.1) | collective-permute-done | bytes 327712 | tf_op jit(solution)/shard_map/ppermute | solution.py:538
  37.0 5.5 %collective-permute-done.2 = bf16[2,80,1024]{2,1,0:T(8,128)(2,1)} collective-permute-done((bf16[2,80,1024]{2,1,0:T(8,128)(2,1)S(1)}, bf16[2,80,1024]{2,1,0:T(8,128)(2,1)}, u32[]{:S(2)}, u32[]{:S(2)}) %collective-permute-start.2) | collective-permute-done | bytes 327712 | tf_op jit(solution)/shard_map/ppermute | solution.py:538
  42.5 1.5 collective-permute-start.6
  44.0 1.5 collective-permute-start.7
  45.5 5.1 %all-to-all-start.1 = ((bf16[4,64,2048]{2,1,0:T(8,128)(2,1)}), bf16[4,64,2048]{2,1,0:T(8,128)(2,1)S(1)}, u32[]{:S(2)}, u32[]{:S(2)}) async-start(bf16[4,64,2048]{2,1,0:T(8,128)(2,1)} %get-tuple-element.203), calls=%async_computation.1 | async-start | bytes 2097152 | tf_op jit(solution)/shard_map/all_to_all | solution.py:565
  50.6 18.7 %collective-permute-done.6.refs_1_.refs_11_.refs_21_ = bf16[4,64,2176]{2,1,0:T(8,128)(2,1)} collective-permute-done((bf16[4,64,2176]{2,1,0:T(8,128)(2,1)S(1)}, bf16[4,64,2176]{2,1,0:T(8,128)(2,1)}, u32[]{:S(2)}, u32[]{:S(2)}) %collective-permute-start.6) | collective-permute-done | bytes 1114144 | tf_op jit(solution)/shard_map/ppermute | solution.py:534
  70.6 1.9 slice.96
  73.0 1.9 slice.97
  75.7 1.6 collective-permute-start.8
  79.7 11.4 %collective-permute-done.8.refs_3_.refs_13_.refs_23_ = bf16[2,64,2176]{2,1,0:T(8,128)(2,1)} collective-permute-done((bf16[2,64,2176]{2,1,0:T(8,128)(2,1)}, bf16[2,64,2176]{2,1,0:T(8,128)(2,1)}, u32[]{:S(2)}, u32[]{:S(2)}) %collective-permute-start.8) | collective-permute-done | bytes 557088 | tf_op jit(solution)/shard_map/ppermute | solution.py:534
  93.9 2.3 pad_maximum_fusion
  97.3 5.3 %all-to-all-start.2 = ((bf16[4,64,2048]{2,1,0:T(8,128)(2,1)}), bf16[4,64,2048]{2,1,0:T(8,128)(2,1)S(1)}, u32[]{:S(2)}, u32[]{:S(2)}) async-start(bf16[4,64,2048]{2,1,0:T(8,128)(2,1)} %get-tuple-element.226), calls=%async_computation.2 | async-start | bytes 2097152 | tf_op jit(solution)/shard_map/all_to_all | solution.py:565
  102.6 10.7 %shard_map.255 = (bf16[640,1024]{1,0:T(8,128)(2,1)}, bf16[640,3072]{1,0:T(8,128)(2,1)}) custom-call(s32[3]{0:T(128)} %pad_add_fusion.place_ref, bf16[4,64,2176]{2,1,0:T(8,128)(2,1)} %copy-done.7, bf16[4,64,2176]{2,1,0:T(8,128)(2,1)} %collective-permute-done.6.refs_1_.refs_11_.refs_21_, bf16[4,64,2176]{2,1,0:T(8,128)(2,1)} %collective-permute-done.7.refs_2_.refs_12_.refs_22_, ...), custom_call_target="tpu_custom_call" | custom-call | flops 12099999744 | tf_op jit(solution)/shard_map/pallas_call | solution.py:265
  113.3 8.1 %collective-permute-done.15.refs_1_.refs_11_ = bf16[4,64,2048]{2,1,0:T(8,128)(2,1)} collective-permute-done((bf16[4,64,2048]{2,1,0:T(8,128)(2,1)S(1)}, bf16[4,64,2048]{2,1,0:T(8,128)(2,1)}, u32[]{:S(2)}, u32[]{:S(2)}) %collective-permute-start.15) | collective-permute-done | bytes 1048608 | tf_op jit(solution)/shard_map/ppermute | solution.py:534
  122.9 1.9 slice.109
  125.8 1.5 collective-permute-start.18
  127.3 15.6 %shard_map.256 = (bf16[2,320,1024]{2,1,0:T(8,128)(2,1)}, f32[2,320,1024]{2,1,0:T(8,128)}) custom-call(f32[2,320,1]{2,1,0:T(8,128)} %compare_select_fusion.bias_ref, bf16[2,320,3072]{2,1,0:T(8,128)(2,1)} %bitcast.168, bf16[2,320,3072]{2,1,0:T(8,128)(2,1)} %bitcast.169, bf16[2,320,3072]{2,1,0:T(8,128)(2,1)} %bitcast.170), custom_call_target="tpu_custom_call" | custom-call | flops 14080000000 | tf_op jit(solution)/shard_map/pallas_call | solution.py:133
  144.6 1.5 collective-permute-start.25
  147.7 19.4 %shard_map.257 = (f32[640,1024]{1,0:T(8,128)}, bf16[640,1024]{1,0:T(8,128)(2,1)}, bf16[640,4096]{1,0:T(8,128)(2,1)}, bf16[640,4096]{1,0:T(8,128)(2,1)}) custom-call(s32[3]{0:T(128)} %pad_add_fusion.place_ref, bf16[4,64,2048]{2,1,0:T(8,128)(2,1)} %copy-done.10, bf16[4,64,2048]{2,1,0:T(8,128)(2,1)} %collective-permute-done.15.refs_1_.refs_11_, ...), custom_call_target="tpu_custom_call" | custom-call | flops 22000001024 | tf_op jit(solution)/shard_map/pallas_call | solution.py:265
  167.1 2.0 collective-permute-done.24.refs_1_
  175.0 8.2 %collective-permute-done.28.g_sib_ref = bf16[640,1024]{1,0:T(8,128)(2,1)S(1)} collective-permute-done((bf16[640,1024]{1,0:T(8,128)(2,1)S(1)}, bf16[640,1024]{1,0:T(8,128)(2,1)S(1)}, u32[]{:S(2)}, u32[]{:S(2)}) %collective-permute-start.28) | collective-permute-done | bytes 1310752 | tf_op jit(solution)/shard_map/ppermute | solution.py:534
  183.2 1.5 collective-permute-start.29
  185.5 11.4 %shard_map.258 = (bf16[4,128,1024]{2,1,0:T(8,128)(2,1)S(1)}, bf16[4,128,1024]{2,1,0:T(8,128)(2,1)}, bf16[4,128,1024]{2,1,0:T(8,128)(2,1)}, bf16[4,128,1024]{2,1,0:T(8,128)(2,1)}) custom-call(s32[3]{0:T(128)S(1)} %copy-done.2, bf16[640,4096]{1,0:T(8,128)(2,1)} %get-tuple-element.332.a0_ref.a1_ref.refs_10_, ...), custom_call_target="tpu_custom_call" | custom-call | flops 10150215680 | tf_op jit(solution)/shard_map/pallas_call | solution.py:712
  200.5 1.8 collective-permute-done.35.refs_9_
  202.4 28.6 %shard_map.259 = (bf16[640,4096]{1,0:T(8,128)(2,1)}, f32[1,4096]{1,0:T(1,128)}, f32[640,1024]{1,0:T(8,128)}, bf16[640,1024]{1,0:T(8,128)(2,1)}, bf16[640,1024]{1,0:T(8,128)(2,1)}, /*index=5*/f32[8,1024]{1,0:T(8,128)}) custom-call(s32[3]{0:T(128)} %pad_add_fusion.place_ref, bf16[4,64,2048]{2,1,0:T(8,128)(2,1)} %copy-done.9, bf16[4,64,2048]{2,1,0:T(8,128)(2,1)} %copy-done.18, ...), custom_call_target="tpu_custom_call" | custom-call | flops 25300000768 | tf_op jit(solution)/shard_map/pallas_call | solution.py:265
  232.5 11.1 %shard_map.260 = bf16[2,320,1536]{2,1,0:T(8,128)(2,1)} custom-call(f32[2,320,1]{2,1,0:T(8,128)} %compare_select_fusion.bias_ref, bf16[2,320,3072]{2,1,0:T(8,128)(2,1)} %bitcast.171, bf16[2,320,3072]{2,1,0:T(8,128)(2,1)} %bitcast.172, bf16[2,320,3072]{2,1,0:T(8,128)(2,1)} %bitcast.173, f32[2,320,1024]{2,1,0:T(8,128)} %get-tuple-element.241.lse_ref, ...), custom_call_target="tpu_custom_call" | custom-call | flops 11440000000 | tf_op jit(solution)/shard_map/pallas_call | solution.py:133
  245.2 8.0 %shard_map.263 = (bf16[4,64,1024]{2,1,0:T(8,128)(2,1)S(1)}, bf16[4,64,1024]{2,1,0:T(8,128)(2,1)S(1)}, bf16[4,64,1024]{2,1,0:T(8,128)(2,1)}, bf16[4,64,1024]{2,1,0:T(8,128)(2,1)}) custom-call(s32[3]{0:T(128)S(1)} %copy-done.3, bf16[640,1024]{1,0:T(8,128)(2,1)} %get-tuple-element.266.refs_0_, bf16[640,1024]{1,0:T(8,128)(2,1)} %copy-done.27, ...), custom_call_target="tpu_custom_call" | custom-call | flops 5075107840 | tf_op jit(solution)/shard_map/pallas_call | solution.py:712
  255.2 12.6 %shard_map.262 = (bf16[4,64,1536]{2,1,0:T(8,128)(2,1)S(1)}, bf16[4,64,1536]{2,1,0:T(8,128)(2,1)S(1)}, bf16[4,64,1536]{2,1,0:T(8,128)(2,1)}, bf16[4,64,1536]{2,1,0:T(8,128)(2,1)}) custom-call(s32[3]{0:T(128)S(1)} %copy-done.3, bf16[640,1024]{1,0:T(8,128)(2,1)} %get-tuple-element.266.refs_0_, bf16[640,1024]{1,0:T(8,128)(2,1)} %copy-done.27, ...), custom_call_target="tpu_custom_call" | custom-call | flops 7612661760 | tf_op jit(solution)/shard_map/pallas_call | solution.py:712
  267.8 2.0 collective-permute-done.43
  269.8 2.8 add_convert_fusion
  272.6 5.1 %all-to-all-start.3 = ((bf16[4,128,1024]{2,1,0:T(8,128)(2,1)}), bf16[4,128,1024]{2,1,0:T(8,128)(2,1)}, u32[]{:S(2)}, u32[]{:S(2)}) async-start(bf16[4,128,1024]{2,1,0:T(8,128)(2,1)} %add_convert_fusion), calls=%async_computation.3 | async-start | bytes 2097152 | tf_op jit(solution)/shard_map/all_to_all | solution.py:565
  277.7 2.1 add_convert_fusion.6
  281.7 6.2 %shard_map.261 = (bf16[4,64,768]{2,1,0:T(8,128)(2,1)S(1)}, bf16[4,64,768]{2,1,0:T(8,128)(2,1)S(1)}, bf16[4,64,768]{2,1,0:T(8,128)(2,1)S(1)}, bf16[4,64,768]{2,1,0:T(8,128)(2,1)}) custom-call(s32[3]{0:T(128)S(1)} %copy-done.3, bf16[640,1024]{1,0:T(8,128)(2,1)} %get-tuple-element.220.refs_0_, bf16[640,1024]{1,0:T(8,128)(2,1)} %copy-done.24, ...), custom_call_target="tpu_custom_call" | custom-call | flops 3806330880 | tf_op jit(solution)/shard_map/pallas_call | solution.py:712
  289.2 11.1 %shard_map.264 = bf16[2,320,1536]{2,1,0:T(8,128)(2,1)} custom-call(f32[2,320,1]{2,1,0:T(8,128)} %compare_select_fusion.bias_ref, bf16[2,320,3072]{2,1,0:T(8,128)(2,1)} %bitcast.174, bf16[2,320,3072]{2,1,0:T(8,128)(2,1)} %bitcast.175, bf16[2,320,3072]{2,1,0:T(8,128)(2,1)} %bitcast.176, f32[2,320,1024]{2,1,0:T(8,128)} %get-tuple-element.241.lse_ref, ...), custom_call_target="tpu_custom_call" | custom-call | flops 11440000000 | tf_op jit(solution)/shard_map/pallas_call | solution.py:133
  300.3 3.1 all-to-all-done.3
  306.5 2.3 add_convert_fusion.5
  308.8 4.3 all-to-all-start.4
  313.1 2.2 add_convert_fusion.4
  316.5 1.9 add_convert_fusion.8
  319.1 2.2 reduce_sum.59.refs_8_
  321.3 5.5 %shard_map.265 = (bf16[4,64,768]{2,1,0:T(8,128)(2,1)S(1)}, bf16[4,64,768]{2,1,0:T(8,128)(2,1)S(1)}, bf16[4,64,768]{2,1,0:T(8,128)(2,1)S(1)}, bf16[4,64,768]{2,1,0:T(8,128)(2,1)S(1)}) custom-call(s32[3]{0:T(128)S(1)} %copy-done.3, bf16[640,1024]{1,0:T(8,128)(2,1)} %get-tuple-element.220.refs_0_, bf16[640,1024]{1,0:T(8,128)(2,1)} %copy-done.24, ...), custom_call_target="tpu_custom_call" | custom-call | flops 3806330880 | tf_op jit(solution)/shard_map/pallas_call | solution.py:712
  326.8 1.4 collective-permute-start.50
  328.2 15.8 %shard_map.266 = (bf16[640,1024]{1,0:T(8,128)(2,1)}, f32[1,3072]{1,0:T(1,128)}, f32[8,1024]{1,0:T(8,128)}) custom-call(s32[3]{0:T(128)} %pad_add_fusion.place_ref, bf16[4,64,2176]{2,1,0:T(8,128)(2,1)} %copy-done.7, bf16[4,64,2176]{2,1,0:T(8,128)(2,1)} %collective-permute-done.6.refs_1_.refs_11_.refs_21_, ...), custom_call_target="tpu_custom_call" | custom-call | flops 15399999488 | tf_op jit(solution)/shard_map/pallas_call | solution.py:265
  344.0 1.5 shard_map.268
  346.9 2.6 add_convert_fusion.3
  349.5 5.1 %all-to-all-start.5 = ((bf16[4,64,1536]{2,1,0:T(8,128)(2,1)}), bf16[4,64,1536]{2,1,0:T(8,128)(2,1)S(1)}, u32[]{:S(2)}, u32[]{:S(2)}) async-start(bf16[4,64,1536]{2,1,0:T(8,128)(2,1)} %add_convert_fusion.3), calls=%async_computation.5 | async-start | bytes 1572864 | tf_op jit(solution)/shard_map/all_to_all | solution.py:565
  354.5 2.3 slice_bitcast_fusion.4
  363.0 15.1 %shard_map.267 = bf16[640,1024]{1,0:T(8,128)(2,1)} custom-call(s32[3]{0:T(128)} %pad_add_fusion.place_ref, bf16[4,64,2048]{2,1,0:T(8,128)(2,1)} %copy-done.9, bf16[4,64,2048]{2,1,0:T(8,128)(2,1)} %copy-done.18, bf16[4,64,2048]{2,1,0:T(8,128)(2,1)} %copy-done.20, bf16[2,64,2048]{2,1,0:T(8,128)(2,1)} %copy-done.31, ...), custom_call_target="tpu_custom_call" | custom-call | flops 12099999744 | tf_op jit(solution)/shard_map/pallas_call | solution.py:265
  378.1 7.3 %collective-permute-done.60.refs_1_ = bf16[64,1024]{1,0:T(8,128)(2,1)S(1)} collective-permute-done((bf16[64,1024]{1,0:T(8,128)(2,1)S(1)}, bf16[64,1024]{1,0:T(8,128)(2,1)S(1)}, u32[]{:S(2)}, u32[]{:S(2)}) %collective-permute-start.60) | collective-permute-done | bytes 131104 | tf_op jit(solution)/shard_map/ppermute | solution.py:534
  385.5 2.4 add_convert_fusion.2
  387.9 5.3 %all-to-all-start.6 = ((bf16[4,64,1536]{2,1,0:T(8,128)(2,1)}), bf16[4,64,1536]{2,1,0:T(8,128)(2,1)S(1)}, u32[]{:S(2)}, u32[]{:S(2)}) async-start(bf16[4,64,1536]{2,1,0:T(8,128)(2,1)} %add_convert_fusion.2), calls=%async_computation.6 | async-start | bytes 1572864 | tf_op jit(solution)/shard_map/all_to_all | solution.py:565
  398.9 1.4 slice_bitcast_fusion
  407.7 6.2 %collective-permute-done.70 = bf16[2,80,1024]{2,1,0:T(8,128)(2,1)S(1)} collective-permute-done((bf16[2,80,1024]{2,1,0:T(8,128)(2,1)S(1)}, bf16[2,80,1024]{2,1,0:T(8,128)(2,1)S(1)}, u32[]{:S(2)}, u32[]{:S(2)}) %collective-permute-start.70) | collective-permute-done | bytes 327712 | tf_op jit(solution)/shard_map/ppermute | solution.py:538
  414.0 6.2 %collective-permute-done.71 = bf16[2,80,1024]{2,1,0:T(8,128)(2,1)S(1)} collective-permute-done((bf16[2,80,1024]{2,1,0:T(8,128)(2,1)S(1)}, bf16[2,80,1024]{2,1,0:T(8,128)(2,1)S(1)}, u32[]{:S(2)}, u32[]{:S(2)}) %collective-permute-start.71) | collective-permute-done | bytes 327712 | tf_op jit(solution)/shard_map/ppermute | solution.py:538
  422.4 2.2 collective-permute-start.75
  424.6 2.4 collective-permute-start.76
  428.7 4.0 shard_map.270
  437.4 2.6 shard_map.269
  (275 shorter events, 69.6 us)
Async XLA Ops:
  5.0 37.5 %all-to-all-start = ((bf16[4,64,2176]{2,1,0:T(8,128)(2,1)}), bf16[4,64,2176]{2,1,0:T(8,128)(2,1)S(1)}, u32[]{:S(2)}, u32[]{:S(2)}) async-start(bf16[4,64,2176]{2,1,0:T(8,128)(2,1)} %get-tuple-element.195), calls=%async_computation | async-start | bytes 2228224 | tf_op jit(solution)/shard_map/all_to_all | solution.py:565
  13.2 15.1 %collective-permute-start.5 = (bf16[2,80,1024]{2,1,0:T(8,128)(2,1)S(1)}, bf16[2,80,1024]{2,1,0:T(8,128)(2,1)S(1)}, u32[]{:S(2)}, u32[]{:S(2)}) collective-permute-start(bf16[2,80,1024]{2,1,0:T(8,128)(2,1)S(1)} %get-tuple-element.402), channel_id=1, source_target_pairs={{0,3},{1,2},{2,1},{3,0},{4,7},{5,6},{6,5},{7,4},{8,11},{9,10},{10,... | collective-permute-start | bytes 983048 | tf_op jit(solution)/shard_map/ppermute | solution.py:538
  13.6 14.7 %collective-permute-start = (bf16[2,80,1024]{2,1,0:T(8,128)(2,1)S(1)}, bf16[2,80,1024]{2,1,0:T(8,128)(2,1)S(1)}, u32[]{:S(2)}, u32[]{:S(2)}) collective-permute-start(bf16[2,80,1024]{2,1,0:T(8,128)(2,1)S(1)} %get-tuple-element.408), channel_id=1, source_target_pairs={{0,1},{1,0},{2,3},{3,2},{4,5},{5,4},{6,7},{7,6},{8,9},{9,8},{10,11... | collective-permute-start | bytes 983048 | tf_op jit(solution)/shard_map/ppermute | solution.py:538
  14.0 22.2 %collective-permute-start.1 = (bf16[2,80,1024]{2,1,0:T(8,128)(2,1)S(1)}, bf16[2,80,1024]{2,1,0:T(8,128)(2,1)S(1)}, u32[]{:S(2)}, u32[]{:S(2)}) collective-permute-start(bf16[2,80,1024]{2,1,0:T(8,128)(2,1)S(1)} %get-tuple-element.407), channel_id=1, source_target_pairs={{0,2},{1,3},{2,0},{3,1},{4,6},{5,7},{6,4},{7,5},{8,10},{9,11},{10,... | collective-permute-start | bytes 983048 | tf_op jit(solution)/shard_map/ppermute | solution.py:538
  15.5 27.0 %collective-permute-start.2 = (bf16[2,80,1024]{2,1,0:T(8,128)(2,1)S(1)}, bf16[2,80,1024]{2,1,0:T(8,128)(2,1)}, u32[]{:S(2)}, u32[]{:S(2)}) collective-permute-start(bf16[2,80,1024]{2,1,0:T(8,128)(2,1)S(1)} %get-tuple-element.406), channel_id=1, source_target_pairs={{0,3},{1,2},{2,1},{3,0},{4,7},{5,6},{6,5},{7,4},{8,11},{9,10},{10,... | collective-permute-start | bytes 983048 | tf_op jit(solution)/shard_map/ppermute | solution.py:538
  42.5 26.9 %collective-permute-start.6 = (bf16[4,64,2176]{2,1,0:T(8,128)(2,1)S(1)}, bf16[4,64,2176]{2,1,0:T(8,128)(2,1)}, u32[]{:S(2)}, u32[]{:S(2)}) collective-permute-start(bf16[4,64,2176]{2,1,0:T(8,128)(2,1)S(1)} %all-to-all-done.refs_0_.refs_10_.refs_20_), channel_id=1, source_target_pairs={{0,2},{2,0},{1,3},{3,1},{4,6},{6,4},{5,7},{7,5},{8,10},{10,8},{9,1... | collective-permute-start | bytes 3342344 | tf_op jit(solution)/shard_map/ppermute | solution.py:534
  44.0 26.6 %collective-permute-start.7 = (bf16[4,64,2176]{2,1,0:T(8,128)(2,1)S(1)}, bf16[4,64,2176]{2,1,0:T(8,128)(2,1)}, u32[]{:S(2)}, u32[]{:S(2)}) collective-permute-start(bf16[4,64,2176]{2,1,0:T(8,128)(2,1)S(1)} %all-to-all-done.refs_0_.refs_10_.refs_20_), channel_id=1, source_target_pairs={{0,4},{4,0},{1,5},{5,1},{2,6},{6,2},{3,7},{7,3},{8,12},{12,8},{9,1... | collective-permute-start | bytes 3342344 | tf_op jit(solution)/shard_map/ppermute | solution.py:534
  45.5 34.2 %all-to-all-start.1 = ((bf16[4,64,2048]{2,1,0:T(8,128)(2,1)}), bf16[4,64,2048]{2,1,0:T(8,128)(2,1)S(1)}, u32[]{:S(2)}, u32[]{:S(2)}) async-start(bf16[4,64,2048]{2,1,0:T(8,128)(2,1)} %get-tuple-element.203), calls=%async_computation.1 | async-start | bytes 2097152 | tf_op jit(solution)/shard_map/all_to_all | solution.py:565
  70.6 21.8 %collective-permute-start.11 = (bf16[4,64,2176]{2,1,0:T(8,128)(2,1)}, bf16[4,64,2176]{2,1,0:T(8,128)(2,1)}, u32[]{:S(2)}, u32[]{:S(2)}) collective-permute-start(bf16[4,64,2176]{2,1,0:T(8,128)(2,1)} %collective-permute-done.6.refs_1_.refs_11_.refs_21_), channel_id=1, source_target_pairs={{0,1},{1,0},{2,3},{3,2},{4,5},{5,4},{6,7},{7,6},{8,9},{9,8},{10,11... | collective-permute-start | bytes 3342344 | tf_op jit(solution)/shard_map/ppermute | solution.py:534
  72.5 19.9 %collective-permute-start.12 = (bf16[4,64,2176]{2,1,0:T(8,128)(2,1)}, bf16[4,64,2176]{2,1,0:T(8,128)(2,1)}, u32[]{:S(2)}, u32[]{:S(2)}) collective-permute-start(bf16[4,64,2176]{2,1,0:T(8,128)(2,1)} %collective-permute-done.7.refs_2_.refs_12_.refs_22_), channel_id=1, source_target_pairs={{0,1},{1,0},{2,3},{3,2},{4,5},{5,4},{6,7},{7,6},{8,9},{9,8},{10,11... | collective-permute-start | bytes 3342344 | tf_op jit(solution)/shard_map/ppermute | solution.py:534
  74.9 17.5 %collective-permute-start.10 = (bf16[4,64,2176]{2,1,0:T(8,128)(2,1)S(1)}, bf16[4,64,2176]{2,1,0:T(8,128)(2,1)}, u32[]{:S(2)}, u32[]{:S(2)}) collective-permute-start(bf16[4,64,2176]{2,1,0:T(8,128)(2,1)S(1)} %all-to-all-done.refs_0_.refs_10_.refs_20_), channel_id=1, source_target_pairs={{0,1},{1,0},{2,3},{3,2},{4,5},{5,4},{6,7},{7,6},{8,9},{9,8},{10,11... | collective-permute-start | bytes 3342344 | tf_op jit(solution)/shard_map/ppermute | solution.py:534
  75.7 15.4 %collective-permute-start.8 = (bf16[2,64,2176]{2,1,0:T(8,128)(2,1)}, bf16[2,64,2176]{2,1,0:T(8,128)(2,1)}, u32[]{:S(2)}, u32[]{:S(2)}) collective-permute-start(bf16[2,64,2176]{2,1,0:T(8,128)(2,1)} %slice.96), channel_id=1, source_target_pairs={{0,4},{4,0},{1,5},{5,1},{2,6},{6,2},{3,7},{7,3},{8,12},{12,8},{9,1... | collective-permute-start | bytes 1671176 | tf_op jit(solution)/shard_map/ppermute | solution.py:534
  77.3 15.1 %collective-permute-start.9 = (bf16[2,64,2176]{2,1,0:T(8,128)(2,1)}, bf16[2,64,2176]{2,1,0:T(8,128)(2,1)}, u32[]{:S(2)}, u32[]{:S(2)}) collective-permute-start(bf16[2,64,2176]{2,1,0:T(8,128)(2,1)} %slice.97), channel_id=1, source_target_pairs={{0,2},{2,0},{1,3},{3,1},{4,6},{6,4},{5,7},{7,5},{8,10},{10,8},{9,1... | collective-permute-start | bytes 1671176 | tf_op jit(solution)/shard_map/ppermute | solution.py:534
  96.2 25.2 %collective-permute-start.15 = (bf16[4,64,2048]{2,1,0:T(8,128)(2,1)S(1)}, bf16[4,64,2048]{2,1,0:T(8,128)(2,1)}, u32[]{:S(2)}, u32[]{:S(2)}) collective-permute-start(bf16[4,64,2048]{2,1,0:T(8,128)(2,1)S(1)} %all-to-all-done.1.refs_0_.refs_10_), channel_id=1, source_target_pairs={{0,2},{2,0},{1,3},{3,1},{4,6},{6,4},{5,7},{7,5},{8,10},{10,8},{9,1... | collective-permute-start | bytes 3145736 | tf_op jit(solution)/shard_map/ppermute | solution.py:534
  96.8 25.0 %collective-permute-start.16 = (bf16[4,64,2048]{2,1,0:T(8,128)(2,1)S(1)}, bf16[4,64,2048]{2,1,0:T(8,128)(2,1)}, u32[]{:S(2)}, u32[]{:S(2)}) collective-permute-start(bf16[4,64,2048]{2,1,0:T(8,128)(2,1)S(1)} %all-to-all-done.1.refs_0_.refs_10_), channel_id=1, source_target_pairs={{0,4},{4,0},{1,5},{5,1},{2,6},{6,2},{3,7},{7,3},{8,12},{12,8},{9,1... | collective-permute-start | bytes 3145736 | tf_op jit(solution)/shard_map/ppermute | solution.py:534
  97.3 45.6 %all-to-all-start.2 = ((bf16[4,64,2048]{2,1,0:T(8,128)(2,1)}), bf16[4,64,2048]{2,1,0:T(8,128)(2,1)S(1)}, u32[]{:S(2)}, u32[]{:S(2)}) async-start(bf16[4,64,2048]{2,1,0:T(8,128)(2,1)} %get-tuple-element.226), calls=%async_computation.2 | async-start | bytes 2097152 | tf_op jit(solution)/shard_map/all_to_all | solution.py:565
  122.8 20.1 %collective-permute-start.20 = (bf16[4,64,2048]{2,1,0:T(8,128)(2,1)}, bf16[4,64,2048]{2,1,0:T(8,128)(2,1)}, u32[]{:S(2)}, u32[]{:S(2)}) collective-permute-start(bf16[4,64,2048]{2,1,0:T(8,128)(2,1)} %collective-permute-done.15.refs_1_.refs_11_), channel_id=1, source_target_pairs={{0,1},{1,0},{2,3},{3,2},{4,5},{5,4},{6,7},{7,6},{8,9},{9,8},{10,11... | collective-permute-start | bytes 3145736 | tf_op jit(solution)/shard_map/ppermute | solution.py:534
  124.8 18.2 %collective-permute-start.21 = (bf16[4,64,2048]{2,1,0:T(8,128)(2,1)}, bf16[4,64,2048]{2,1,0:T(8,128)(2,1)}, u32[]{:S(2)}, u32[]{:S(2)}) collective-permute-start(bf16[4,64,2048]{2,1,0:T(8,128)(2,1)} %collective-permute-done.16.refs_2_.refs_12_), channel_id=1, source_target_pairs={{0,1},{1,0},{2,3},{3,2},{4,5},{5,4},{6,7},{7,6},{8,9},{9,8},{10,11... | collective-permute-start | bytes 3145736 | tf_op jit(solution)/shard_map/ppermute | solution.py:534
  125.3 17.6 %collective-permute-start.17 = (bf16[2,64,2048]{2,1,0:T(8,128)(2,1)S(1)}, bf16[2,64,2048]{2,1,0:T(8,128)(2,1)}, u32[]{:S(2)}, u32[]{:S(2)}) collective-permute-start(bf16[2,64,2048]{2,1,0:T(8,128)(2,1)S(1)} %slice.108), channel_id=1, source_target_pairs={{0,4},{4,0},{1,5},{5,1},{2,6},{6,2},{3,7},{7,3},{8,12},{12,8},{9,1... | collective-permute-start | bytes 1572872 | tf_op jit(solution)/shard_map/ppermute | solution.py:534
  125.8 17.1 %collective-permute-start.18 = (bf16[2,64,2048]{2,1,0:T(8,128)(2,1)}, bf16[2,64,2048]{2,1,0:T(8,128)(2,1)}, u32[]{:S(2)}, u32[]{:S(2)}) collective-permute-start(bf16[2,64,2048]{2,1,0:T(8,128)(2,1)} %slice.109), channel_id=1, source_target_pairs={{0,2},{2,0},{1,3},{3,1},{4,6},{6,4},{5,7},{7,5},{8,10},{10,8},{9,1... | collective-permute-start | bytes 1572872 | tf_op jit(solution)/shard_map/ppermute | solution.py:534
  127.3 15.7 %collective-permute-start.19 = (bf16[4,64,2048]{2,1,0:T(8,128)(2,1)S(1)}, bf16[4,64,2048]{2,1,0:T(8,128)(2,1)}, u32[]{:S(2)}, u32[]{:S(2)}) collective-permute-start(bf16[4,64,2048]{2,1,0:T(8,128)(2,1)S(1)} %all-to-all-done.1.refs_0_.refs_10_), channel_id=1, source_target_pairs={{0,1},{1,0},{2,3},{3,2},{4,5},{5,4},{6,7},{7,6},{8,9},{9,8},{10,11... | collective-permute-start | bytes 3145736 | tf_op jit(solution)/shard_map/ppermute | solution.py:534
  143.6 23.5 %collective-permute-start.26 = (bf16[640,1024]{1,0:T(8,128)(2,1)}, bf16[640,1024]{1,0:T(8,128)(2,1)S(1)}, u32[]{:S(2)}, u32[]{:S(2)}) collective-permute-start(bf16[640,1024]{1,0:T(8,128)(2,1)} %get-tuple-element.220.refs_0_), channel_id=1, source_target_pairs={{0,1},{1,0},{2,3},{3,2},{4,5},{5,4},{6,7},{7,6},{8,9},{9,8},{10,11... | collective-permute-start | bytes 3932168 | tf_op jit(solution)/shard_map/ppermute | solution.py:534
  144.0 25.1 %collective-permute-start.24 = (bf16[4,64,2048]{2,1,0:T(8,128)(2,1)S(1)}, bf16[4,64,2048]{2,1,0:T(8,128)(2,1)S(1)}, u32[]{:S(2)}, u32[]{:S(2)}) collective-permute-start(bf16[4,64,2048]{2,1,0:T(8,128)(2,1)S(1)} %all-to-all-done.2.refs_0_), channel_id=1, source_target_pairs={{0,2},{2,0},{1,3},{3,1},{4,6},{6,4},{5,7},{7,5},{8,10},{10,8},{9,1... | collective-permute-start | bytes 3145736 | tf_op jit(solution)/shard_map/ppermute | solution.py:534
  144.6 24.9 %collective-permute-start.25 = (bf16[4,64,2048]{2,1,0:T(8,128)(2,1)S(1)}, bf16[4,64,2048]{2,1,0:T(8,128)(2,1)S(1)}, u32[]{:S(2)}, u32[]{:S(2)}) collective-permute-start(bf16[4,64,2048]{2,1,0:T(8,128)(2,1)S(1)} %all-to-all-done.2.refs_0_), channel_id=1, source_target_pairs={{0,4},{4,0},{1,5},{5,1},{2,6},{6,2},{3,7},{7,3},{8,12},{12,8},{9,1... | collective-permute-start | bytes 3145736 | tf_op jit(solution)/shard_map/ppermute | solution.py:534
  171.2 13.6 %collective-permute-start.27 = (bf16[640,4096]{1,0:T(8,128)(2,1)}, bf16[640,4096]{1,0:T(8,128)(2,1)}, u32[]{:S(2)}, u32[]{:S(2)}) collective-permute-start(bf16[640,4096]{1,0:T(8,128)(2,1)} %get-tuple-element.332.a0_ref.a1_ref.refs_10_), channel_id=1, source_target_pairs={{0,1},{1,0},{2,3},{3,2},{4,5},{5,4},{6,7},{7,6},{8,9},{9,8},{10,11... | collective-permute-start | bytes 15728648 | tf_op jit(solution)/shard_map/ppermute | solution.py:534
  173.2 25.3 %collective-permute-start.31 = (bf16[4,64,2048]{2,1,0:T(8,128)(2,1)S(1)}, bf16[4,64,2048]{2,1,0:T(8,128)(2,1)S(1)}, u32[]{:S(2)}, u32[]{:S(2)}) collective-permute-start(bf16[4,64,2048]{2,1,0:T(8,128)(2,1)S(1)} %all-to-all-done.2.refs_0_), channel_id=1, source_target_pairs={{0,1},{1,0},{2,3},{3,2},{4,5},{5,4},{6,7},{7,6},{8,9},{9,8},{10,11... | collective-permute-start | bytes 3145736 | tf_op jit(solution)/shard_map/ppermute | solution.py:534
  173.7 24.8 %collective-permute-start.32 = (bf16[4,64,2048]{2,1,0:T(8,128)(2,1)S(1)}, bf16[4,64,2048]{2,1,0:T(8,128)(2,1)S(1)}, u32[]{:S(2)}, u32[]{:S(2)}) collective-permute-start(bf16[4,64,2048]{2,1,0:T(8,128)(2,1)S(1)} %copy-done.19), channel_id=1, source_target_pairs={{0,1},{1,0},{2,3},{3,2},{4,5},{5,4},{6,7},{7,6},{8,9},{9,8},{10,11... | collective-permute-start | bytes 3145736 | tf_op jit(solution)/shard_map/ppermute | solution.py:534
  174.4 24.1 %collective-permute-start.33 = (bf16[4,64,2048]{2,1,0:T(8,128)(2,1)S(1)}, bf16[4,64,2048]{2,1,0:T(8,128)(2,1)}, u32[]{:S(2)}, u32[]{:S(2)}) collective-permute-start(bf16[4,64,2048]{2,1,0:T(8,128)(2,1)S(1)} %copy-done.21), channel_id=1, source_target_pairs={{0,1},{1,0},{2,3},{3,2},{4,5},{5,4},{6,7},{7,6},{8,9},{9,8},{10,11... | collective-permute-start | bytes 3145736 | tf_op jit(solution)/shard_map/ppermute | solution.py:534
  183.2 14.0 %collective-permute-start.29 = (bf16[2,64,2048]{2,1,0:T(8,128)(2,1)S(1)}, bf16[2,64,2048]{2,1,0:T(8,128)(2,1)S(1)}, u32[]{:S(2)}, u32[]{:S(2)}) collective-permute-start(bf16[2,64,2048]{2,1,0:T(8,128)(2,1)S(1)} %slice.110), channel_id=1, source_target_pairs={{0,4},{4,0},{1,5},{5,1},{2,6},{6,2},{3,7},{7,3},{8,12},{12,8},{9,1... | collective-permute-start | bytes 1572872 | tf_op jit(solution)/shard_map/ppermute | solution.py:534
  184.7 13.8 %collective-permute-start.30 = (bf16[2,64,2048]{2,1,0:T(8,128)(2,1)S(1)}, bf16[2,64,2048]{2,1,0:T(8,128)(2,1)}, u32[]{:S(2)}, u32[]{:S(2)}) collective-permute-start(bf16[2,64,2048]{2,1,0:T(8,128)(2,1)S(1)} %slice.111), channel_id=1, source_target_pairs={{0,2},{2,0},{1,3},{3,1},{4,6},{6,4},{5,7},{7,5},{8,10},{10,8},{9,1... | collective-permute-start | bytes 1572872 | tf_op jit(solution)/shard_map/ppermute | solution.py:534
  199.1 31.9 %collective-permute-start.37 = (bf16[640,1024]{1,0:T(8,128)(2,1)S(1)}, bf16[640,1024]{1,0:T(8,128)(2,1)S(1)}, u32[]{:S(2)}, u32[]{:S(2)}) collective-permute-start(bf16[640,1024]{1,0:T(8,128)(2,1)S(1)} %bitcast.159), channel_id=1, source_target_pairs={{0,1},{1,0},{2,3},{3,2},{4,5},{5,4},{6,7},{7,6},{8,9},{9,8},{10,11... | collective-permute-start | bytes 3932168 | tf_op jit(solution)/shard_map/ppermute | solution.py:534
  199.6 31.5 %collective-permute-start.38 = (bf16[640,1024]{1,0:T(8,128)(2,1)}, bf16[640,1024]{1,0:T(8,128)(2,1)S(1)}, u32[]{:S(2)}, u32[]{:S(2)}) collective-permute-start(bf16[640,1024]{1,0:T(8,128)(2,1)} %get-tuple-element.266.refs_0_), channel_id=1, source_target_pairs={{0,1},{1,0},{2,3},{3,2},{4,5},{5,4},{6,7},{7,6},{8,9},{9,8},{10,11... | collective-permute-start | bytes 3932168 | tf_op jit(solution)/shard_map/ppermute | solution.py:534
  199.6 31.4 %collective-permute-start.36 = (bf16[4,128,1024]{2,1,0:T(8,128)(2,1)}, bf16[4,128,1024]{2,1,0:T(8,128)(2,1)S(1)}, u32[]{:S(2)}, u32[]{:S(2)}) collective-permute-start(bf16[4,128,1024]{2,1,0:T(8,128)(2,1)} %get-tuple-element.263), channel_id=1, source_target_pairs={{0,4},{4,0},{1,5},{5,1},{2,6},{6,2},{3,7},{7,3},{8,12},{12,8},{9,1... | collective-permute-start | bytes 3145736 | tf_op jit(solution)/shard_map/ppermute | solution.py:534
  231.1 12.6 %collective-permute-start.39 = (bf16[640,4096]{1,0:T(8,128)(2,1)}, bf16[640,4096]{1,0:T(8,128)(2,1)}, u32[]{:S(2)}, u32[]{:S(2)}) collective-permute-start(bf16[640,4096]{1,0:T(8,128)(2,1)} %get-tuple-element.268.refs_2_), channel_id=1, source_target_pairs={{0,1},{1,0},{2,3},{3,2},{4,5},{5,4},{6,7},{7,6},{8,9},{9,8},{10,11... | collective-permute-start | bytes 15728648 | tf_op jit(solution)/shard_map/ppermute | solution.py:534
  231.3 12.4 %collective-permute-start.40 = (bf16[640,1024]{1,0:T(8,128)(2,1)}, bf16[640,1024]{1,0:T(8,128)(2,1)}, u32[]{:S(2)}, u32[]{:S(2)}) collective-permute-start(bf16[640,1024]{1,0:T(8,128)(2,1)} %get-tuple-element.269.refs_6_), channel_id=1, source_target_pairs={{0,1},{1,0},{2,3},{3,2},{4,5},{5,4},{6,7},{7,6},{8,9},{9,8},{10,11... | collective-permute-start | bytes 3932168 | tf_op jit(solution)/shard_map/ppermute | solution.py:534
  231.6 36.1 %collective-permute-start.44 = (bf16[4,128,1024]{2,1,0:T(8,128)(2,1)}, bf16[4,128,1024]{2,1,0:T(8,128)(2,1)}, u32[]{:S(2)}, u32[]{:S(2)}) collective-permute-start(bf16[4,128,1024]{2,1,0:T(8,128)(2,1)} %get-tuple-element.292), channel_id=1, source_target_pairs={{0,4},{4,0},{1,5},{5,1},{2,6},{6,2},{3,7},{7,3},{8,12},{12,8},{9,1... | collective-permute-start | bytes 3145736 | tf_op jit(solution)/shard_map/ppermute | solution.py:534
  243.7 38.0 %collective-permute-start.41 = (bf16[640,1536]{1,0:T(8,128)(2,1)}, bf16[640,1536]{1,0:T(8,128)(2,1)}, u32[]{:S(2)}, u32[]{:S(2)}) collective-permute-start(bf16[640,1536]{1,0:T(8,128)(2,1)} %bitcast.151), channel_id=1, source_target_pairs={{0,1},{1,0},{2,3},{3,2},{4,5},{5,4},{6,7},{7,6},{8,9},{9,8},{10,11... | collective-permute-start | bytes 5898248 | tf_op jit(solution)/shard_map/ppermute | solution.py:534
  244.4 25.5 %collective-permute-start.43 = (bf16[4,128,1024]{2,1,0:T(8,128)(2,1)S(1)}, bf16[4,128,1024]{2,1,0:T(8,128)(2,1)S(1)}, u32[]{:S(2)}, u32[]{:S(2)}) collective-permute-start(bf16[4,128,1024]{2,1,0:T(8,128)(2,1)S(1)} %add_convert_fusion.1), channel_id=1, source_target_pairs={{0,2},{2,0},{1,3},{3,1},{4,6},{6,4},{5,7},{7,5},{8,10},{10,8},{9,1... | collective-permute-start | bytes 3145736 | tf_op jit(solution)/shard_map/ppermute | solution.py:534
  253.2 16.6 %collective-permute-start.42 = (bf16[4,64,1024]{2,1,0:T(8,128)(2,1)}, bf16[4,64,1024]{2,1,0:T(8,128)(2,1)}, u32[]{:S(2)}, u32[]{:S(2)}) collective-permute-start(bf16[4,64,1024]{2,1,0:T(8,128)(2,1)} %get-tuple-element.289), channel_id=1, source_target_pairs={{0,4},{4,0},{1,5},{5,1},{2,6},{6,2},{3,7},{7,3},{8,12},{12,8},{9,1... | collective-permute-start | bytes 1572872 | tf_op jit(solution)/shard_map/ppermute | solution.py:534
  254.2 46.1 %collective-permute-start.47 = (bf16[4,64,1024]{2,1,0:T(8,128)(2,1)}, bf16[4,64,1024]{2,1,0:T(8,128)(2,1)}, u32[]{:S(2)}, u32[]{:S(2)}) collective-permute-start(bf16[4,64,1024]{2,1,0:T(8,128)(2,1)} %get-tuple-element.299), channel_id=1, source_target_pairs={{0,4},{4,0},{1,5},{5,1},{2,6},{6,2},{3,7},{7,3},{8,12},{12,8},{9,1... | collective-permute-start | bytes 1572872 | tf_op jit(solution)/shard_map/ppermute | solution.py:534
  272.6 30.7 %all-to-all-start.3 = ((bf16[4,128,1024]{2,1,0:T(8,128)(2,1)}), bf16[4,128,1024]{2,1,0:T(8,128)(2,1)}, u32[]{:S(2)}, u32[]{:S(2)}) async-start(bf16[4,128,1024]{2,1,0:T(8,128)(2,1)} %add_convert_fusion), calls=%async_computation.3 | async-start | bytes 2097152 | tf_op jit(solution)/shard_map/all_to_all | solution.py:565
  279.8 20.5 %collective-permute-start.46 = (bf16[4,64,1024]{2,1,0:T(8,128)(2,1)}, bf16[4,64,1024]{2,1,0:T(8,128)(2,1)}, u32[]{:S(2)}, u32[]{:S(2)}) collective-permute-start(bf16[4,64,1024]{2,1,0:T(8,128)(2,1)} %add_convert_fusion.6), channel_id=1, source_target_pairs={{0,2},{2,0},{1,3},{3,1},{4,6},{6,4},{5,7},{7,5},{8,10},{10,8},{9,1... | collective-permute-start | bytes 1572872 | tf_op jit(solution)/shard_map/ppermute | solution.py:534
  280.6 19.8 %collective-permute-start.48 = (bf16[4,64,1536]{2,1,0:T(8,128)(2,1)}, bf16[4,64,1536]{2,1,0:T(8,128)(2,1)}, u32[]{:S(2)}, u32[]{:S(2)}) collective-permute-start(bf16[4,64,1536]{2,1,0:T(8,128)(2,1)} %get-tuple-element.300), channel_id=1, source_target_pairs={{0,4},{4,0},{1,5},{5,1},{2,6},{6,2},{3,7},{7,3},{8,12},{12,8},{9,1... | collective-permute-start | bytes 2359304 | tf_op jit(solution)/shard_map/ppermute | solution.py:534
  288.0 15.4 %collective-permute-start.45 = (bf16[4,64,768]{2,1,0:T(8,128)(2,1)}, bf16[4,64,768]{2,1,0:T(8,128)(2,1)}, u32[]{:S(2)}, u32[]{:S(2)}) collective-permute-start(bf16[4,64,768]{2,1,0:T(8,128)(2,1)} %get-tuple-element.296), channel_id=1, source_target_pairs={{0,2},{2,0},{1,3},{3,1},{4,6},{6,4},{5,7},{7,5},{8,10},{10,8},{9,1... | collective-permute-start | bytes 1179656 | tf_op jit(solution)/shard_map/ppermute | solution.py:534
  303.4 17.9 %collective-permute-start.49 = (bf16[640,1536]{1,0:T(8,128)(2,1)}, bf16[640,1536]{1,0:T(8,128)(2,1)}, u32[]{:S(2)}, u32[]{:S(2)}) collective-permute-start(bf16[640,1536]{1,0:T(8,128)(2,1)} %bitcast.154), channel_id=1, source_target_pairs={{0,1},{1,0},{2,3},{3,2},{4,5},{5,4},{6,7},{7,6},{8,9},{9,8},{10,11... | collective-permute-start | bytes 5898248 | tf_op jit(solution)/shard_map/ppermute | solution.py:534
  304.4 41.0 %collective-permute-start.54 = (bf16[4,64,1536]{2,1,0:T(8,128)(2,1)}, bf16[4,64,1536]{2,1,0:T(8,128)(2,1)}, u32[]{:S(2)}, u32[]{:S(2)}) collective-permute-start(bf16[4,64,1536]{2,1,0:T(8,128)(2,1)} %get-tuple-element.320), channel_id=1, source_target_pairs={{0,4},{4,0},{1,5},{5,1},{2,6},{6,2},{3,7},{7,3},{8,12},{12,8},{9,1... | collective-permute-start | bytes 2359304 | tf_op jit(solution)/shard_map/ppermute | solution.py:534
  305.7 40.5 %collective-permute-start.51 = (bf16[4,64,768]{2,1,0:T(8,128)(2,1)S(1)}, bf16[4,64,768]{2,1,0:T(8,128)(2,1)}, u32[]{:S(2)}, u32[]{:S(2)}) collective-permute-start(bf16[4,64,768]{2,1,0:T(8,128)(2,1)S(1)} %get-tuple-element.315), channel_id=1, source_target_pairs={{0,2},{2,0},{1,3},{3,1},{4,6},{6,4},{5,7},{7,5},{8,10},{10,8},{9,1... | collective-permute-start | bytes 1179656 | tf_op jit(solution)/shard_map/ppermute | solution.py:534
  308.8 38.2 %all-to-all-start.4 = ((bf16[4,64,1024]{2,1,0:T(8,128)(2,1)}), bf16[4,64,1024]{2,1,0:T(8,128)(2,1)}, u32[]{:S(2)}, u32[]{:S(2)}) async-start(bf16[4,64,1024]{2,1,0:T(8,128)(2,1)} %add_convert_fusion.5), calls=%async_computation.4 | async-start | bytes 1048576 | tf_op jit(solution)/shard_map/all_to_all | solution.py:565
  315.3 31.6 %collective-permute-start.53 = (bf16[4,64,1536]{2,1,0:T(8,128)(2,1)}, bf16[4,64,1536]{2,1,0:T(8,128)(2,1)}, u32[]{:S(2)}, u32[]{:S(2)}) collective-permute-start(bf16[4,64,1536]{2,1,0:T(8,128)(2,1)} %add_convert_fusion.4), channel_id=1, source_target_pairs={{0,2},{2,0},{1,3},{3,1},{4,6},{6,4},{5,7},{7,5},{8,10},{10,8},{9,1... | collective-permute-start | bytes 2359304 | tf_op jit(solution)/shard_map/ppermute | solution.py:534
  318.4 28.5 %collective-permute-start.52 = (bf16[4,64,768]{2,1,0:T(8,128)(2,1)}, bf16[4,64,768]{2,1,0:T(8,128)(2,1)}, u32[]{:S(2)}, u32[]{:S(2)}) collective-permute-start(bf16[4,64,768]{2,1,0:T(8,128)(2,1)} %add_convert_fusion.8), channel_id=1, source_target_pairs={{0,4},{4,0},{1,5},{5,1},{2,6},{6,2},{3,7},{7,3},{8,12},{12,8},{9,1... | collective-permute-start | bytes 1179656 | tf_op jit(solution)/shard_map/ppermute | solution.py:534
  326.8 20.1 %collective-permute-start.50 = (bf16[4,64,768]{2,1,0:T(8,128)(2,1)S(1)}, bf16[4,64,768]{2,1,0:T(8,128)(2,1)}, u32[]{:S(2)}, u32[]{:S(2)}) collective-permute-start(bf16[4,64,768]{2,1,0:T(8,128)(2,1)S(1)} %get-tuple-element.314), channel_id=1, source_target_pairs={{0,4},{4,0},{1,5},{5,1},{2,6},{6,2},{3,7},{7,3},{8,12},{12,8},{9,1... | collective-permute-start | bytes 1179656 | tf_op jit(solution)/shard_map/ppermute | solution.py:534
  345.4 15.5 %collective-permute-start.61 = (bf16[128,1024]{1,0:T(8,128)(2,1)}, bf16[128,1024]{1,0:T(8,128)(2,1)}, u32[]{:S(2)}, u32[]{:S(2)}) collective-permute-start(bf16[128,1024]{1,0:T(8,128)(2,1)} %reduce_sum.59.refs_8_), channel_id=1, source_target_pairs={{0,2},{2,0},{1,3},{3,1},{4,6},{6,4},{5,7},{7,5},{8,10},{10,8},{9,1... | collective-permute-start | bytes 786440 | tf_op jit(solution)/shard_map/ppermute | solution.py:534
  346.2 16.1 %collective-permute-start.56 = (bf16[4,64,768]{2,1,0:T(8,128)(2,1)S(1)}, bf16[4,64,768]{2,1,0:T(8,128)(2,1)}, u32[]{:S(2)}, u32[]{:S(2)}) collective-permute-start(bf16[4,64,768]{2,1,0:T(8,128)(2,1)S(1)} %get-tuple-element.328), channel_id=1, source_target_pairs={{0,4},{4,0},{1,5},{5,1},{2,6},{6,2},{3,7},{7,3},{8,12},{12,8},{9,1... | collective-permute-start | bytes 1179656 | tf_op jit(solution)/shard_map/ppermute | solution.py:534
  349.5 36.0 %all-to-all-start.5 = ((bf16[4,64,1536]{2,1,0:T(8,128)(2,1)}), bf16[4,64,1536]{2,1,0:T(8,128)(2,1)S(1)}, u32[]{:S(2)}, u32[]{:S(2)}) async-start(bf16[4,64,1536]{2,1,0:T(8,128)(2,1)} %add_convert_fusion.3), calls=%async_computation.5 | async-start | bytes 1572864 | tf_op jit(solution)/shard_map/all_to_all | solution.py:565
  356.8 28.6 %collective-permute-start.57 = (bf16[2,80,1024]{2,1,0:T(8,128)(2,1)}, bf16[2,80,1024]{2,1,0:T(8,128)(2,1)}, u32[]{:S(2)}, u32[]{:S(2)}) collective-permute-start(bf16[2,80,1024]{2,1,0:T(8,128)(2,1)} %get-tuple-element.399), channel_id=1, source_target_pairs={{0,1},{1,0},{2,3},{3,2},{4,5},{5,4},{6,7},{7,6},{8,9},{9,8},{10,11... | collective-permute-start | bytes 983048 | tf_op jit(solution)/shard_map/ppermute | solution.py:538
  356.8 28.6 %collective-permute-start.58 = (bf16[2,80,1024]{2,1,0:T(8,128)(2,1)}, bf16[2,80,1024]{2,1,0:T(8,128)(2,1)}, u32[]{:S(2)}, u32[]{:S(2)}) collective-permute-start(bf16[2,80,1024]{2,1,0:T(8,128)(2,1)} %get-tuple-element.401), channel_id=1, source_target_pairs={{0,2},{1,3},{2,0},{3,1},{4,6},{5,7},{6,4},{7,5},{8,10},{9,11},{10,... | collective-permute-start | bytes 983048 | tf_op jit(solution)/shard_map/ppermute | solution.py:538
  358.1 27.3 %collective-permute-start.59 = (bf16[2,80,1024]{2,1,0:T(8,128)(2,1)}, bf16[2,80,1024]{2,1,0:T(8,128)(2,1)}, u32[]{:S(2)}, u32[]{:S(2)}) collective-permute-start(bf16[2,80,1024]{2,1,0:T(8,128)(2,1)} %get-tuple-element.398), channel_id=1, source_target_pairs={{0,3},{1,2},{2,1},{3,0},{4,7},{5,6},{6,5},{7,4},{8,11},{9,10},{10,... | collective-permute-start | bytes 983048 | tf_op jit(solution)/shard_map/ppermute | solution.py:538
  360.9 24.5 %collective-permute-start.55 = (bf16[4,64,768]{2,1,0:T(8,128)(2,1)S(1)}, bf16[4,64,768]{2,1,0:T(8,128)(2,1)S(1)}, u32[]{:S(2)}, u32[]{:S(2)}) collective-permute-start(bf16[4,64,768]{2,1,0:T(8,128)(2,1)S(1)} %add_convert_fusion.7), channel_id=1, source_target_pairs={{0,2},{2,0},{1,3},{3,1},{4,6},{6,4},{5,7},{7,5},{8,10},{10,8},{9,1... | collective-permute-start | bytes 1179656 | tf_op jit(solution)/shard_map/ppermute | solution.py:534
  362.3 23.1 %collective-permute-start.60 = (bf16[64,1024]{1,0:T(8,128)(2,1)S(1)}, bf16[64,1024]{1,0:T(8,128)(2,1)S(1)}, u32[]{:S(2)}, u32[]{:S(2)}) collective-permute-start(bf16[64,1024]{1,0:T(8,128)(2,1)S(1)} %reduce_sum.58.refs_0_), channel_id=1, source_target_pairs={{0,2},{2,0},{1,3},{3,1},{4,6},{6,4},{5,7},{7,5},{8,10},{10,8},{9,1... | collective-permute-start | bytes 393224 | tf_op jit(solution)/shard_map/ppermute | solution.py:534
  387.9 32.3 %all-to-all-start.6 = ((bf16[4,64,1536]{2,1,0:T(8,128)(2,1)}), bf16[4,64,1536]{2,1,0:T(8,128)(2,1)S(1)}, u32[]{:S(2)}, u32[]{:S(2)}) async-start(bf16[4,64,1536]{2,1,0:T(8,128)(2,1)} %add_convert_fusion.2), calls=%async_computation.6 | async-start | bytes 1572864 | tf_op jit(solution)/shard_map/all_to_all | solution.py:565
  405.4 14.8 %collective-permute-start.71 = (bf16[2,80,1024]{2,1,0:T(8,128)(2,1)S(1)}, bf16[2,80,1024]{2,1,0:T(8,128)(2,1)S(1)}, u32[]{:S(2)}, u32[]{:S(2)}) collective-permute-start(bf16[2,80,1024]{2,1,0:T(8,128)(2,1)S(1)} %get-tuple-element.394), channel_id=1, source_target_pairs={{0,3},{1,2},{2,1},{3,0},{4,7},{5,6},{6,5},{7,4},{8,11},{9,10},{10,... | collective-permute-start | bytes 983048 | tf_op jit(solution)/shard_map/ppermute | solution.py:538
  406.3 13.9 %collective-permute-start.66 = (bf16[64,1536]{1,0:T(8,128)(2,1)}, bf16[64,1536]{1,0:T(8,128)(2,1)}, u32[]{:S(2)}, u32[]{:S(2)}) collective-permute-start(bf16[64,1536]{1,0:T(8,128)(2,1)} %copy-done.36), channel_id=1, source_target_pairs={{0,1},{1,0},{2,3},{3,2},{4,5},{5,4},{6,7},{7,6},{8,9},{9,8},{10,11... | collective-permute-start | bytes 589832 | tf_op jit(solution)/shard_map/ppermute | solution.py:534
  421.0 14.0 %collective-permute-start.78 = (bf16[64,1536]{1,0:T(8,128)(2,1)}, bf16[64,1536]{1,0:T(8,128)(2,1)}, u32[]{:S(2)}, u32[]{:S(2)}) collective-permute-start(bf16[64,1536]{1,0:T(8,128)(2,1)} %reduce_sum.61.refs_0_), channel_id=1, source_target_pairs={{0,2},{2,0},{1,3},{3,1},{4,6},{6,4},{5,7},{7,5},{8,10},{10,8},{9,1... | collective-permute-start | bytes 589832 | tf_op jit(solution)/shard_map/ppermute | solution.py:534
  422.3 13.3 %collective-permute-start.79 = (bf16[64,1536]{1,0:T(8,128)(2,1)}, bf16[64,1536]{1,0:T(8,128)(2,1)}, u32[]{:S(2)}, u32[]{:S(2)}) collective-permute-start(bf16[64,1536]{1,0:T(8,128)(2,1)} %reduce_sum.61.refs_0_), channel_id=1, source_target_pairs={{0,1},{1,0},{2,3},{3,2},{4,5},{5,4},{6,7},{7,6},{8,9},{9,8},{10,11... | collective-permute-start | bytes 589832 | tf_op jit(solution)/shard_map/ppermute | solution.py:534
  (66 other events, 702.7 us)
where the time goes:
time: 446 us; the launch traced here: 440 us
  Pallas kernels  183 us (41%)
  waiting for transfers between devices  111 us (25%)
  starting transfers between devices  89.8 us (20%)
  other arithmetic  32.5 us (7%)
  local copies, waits for them, and re-layouts  22.8 us (5%)
    pallas_call x5, Pallas kernels, stepped(): pl.pallas_call(functools.partial(kernel, weights), grid_spec=pltpu.Prefet...  89.7 us
    ppermute x66, waiting for transfers between devices, swap(): return lax.ppermute(value, axis, [(0, 1), (1, 0)])  68.8 us
    pallas_call x5, Pallas kernels, grad_parts(): pl.pallas_call(kernel, grid_spec=pltpu.PrefetchScalarGridSpec(num_scalar_...  43.7 us
    ppermute x66, starting transfers between devices, swap(): return lax.ppermute(value, axis, [(0, 1), (1, 0)])  40.4 us
    ppermute x15, waiting for transfers between devices, send(): lax.ppermute(value, axis, [(i, i ^ step) for i in range(lax.axis_size(axi...  38.7 us
    pallas_call x3, Pallas kernels, attention(): pl.pallas_call(attend_back_kernel if back else attend_kernel, grid=(image...  37.8 us
    all_to_all x7, starting transfers between devices, exchange(): return lax.all_to_all(blocks, axis, split_axis=0, concat_axis=0, tiled=True)  36.6 us
    ppermute x15, starting transfers between devices, send(): lax.ppermute(value, axis, [(i, i ^ step) for i in range(lax.axis_size(axi...  12.8 us
  transfers between devices with their start and end apart: 88, of which 26 were waited for; matrix products, arithmetic and copies ran while one was open for 11% of the time, Pallas kernels for 40%

commit v1 on v0

--- a/solution.py
+++ b/solution.py
@@ -140,7 +140,7 @@
     )(key_bias, joint, joint, joint, *saved)
 
 
-STEP = 512
+STEP = 1024
 
 
 def stats(values):
@@ -165,13 +165,13 @@
     return block_spec(array.shape)
 
 
-def columns_spec(rows, index=lambda j: j):
-    return block_spec((rows, STEP), index)
+def columns_spec(rows, index=lambda j: j, step=STEP):
+    return block_spec((rows, step), index)
 
 
 class Weight:
-    def __init__(self, arrays, by_rows=False, base=0, blocks=None):
-        self.arrays, self.by_rows, self.base, self.blocks = tuple(arrays), by_rows, base, blocks
+    def __init__(self, arrays, by_rows=False, base=0, blocks=None, step=STEP):
+        self.arrays, self.by_rows, self.base, self.blocks, self.step = tuple(arrays), by_rows, base, blocks, step
 
     def specs(self):
         return [pl.BlockSpec(memory_space=pl.ANY)] * len(self.arrays)
@@ -179,7 +179,7 @@
     def copies(self, refs, place_ref, j, block, buf, sem):
         copy = lambda source, target: pltpu.make_async_copy(source, target, sem)
         if len(refs) == 1:
-            at = pl.ds(pl.multiple_of(block * STEP, STEP), STEP)
+            at = pl.ds(pl.multiple_of(block * self.step, self.step), self.step)
             return [(None, [copy(refs[0].at[at] if self.by_rows else refs[0].at[:, at], buf)])]
         y, x, c = place_ref[0], place_ref[1], place_ref[2]
         depth, rows = refs[0].shape[0], refs[0].shape[1]
@@ -193,7 +193,7 @@
         found = []
         if not self.by_rows:
             half = self.blocks // 2
-            lanes = pl.ds(pl.multiple_of(self.base + block % half * STEP, LANES), STEP)
+            lanes = pl.ds(pl.multiple_of(self.base + block % half * self.step, LANES), self.step)
             for owner in range(2):
                 some = []
                 for i in range(4):
@@ -206,15 +206,14 @@
         width = buf.shape[1]
         segments = refs[0].shape[2] // width
         for z in range(depth):
-            for far in range(2):
-                some = []
-                for owner in range(2):
-                    for i in range(2):
-                        for k in range(segments):
-                            row = ((c ^ owner) * 2 + (x ^ i)) * segments * rows + k * rows
-                            source = piece(owner, 2 * far + i, z).at[:, pl.ds(k * width, width)]
-                            some.append(copy(source, buf.at[pl.ds(pl.multiple_of(row, rows), rows)]))
-                found.append((j == 2 * z + far, some))
+            some = []
+            for owner in range(2):
+                for i in range(4):
+                    for k in range(segments):
+                        row = (((y ^ (i // 2)) * 2 + (c ^ owner)) * 2 + (x ^ (i % 2))) * segments * rows + k * rows
+                        source = piece(owner, i, z).at[:, pl.ds(k * width, width)]
+                        some.append(copy(source, buf.at[pl.ds(pl.multiple_of(row, rows), rows)]))
+            found.append((j == z, some))
         return found
 
     def start(self, *where):
@@ -228,16 +227,12 @@
             go() if condition is None else pl.when(condition)(go)
 
 
-def shard_block(j, place):
-    return j // 2 * 2 + (place[0] ^ (j % 2))
-
-
-def stream(weight, refs, place_ref, block, buf, sems):
+def stream(weight, refs, place_ref, buf, sems):
     j = pl.program_id(0)
 
     def where(step):
         slot = step % 2
-        return refs, place_ref, step, block(step), buf.at[slot], sems.at[slot]
+        return refs, place_ref, step, step, buf.at[slot], sems.at[slot]
 
     @pl.when(j == 0)
     def _():
@@ -283,34 +278,33 @@
 
 def project_kernel(weights, place_ref, *refs):
     (weight_refs,), refs = split_refs(refs, weights)
-    tokens_ref, gain_ref, shift_ref, bias_ref, normed_ref, joint_ref, buf, sems = refs
-    j = pl.program_id(0)
-
-    @pl.when(j == 0)
+    tokens_ref, gain_ref, shift_ref, query_ref, value_ref, normed_ref, joint_ref, buf, sems = refs
+
+    @pl.when(pl.program_id(0) == 0)
     def _():
         normal, _ = stats(tokens_ref[...].astype(F32))
         normed_ref[...] = (normal * gain_ref[...] + shift_ref[...]).astype(BF16)
 
-    weight = stream(weights[0], weight_refs, place_ref, lambda step: step, buf, sems)
-    bias = jnp.where(j % 3 == 1, 0.0, bias_ref[...])
+    weight = stream(weights[0], weight_refs, place_ref, buf, sems)
+    bias = jnp.concatenate([query_ref[...], jnp.zeros_like(query_ref[...]), value_ref[...]], axis=1)
     joint_ref[...] = (contract(normed_ref[...], weight, 1, 0) + bias).astype(BF16)
 
 
 def project(place, tokens, gain, shift, weight, bias_qv):
     rows, width = tokens.shape
-    assert width // GROUPS == STEP
+    part = width // GROUPS
     return stepped(
         project_kernel,
-        3 * width // STEP,
+        GROUPS,
         place,
         [weight],
         [whole_spec(tokens), whole_spec(gain), whole_spec(shift)]
-        + [columns_spec(1, lambda j: j // 3 + jnp.where(j % 3 == 2, GROUPS, 0))],
-        (tokens, gain, shift, bias_qv),
-        [whole_spec(tokens), columns_spec(rows)],
+        + [columns_spec(1, index, part) for index in (lambda j: j, lambda j: GROUPS + j)],
+        (tokens, gain, shift, bias_qv, bias_qv),
+        [whole_spec(tokens), columns_spec(rows, step=3 * part)],
         [jax.ShapeDtypeStruct((rows, width), BF16), jax.ShapeDtypeStruct((rows, 3 * width), BF16)],
-        streamed(width, STEP),
-        11,
+        streamed(width, 3 * part),
+        10,
     )
 
 
@@ -338,7 +332,7 @@
         normal, _ = stats(middle)
         normed_ref[...] = (normal * gain_ref[...] + shift_ref[...]).astype(BF16)
 
-    weight = stream(weights[0], up_refs, place_ref, lambda step: step, buf, sems)
+    weight = stream(weights[0], up_refs, place_ref, buf, sems)
     pre = contract(normed_ref[...], weight, 1, 0) + bias_ref[...]
     cumul = 0.5 * (1.0 + lax.erf(pre * 0.7071067811865476))
     hidden_ref[...] = (pre * cumul).astype(BF16)
@@ -359,7 +353,7 @@
         [whole_spec(tokens)] * 2 + [columns_spec(rows)] * 2,
         [jax.ShapeDtypeStruct((rows, width), F32), jax.ShapeDtypeStruct((rows, width), BF16)]
         + [jax.ShapeDtypeStruct((rows, hidden), BF16)] * 2,
-        streamed(width, STEP) + [pltpu.VMEM((width // STEP, width, STEP), BF16), pltpu.SemaphoreType.DMA],
+        streamed(width, STEP) + [pltpu.VMEM((width // out_weight.step, width, out_weight.step), BF16), pltpu.SemaphoreType.DMA],
         20,
     )
 
@@ -379,8 +373,7 @@
 def finish_kernel(weights, place_ref, *refs):
     (down_refs,), refs = split_refs(refs, weights)
     hidden_ref, middle_ref, bias_ref, valid_ref, result_ref, total_ref, buf, sems = refs
-    block = lambda step: shard_block(step, place_ref)
-    weight = stream(weights[0], down_refs, place_ref, block, buf, sems)
+    weight = stream(weights[0], down_refs, place_ref, buf, sems)
     part = contract(hidden_ref[...], weight, 1, 0)
     accumulate(total_ref, part, lambda: middle_ref[...] + bias_ref[...])
 
@@ -396,7 +389,7 @@
         hidden.shape[1] // STEP,
         place,
         [down],
-        [columns_spec(rows, shard_block)] + [whole_spec(v) for v in (middle, bias_down, valid)],
+        [columns_spec(rows)] + [whole_spec(v) for v in (middle, bias_down, valid)],
         (hidden, middle, bias_down, valid),
         whole_spec(middle),
         jax.ShapeDtypeStruct((rows, width), BF16),
@@ -418,9 +411,8 @@
         for weight, where in blocks():
             weight.start(*where)
 
-    block = lambda step: shard_block(step, place_ref)
-    down = stream(weights[0], down_refs, place_ref, block, down_buf, down_sems)
-    up = stream(weights[1], up_refs, place_ref, block, up_buf, up_sems)
+    down = stream(weights[0], down_refs, place_ref, down_buf, down_sems)
+    up = stream(weights[1], up_refs, place_ref, up_buf, up_sems)
     pre = (contract(grad_ref[...], down, 1, 1) * slope_ref[...].astype(F32)).astype(BF16)
     pre_ref[...] = pre
     bias_up_ref[...] = column_sums(pre.astype(F32))
@@ -437,7 +429,8 @@
         branch = grad_middle.astype(BF16)
         branch_ref[...] = branch
         context_ref[...] = sum(
-            contract(branch[:, b * STEP : (b + 1) * STEP], out_buf[b], 1, 1) for b in range(out_buf.shape[0])
+            contract(branch[:, b * out_buf.shape[2] : (b + 1) * out_buf.shape[2]], out_buf[b], 1, 1)
+            for b in range(out_buf.shape[0])
         ).astype(BF16)
         sums_ref[0:1] = column_sums(total * normal)
         sums_ref[1:2] = column_sums(total)
@@ -452,9 +445,9 @@
         hidden // STEP,
         place,
         [down, up, out_weight],
-        [whole_spec(grad_out), columns_spec(rows, shard_block), whole_spec(middle), whole_spec(gain)],
+        [whole_spec(grad_out), columns_spec(rows), whole_spec(middle), whole_spec(gain)],
         (grad_out, slope, middle, gain),
-        [columns_spec(rows, shard_block), columns_spec(1, shard_block)]
+        [columns_spec(rows), columns_spec(1)]
         + [whole_spec(middle)] * 3
         + [block_spec((8, width))],
         [
@@ -468,7 +461,7 @@
         [pltpu.VMEM((rows, width), F32)]
         + streamed(STEP, width)
         + streamed(width, STEP)
-        + [pltpu.VMEM((width // STEP, width, STEP), BF16), pltpu.SemaphoreType.DMA],
+        + [pltpu.VMEM((width // out_weight.step, width, out_weight.step), BF16), pltpu.SemaphoreType.DMA],
         23,
     )
 
@@ -478,10 +471,10 @@
     joint_0_ref, joint_1_ref, tokens_ref, gain_ref, grad_middle_ref, *refs = refs
     input_ref, bias_ref, sums_ref, total_ref, buf, sems = refs
     j = pl.program_id(0)
-    first = jnp.broadcast_to(j < 3, joint_0_ref.shape)
+    first = jnp.broadcast_to(j == 0, joint_0_ref.shape)
     joint = jnp.where(first, joint_0_ref[...], joint_1_ref[...])
     bias_ref[...] = column_sums(joint.astype(F32))
-    weight = stream(weights[0], weight_refs, place_ref, lambda step: step, buf, sems)
+    weight = stream(weights[0], weight_refs, place_ref, buf, sems)
     accumulate(total_ref, contract(joint, weight, 1, 1))
 
     @pl.when(j == pl.num_programs(0) - 1)
@@ -496,22 +489,22 @@
 
 def back_input(place, joint_0, joint_1, weight, tokens, gain, grad_middle):
     rows, width = tokens.shape
+    group = 3 * width // GROUPS
     return stepped(
         input_kernel,
-        3 * width // STEP,
+        GROUPS,
         place,
         [weight],
-        [columns_spec(rows, lambda j: jnp.minimum(j, 2)), columns_spec(rows, lambda j: jnp.maximum(j - 3, 0))]
-        + [whole_spec(v) for v in (tokens, gain, grad_middle)],
+        [whole_spec(v) for v in (joint_0, joint_1, tokens, gain, grad_middle)],
         (joint_0, joint_1, tokens, gain, grad_middle),
-        [whole_spec(tokens), columns_spec(1), block_spec((8, width))],
+        [whole_spec(tokens), columns_spec(1, step=group), block_spec((8, width))],
         [
             jax.ShapeDtypeStruct((rows, width), BF16),
             jax.ShapeDtypeStruct((1, 3 * width), F32),
             jax.ShapeDtypeStruct((8, width), F32),
         ],
-        [pltpu.VMEM((rows, width), F32)] + streamed(width, STEP),
-        14,
+        [pltpu.VMEM((rows, width), F32)] + streamed(width, group),
+        13,
     )
 
 
@@ -828,10 +821,8 @@
     return jnp.stack(rows, axis=1).reshape(2 * own_y.shape[0], -1)
 
 
-def over_pairs(packed):
+def over_rows(packed):
     y = lax.axis_index("y")
-    packed = packed + swap(packed, "c")
-    packed = packed + swap(packed, "x")
     packed = packed.reshape(lax.axis_size("z"), 2, -1)
     row = lambda yy: lax.dynamic_index_in_dim(packed, yy, 1, keepdims=False)
     return row(y) + swap(row(1 - y), "y")
@@ -885,12 +876,12 @@
     key_bias = jnp.where(valid, 0.0, -1000000000.0)[:, :, None]
     valid = valid.reshape(rows, 1)
 
-    def by_image(value):
+    def by_image(value, which=range(members)):
         value = value.reshape(members, images, few, width)
-        return [send(pick(value, here ^ k), SEQ, k) if k else pick(value, here) for k in range(members)]
-
-    def by_slot(value):
-        value = value.reshape(images, members, few, width)
+        return [send(pick(value, here ^ k), SEQ, k) if k else pick(value, here) for k in which]
+
+    def by_slot(*values):
+        value = jnp.concatenate([v.reshape(images, members, few, width) for v in values])
         return [send(value[:, k], SEQ, k) if k else value[:, 0] for k in range(members)]
 
     def in_images(blocks):
@@ -898,7 +889,9 @@
 
     def in_slots(blocks):
         blocks = jnp.stack(blocks)
-        return jnp.concatenate([pick(blocks, here ^ k) for k in range(members)], axis=0)
+        kinds = blocks.shape[1] // images
+        blocks = jnp.concatenate([pick(blocks, here ^ k).reshape(kinds, images, few, width) for k in range(members)], axis=1)
+        return [blocks[i] for i in range(kinds)]
 
     def unpack(vectors):
         vectors = vectors.astype(F32)
@@ -910,10 +903,11 @@
         cut_group = Split(attn_weight.shape, columns=3 * width // GROUPS)
         place = my_place()
         first, second, third = pieces(attn_weight, out_weight, up_weight, down_weight, small)
-        tokens, cot, z1, second, third = tie(
-            by_image(tokens), by_image(cotangent), exchange(first, "z"), second, third
-        )
-        tokens, cot = in_images(tokens), in_images(cot)
+        cot = by_image(cotangent, range(members - 1))
+        tokens, cot, cotangent, z1, second, third = tie(
+            by_image(tokens), cot, cotangent, exchange(first, "z"), second, third
+        )
+        tokens = in_images(tokens)
         x1, y1 = swap(z1, "x"), swap(z1, "y")
         z2 = exchange(second, "z")
         x1, y1, z1, third = tie(x1, y1, z1, third)
@@ -922,21 +916,29 @@
         d1, c1, z2, vectors, third = tie(corner(x1, y1), core_swap(z1, x1, y1), z2, vectors, third)
         gain_a, shift_a, bias_qv, bias_out, gain_b, shift_b, bias_up, bias_down = vectors
         arrays = (z1, x1, y1, *d1, *c1, *core_swap(*d1))
-        qkv_full = Weight(arrays, blocks=3 * width // STEP)
-        out_full = Weight(arrays, base=cut_qkv.wide, blocks=width // STEP)
-        x2, y2, z3 = swap(z2, "x"), swap(z2, "y"), exchange(third, "z")
+        qkv_full = Weight(arrays, blocks=GROUPS, step=3 * width // GROUPS)
+        out_full = Weight(arrays, base=cut_qkv.wide, blocks=2, step=cut_out.wide)
+        x2, y2 = swap(z2, "x"), swap(z2, "y")
         normed_a, joint = project(place, tokens, gain_a, shift_a, qkv_full, bias_qv)
-        joint, x2, y2, z2, normed_a = tie(joint, x2, y2, z2, normed_a)
+        joint, third = tie(joint, third)
+        z3 = exchange(third, "z")
+        joint, x2, y2, z2, normed_a, cotangent = tie(joint, x2, y2, z2, normed_a, cotangent)
         joint = joint.reshape(images, slots, 3 * width)
         d2, c2 = corner(x2, y2), core_swap(z2, x2, y2)
         context, lse = attention(key_bias, joint)
-        context, d2, c2, z3 = tie(context.reshape(rows, width), d2, c2, z3)
+        context, d2, c2, z3, cot = tie(
+            context.reshape(rows, width), d2, c2, z3, cot + by_image(cotangent, [members - 1])
+        )
+        cot = in_images(cot)
         x3, y3 = swap(z3, "x"), swap(z3, "y")
         up_full = Weight((z2, x2, y2, *d2, *c2, *core_swap(*d2)), blocks=cut_up.columns // STEP)
         middle, normed_b, hidden, slope = expand(
             place, tokens, context, out_full, bias_out, gain_b, shift_b, up_full, bias_up
         )
-        hidden, slope, x3, y3, z3, normed_sib = tie(hidden, slope, x3, y3, z3, swap(normed_a, "c"))
+        grad_out = jnp.where(valid, cot, jnp.zeros_like(cot))
+        hidden, slope, x3, y3, z3, normed_sib, out_sib = tie(
+            hidden, slope, x3, y3, z3, swap(normed_a, "c"), swap(grad_out, "c")
+        )
     else:
         vectors = unpack(lax.all_gather(packed, FSDP, axis=0))
         gain_a, shift_a, bias_qv, bias_out, gain_b, shift_b, bias_up, bias_down = vectors
@@ -945,8 +947,10 @@
             Weight([lax.all_gather(w, FSDP, axis=0, tiled=True)], by_rows=w is down_weight)
             for w in (grouped(attn_weight), out_weight, up_weight, down_weight)
         )
+        qkv_full.step, out_full.step = 3 * width // GROUPS, width // 2
         tokens = in_images(by_image(tokens))
         cot = in_images(by_image(cotangent))
+        grad_out = jnp.where(valid, cot, jnp.zeros_like(cot))
         normed_a, joint = project(place, tokens, gain_a, shift_a, qkv_full, bias_qv)
         joint = joint.reshape(images, slots, 3 * width)
         context, lse = attention(key_bias, joint)
@@ -955,7 +959,6 @@
             place, tokens, context, out_full, bias_out, gain_b, shift_b, up_full, bias_up
         )
 
-    grad_out = jnp.where(valid, cot, jnp.zeros_like(cot))
     g_bias_down = jnp.sum(grad_out.astype(F32), axis=0, keepdims=True)
     valid_wide = valid.astype(F32)
 
@@ -968,7 +971,7 @@
     depth = lax.axis_size("z")
     if staged:
         d3, c3 = corner(x3, y3), core_swap(z3, x3, y3)
-        down_parts = grad_parts([(hidden, swap(hidden, "c"), grad_out, swap(grad_out, "c"), 0, 0)], cut_down, depth)
+        down_parts = grad_parts([(hidden, swap(hidden, "c"), grad_out, out_sib, 0, 0)], cut_down, depth)
         down_parts, slope, d3, c3, hidden = tie(down_parts, slope, d3, c3, hidden)
         down_full = Weight((z3, x3, y3, *d3, *c3, *core_swap(*d3)), by_rows=True)
         down_e = swap(down_parts[3], "y")
@@ -983,13 +986,13 @@
         down_x, down_y = swap(add(down_parts[1], down_e), "x"), swap(down_parts[2], "y")
         joint_0 = back_attention(grad_context, 0)
         joint_0, grad_context, pre_sib, branch_sib = tie(joint_0, grad_context, pre_sib, branch_sib)
-        half = cut_up.wide // STEP // 2
+        half = cut_up.wide // 512 // 2
         up_job = (normed_b, normed_sib_b, grad_pre, pre_sib)
         a_parts = grad_parts([up_job + (0, half)], cut_up, depth)
         joint_0_sib = swap(joint_0, "c")
         a_parts, grad_context = tie(a_parts, grad_context)
         a_e = swap(a_parts[3], "y")
-        out_job = (context, context_sib, grad_branch, branch_sib, 0, cut_out.wide // STEP)
+        out_job = (context, context_sib, grad_branch, branch_sib, 0, cut_out.wide // 512)
         b_parts = grad_parts([up_job + (half, half), out_job], cut_up, depth)
         b_parts, grad_context, a_e, down_x, down_y = tie(b_parts, grad_context, a_e, down_x, down_y)
         a_x, a_y = swap(add(a_parts[1], a_e), "x"), swap(a_parts[2], "y")
@@ -1008,7 +1011,10 @@
         parts_1, joint_1 = tie(parts_1, joint_1)
         e_1 = swap(parts_1[3], "y")
         input_grad, joint_sums, sums_a = back_input(place, joint_0, joint_1, qkv_full, tokens, gain_a, grad_middle)
-        input_grad, e_1, x_0, y_0, b_x, b_y, a_z, hidden = tie(input_grad, e_1, x_0, y_0, b_x, b_y, a_z, hidden)
+        packed = pack(shard_count, sums_a, joint_sums, sums_b, bias_up_sums, g_bias_down)
+        input_grad, e_1, x_0, y_0, b_x, b_y, a_z, hidden, down_b, packed = tie(
+            input_grad, e_1, x_0, y_0, b_x, b_y, a_z, hidden, down_b, packed
+        )
         x_1, y_1 = swap(add(parts_1[1], e_1), "x"), swap(parts_1[2], "y")
         b_z = grad_z(b_parts, b_x, b_y)
         result = finish(place, hidden, down_full, middle, bias_down, valid_wide)
@@ -1021,29 +1027,30 @@
         joint_0, joint_1 = (back_attention(grad_context, g) for g in range(GROUPS))
         input_grad, joint_sums, sums_a = back_input(place, joint_0, joint_1, qkv_full, tokens, gain_a, grad_middle)
         grad_joint = jnp.concatenate([joint_0, joint_1], axis=1)
-        layer_out = by_slot(finish(place, hidden, down_full, middle, bias_down, valid_wide))
-
-    if staged:
-        packed = pack(shard_count, sums_a, joint_sums, sums_b, bias_up_sums, g_bias_down)
-    else:
+        result = finish(place, hidden, down_full, middle, bias_down, valid_wide)
+
+    if not staged:
         group = 3 * width // GROUPS
         joint_sums = ungrouped([joint_sums[:, g * group : (g + 1) * group] for g in range(GROUPS)])
         g_bias_qv = jnp.concatenate([joint_sums[:, :width], joint_sums[:, 2 * width :]], axis=1)
         small_grads = (sums_a[0], sums_a[1], g_bias_qv, sums_b[2], sums_b[0], sums_b[1], bias_up_sums, g_bias_down)
         packed = jnp.concatenate([v.reshape(shard_count, -1) for v in small_grads], axis=1)
     if staged:
+        packed = packed + swap(packed, "c")
+        packed = packed + swap(packed, "x")
         x_1, y_1, b_z, result, input_grad, packed, a_g, down_g = tie(
-            x_1, y_1, b_z, result, by_slot(input_grad), packed, grad_x(a_z), grad_x(down_b)
+            x_1, y_1, b_z, result, input_grad, packed, grad_x(a_z), grad_x(down_b)
         )
         qkv_b = grad_z(
             tuple(jnp.concatenate([p, q], axis=2) for p, q in zip(parts_0[:1], parts_1[:1])),
             jnp.concatenate([x_0, x_1], axis=2),
             jnp.concatenate([y_0, y_1], axis=2),
         )
-        qkv_b, a_g, b_g, down_g, layer_out, packed = tie(
-            qkv_b, grad_core(*a_g), grad_core(*grad_x(b_z)), grad_core(*down_g), by_slot(result), over_pairs(packed)
-        )
-        packed = over_line(packed)
+        outs = by_slot(input_grad, result)
+        early, late = outs[:-1], outs[-1]
+        qkv_b, b_g, packed, a_g, down_g, early = tie(qkv_b, grad_x(b_z), over_rows(packed), a_g, down_g, early)
+        b_g, a_g, down_g = (grad_core(*v) for v in (b_g, a_g, down_g))
+        mine, from_x = grad_x(qkv_b)
         half, n_out, n_qkv = cut_up.wide // 2, cut_out.wide, cut_group.wide
         up_plan = [(0, 0, half, (0, 2 * half)), (1, 0, half, (half, 3 * half))]
         g_up, g_out, g_down = shards_of(
@@ -1054,6 +1061,10 @@
                 (True, down_weight.shape, [(2, 0, width, None)]),
             ],
         )
+        g_up, g_out, g_down, packed, late, from_x = tie(g_up, g_out, g_down, packed, late, from_x)
+        outs = early + [late]
+        qkv_g = grad_core(mine, from_x)
+        packed = over_line(packed)
         part = width // GROUPS
         qkv_plan = []
         for g in range(GROUPS):
@@ -1061,9 +1072,9 @@
                 places = [divmod(c * n_qkv + low, part) for c in range(2)]
                 places = [t * width + g * part + at for t, at in places]
                 qkv_plan.append((0, g * n_qkv + low, LANES, places))
-        (g_qkv,) = shards_of([grad_core(*grad_x(qkv_b))], [(False, attn_weight.shape, qkv_plan)])
+        (g_qkv,) = shards_of([qkv_g], [(False, attn_weight.shape, qkv_plan)])
     else:
-        input_grad = by_slot(input_grad)
+        outs = by_slot(input_grad, result)
         packed = lax.psum_scatter(packed, FSDP, scatter_dimension=0)
         packed = lax.psum(packed, SEQ)
         g_qkv, g_out, g_up, g_down = (
@@ -1071,7 +1082,7 @@
             for a, g in ((normed_a, grad_joint), (context, grad_branch), (normed_b, grad_pre), (hidden, grad_out))
         )
         g_qkv = ungrouped([g_qkv[:, : 3 * width // GROUPS], g_qkv[:, 3 * width // GROUPS :]])
-    layer_out, input_grad = in_slots(layer_out), in_slots(input_grad)
+    input_grad, layer_out = in_slots(outs)
     (g_gain_a, g_shift_a, g_bias_qv, g_bias_out, g_gain_b, g_shift_b, g_bias_up, g_bias_down) = (
         packed[c : c + n] for c, n in zip(cuts, sizes)
     )

time: 446 us -> 439 us (0.984)
  Pallas kernels: 183 us -> 176 us
  starting transfers between devices: 89.8 us -> 83.7 us
  waiting for transfers between devices: 111 us -> 116 us
    ppermute x66, waiting for transfers between devices: 68.8 us -> 79.7 us  [swap(): return lax.ppermute(value, axis, [(0, 1), (1, 0)])]
    ppermute x15 -> x12, waiting for transfers between devices: 38.7 us -> 30.3 us  [send(): lax.ppermute(value, axis, [(i, i ^ step) for i in range(lax.axis_size(axi...]
    pallas_call x5, Pallas kernels: 89.7 us -> 82.5 us  [stepped(): pl.pallas_call(functools.partial(kernel, weights), grid_spec=pltpu.Prefet...]
    ppermute x15 -> x12, starting transfers between devices: 12.8 us -> 9.5 us  [send(): lax.ppermute(value, axis, [(i, i ^ step) for i in range(lax.axis_size(axi...]
    unnamed x89 -> x93, local copies, waits for them, and re-layouts: 8.15 us -> 9.75 us
  transfers between devices with their start and end apart: 88 -> 85, of which waited for: 26 -> 29; matrix products, arithmetic and copies ran while one was open for 11% -> 10% of each run, Pallas kernels for 40% -> 39%
where the time goes in v1:
time: 439 us; the launch traced here: 433 us
  Pallas kernels  176 us (40%)
  waiting for transfers between devices  116 us (26%)
  starting transfers between devices  83.7 us (19%)
  other arithmetic  32.8 us (7%)
  local copies, waits for them, and re-layouts  22.9 us (5%)
    pallas_call x5, Pallas kernels, stepped(): pl.pallas_call(functools.partial(kernel, weights), grid_spec=pltpu.Prefet...  82.5 us
    ppermute x66, waiting for transfers between devices, swap(): return lax.ppermute(value, axis, [(0, 1), (1, 0)])  79.7 us
    pallas_call x5, Pallas kernels, grad_parts(): pl.pallas_call(kernel, grid_spec=pltpu.PrefetchScalarGridSpec(num_scalar_...  43.7 us
    ppermute x66, starting transfers between devices, swap(): return lax.ppermute(value, axis, [(0, 1), (1, 0)])  40.2 us
    pallas_call x3, Pallas kernels, attention(): pl.pallas_call(attend_back_kernel if back else attend_kernel, grid=(image...  38 us
    all_to_all x7, starting transfers between devices, exchange(): return lax.all_to_all(blocks, axis, split_axis=0, concat_axis=0, tiled=True)  34 us
    ppermute x12, waiting for transfers between devices, send(): lax.ppermute(value, axis, [(i, i ^ step) for i in range(lax.axis_size(axi...  30.3 us
    convert_element_type x4, other arithmetic, grad_z(): sum((v.astype(F32) for v in (parts[0], from_x, from_y))).astype(BF16)  10.4 us
  transfers between devices with their start and end apart: 85, of which 29 were waited for; matrix products, arithmetic and copies ran while one was open for 10% of the time, Pallas kernels for 39%

profile of v1, /device:TPU:0, one launch (start us, length us, event | category | flops | bytes accessed | tf_op | source)
XLA Modules:
  0.0 432.7 jit_solution(561402301661127796)
XLA Ops:
  1.2 3.7 shard_map.254
  4.9 6.4 %all-to-all-start = ((bf16[4,64,2176]{2,1,0:T(8,128)(2,1)}), bf16[4,64,2176]{2,1,0:T(8,128)(2,1)}, u32[]{:S(2)}, u32[]{:S(2)}) async-start(bf16[4,64,2176]{2,1,0:T(8,128)(2,1)} %get-tuple-element.201), calls=%async_computation | async-start | bytes 2228224 | tf_op jit(solution)/shard_map/all_to_all | solution.py:558
  11.6 1.6 collective-permute-start.1
  15.4 6.7 %collective-permute-done.1 = bf16[2,80,1024]{2,1,0:T(8,128)(2,1)S(1)} collective-permute-done((bf16[2,80,1024]{2,1,0:T(8,128)(2,1)S(1)}, bf16[2,80,1024]{2,1,0:T(8,128)(2,1)S(1)}, u32[]{:S(2)}, u32[]{:S(2)}) %collective-permute-start.1) | collective-permute-done | bytes 327712 | tf_op jit(solution)/shard_map/ppermute | solution.py:531
  22.1 6.1 %collective-permute-done.2 = bf16[2,80,1024]{2,1,0:T(8,128)(2,1)S(1)} collective-permute-done((bf16[2,80,1024]{2,1,0:T(8,128)(2,1)S(1)}, bf16[2,80,1024]{2,1,0:T(8,128)(2,1)S(1)}, u32[]{:S(2)}, u32[]{:S(2)}) %collective-permute-start.2) | collective-permute-done | bytes 327712 | tf_op jit(solution)/shard_map/ppermute | solution.py:531
  29.0 6.8 %collective-permute-done.4 = bf16[2,80,1024]{2,1,0:T(8,128)(2,1)S(1)} collective-permute-done((bf16[2,80,1024]{2,1,0:T(8,128)(2,1)S(1)}, bf16[2,80,1024]{2,1,0:T(8,128)(2,1)S(1)}, u32[]{:S(2)}, u32[]{:S(2)}) %collective-permute-start.4) | collective-permute-done | bytes 327712 | tf_op jit(solution)/shard_map/ppermute | solution.py:531
  35.7 2.9 all-to-all-done.refs_0_.refs_10_.refs_20_
  40.1 1.5 collective-permute-start.6
  41.6 4.3 all-to-all-start.1
  46.0 18.5 %collective-permute-done.5.refs_1_.refs_11_.refs_21_ = bf16[4,64,2176]{2,1,0:T(8,128)(2,1)} collective-permute-done((bf16[4,64,2176]{2,1,0:T(8,128)(2,1)}, bf16[4,64,2176]{2,1,0:T(8,128)(2,1)}, u32[]{:S(2)}, u32[]{:S(2)}) %collective-permute-start.5) | collective-permute-done | bytes 1114144 | tf_op jit(solution)/shard_map/ppermute | solution.py:527
  69.4 1.6 collective-permute-start.7
  73.4 11.2 %collective-permute-done.7.refs_3_.refs_13_.refs_23_ = bf16[2,64,2176]{2,1,0:T(8,128)(2,1)} collective-permute-done((bf16[2,64,2176]{2,1,0:T(8,128)(2,1)S(1)}, bf16[2,64,2176]{2,1,0:T(8,128)(2,1)}, u32[]{:S(2)}, u32[]{:S(2)}) %collective-permute-start.7) | collective-permute-done | bytes 557088 | tf_op jit(solution)/shard_map/ppermute | solution.py:527
  87.6 2.3 pad_maximum_fusion.2
  90.9 9.8 %shard_map.255 = (bf16[640,1024]{1,0:T(8,128)(2,1)}, bf16[640,3072]{1,0:T(8,128)(2,1)}) custom-call(s32[3]{0:T(128)} %pad_add_fusion.place_ref, bf16[4,64,2176]{2,1,0:T(8,128)(2,1)} %all-to-all-done.refs_0_.refs_10_.refs_20_, bf16[4,64,2176]{2,1,0:T(8,128)(2,1)} %collective-permute-done.5.refs_1_.refs_11_.refs_21_, ...), custom_call_target="tpu_custom_call" | custom-call | flops 11000000512 | tf_op jit(solution)/shard_map/pallas_call | solution.py:260
  100.7 4.5 %all-to-all-start.2 = ((bf16[4,64,2048]{2,1,0:T(8,128)(2,1)}), bf16[4,64,2048]{2,1,0:T(8,128)(2,1)}, u32[]{:S(2)}, u32[]{:S(2)}) async-start(bf16[4,64,2048]{2,1,0:T(8,128)(2,1)} %get-tuple-element.235), calls=%async_computation.2 | async-start | bytes 2097152 | tf_op jit(solution)/shard_map/all_to_all | solution.py:558
  105.2 6.8 %collective-permute-done.14.refs_1_.refs_11_ = bf16[4,64,2048]{2,1,0:T(8,128)(2,1)} collective-permute-done((bf16[4,64,2048]{2,1,0:T(8,128)(2,1)}, bf16[4,64,2048]{2,1,0:T(8,128)(2,1)}, u32[]{:S(2)}, u32[]{:S(2)}) %collective-permute-start.14) | collective-permute-done | bytes 1048608 | tf_op jit(solution)/shard_map/ppermute | solution.py:527
  114.5 1.7 collective-permute-start.19
  118.4 3.9 collective-permute-done.21
  122.6 15.8 %shard_map.256 = (bf16[2,320,1024]{2,1,0:T(8,128)(2,1)}, f32[2,320,1024]{2,1,0:T(8,128)}) custom-call(f32[2,320,1]{2,1,0:T(8,128)} %compare_select_fusion.bias_ref, bf16[2,320,3072]{2,1,0:T(8,128)(2,1)} %bitcast.148, bf16[2,320,3072]{2,1,0:T(8,128)(2,1)} %bitcast.149, bf16[2,320,3072]{2,1,0:T(8,128)(2,1)} %bitcast.150), custom_call_target="tpu_custom_call" | custom-call | flops 14080000000 | tf_op jit(solution)/shard_map/pallas_call | solution.py:133
  138.7 1.6 collective-permute-start.24
  144.0 17.8 %shard_map.257 = (f32[640,1024]{1,0:T(8,128)}, bf16[640,1024]{1,0:T(8,128)(2,1)}, bf16[640,4096]{1,0:T(8,128)(2,1)}, bf16[640,4096]{1,0:T(8,128)(2,1)}) custom-call(s32[3]{0:T(128)} %pad_add_fusion.place_ref, bf16[4,64,2048]{2,1,0:T(8,128)(2,1)} %all-to-all-done.1.refs_0_.refs_10_, bf16[4,64,2048]{2,1,0:T(8,128)(2,1)} %collective-permute-done.14.refs_1_.refs_11_, ...), custom_call_target="tpu_custom_call" | custom-call | flops 22000001024 | tf_op jit(solution)/shard_map/pallas_call | solution.py:260
  161.9 2.5 collective-permute-done.24.refs_1_
  166.9 9.7 %collective-permute-done.28.a0_sib_ref.a1_sib_ref = bf16[640,4096]{1,0:T(8,128)(2,1)S(1)} collective-permute-done((bf16[640,4096]{1,0:T(8,128)(2,1)}, bf16[640,4096]{1,0:T(8,128)(2,1)S(1)}, u32[]{:S(2)}, u32[]{:S(2)}) %collective-permute-start.28) | collective-permute-done | bytes 5242912 | tf_op jit(solution)/shard_map/ppermute | solution.py:527
  176.7 2.3 copy-done.22
  179.8 11.4 %shard_map.258 = (bf16[4,128,1024]{2,1,0:T(8,128)(2,1)S(1)}, bf16[4,128,1024]{2,1,0:T(8,128)(2,1)}, bf16[4,128,1024]{2,1,0:T(8,128)(2,1)}, bf16[4,128,1024]{2,1,0:T(8,128)(2,1)}) custom-call(s32[3]{0:T(128)S(1)} %copy-done.2, bf16[640,4096]{1,0:T(8,128)(2,1)} %get-tuple-element.351.a0_ref.a1_ref.refs_10_, ...), custom_call_target="tpu_custom_call" | custom-call | flops 10150215680 | tf_op jit(solution)/shard_map/pallas_call | solution.py:705
  191.2 1.9 collective-permute-done.30.refs_4_
  195.1 2.5 collective-permute-done.35.refs_9_
  198.3 26.8 %shard_map.259 = (bf16[640,4096]{1,0:T(8,128)(2,1)}, f32[1,4096]{1,0:T(1,128)}, f32[640,1024]{1,0:T(8,128)}, bf16[640,1024]{1,0:T(8,128)(2,1)}, bf16[640,1024]{1,0:T(8,128)(2,1)}, /*index=5*/f32[8,1024]{1,0:T(8,128)}) custom-call(s32[3]{0:T(128)} %pad_add_fusion.place_ref, bf16[4,64,2048]{2,1,0:T(8,128)(2,1)} %all-to-all-done.2.refs_0_, ...), custom_call_target="tpu_custom_call" | custom-call | flops 25300000768 | tf_op jit(solution)/shard_map/pallas_call | solution.py:260
  226.2 11.1 %shard_map.260 = bf16[2,320,1536]{2,1,0:T(8,128)(2,1)} custom-call(f32[2,320,1]{2,1,0:T(8,128)} %compare_select_fusion.bias_ref, bf16[2,320,3072]{2,1,0:T(8,128)(2,1)} %bitcast.151, bf16[2,320,3072]{2,1,0:T(8,128)(2,1)} %bitcast.152, bf16[2,320,3072]{2,1,0:T(8,128)(2,1)} %bitcast.153, f32[2,320,1024]{2,1,0:T(8,128)} %get-tuple-element.258.lse_ref, ...), custom_call_target="tpu_custom_call" | custom-call | flops 11440000000 | tf_op jit(solution)/shard_map/pallas_call | solution.py:133
  238.9 8.0 %shard_map.263 = (bf16[4,64,1024]{2,1,0:T(8,128)(2,1)S(1)}, bf16[4,64,1024]{2,1,0:T(8,128)(2,1)S(1)}, bf16[4,64,1024]{2,1,0:T(8,128)(2,1)}, bf16[4,64,1024]{2,1,0:T(8,128)(2,1)}) custom-call(s32[3]{0:T(128)S(1)} %copy-done.3, bf16[640,1024]{1,0:T(8,128)(2,1)} %get-tuple-element.280.refs_0_, bf16[640,1024]{1,0:T(8,128)(2,1)} %collective-permute-done.38.refs_1_, ...), custom_call_target="tpu_custom_call" | custom-call | flops 5075107840 | tf_op jit(solution)/shard_map/pallas_call | solution.py:705
  248.9 12.6 %shard_map.262 = (bf16[4,64,1536]{2,1,0:T(8,128)(2,1)S(1)}, bf16[4,64,1536]{2,1,0:T(8,128)(2,1)S(1)}, bf16[4,64,1536]{2,1,0:T(8,128)(2,1)}, bf16[4,64,1536]{2,1,0:T(8,128)(2,1)}) custom-call(s32[3]{0:T(128)S(1)} %copy-done.3, bf16[640,1024]{1,0:T(8,128)(2,1)} %get-tuple-element.280.refs_0_, bf16[640,1024]{1,0:T(8,128)(2,1)} %collective-permute-done.38.refs_1_, ...), custom_call_target="tpu_custom_call" | custom-call | flops 7612661760 | tf_op jit(solution)/shard_map/pallas_call | solution.py:705
  261.5 2.0 collective-permute-done.43
  263.5 2.9 add_convert_fusion
  266.4 4.3 all-to-all-start.3
  270.6 2.1 add_convert_fusion.6
  273.6 1.5 collective-permute-start.48
  275.1 6.3 %shard_map.261 = (bf16[4,64,768]{2,1,0:T(8,128)(2,1)S(1)}, bf16[4,64,768]{2,1,0:T(8,128)(2,1)S(1)}, bf16[4,64,768]{2,1,0:T(8,128)(2,1)S(1)}, bf16[4,64,768]{2,1,0:T(8,128)(2,1)}) custom-call(s32[3]{0:T(128)S(1)} %copy-done.3, bf16[640,1024]{1,0:T(8,128)(2,1)} %get-tuple-element.229.refs_0_, bf16[640,1024]{1,0:T(8,128)(2,1)} %collective-permute-done.26.refs_1_, ...), custom_call_target="tpu_custom_call" | custom-call | flops 3806330880 | tf_op jit(solution)/shard_map/pallas_call | solution.py:705
  282.6 11.1 %shard_map.264 = bf16[2,320,1536]{2,1,0:T(8,128)(2,1)} custom-call(f32[2,320,1]{2,1,0:T(8,128)} %compare_select_fusion.bias_ref, bf16[2,320,3072]{2,1,0:T(8,128)(2,1)} %bitcast.154, bf16[2,320,3072]{2,1,0:T(8,128)(2,1)} %bitcast.155, bf16[2,320,3072]{2,1,0:T(8,128)(2,1)} %bitcast.156, f32[2,320,1024]{2,1,0:T(8,128)} %get-tuple-element.258.lse_ref, ...), custom_call_target="tpu_custom_call" | custom-call | flops 11440000000 | tf_op jit(solution)/shard_map/pallas_call | solution.py:133
  293.7 2.8 all-to-all-done.3
  297.5 1.8 collective-permute-start.54
  300.0 2.3 add_convert_fusion.5
  302.3 4.3 all-to-all-start.4
  306.6 2.2 add_convert_fusion.4
  310.1 1.8 add_convert_fusion.8
  312.2 5.5 %shard_map.265 = (bf16[4,64,768]{2,1,0:T(8,128)(2,1)S(1)}, bf16[4,64,768]{2,1,0:T(8,128)(2,1)S(1)}, bf16[4,64,768]{2,1,0:T(8,128)(2,1)S(1)}, bf16[4,64,768]{2,1,0:T(8,128)(2,1)S(1)}) custom-call(s32[3]{0:T(128)S(1)} %copy-done.3, bf16[640,1024]{1,0:T(8,128)(2,1)} %get-tuple-element.229.refs_0_, bf16[640,1024]{1,0:T(8,128)(2,1)} %collective-permute-done.26.refs_1_, ...), custom_call_target="tpu_custom_call" | custom-call | flops 3806330880 | tf_op jit(solution)/shard_map/pallas_call | solution.py:705
  317.7 1.8 collective-permute-start.50
  319.5 14.9 %shard_map.266 = (bf16[640,1024]{1,0:T(8,128)(2,1)}, f32[1,3072]{1,0:T(1,128)}, f32[8,1024]{1,0:T(8,128)}) custom-call(s32[3]{0:T(128)} %pad_add_fusion.place_ref, bf16[4,64,2176]{2,1,0:T(8,128)(2,1)} %all-to-all-done.refs_0_.refs_10_.refs_20_, bf16[4,64,2176]{2,1,0:T(8,128)(2,1)} %collective-permute-done.5.refs_1_.refs_11_.refs_21_, ...), custom_call_target="tpu_custom_call" | custom-call | flops 14300000256 | tf_op jit(solution)/shard_map/pallas_call | solution.py:260
  336.2 2.6 add_convert_fusion.3
  338.8 5.1 %all-to-all-start.5 = ((bf16[4,64,1536]{2,1,0:T(8,128)(2,1)}), bf16[4,64,1536]{2,1,0:T(8,128)(2,1)S(1)}, u32[]{:S(2)}, u32[]{:S(2)}) async-start(bf16[4,64,1536]{2,1,0:T(8,128)(2,1)} %add_convert_fusion.3), calls=%async_computation.5 | async-start | bytes 1572864 | tf_op jit(solution)/shard_map/all_to_all | solution.py:558
  351.9 13.2 %shard_map.268 = bf16[640,1024]{1,0:T(8,128)(2,1)} custom-call(s32[3]{0:T(128)} %pad_add_fusion.place_ref, bf16[4,64,2048]{2,1,0:T(8,128)(2,1)} %all-to-all-done.2.refs_0_, bf16[4,64,2048]{2,1,0:T(8,128)(2,1)} %copy-done.18, bf16[4,64,2048]{2,1,0:T(8,128)(2,1)} %copy-done.19, bf16[2,64,2048]{2,1,0:T(8,128)(2,1)} %copy-done.33, ...), custom_call_target="tpu_custom_call" | custom-call | flops 12099999744 | tf_op jit(solution)/shard_map/pallas_call | solution.py:260
  366.4 2.7 add_convert_fusion.2
  369.1 5.2 %all-to-all-start.6 = ((bf16[4,64,1536]{2,1,0:T(8,128)(2,1)}), bf16[4,64,1536]{2,1,0:T(8,128)(2,1)S(1)}, u32[]{:S(2)}, u32[]{:S(2)}) async-start(bf16[4,64,1536]{2,1,0:T(8,128)(2,1)} %add_convert_fusion.2), calls=%async_computation.6 | async-start | bytes 1572864 | tf_op jit(solution)/shard_map/all_to_all | solution.py:558
  374.3 2.7 fusion.6
  379.5 1.5 constant_dynamic-slice_fusion.5
  381.6 1.5 collective-permute-start.62
  386.5 12.4 %collective-permute-done.61.refs_5_ = bf16[64,1536]{1,0:T(8,128)(2,1)S(1)} collective-permute-done((bf16[64,1536]{1,0:T(8,128)(2,1)}, bf16[64,1536]{1,0:T(8,128)(2,1)S(1)}, u32[]{:S(2)}, u32[]{:S(2)}) %collective-permute-start.61) | collective-permute-done | bytes 196640 | tf_op jit(solution)/shard_map/ppermute | solution.py:527
  404.1 4.0 shard_map.269
  408.1 4.1 collective-permute-done.71
  412.2 4.6 %collective-permute-done.72.refs_1_ = bf16[64,1536]{1,0:T(8,128)(2,1)S(1)} collective-permute-done((bf16[64,1536]{1,0:T(8,128)(2,1)}, bf16[64,1536]{1,0:T(8,128)(2,1)S(1)}, u32[]{:S(2)}, u32[]{:S(2)}) %collective-permute-start.72) | collective-permute-done | bytes 196640 | tf_op jit(solution)/shard_map/ppermute | solution.py:527
  416.9 2.1 collective-permute-start.73
  419.0 2.4 collective-permute-start.74
  422.5 1.7 slice_bitcast_fusion
  424.2 2.6 collective-permute-done.75
  429.9 2.6 shard_map.270
  (272 shorter events, 68.6 us)
Async XLA Ops:
  4.9 33.7 %all-to-all-start = ((bf16[4,64,2176]{2,1,0:T(8,128)(2,1)}), bf16[4,64,2176]{2,1,0:T(8,128)(2,1)}, u32[]{:S(2)}, u32[]{:S(2)}) async-start(bf16[4,64,2176]{2,1,0:T(8,128)(2,1)} %get-tuple-element.201), calls=%async_computation | async-start | bytes 2228224 | tf_op jit(solution)/shard_map/all_to_all | solution.py:558
  13.1 15.1 %collective-permute-start.2 = (bf16[2,80,1024]{2,1,0:T(8,128)(2,1)S(1)}, bf16[2,80,1024]{2,1,0:T(8,128)(2,1)S(1)}, u32[]{:S(2)}, u32[]{:S(2)}) collective-permute-start(bf16[2,80,1024]{2,1,0:T(8,128)(2,1)S(1)} %get-tuple-element.411), channel_id=1, source_target_pairs={{0,3},{1,2},{2,1},{3,0},{4,7},{5,6},{6,5},{7,4},{8,11},{9,10},{10,... | collective-permute-start | bytes 983048 | tf_op jit(solution)/shard_map/ppermute | solution.py:531
  13.5 14.7 %collective-permute-start.3 = (bf16[2,80,1024]{2,1,0:T(8,128)(2,1)S(1)}, bf16[2,80,1024]{2,1,0:T(8,128)(2,1)S(1)}, u32[]{:S(2)}, u32[]{:S(2)}) collective-permute-start(bf16[2,80,1024]{2,1,0:T(8,128)(2,1)S(1)} %get-tuple-element.409), channel_id=1, source_target_pairs={{0,1},{1,0},{2,3},{3,2},{4,5},{5,4},{6,7},{7,6},{8,9},{9,8},{10,11... | collective-permute-start | bytes 983048 | tf_op jit(solution)/shard_map/ppermute | solution.py:531
  13.9 21.8 %collective-permute-start.4 = (bf16[2,80,1024]{2,1,0:T(8,128)(2,1)S(1)}, bf16[2,80,1024]{2,1,0:T(8,128)(2,1)S(1)}, u32[]{:S(2)}, u32[]{:S(2)}) collective-permute-start(bf16[2,80,1024]{2,1,0:T(8,128)(2,1)S(1)} %get-tuple-element.408), channel_id=1, source_target_pairs={{0,2},{1,3},{2,0},{3,1},{4,6},{5,7},{6,4},{7,5},{8,10},{9,11},{10,... | collective-permute-start | bytes 983048 | tf_op jit(solution)/shard_map/ppermute | solution.py:531
  38.6 25.8 %collective-permute-start.5 = (bf16[4,64,2176]{2,1,0:T(8,128)(2,1)}, bf16[4,64,2176]{2,1,0:T(8,128)(2,1)}, u32[]{:S(2)}, u32[]{:S(2)}) collective-permute-start(bf16[4,64,2176]{2,1,0:T(8,128)(2,1)} %all-to-all-done.refs_0_.refs_10_.refs_20_), channel_id=1, source_target_pairs={{0,2},{2,0},{1,3},{3,1},{4,6},{6,4},{5,7},{7,5},{8,10},{10,8},{9,1... | collective-permute-start | bytes 3342344 | tf_op jit(solution)/shard_map/ppermute | solution.py:527
  40.1 25.6 %collective-permute-start.6 = (bf16[4,64,2176]{2,1,0:T(8,128)(2,1)}, bf16[4,64,2176]{2,1,0:T(8,128)(2,1)}, u32[]{:S(2)}, u32[]{:S(2)}) collective-permute-start(bf16[4,64,2176]{2,1,0:T(8,128)(2,1)} %all-to-all-done.refs_0_.refs_10_.refs_20_), channel_id=1, source_target_pairs={{0,4},{4,0},{1,5},{5,1},{2,6},{6,2},{3,7},{7,3},{8,12},{12,8},{9,1... | collective-permute-start | bytes 3342344 | tf_op jit(solution)/shard_map/ppermute | solution.py:527
  41.6 31.8 %all-to-all-start.1 = ((bf16[4,64,2048]{2,1,0:T(8,128)(2,1)}), bf16[4,64,2048]{2,1,0:T(8,128)(2,1)}, u32[]{:S(2)}, u32[]{:S(2)}) async-start(bf16[4,64,2048]{2,1,0:T(8,128)(2,1)} %get-tuple-element.209), calls=%async_computation.1 | async-start | bytes 2097152 | tf_op jit(solution)/shard_map/all_to_all | solution.py:558
  65.7 20.2 %collective-permute-start.10 = (bf16[4,64,2176]{2,1,0:T(8,128)(2,1)}, bf16[4,64,2176]{2,1,0:T(8,128)(2,1)}, u32[]{:S(2)}, u32[]{:S(2)}) collective-permute-start(bf16[4,64,2176]{2,1,0:T(8,128)(2,1)} %collective-permute-done.5.refs_1_.refs_11_.refs_21_), channel_id=1, source_target_pairs={{0,1},{1,0},{2,3},{3,2},{4,5},{5,4},{6,7},{7,6},{8,9},{9,8},{10,11... | collective-permute-start | bytes 3342344 | tf_op jit(solution)/shard_map/ppermute | solution.py:527
  66.8 19.1 %collective-permute-start.11 = (bf16[4,64,2176]{2,1,0:T(8,128)(2,1)}, bf16[4,64,2176]{2,1,0:T(8,128)(2,1)}, u32[]{:S(2)}, u32[]{:S(2)}) collective-permute-start(bf16[4,64,2176]{2,1,0:T(8,128)(2,1)} %collective-permute-done.6.refs_2_.refs_12_.refs_22_), channel_id=1, source_target_pairs={{0,1},{1,0},{2,3},{3,2},{4,5},{5,4},{6,7},{7,6},{8,9},{9,8},{10,11... | collective-permute-start | bytes 3342344 | tf_op jit(solution)/shard_map/ppermute | solution.py:527
  68.5 17.4 %collective-permute-start.9 = (bf16[4,64,2176]{2,1,0:T(8,128)(2,1)}, bf16[4,64,2176]{2,1,0:T(8,128)(2,1)}, u32[]{:S(2)}, u32[]{:S(2)}) collective-permute-start(bf16[4,64,2176]{2,1,0:T(8,128)(2,1)} %all-to-all-done.refs_0_.refs_10_.refs_20_), channel_id=1, source_target_pairs={{0,1},{1,0},{2,3},{3,2},{4,5},{5,4},{6,7},{7,6},{8,9},{9,8},{10,11... | collective-permute-start | bytes 3342344 | tf_op jit(solution)/shard_map/ppermute | solution.py:527
  69.4 15.2 %collective-permute-start.7 = (bf16[2,64,2176]{2,1,0:T(8,128)(2,1)S(1)}, bf16[2,64,2176]{2,1,0:T(8,128)(2,1)}, u32[]{:S(2)}, u32[]{:S(2)}) collective-permute-start(bf16[2,64,2176]{2,1,0:T(8,128)(2,1)S(1)} %slice.90), channel_id=1, source_target_pairs={{0,4},{4,0},{1,5},{5,1},{2,6},{6,2},{3,7},{7,3},{8,12},{12,8},{9,1... | collective-permute-start | bytes 1671176 | tf_op jit(solution)/shard_map/ppermute | solution.py:527
  71.0 14.8 %collective-permute-start.8 = (bf16[2,64,2176]{2,1,0:T(8,128)(2,1)S(1)}, bf16[2,64,2176]{2,1,0:T(8,128)(2,1)}, u32[]{:S(2)}, u32[]{:S(2)}) collective-permute-start(bf16[2,64,2176]{2,1,0:T(8,128)(2,1)S(1)} %slice.91), channel_id=1, source_target_pairs={{0,2},{2,0},{1,3},{3,1},{4,6},{6,4},{5,7},{7,5},{8,10},{10,8},{9,1... | collective-permute-start | bytes 1671176 | tf_op jit(solution)/shard_map/ppermute | solution.py:527
  86.6 25.5 %collective-permute-start.14 = (bf16[4,64,2048]{2,1,0:T(8,128)(2,1)}, bf16[4,64,2048]{2,1,0:T(8,128)(2,1)}, u32[]{:S(2)}, u32[]{:S(2)}) collective-permute-start(bf16[4,64,2048]{2,1,0:T(8,128)(2,1)} %all-to-all-done.1.refs_0_.refs_10_), channel_id=1, source_target_pairs={{0,2},{2,0},{1,3},{3,1},{4,6},{6,4},{5,7},{7,5},{8,10},{10,8},{9,1... | collective-permute-start | bytes 3145736 | tf_op jit(solution)/shard_map/ppermute | solution.py:527
  87.1 25.2 %collective-permute-start.15 = (bf16[4,64,2048]{2,1,0:T(8,128)(2,1)}, bf16[4,64,2048]{2,1,0:T(8,128)(2,1)}, u32[]{:S(2)}, u32[]{:S(2)}) collective-permute-start(bf16[4,64,2048]{2,1,0:T(8,128)(2,1)} %all-to-all-done.1.refs_0_.refs_10_), channel_id=1, source_target_pairs={{0,4},{4,0},{1,5},{5,1},{2,6},{6,2},{3,7},{7,3},{8,12},{12,8},{9,1... | collective-permute-start | bytes 3145736 | tf_op jit(solution)/shard_map/ppermute | solution.py:527
  100.7 38.0 %all-to-all-start.2 = ((bf16[4,64,2048]{2,1,0:T(8,128)(2,1)}), bf16[4,64,2048]{2,1,0:T(8,128)(2,1)}, u32[]{:S(2)}, u32[]{:S(2)}) async-start(bf16[4,64,2048]{2,1,0:T(8,128)(2,1)} %get-tuple-element.235), calls=%async_computation.2 | async-start | bytes 2097152 | tf_op jit(solution)/shard_map/all_to_all | solution.py:558
  114.5 24.2 %collective-permute-start.19 = (bf16[4,64,2048]{2,1,0:T(8,128)(2,1)}, bf16[4,64,2048]{2,1,0:T(8,128)(2,1)S(1)}, u32[]{:S(2)}, u32[]{:S(2)}) collective-permute-start(bf16[4,64,2048]{2,1,0:T(8,128)(2,1)} %collective-permute-done.14.refs_1_.refs_11_), channel_id=1, source_target_pairs={{0,1},{1,0},{2,3},{3,2},{4,5},{5,4},{6,7},{7,6},{8,9},{9,8},{10,11... | collective-permute-start | bytes 3145736 | tf_op jit(solution)/shard_map/ppermute | solution.py:527
  117.2 21.5 %collective-permute-start.20 = (bf16[4,64,2048]{2,1,0:T(8,128)(2,1)}, bf16[4,64,2048]{2,1,0:T(8,128)(2,1)}, u32[]{:S(2)}, u32[]{:S(2)}) collective-permute-start(bf16[4,64,2048]{2,1,0:T(8,128)(2,1)} %collective-permute-done.15.refs_2_.refs_12_), channel_id=1, source_target_pairs={{0,1},{1,0},{2,3},{3,2},{4,5},{5,4},{6,7},{7,6},{8,9},{9,8},{10,11... | collective-permute-start | bytes 3145736 | tf_op jit(solution)/shard_map/ppermute | solution.py:527
  117.3 21.1 %collective-permute-start.16 = (bf16[2,64,2048]{2,1,0:T(8,128)(2,1)S(1)}, bf16[2,64,2048]{2,1,0:T(8,128)(2,1)}, u32[]{:S(2)}, u32[]{:S(2)}) collective-permute-start(bf16[2,64,2048]{2,1,0:T(8,128)(2,1)S(1)} %slice.102), channel_id=1, source_target_pairs={{0,4},{4,0},{1,5},{5,1},{2,6},{6,2},{3,7},{7,3},{8,12},{12,8},{9,1... | collective-permute-start | bytes 1572872 | tf_op jit(solution)/shard_map/ppermute | solution.py:527
  117.9 20.8 %collective-permute-start.17 = (bf16[2,64,2048]{2,1,0:T(8,128)(2,1)S(1)}, bf16[2,64,2048]{2,1,0:T(8,128)(2,1)}, u32[]{:S(2)}, u32[]{:S(2)}) collective-permute-start(bf16[2,64,2048]{2,1,0:T(8,128)(2,1)S(1)} %slice.103), channel_id=1, source_target_pairs={{0,2},{2,0},{1,3},{3,1},{4,6},{6,4},{5,7},{7,5},{8,10},{10,8},{9,1... | collective-permute-start | bytes 1572872 | tf_op jit(solution)/shard_map/ppermute | solution.py:527
  122.3 16.3 %collective-permute-start.18 = (bf16[4,64,2048]{2,1,0:T(8,128)(2,1)}, bf16[4,64,2048]{2,1,0:T(8,128)(2,1)}, u32[]{:S(2)}, u32[]{:S(2)}) collective-permute-start(bf16[4,64,2048]{2,1,0:T(8,128)(2,1)} %all-to-all-done.1.refs_0_.refs_10_), channel_id=1, source_target_pairs={{0,1},{1,0},{2,3},{3,2},{4,5},{5,4},{6,7},{7,6},{8,9},{9,8},{10,11... | collective-permute-start | bytes 3145736 | tf_op jit(solution)/shard_map/ppermute | solution.py:527
  138.4 23.5 %collective-permute-start.26 = (bf16[640,1024]{1,0:T(8,128)(2,1)}, bf16[640,1024]{1,0:T(8,128)(2,1)}, u32[]{:S(2)}, u32[]{:S(2)}) collective-permute-start(bf16[640,1024]{1,0:T(8,128)(2,1)} %get-tuple-element.229.refs_0_), channel_id=1, source_target_pairs={{0,1},{1,0},{2,3},{3,2},{4,5},{5,4},{6,7},{7,6},{8,9},{9,8},{10,11... | collective-permute-start | bytes 3932168 | tf_op jit(solution)/shard_map/ppermute | solution.py:527
  138.7 25.7 %collective-permute-start.24 = (bf16[4,64,2048]{2,1,0:T(8,128)(2,1)}, bf16[4,64,2048]{2,1,0:T(8,128)(2,1)S(1)}, u32[]{:S(2)}, u32[]{:S(2)}) collective-permute-start(bf16[4,64,2048]{2,1,0:T(8,128)(2,1)} %all-to-all-done.2.refs_0_), channel_id=1, source_target_pairs={{0,2},{2,0},{1,3},{3,1},{4,6},{6,4},{5,7},{7,5},{8,10},{10,8},{9,1... | collective-permute-start | bytes 3145736 | tf_op jit(solution)/shard_map/ppermute | solution.py:527
  140.3 25.0 %collective-permute-start.25 = (bf16[4,64,2048]{2,1,0:T(8,128)(2,1)}, bf16[4,64,2048]{2,1,0:T(8,128)(2,1)S(1)}, u32[]{:S(2)}, u32[]{:S(2)}) collective-permute-start(bf16[4,64,2048]{2,1,0:T(8,128)(2,1)} %all-to-all-done.2.refs_0_), channel_id=1, source_target_pairs={{0,4},{4,0},{1,5},{5,1},{2,6},{6,2},{3,7},{7,3},{8,12},{12,8},{9,1... | collective-permute-start | bytes 3145736 | tf_op jit(solution)/shard_map/ppermute | solution.py:527
  142.5 22.9 %collective-permute-start.27 = (bf16[640,1024]{1,0:T(8,128)(2,1)S(1)}, bf16[640,1024]{1,0:T(8,128)(2,1)S(1)}, u32[]{:S(2)}, u32[]{:S(2)}) collective-permute-start(bf16[640,1024]{1,0:T(8,128)(2,1)S(1)} %bitcast_select_fusion.g_ref.refs_30_), channel_id=1, source_target_pairs={{0,1},{1,0},{2,3},{3,2},{4,5},{5,4},{6,7},{7,6},{8,9},{9,8},{10,11... | collective-permute-start | bytes 3932168 | tf_op jit(solution)/shard_map/ppermute | solution.py:527
  165.4 27.6 %collective-permute-start.31 = (bf16[4,64,2048]{2,1,0:T(8,128)(2,1)}, bf16[4,64,2048]{2,1,0:T(8,128)(2,1)S(1)}, u32[]{:S(2)}, u32[]{:S(2)}) collective-permute-start(bf16[4,64,2048]{2,1,0:T(8,128)(2,1)} %all-to-all-done.2.refs_0_), channel_id=1, source_target_pairs={{0,1},{1,0},{2,3},{3,2},{4,5},{5,4},{6,7},{7,6},{8,9},{9,8},{10,11... | collective-permute-start | bytes 3145736 | tf_op jit(solution)/shard_map/ppermute | solution.py:527
  165.9 27.1 %collective-permute-start.32 = (bf16[4,64,2048]{2,1,0:T(8,128)(2,1)S(1)}, bf16[4,64,2048]{2,1,0:T(8,128)(2,1)S(1)}, u32[]{:S(2)}, u32[]{:S(2)}) collective-permute-start(bf16[4,64,2048]{2,1,0:T(8,128)(2,1)S(1)} %collective-permute-done.24.refs_1_), channel_id=1, source_target_pairs={{0,1},{1,0},{2,3},{3,2},{4,5},{5,4},{6,7},{7,6},{8,9},{9,8},{10,11... | collective-permute-start | bytes 3145736 | tf_op jit(solution)/shard_map/ppermute | solution.py:527
  166.0 27.1 %collective-permute-start.33 = (bf16[4,64,2048]{2,1,0:T(8,128)(2,1)S(1)}, bf16[4,64,2048]{2,1,0:T(8,128)(2,1)S(1)}, u32[]{:S(2)}, u32[]{:S(2)}) collective-permute-start(bf16[4,64,2048]{2,1,0:T(8,128)(2,1)S(1)} %collective-permute-done.25.refs_2_), channel_id=1, source_target_pairs={{0,1},{1,0},{2,3},{3,2},{4,5},{5,4},{6,7},{7,6},{8,9},{9,8},{10,11... | collective-permute-start | bytes 3145736 | tf_op jit(solution)/shard_map/ppermute | solution.py:527
  166.5 24.6 %collective-permute-start.29 = (bf16[2,64,2048]{2,1,0:T(8,128)(2,1)S(1)}, bf16[2,64,2048]{2,1,0:T(8,128)(2,1)S(1)}, u32[]{:S(2)}, u32[]{:S(2)}) collective-permute-start(bf16[2,64,2048]{2,1,0:T(8,128)(2,1)S(1)} %slice.104), channel_id=1, source_target_pairs={{0,4},{4,0},{1,5},{5,1},{2,6},{6,2},{3,7},{7,3},{8,12},{12,8},{9,1... | collective-permute-start | bytes 1572872 | tf_op jit(solution)/shard_map/ppermute | solution.py:527
  179.0 14.1 %collective-permute-start.30 = (bf16[2,64,2048]{2,1,0:T(8,128)(2,1)S(1)}, bf16[2,64,2048]{2,1,0:T(8,128)(2,1)}, u32[]{:S(2)}, u32[]{:S(2)}) collective-permute-start(bf16[2,64,2048]{2,1,0:T(8,128)(2,1)S(1)} %slice.105), channel_id=1, source_target_pairs={{0,2},{2,0},{1,3},{3,1},{4,6},{6,4},{5,7},{7,5},{8,10},{10,8},{9,1... | collective-permute-start | bytes 1572872 | tf_op jit(solution)/shard_map/ppermute | solution.py:527
  193.7 31.5 %collective-permute-start.37 = (bf16[640,1024]{1,0:T(8,128)(2,1)S(1)}, bf16[640,1024]{1,0:T(8,128)(2,1)S(1)}, u32[]{:S(2)}, u32[]{:S(2)}) collective-permute-start(bf16[640,1024]{1,0:T(8,128)(2,1)S(1)} %bitcast.139), channel_id=1, source_target_pairs={{0,1},{1,0},{2,3},{3,2},{4,5},{5,4},{6,7},{7,6},{8,9},{9,8},{10,11... | collective-permute-start | bytes 3932168 | tf_op jit(solution)/shard_map/ppermute | solution.py:527
  193.7 31.4 %collective-permute-start.38 = (bf16[640,1024]{1,0:T(8,128)(2,1)S(1)}, bf16[640,1024]{1,0:T(8,128)(2,1)}, u32[]{:S(2)}, u32[]{:S(2)}) collective-permute-start(bf16[640,1024]{1,0:T(8,128)(2,1)S(1)} %copy-done.24), channel_id=1, source_target_pairs={{0,1},{1,0},{2,3},{3,2},{4,5},{5,4},{6,7},{7,6},{8,9},{9,8},{10,11... | collective-permute-start | bytes 3932168 | tf_op jit(solution)/shard_map/ppermute | solution.py:527
  194.2 31.0 %collective-permute-start.36 = (bf16[4,128,1024]{2,1,0:T(8,128)(2,1)}, bf16[4,128,1024]{2,1,0:T(8,128)(2,1)S(1)}, u32[]{:S(2)}, u32[]{:S(2)}) collective-permute-start(bf16[4,128,1024]{2,1,0:T(8,128)(2,1)} %get-tuple-element.277), channel_id=1, source_target_pairs={{0,4},{4,0},{1,5},{5,1},{2,6},{6,2},{3,7},{7,3},{8,12},{12,8},{9,1... | collective-permute-start | bytes 3145736 | tf_op jit(solution)/shard_map/ppermute | solution.py:527
  225.2 12.2 %collective-permute-start.39 = (bf16[640,4096]{1,0:T(8,128)(2,1)}, bf16[640,4096]{1,0:T(8,128)(2,1)}, u32[]{:S(2)}, u32[]{:S(2)}) collective-permute-start(bf16[640,4096]{1,0:T(8,128)(2,1)} %get-tuple-element.282.refs_2_), channel_id=1, source_target_pairs={{0,1},{1,0},{2,3},{3,2},{4,5},{5,4},{6,7},{7,6},{8,9},{9,8},{10,11... | collective-permute-start | bytes 15728648 | tf_op jit(solution)/shard_map/ppermute | solution.py:527
  225.4 11.9 %collective-permute-start.40 = (bf16[640,1024]{1,0:T(8,128)(2,1)}, bf16[640,1024]{1,0:T(8,128)(2,1)}, u32[]{:S(2)}, u32[]{:S(2)}) collective-permute-start(bf16[640,1024]{1,0:T(8,128)(2,1)} %get-tuple-element.283.refs_6_), channel_id=1, source_target_pairs={{0,1},{1,0},{2,3},{3,2},{4,5},{5,4},{6,7},{7,6},{8,9},{9,8},{10,11... | collective-permute-start | bytes 3932168 | tf_op jit(solution)/shard_map/ppermute | solution.py:527
  225.8 35.7 %collective-permute-start.44 = (bf16[4,128,1024]{2,1,0:T(8,128)(2,1)}, bf16[4,128,1024]{2,1,0:T(8,128)(2,1)}, u32[]{:S(2)}, u32[]{:S(2)}) collective-permute-start(bf16[4,128,1024]{2,1,0:T(8,128)(2,1)} %get-tuple-element.306), channel_id=1, source_target_pairs={{0,4},{4,0},{1,5},{5,1},{2,6},{6,2},{3,7},{7,3},{8,12},{12,8},{9,1... | collective-permute-start | bytes 3145736 | tf_op jit(solution)/shard_map/ppermute | solution.py:527
  237.4 37.7 %collective-permute-start.41 = (bf16[640,1536]{1,0:T(8,128)(2,1)}, bf16[640,1536]{1,0:T(8,128)(2,1)}, u32[]{:S(2)}, u32[]{:S(2)}) collective-permute-start(bf16[640,1536]{1,0:T(8,128)(2,1)} %bitcast.131), channel_id=1, source_target_pairs={{0,1},{1,0},{2,3},{3,2},{4,5},{5,4},{6,7},{7,6},{8,9},{9,8},{10,11... | collective-permute-start | bytes 5898248 | tf_op jit(solution)/shard_map/ppermute | solution.py:527
  238.0 25.5 %collective-permute-start.43 = (bf16[4,128,1024]{2,1,0:T(8,128)(2,1)S(1)}, bf16[4,128,1024]{2,1,0:T(8,128)(2,1)S(1)}, u32[]{:S(2)}, u32[]{:S(2)}) collective-permute-start(bf16[4,128,1024]{2,1,0:T(8,128)(2,1)S(1)} %add_convert_fusion.1), channel_id=1, source_target_pairs={{0,2},{2,0},{1,3},{3,1},{4,6},{6,4},{5,7},{7,5},{8,10},{10,8},{9,1... | collective-permute-start | bytes 3145736 | tf_op jit(solution)/shard_map/ppermute | solution.py:527
  246.9 16.6 %collective-permute-start.42 = (bf16[4,64,1024]{2,1,0:T(8,128)(2,1)}, bf16[4,64,1024]{2,1,0:T(8,128)(2,1)}, u32[]{:S(2)}, u32[]{:S(2)}) collective-permute-start(bf16[4,64,1024]{2,1,0:T(8,128)(2,1)} %get-tuple-element.303), channel_id=1, source_target_pairs={{0,4},{4,0},{1,5},{5,1},{2,6},{6,2},{3,7},{7,3},{8,12},{12,8},{9,1... | collective-permute-start | bytes 1572872 | tf_op jit(solution)/shard_map/ppermute | solution.py:527
  248.3 45.3 %collective-permute-start.47 = (bf16[4,64,1024]{2,1,0:T(8,128)(2,1)}, bf16[4,64,1024]{2,1,0:T(8,128)(2,1)}, u32[]{:S(2)}, u32[]{:S(2)}) collective-permute-start(bf16[4,64,1024]{2,1,0:T(8,128)(2,1)} %get-tuple-element.313), channel_id=1, source_target_pairs={{0,4},{4,0},{1,5},{5,1},{2,6},{6,2},{3,7},{7,3},{8,12},{12,8},{9,1... | collective-permute-start | bytes 1572872 | tf_op jit(solution)/shard_map/ppermute | solution.py:527
  266.4 30.1 %all-to-all-start.3 = ((bf16[4,128,1024]{2,1,0:T(8,128)(2,1)}), bf16[4,128,1024]{2,1,0:T(8,128)(2,1)}, u32[]{:S(2)}, u32[]{:S(2)}) async-start(bf16[4,128,1024]{2,1,0:T(8,128)(2,1)} %add_convert_fusion), calls=%async_computation.3 | async-start | bytes 2097152 | tf_op jit(solution)/shard_map/all_to_all | solution.py:558
  272.7 21.0 %collective-permute-start.46 = (bf16[4,64,1024]{2,1,0:T(8,128)(2,1)}, bf16[4,64,1024]{2,1,0:T(8,128)(2,1)}, u32[]{:S(2)}, u32[]{:S(2)}) collective-permute-start(bf16[4,64,1024]{2,1,0:T(8,128)(2,1)} %add_convert_fusion.6), channel_id=1, source_target_pairs={{0,2},{2,0},{1,3},{3,1},{4,6},{6,4},{5,7},{7,5},{8,10},{10,8},{9,1... | collective-permute-start | bytes 1572872 | tf_op jit(solution)/shard_map/ppermute | solution.py:527
  273.6 20.1 %collective-permute-start.48 = (bf16[4,64,1536]{2,1,0:T(8,128)(2,1)}, bf16[4,64,1536]{2,1,0:T(8,128)(2,1)}, u32[]{:S(2)}, u32[]{:S(2)}) collective-permute-start(bf16[4,64,1536]{2,1,0:T(8,128)(2,1)} %get-tuple-element.314), channel_id=1, source_target_pairs={{0,4},{4,0},{1,5},{5,1},{2,6},{6,2},{3,7},{7,3},{8,12},{12,8},{9,1... | collective-permute-start | bytes 2359304 | tf_op jit(solution)/shard_map/ppermute | solution.py:527
  281.4 15.2 %collective-permute-start.45 = (bf16[4,64,768]{2,1,0:T(8,128)(2,1)}, bf16[4,64,768]{2,1,0:T(8,128)(2,1)}, u32[]{:S(2)}, u32[]{:S(2)}) collective-permute-start(bf16[4,64,768]{2,1,0:T(8,128)(2,1)} %get-tuple-element.310), channel_id=1, source_target_pairs={{0,2},{2,0},{1,3},{3,1},{4,6},{6,4},{5,7},{7,5},{8,10},{10,8},{9,1... | collective-permute-start | bytes 1179656 | tf_op jit(solution)/shard_map/ppermute | solution.py:527
  296.5 15.7 %collective-permute-start.49 = (bf16[640,1536]{1,0:T(8,128)(2,1)}, bf16[640,1536]{1,0:T(8,128)(2,1)}, u32[]{:S(2)}, u32[]{:S(2)}) collective-permute-start(bf16[640,1536]{1,0:T(8,128)(2,1)} %bitcast.134), channel_id=1, source_target_pairs={{0,1},{1,0},{2,3},{3,2},{4,5},{5,4},{6,7},{7,6},{8,9},{9,8},{10,11... | collective-permute-start | bytes 5898248 | tf_op jit(solution)/shard_map/ppermute | solution.py:527
  297.5 38.4 %collective-permute-start.54 = (bf16[4,64,1536]{2,1,0:T(8,128)(2,1)}, bf16[4,64,1536]{2,1,0:T(8,128)(2,1)}, u32[]{:S(2)}, u32[]{:S(2)}) collective-permute-start(bf16[4,64,1536]{2,1,0:T(8,128)(2,1)} %get-tuple-element.334), channel_id=1, source_target_pairs={{0,4},{4,0},{1,5},{5,1},{2,6},{6,2},{3,7},{7,3},{8,12},{12,8},{9,1... | collective-permute-start | bytes 2359304 | tf_op jit(solution)/shard_map/ppermute | solution.py:527
  299.2 36.9 %collective-permute-start.51 = (bf16[4,64,768]{2,1,0:T(8,128)(2,1)S(1)}, bf16[4,64,768]{2,1,0:T(8,128)(2,1)}, u32[]{:S(2)}, u32[]{:S(2)}) collective-permute-start(bf16[4,64,768]{2,1,0:T(8,128)(2,1)S(1)} %get-tuple-element.329), channel_id=1, source_target_pairs={{0,2},{2,0},{1,3},{3,1},{4,6},{6,4},{5,7},{7,5},{8,10},{10,8},{9,1... | collective-permute-start | bytes 1179656 | tf_op jit(solution)/shard_map/ppermute | solution.py:527
  302.3 33.8 %all-to-all-start.4 = ((bf16[4,64,1024]{2,1,0:T(8,128)(2,1)}), bf16[4,64,1024]{2,1,0:T(8,128)(2,1)}, u32[]{:S(2)}, u32[]{:S(2)}) async-start(bf16[4,64,1024]{2,1,0:T(8,128)(2,1)} %add_convert_fusion.5), calls=%async_computation.4 | async-start | bytes 1048576 | tf_op jit(solution)/shard_map/all_to_all | solution.py:558
  308.8 27.3 %collective-permute-start.53 = (bf16[4,64,1536]{2,1,0:T(8,128)(2,1)}, bf16[4,64,1536]{2,1,0:T(8,128)(2,1)}, u32[]{:S(2)}, u32[]{:S(2)}) collective-permute-start(bf16[4,64,1536]{2,1,0:T(8,128)(2,1)} %add_convert_fusion.4), channel_id=1, source_target_pairs={{0,2},{2,0},{1,3},{3,1},{4,6},{6,4},{5,7},{7,5},{8,10},{10,8},{9,1... | collective-permute-start | bytes 2359304 | tf_op jit(solution)/shard_map/ppermute | solution.py:527
  311.9 24.2 %collective-permute-start.52 = (bf16[4,64,768]{2,1,0:T(8,128)(2,1)}, bf16[4,64,768]{2,1,0:T(8,128)(2,1)}, u32[]{:S(2)}, u32[]{:S(2)}) collective-permute-start(bf16[4,64,768]{2,1,0:T(8,128)(2,1)} %add_convert_fusion.8), channel_id=1, source_target_pairs={{0,4},{4,0},{1,5},{5,1},{2,6},{6,2},{3,7},{7,3},{8,12},{12,8},{9,1... | collective-permute-start | bytes 1179656 | tf_op jit(solution)/shard_map/ppermute | solution.py:527
  317.7 18.5 %collective-permute-start.50 = (bf16[4,64,768]{2,1,0:T(8,128)(2,1)S(1)}, bf16[4,64,768]{2,1,0:T(8,128)(2,1)}, u32[]{:S(2)}, u32[]{:S(2)}) collective-permute-start(bf16[4,64,768]{2,1,0:T(8,128)(2,1)S(1)} %get-tuple-element.328), channel_id=1, source_target_pairs={{0,4},{4,0},{1,5},{5,1},{2,6},{6,2},{3,7},{7,3},{8,12},{12,8},{9,1... | collective-permute-start | bytes 1179656 | tf_op jit(solution)/shard_map/ppermute | solution.py:527
  335.9 30.5 %collective-permute-start.56 = (bf16[4,64,768]{2,1,0:T(8,128)(2,1)S(1)}, bf16[4,64,768]{2,1,0:T(8,128)(2,1)}, u32[]{:S(2)}, u32[]{:S(2)}) collective-permute-start(bf16[4,64,768]{2,1,0:T(8,128)(2,1)S(1)} %get-tuple-element.347), channel_id=1, source_target_pairs={{0,4},{4,0},{1,5},{5,1},{2,6},{6,2},{3,7},{7,3},{8,12},{12,8},{9,1... | collective-permute-start | bytes 1179656 | tf_op jit(solution)/shard_map/ppermute | solution.py:527
  336.2 14.6 %collective-permute-start.57 = (f32[8,1536]{1,0:T(8,128)}, f32[8,1536]{1,0:T(8,128)S(1)}, u32[]{:S(2)}, u32[]{:S(2)}) collective-permute-start(f32[8,1536]{1,0:T(8,128)} %shard_map.267), channel_id=1, source_target_pairs={{0,1},{1,0},{2,3},{3,2},{4,5},{5,4},{6,7},{7,6},{8,9},{9,8},{10,11... | collective-permute-start | bytes 147464 | tf_op jit(solution)/shard_map/ppermute | solution.py:527
  338.8 27.6 %all-to-all-start.5 = ((bf16[4,64,1536]{2,1,0:T(8,128)(2,1)}), bf16[4,64,1536]{2,1,0:T(8,128)(2,1)S(1)}, u32[]{:S(2)}, u32[]{:S(2)}) async-start(bf16[4,64,1536]{2,1,0:T(8,128)(2,1)} %add_convert_fusion.3), calls=%async_computation.5 | async-start | bytes 1572864 | tf_op jit(solution)/shard_map/all_to_all | solution.py:558
  345.0 21.4 %collective-permute-start.55 = (bf16[4,64,768]{2,1,0:T(8,128)(2,1)S(1)}, bf16[4,64,768]{2,1,0:T(8,128)(2,1)S(1)}, u32[]{:S(2)}, u32[]{:S(2)}) collective-permute-start(bf16[4,64,768]{2,1,0:T(8,128)(2,1)S(1)} %add_convert_fusion.7), channel_id=1, source_target_pairs={{0,2},{2,0},{1,3},{3,1},{4,6},{6,4},{5,7},{7,5},{8,10},{10,8},{9,1... | collective-permute-start | bytes 1179656 | tf_op jit(solution)/shard_map/ppermute | solution.py:527
  347.5 18.9 %collective-permute-start.60 = (bf16[128,1024]{1,0:T(8,128)(2,1)S(1)}, bf16[128,1024]{1,0:T(8,128)(2,1)}, u32[]{:S(2)}, u32[]{:S(2)}) collective-permute-start(bf16[128,1024]{1,0:T(8,128)(2,1)S(1)} %reduce_sum.59.refs_8_), channel_id=1, source_target_pairs={{0,2},{2,0},{1,3},{3,1},{4,6},{6,4},{5,7},{7,5},{8,10},{10,8},{9,1... | collective-permute-start | bytes 786440 | tf_op jit(solution)/shard_map/ppermute | solution.py:527
  349.7 16.7 %collective-permute-start.59 = (bf16[64,1024]{1,0:T(8,128)(2,1)S(1)}, bf16[64,1024]{1,0:T(8,128)(2,1)S(1)}, u32[]{:S(2)}, u32[]{:S(2)}) collective-permute-start(bf16[64,1024]{1,0:T(8,128)(2,1)S(1)} %reduce_sum.58.refs_0_), channel_id=1, source_target_pairs={{0,2},{2,0},{1,3},{3,1},{4,6},{6,4},{5,7},{7,5},{8,10},{10,8},{9,1... | collective-permute-start | bytes 393224 | tf_op jit(solution)/shard_map/ppermute | solution.py:527
  350.8 15.0 %collective-permute-start.58 = (f32[8,1536]{1,0:T(8,128)S(1)}, f32[8,1536]{1,0:T(8,128)S(1)}, u32[]{:S(2)}, u32[]{:S(2)}) collective-permute-start(f32[8,1536]{1,0:T(8,128)S(1)} %add.159), channel_id=1, source_target_pairs={{0,2},{2,0},{1,3},{3,1},{4,6},{6,4},{5,7},{7,5},{8,10},{10,8},{9,1... | collective-permute-start | bytes 147464 | tf_op jit(solution)/shard_map/ppermute | solution.py:527
  369.1 30.5 %all-to-all-start.6 = ((bf16[4,64,1536]{2,1,0:T(8,128)(2,1)}), bf16[4,64,1536]{2,1,0:T(8,128)(2,1)S(1)}, u32[]{:S(2)}, u32[]{:S(2)}) async-start(bf16[4,64,1536]{2,1,0:T(8,128)(2,1)} %add_convert_fusion.2), calls=%async_computation.6 | async-start | bytes 1572864 | tf_op jit(solution)/shard_map/all_to_all | solution.py:558
  377.0 22.0 %collective-permute-start.63 = (bf16[4,80,1024]{2,1,0:T(8,128)(2,1)}, bf16[4,80,1024]{2,1,0:T(8,128)(2,1)S(1)}, u32[]{:S(2)}, u32[]{:S(2)}) collective-permute-start(bf16[4,80,1024]{2,1,0:T(8,128)(2,1)} %get-tuple-element.404), channel_id=1, source_target_pairs={{0,1},{1,0},{2,3},{3,2},{4,5},{5,4},{6,7},{7,6},{8,9},{9,8},{10,11... | collective-permute-start | bytes 1966088 | tf_op jit(solution)/shard_map/ppermute | solution.py:531
  377.0 22.6 %collective-permute-start.64 = (bf16[4,80,1024]{2,1,0:T(8,128)(2,1)}, bf16[4,80,1024]{2,1,0:T(8,128)(2,1)S(1)}, u32[]{:S(2)}, u32[]{:S(2)}) collective-permute-start(bf16[4,80,1024]{2,1,0:T(8,128)(2,1)} %get-tuple-element.405), channel_id=1, source_target_pairs={{0,2},{1,3},{2,0},{3,1},{4,6},{5,7},{6,4},{7,5},{8,10},{9,11},{10,... | collective-permute-start | bytes 1966088 | tf_op jit(solution)/shard_map/ppermute | solution.py:531
  384.0 15.0 %collective-permute-start.61 = (bf16[64,1536]{1,0:T(8,128)(2,1)}, bf16[64,1536]{1,0:T(8,128)(2,1)S(1)}, u32[]{:S(2)}, u32[]{:S(2)}) collective-permute-start(bf16[64,1536]{1,0:T(8,128)(2,1)} %reduce_sum.60.refs_4_), channel_id=1, source_target_pairs={{0,2},{2,0},{1,3},{3,1},{4,6},{6,4},{5,7},{7,5},{8,10},{10,8},{9,1... | collective-permute-start | bytes 589832 | tf_op jit(solution)/shard_map/ppermute | solution.py:527
  385.2 27.0 %collective-permute-start.71 = (bf16[4,80,1024]{2,1,0:T(8,128)(2,1)}, bf16[4,80,1024]{2,1,0:T(8,128)(2,1)S(1)}, u32[]{:S(2)}, u32[]{:S(2)}) collective-permute-start(bf16[4,80,1024]{2,1,0:T(8,128)(2,1)} %get-tuple-element.402), channel_id=1, source_target_pairs={{0,3},{1,2},{2,1},{3,0},{4,7},{5,6},{6,5},{7,4},{8,11},{9,10},{10,... | collective-permute-start | bytes 1966088 | tf_op jit(solution)/shard_map/ppermute | solution.py:531
  403.1 13.7 %collective-permute-start.72 = (bf16[64,1536]{1,0:T(8,128)(2,1)}, bf16[64,1536]{1,0:T(8,128)(2,1)S(1)}, u32[]{:S(2)}, u32[]{:S(2)}) collective-permute-start(bf16[64,1536]{1,0:T(8,128)(2,1)} %reduce_sum.61.refs_0_), channel_id=1, source_target_pairs={{0,2},{2,0},{1,3},{3,1},{4,6},{6,4},{5,7},{7,5},{8,10},{10,8},{9,1... | collective-permute-start | bytes 589832 | tf_op jit(solution)/shard_map/ppermute | solution.py:527
  404.1 24.4 %collective-permute-start.76 = (bf16[64,1536]{1,0:T(8,128)(2,1)}, bf16[64,1536]{1,0:T(8,128)(2,1)S(1)}, u32[]{:S(2)}, u32[]{:S(2)}) collective-permute-start(bf16[64,1536]{1,0:T(8,128)(2,1)} %reduce_sum.61.refs_0_), channel_id=1, source_target_pairs={{0,1},{1,0},{2,3},{3,2},{4,5},{5,4},{6,7},{7,6},{8,9},{9,8},{10,11... | collective-permute-start | bytes 589832 | tf_op jit(solution)/shard_map/ppermute | solution.py:527
  (65 other events, 553.2 us)

commit v2 on v1

--- a/solution.py
+++ b/solution.py
@@ -316,7 +316,7 @@
 def expand_kernel(weights, place_ref, *refs):
     (up_refs, out_w_refs), refs = split_refs(refs, weights)
     tokens_ref, context_ref, bias_out_ref, gain_ref, shift_ref, bias_ref, *refs = refs
-    middle_ref, normed_ref, hidden_ref, slope_ref, buf, sems, out_buf, out_sem = refs
+    middle_ref, normed_ref, hidden_ref, slope_ref, other_ref, buf, sems, out_buf, out_sem = refs
 
     @pl.when(pl.program_id(0) == 0)
     def _():
@@ -335,7 +335,12 @@
     weight = stream(weights[0], up_refs, place_ref, buf, sems)
     pre = contract(normed_ref[...], weight, 1, 0) + bias_ref[...]
     cumul = 0.5 * (1.0 + lax.erf(pre * 0.7071067811865476))
-    hidden_ref[...] = (pre * cumul).astype(BF16)
+    hidden = (pre * cumul).astype(BF16)
+    hidden_ref[...] = hidden
+    half = 2 * LANES
+    for i in range(other_ref.shape[1] // half):
+        low, high = (hidden[:, (2 * i + k) * half : (2 * i + k + 1) * half] for k in range(2))
+        other_ref[:, i * half : (i + 1) * half] = jnp.where(place_ref[2] == 0, high, low)
     slope = cumul + pre * (jnp.exp(-0.5 * pre * pre) * 0.3989422804014327)
     slope_ref[...] = slope.astype(BF16)
 
@@ -350,9 +355,9 @@
         [up, out_weight],
         [whole_spec(v) for v in (tokens, context, bias_out, gain, shift)] + [columns_spec(1)],
         (tokens, context, bias_out, gain, shift, bias_up),
-        [whole_spec(tokens)] * 2 + [columns_spec(rows)] * 2,
+        [whole_spec(tokens)] * 2 + [columns_spec(rows)] * 2 + [columns_spec(rows, step=STEP // 2)],
         [jax.ShapeDtypeStruct((rows, width), F32), jax.ShapeDtypeStruct((rows, width), BF16)]
-        + [jax.ShapeDtypeStruct((rows, hidden), BF16)] * 2,
+        + [jax.ShapeDtypeStruct((rows, n), BF16) for n in (hidden, hidden, hidden // 2)],
         streamed(width, STEP) + [pltpu.VMEM((width // out_weight.step, width, out_weight.step), BF16), pltpu.SemaphoreType.DMA],
         20,
     )
@@ -675,8 +680,8 @@
         specs = [
             pl.BlockSpec((tokens, half), lambda j, place: (0, 4 * j + place[2])),
             pl.BlockSpec((tokens, half), lambda j, place: (0, 4 * j + 2 + place[2])),
-            pl.BlockSpec((tokens, half), lambda j, place: (0, 4 * j + place[2])),
-            pl.BlockSpec((tokens, half), lambda j, place: (0, 4 * j + 2 + place[2])),
+            pl.BlockSpec((tokens, half), lambda j, place: (0, 2 * j)),
+            pl.BlockSpec((tokens, half), lambda j, place: (0, 2 * j + 1)),
             every,
             every,
         ]
@@ -913,7 +918,9 @@
         x1, y1, z1, third = tie(x1, y1, z1, third)
         vec_z, vec_y = (v[:, : sum(sizes) // LANES, -LANES:].reshape(v.shape[0], -1) for v in (z1, y1))
         vectors = unpack(order_vectors(vec_z, vec_y))
-        d1, c1, z2, vectors, third = tie(corner(x1, y1), core_swap(z1, x1, y1), z2, vectors, third)
+        d1, c1, z2, vectors, third, tokens = tie(
+            corner(x1, y1), core_swap(z1, x1, y1), z2, vectors, third, tokens
+        )
         gain_a, shift_a, bias_qv, bias_out, gain_b, shift_b, bias_up, bias_down = vectors
         arrays = (z1, x1, y1, *d1, *c1, *core_swap(*d1))
         qkv_full = Weight(arrays, blocks=GROUPS, step=3 * width // GROUPS)
@@ -922,9 +929,9 @@
         normed_a, joint = project(place, tokens, gain_a, shift_a, qkv_full, bias_qv)
         joint, third = tie(joint, third)
         z3 = exchange(third, "z")
-        joint, x2, y2, z2, normed_a, cotangent = tie(joint, x2, y2, z2, normed_a, cotangent)
+        joint, x2, y2, c_z2, normed_a, cotangent = tie(joint, x2, y2, swap(z2, "c"), normed_a, cotangent)
         joint = joint.reshape(images, slots, 3 * width)
-        d2, c2 = corner(x2, y2), core_swap(z2, x2, y2)
+        d2, c2 = corner(x2, y2), (c_z2, *core_swap(x2, y2))
         context, lse = attention(key_bias, joint)
         context, d2, c2, z3, cot = tie(
             context.reshape(rows, width), d2, c2, z3, cot + by_image(cotangent, [members - 1])
@@ -932,12 +939,12 @@
         cot = in_images(cot)
         x3, y3 = swap(z3, "x"), swap(z3, "y")
         up_full = Weight((z2, x2, y2, *d2, *c2, *core_swap(*d2)), blocks=cut_up.columns // STEP)
-        middle, normed_b, hidden, slope = expand(
+        middle, normed_b, hidden, slope, hidden_other = expand(
             place, tokens, context, out_full, bias_out, gain_b, shift_b, up_full, bias_up
         )
         grad_out = jnp.where(valid, cot, jnp.zeros_like(cot))
-        hidden, slope, x3, y3, z3, normed_sib, out_sib = tie(
-            hidden, slope, x3, y3, z3, swap(normed_a, "c"), swap(grad_out, "c")
+        hidden, hidden_other, slope, x3, y3, c_z3, grad_out, out_sib = tie(
+            hidden, hidden_other, slope, x3, y3, swap(z3, "c"), grad_out, swap(grad_out, "c")
         )
     else:
         vectors = unpack(lax.all_gather(packed, FSDP, axis=0))
@@ -955,7 +962,7 @@
         joint = joint.reshape(images, slots, 3 * width)
         context, lse = attention(key_bias, joint)
         context = context.reshape(rows, width)
-        middle, normed_b, hidden, slope = expand(
+        middle, normed_b, hidden, slope, hidden_other = expand(
             place, tokens, context, out_full, bias_out, gain_b, shift_b, up_full, bias_up
         )
 
@@ -970,16 +977,18 @@
     shard_count = lax.axis_size(FSDP)
     depth = lax.axis_size("z")
     if staged:
-        d3, c3 = corner(x3, y3), core_swap(z3, x3, y3)
-        down_parts = grad_parts([(hidden, swap(hidden, "c"), grad_out, out_sib, 0, 0)], cut_down, depth)
-        down_parts, slope, d3, c3, hidden = tie(down_parts, slope, d3, c3, hidden)
+        d3, c3 = corner(x3, y3), (c_z3, *core_swap(x3, y3))
+        down_parts = grad_parts([(hidden, swap(hidden_other, "c"), grad_out, out_sib, 0, 0)], cut_down, depth)
+        down_parts, slope, d3, c3, hidden, g_bias_down, valid_wide = tie(
+            down_parts, slope, d3, c3, hidden, g_bias_down, valid_wide
+        )
         down_full = Weight((z3, x3, y3, *d3, *c3, *core_swap(*d3)), by_rows=True)
         down_e = swap(down_parts[3], "y")
         grad_pre, bias_up_sums, grad_middle, grad_branch, grad_context, sums_b = back(
             place, grad_out, down_full, slope, up_full, middle, gain_b, out_full
         )
-        grad_pre, down_e, grad_context, grad_branch, context_sib, normed_sib_b = tie(
-            grad_pre, down_e, grad_context, grad_branch, swap(context, "c"), swap(normed_b, "c")
+        grad_pre, down_e, grad_context, grad_branch, context_sib, normed_sib_b, normed_sib = tie(
+            grad_pre, down_e, grad_context, grad_branch, swap(context, "c"), swap(normed_b, "c"), swap(normed_a, "c")
         )
         grad_context = grad_context.reshape(images, slots, width)
         pre_sib, branch_sib = swap(grad_pre, "c"), swap(grad_branch, "c")

time: 439 us -> 428 us (0.975)
  waiting for transfers between devices: 116 us -> 103 us
    ppermute x66, waiting for transfers between devices: 79.7 us -> 67.5 us  [swap(): return lax.ppermute(value, axis, [(0, 1), (1, 0)])]
    unnamed x93 -> x83, local copies, waits for them, and re-layouts: 9.75 us -> 8.57 us
  transfers between devices with their start and end apart: 85 -> 85, of which waited for: 29 -> 27; matrix products, arithmetic and copies ran while one was open for 10% -> 11% of each run, Pallas kernels for 39% -> 40%
where the time goes in v2:
time: 428 us; the launch traced here: 422 us
  Pallas kernels  177 us (41%)
  waiting for transfers between devices  103 us (24%)
  starting transfers between devices  84.3 us (20%)
  other arithmetic  32.8 us (8%)
  local copies, waits for them, and re-layouts  23.6 us (6%)
    pallas_call x5, Pallas kernels, stepped(): pl.pallas_call(functools.partial(kernel, weights), grid_spec=pltpu.Prefet...  83.2 us
    ppermute x66, waiting for transfers between devices, swap(): return lax.ppermute(value, axis, [(0, 1), (1, 0)])  67.5 us
    pallas_call x5, Pallas kernels, grad_parts(): pl.pallas_call(kernel, grid_spec=pltpu.PrefetchScalarGridSpec(num_scalar_...  43.8 us
    ppermute x66, starting transfers between devices, swap(): return lax.ppermute(value, axis, [(0, 1), (1, 0)])  41.2 us
    pallas_call x3, Pallas kernels, attention(): pl.pallas_call(attend_back_kernel if back else attend_kernel, grid=(image...  37.9 us
    all_to_all x7, starting transfers between devices, exchange(): return lax.all_to_all(blocks, axis, split_axis=0, concat_axis=0, tiled=True)  33.9 us
    ppermute x12, waiting for transfers between devices, send(): lax.ppermute(value, axis, [(i, i ^ step) for i in range(lax.axis_size(axi...  28.4 us
    convert_element_type x4, other arithmetic, grad_z(): sum((v.astype(F32) for v in (parts[0], from_x, from_y))).astype(BF16)  10.4 us
  transfers between devices with their start and end apart: 85, of which 27 were waited for; matrix products, arithmetic and copies ran while one was open for 11% of the time, Pallas kernels for 40%

profile of v2, /device:TPU:0, one launch (start us, length us, event | category | flops | bytes accessed | tf_op | source)
XLA Modules:
  0.0 421.6 jit_solution(857006561085215296)
XLA Ops:
  1.3 3.7 shard_map.254
  5.0 6.4 %all-to-all-start = ((bf16[4,64,2176]{2,1,0:T(8,128)(2,1)}), bf16[4,64,2176]{2,1,0:T(8,128)(2,1)}, u32[]{:S(2)}, u32[]{:S(2)}) async-start(bf16[4,64,2176]{2,1,0:T(8,128)(2,1)} %get-tuple-element.207), calls=%async_computation | async-start | bytes 2228224 | tf_op jit(solution)/shard_map/all_to_all | solution.py:563
  11.7 1.6 collective-permute-start.1
  14.0 1.5 collective-permute-start.4
  15.5 6.7 %collective-permute-done.1 = bf16[2,80,1024]{2,1,0:T(8,128)(2,1)S(1)} collective-permute-done((bf16[2,80,1024]{2,1,0:T(8,128)(2,1)S(1)}, bf16[2,80,1024]{2,1,0:T(8,128)(2,1)S(1)}, u32[]{:S(2)}, u32[]{:S(2)}) %collective-permute-start.1) | collective-permute-done | bytes 327712 | tf_op jit(solution)/shard_map/ppermute | solution.py:536
  22.2 6.1 %collective-permute-done.2 = bf16[2,80,1024]{2,1,0:T(8,128)(2,1)S(1)} collective-permute-done((bf16[2,80,1024]{2,1,0:T(8,128)(2,1)S(1)}, bf16[2,80,1024]{2,1,0:T(8,128)(2,1)S(1)}, u32[]{:S(2)}, u32[]{:S(2)}) %collective-permute-start.2) | collective-permute-done | bytes 327712 | tf_op jit(solution)/shard_map/ppermute | solution.py:536
  29.1 6.8 %collective-permute-done.4 = bf16[2,80,1024]{2,1,0:T(8,128)(2,1)S(1)} collective-permute-done((bf16[2,80,1024]{2,1,0:T(8,128)(2,1)S(1)}, bf16[2,80,1024]{2,1,0:T(8,128)(2,1)S(1)}, u32[]{:S(2)}, u32[]{:S(2)}) %collective-permute-start.4) | collective-permute-done | bytes 327712 | tf_op jit(solution)/shard_map/ppermute | solution.py:536
  35.8 2.9 all-to-all-done.refs_0_.refs_10_.refs_20_
  38.7 1.5 collective-permute-start.5
  40.2 1.5 collective-permute-start.6
  41.7 4.2 %all-to-all-start.1 = ((bf16[4,64,2048]{2,1,0:T(8,128)(2,1)}), bf16[4,64,2048]{2,1,0:T(8,128)(2,1)}, u32[]{:S(2)}, u32[]{:S(2)}) async-start(bf16[4,64,2048]{2,1,0:T(8,128)(2,1)} %get-tuple-element.215), calls=%async_computation.1 | async-start | bytes 2097152 | tf_op jit(solution)/shard_map/all_to_all | solution.py:563
  46.0 2.3 pad_maximum_fusion.2
  48.3 16.3 %collective-permute-done.5.refs_1_.refs_11_.refs_21_ = bf16[4,64,2176]{2,1,0:T(8,128)(2,1)} collective-permute-done((bf16[4,64,2176]{2,1,0:T(8,128)(2,1)}, bf16[4,64,2176]{2,1,0:T(8,128)(2,1)}, u32[]{:S(2)}, u32[]{:S(2)}) %collective-permute-start.5) | collective-permute-done | bytes 1114144 | tf_op jit(solution)/shard_map/ppermute | solution.py:532
  69.5 1.6 collective-permute-start.7
  73.5 11.2 %collective-permute-done.7.refs_3_.refs_13_.refs_23_ = bf16[2,64,2176]{2,1,0:T(8,128)(2,1)} collective-permute-done((bf16[2,64,2176]{2,1,0:T(8,128)(2,1)S(1)}, bf16[2,64,2176]{2,1,0:T(8,128)(2,1)}, u32[]{:S(2)}, u32[]{:S(2)}) %collective-permute-start.7) | collective-permute-done | bytes 557088 | tf_op jit(solution)/shard_map/ppermute | solution.py:532
  89.1 9.8 %shard_map.255 = (bf16[640,1024]{1,0:T(8,128)(2,1)}, bf16[640,3072]{1,0:T(8,128)(2,1)}) custom-call(s32[3]{0:T(128)} %pad_add_fusion.place_ref, bf16[4,64,2176]{2,1,0:T(8,128)(2,1)} %all-to-all-done.refs_0_.refs_10_.refs_20_, bf16[4,64,2176]{2,1,0:T(8,128)(2,1)} %collective-permute-done.5.refs_1_.refs_11_.refs_21_, ...), custom_call_target="tpu_custom_call" | custom-call | flops 11000000512 | tf_op jit(solution)/shard_map/pallas_call | solution.py:260
  98.9 4.5 %all-to-all-start.2 = ((bf16[4,64,2048]{2,1,0:T(8,128)(2,1)}), bf16[4,64,2048]{2,1,0:T(8,128)(2,1)}, u32[]{:S(2)}, u32[]{:S(2)}) async-start(bf16[4,64,2048]{2,1,0:T(8,128)(2,1)} %get-tuple-element.242), calls=%async_computation.2 | async-start | bytes 2097152 | tf_op jit(solution)/shard_map/all_to_all | solution.py:563
  104.2 7.9 %collective-permute-done.14.refs_1_.refs_11_ = bf16[4,64,2048]{2,1,0:T(8,128)(2,1)} collective-permute-done((bf16[4,64,2048]{2,1,0:T(8,128)(2,1)}, bf16[4,64,2048]{2,1,0:T(8,128)(2,1)}, u32[]{:S(2)}, u32[]{:S(2)}) %collective-permute-start.14) | collective-permute-done | bytes 1048608 | tf_op jit(solution)/shard_map/ppermute | solution.py:532
  115.7 1.5 collective-permute-start.18
  117.9 15.7 %shard_map.256 = (bf16[2,320,1024]{2,1,0:T(8,128)(2,1)}, f32[2,320,1024]{2,1,0:T(8,128)}) custom-call(f32[2,320,1]{2,1,0:T(8,128)} %compare_select_fusion.bias_ref, bf16[2,320,3072]{2,1,0:T(8,128)(2,1)} %bitcast.148, bf16[2,320,3072]{2,1,0:T(8,128)(2,1)} %bitcast.149, bf16[2,320,3072]{2,1,0:T(8,128)(2,1)} %bitcast.150), custom_call_target="tpu_custom_call" | custom-call | flops 14080000000 | tf_op jit(solution)/shard_map/pallas_call | solution.py:133
  133.6 1.8 collective-permute-done.21
  136.5 1.5 collective-permute-start.24
  138.0 1.5 collective-permute-start.25
  140.5 18.4 %shard_map.257 = (f32[640,1024]{1,0:T(8,128)}, bf16[640,1024]{1,0:T(8,128)(2,1)}, bf16[640,4096]{1,0:T(8,128)(2,1)}, bf16[640,4096]{1,0:T(8,128)(2,1)}, bf16[640,2048]{1,0:T(8,128)(2,1)}) custom-call(s32[3]{0:T(128)} %pad_add_fusion.place_ref, bf16[4,64,2048]{2,1,0:T(8,128)(2,1)} %all-to-all-done.1.refs_0_.refs_10_, ...), custom_call_target="tpu_custom_call" | custom-call | flops 22000001024 | tf_op jit(solution)/shard_map/pallas_call | solution.py:260
  158.9 3.3 collective-permute-done.24.refs_1_
  167.4 1.5 collective-permute-start.29
  170.4 11.5 %shard_map.258 = (bf16[4,128,1024]{2,1,0:T(8,128)(2,1)S(1)}, bf16[4,128,1024]{2,1,0:T(8,128)(2,1)}, bf16[4,128,1024]{2,1,0:T(8,128)(2,1)}, bf16[4,128,1024]{2,1,0:T(8,128)(2,1)}) custom-call(s32[3]{0:T(128)S(1)} %copy-done.2, bf16[640,4096]{1,0:T(8,128)(2,1)} %get-tuple-element.362.a0_ref.a1_ref.refs_10_, ...), custom_call_target="tpu_custom_call" | custom-call | flops 10150215680 | tf_op jit(solution)/shard_map/pallas_call | solution.py:710
  186.3 26.9 %shard_map.259 = (bf16[640,4096]{1,0:T(8,128)(2,1)}, f32[1,4096]{1,0:T(1,128)}, f32[640,1024]{1,0:T(8,128)}, bf16[640,1024]{1,0:T(8,128)(2,1)}, bf16[640,1024]{1,0:T(8,128)(2,1)}, /*index=5*/f32[8,1024]{1,0:T(8,128)}) custom-call(s32[3]{0:T(128)} %pad_add_fusion.place_ref, bf16[4,64,2048]{2,1,0:T(8,128)(2,1)} %all-to-all-done.2.refs_0_, ...), custom_call_target="tpu_custom_call" | custom-call | flops 25300000768 | tf_op jit(solution)/shard_map/pallas_call | solution.py:260
  215.1 11.2 %shard_map.260 = bf16[2,320,1536]{2,1,0:T(8,128)(2,1)} custom-call(f32[2,320,1]{2,1,0:T(8,128)} %compare_select_fusion.bias_ref, bf16[2,320,3072]{2,1,0:T(8,128)(2,1)} %bitcast.151, bf16[2,320,3072]{2,1,0:T(8,128)(2,1)} %bitcast.152, bf16[2,320,3072]{2,1,0:T(8,128)(2,1)} %bitcast.153, f32[2,320,1024]{2,1,0:T(8,128)} %get-tuple-element.290.lse_ref, ...), custom_call_target="tpu_custom_call" | custom-call | flops 11440000000 | tf_op jit(solution)/shard_map/pallas_call | solution.py:133
  227.6 8.0 %shard_map.263 = (bf16[4,64,1024]{2,1,0:T(8,128)(2,1)S(1)}, bf16[4,64,1024]{2,1,0:T(8,128)(2,1)S(1)}, bf16[4,64,1024]{2,1,0:T(8,128)(2,1)}, bf16[4,64,1024]{2,1,0:T(8,128)(2,1)}) custom-call(s32[3]{0:T(128)S(1)} %copy-done.3, bf16[640,1024]{1,0:T(8,128)(2,1)} %get-tuple-element.288.refs_0_, bf16[640,1024]{1,0:T(8,128)(2,1)} %collective-permute-done.37.refs_1_, ...), custom_call_target="tpu_custom_call" | custom-call | flops 5075107840 | tf_op jit(solution)/shard_map/pallas_call | solution.py:710
  237.7 12.6 %shard_map.262 = (bf16[4,64,1536]{2,1,0:T(8,128)(2,1)S(1)}, bf16[4,64,1536]{2,1,0:T(8,128)(2,1)S(1)}, bf16[4,64,1536]{2,1,0:T(8,128)(2,1)}, bf16[4,64,1536]{2,1,0:T(8,128)(2,1)}) custom-call(s32[3]{0:T(128)S(1)} %copy-done.3, bf16[640,1024]{1,0:T(8,128)(2,1)} %get-tuple-element.288.refs_0_, bf16[640,1024]{1,0:T(8,128)(2,1)} %collective-permute-done.37.refs_1_, ...), custom_call_target="tpu_custom_call" | custom-call | flops 7612661760 | tf_op jit(solution)/shard_map/pallas_call | solution.py:710
  250.3 2.1 collective-permute-done.43
  252.4 2.8 add_convert_fusion
  255.2 4.2 %all-to-all-start.3 = ((bf16[4,128,1024]{2,1,0:T(8,128)(2,1)}), bf16[4,128,1024]{2,1,0:T(8,128)(2,1)}, u32[]{:S(2)}, u32[]{:S(2)}) async-start(bf16[4,128,1024]{2,1,0:T(8,128)(2,1)} %add_convert_fusion), calls=%async_computation.3 | async-start | bytes 2097152 | tf_op jit(solution)/shard_map/all_to_all | solution.py:563
  259.5 2.0 add_convert_fusion.6
  263.1 6.2 %shard_map.261 = (bf16[4,64,768]{2,1,0:T(8,128)(2,1)S(1)}, bf16[4,64,768]{2,1,0:T(8,128)(2,1)S(1)}, bf16[4,64,768]{2,1,0:T(8,128)(2,1)S(1)}, bf16[4,64,768]{2,1,0:T(8,128)(2,1)}) custom-call(s32[3]{0:T(128)S(1)} %copy-done.3, bf16[640,1024]{1,0:T(8,128)(2,1)} %get-tuple-element.236.refs_0_, bf16[640,1024]{1,0:T(8,128)(2,1)} %copy-done.23, ...), custom_call_target="tpu_custom_call" | custom-call | flops 3806330880 | tf_op jit(solution)/shard_map/pallas_call | solution.py:710
  270.6 11.1 %shard_map.264 = bf16[2,320,1536]{2,1,0:T(8,128)(2,1)} custom-call(f32[2,320,1]{2,1,0:T(8,128)} %compare_select_fusion.bias_ref, bf16[2,320,3072]{2,1,0:T(8,128)(2,1)} %bitcast.154, bf16[2,320,3072]{2,1,0:T(8,128)(2,1)} %bitcast.155, bf16[2,320,3072]{2,1,0:T(8,128)(2,1)} %bitcast.156, f32[2,320,1024]{2,1,0:T(8,128)} %get-tuple-element.290.lse_ref, ...), custom_call_target="tpu_custom_call" | custom-call | flops 11440000000 | tf_op jit(solution)/shard_map/pallas_call | solution.py:133
  281.7 3.9 all-to-all-done.3
  288.0 2.3 add_convert_fusion.5
  290.3 4.3 %all-to-all-start.4 = ((bf16[4,64,1024]{2,1,0:T(8,128)(2,1)}), bf16[4,64,1024]{2,1,0:T(8,128)(2,1)}, u32[]{:S(2)}, u32[]{:S(2)}) async-start(bf16[4,64,1024]{2,1,0:T(8,128)(2,1)} %add_convert_fusion.5), calls=%async_computation.4 | async-start | bytes 1048576 | tf_op jit(solution)/shard_map/all_to_all | solution.py:563
  294.7 2.2 add_convert_fusion.4
  298.1 1.8 add_convert_fusion.8
  301.2 5.5 %shard_map.265 = (bf16[4,64,768]{2,1,0:T(8,128)(2,1)S(1)}, bf16[4,64,768]{2,1,0:T(8,128)(2,1)S(1)}, bf16[4,64,768]{2,1,0:T(8,128)(2,1)S(1)}, bf16[4,64,768]{2,1,0:T(8,128)(2,1)S(1)}) custom-call(s32[3]{0:T(128)S(1)} %copy-done.3, bf16[640,1024]{1,0:T(8,128)(2,1)} %get-tuple-element.236.refs_0_, bf16[640,1024]{1,0:T(8,128)(2,1)} %copy-done.23, ...), custom_call_target="tpu_custom_call" | custom-call | flops 3806330880 | tf_op jit(solution)/shard_map/pallas_call | solution.py:710
  307.5 14.9 %shard_map.266 = (bf16[640,1024]{1,0:T(8,128)(2,1)}, f32[1,3072]{1,0:T(1,128)}, f32[8,1024]{1,0:T(8,128)}) custom-call(s32[3]{0:T(128)} %pad_add_fusion.place_ref, bf16[4,64,2176]{2,1,0:T(8,128)(2,1)} %all-to-all-done.refs_0_.refs_10_.refs_20_, bf16[4,64,2176]{2,1,0:T(8,128)(2,1)} %collective-permute-done.5.refs_1_.refs_11_.refs_21_, ...), custom_call_target="tpu_custom_call" | custom-call | flops 14300000256 | tf_op jit(solution)/shard_map/pallas_call | solution.py:260
  322.4 1.5 shard_map.267
  325.2 2.6 add_convert_fusion.3
  327.8 5.0 %all-to-all-start.5 = ((bf16[4,64,1536]{2,1,0:T(8,128)(2,1)}), bf16[4,64,1536]{2,1,0:T(8,128)(2,1)S(1)}, u32[]{:S(2)}, u32[]{:S(2)}) async-start(bf16[4,64,1536]{2,1,0:T(8,128)(2,1)} %add_convert_fusion.3), calls=%async_computation.5 | async-start | bytes 1572864 | tf_op jit(solution)/shard_map/all_to_all | solution.py:563
  334.8 1.4 reduce_sum.59.refs_8_
  336.3 1.3 collective-permute-start.60
  340.9 13.2 %shard_map.268 = bf16[640,1024]{1,0:T(8,128)(2,1)} custom-call(s32[3]{0:T(128)} %pad_add_fusion.place_ref, bf16[4,64,2048]{2,1,0:T(8,128)(2,1)} %all-to-all-done.2.refs_0_, bf16[4,64,2048]{2,1,0:T(8,128)(2,1)} %copy-done.16, bf16[4,64,2048]{2,1,0:T(8,128)(2,1)} %copy-done.17, bf16[2,64,2048]{2,1,0:T(8,128)(2,1)} %copy-done.29, ...), custom_call_target="tpu_custom_call" | custom-call | flops 12099999744 | tf_op jit(solution)/shard_map/pallas_call | solution.py:260
  355.4 2.7 add_convert_fusion.2
  358.1 5.2 %all-to-all-start.6 = ((bf16[4,64,1536]{2,1,0:T(8,128)(2,1)}), bf16[4,64,1536]{2,1,0:T(8,128)(2,1)S(1)}, u32[]{:S(2)}, u32[]{:S(2)}) async-start(bf16[4,64,1536]{2,1,0:T(8,128)(2,1)} %add_convert_fusion.2), calls=%async_computation.6 | async-start | bytes 1572864 | tf_op jit(solution)/shard_map/all_to_all | solution.py:563
  363.3 2.7 fusion.6
  366.8 1.4 reshape.311
  368.2 1.5 constant_dynamic-slice_fusion.5
  375.3 12.7 %collective-permute-done.61.refs_5_ = bf16[64,1536]{1,0:T(8,128)(2,1)S(1)} collective-permute-done((bf16[64,1536]{1,0:T(8,128)(2,1)}, bf16[64,1536]{1,0:T(8,128)(2,1)S(1)}, u32[]{:S(2)}, u32[]{:S(2)}) %collective-permute-start.61) | collective-permute-done | bytes 196640 | tf_op jit(solution)/shard_map/ppermute | solution.py:532
  392.9 4.0 shard_map.269
  396.9 4.3 %collective-permute-done.71 = bf16[4,80,1024]{2,1,0:T(8,128)(2,1)S(1)} collective-permute-done((bf16[4,80,1024]{2,1,0:T(8,128)(2,1)}, bf16[4,80,1024]{2,1,0:T(8,128)(2,1)S(1)}, u32[]{:S(2)}, u32[]{:S(2)}) %collective-permute-start.71) | collective-permute-done | bytes 655392 | tf_op jit(solution)/shard_map/ppermute | solution.py:536
  401.2 4.6 %collective-permute-done.72.refs_1_ = bf16[64,1536]{1,0:T(8,128)(2,1)S(1)} collective-permute-done((bf16[64,1536]{1,0:T(8,128)(2,1)}, bf16[64,1536]{1,0:T(8,128)(2,1)S(1)}, u32[]{:S(2)}, u32[]{:S(2)}) %collective-permute-start.72) | collective-permute-done | bytes 196640 | tf_op jit(solution)/shard_map/ppermute | solution.py:532
  405.9 2.1 collective-permute-start.73
  408.0 2.4 collective-permute-start.74
  411.4 1.7 slice_bitcast_fusion
  413.2 2.6 collective-permute-done.75
  418.8 2.6 shard_map.270
  (262 shorter events, 69.4 us)
Async XLA Ops:
  5.0 33.7 %all-to-all-start = ((bf16[4,64,2176]{2,1,0:T(8,128)(2,1)}), bf16[4,64,2176]{2,1,0:T(8,128)(2,1)}, u32[]{:S(2)}, u32[]{:S(2)}) async-start(bf16[4,64,2176]{2,1,0:T(8,128)(2,1)} %get-tuple-element.207), calls=%async_computation | async-start | bytes 2228224 | tf_op jit(solution)/shard_map/all_to_all | solution.py:563
  13.2 15.1 %collective-permute-start.2 = (bf16[2,80,1024]{2,1,0:T(8,128)(2,1)S(1)}, bf16[2,80,1024]{2,1,0:T(8,128)(2,1)S(1)}, u32[]{:S(2)}, u32[]{:S(2)}) collective-permute-start(bf16[2,80,1024]{2,1,0:T(8,128)(2,1)S(1)} %get-tuple-element.421), channel_id=1, source_target_pairs={{0,3},{1,2},{2,1},{3,0},{4,7},{5,6},{6,5},{7,4},{8,11},{9,10},{10,... | collective-permute-start | bytes 983048 | tf_op jit(solution)/shard_map/ppermute | solution.py:536
  13.6 14.8 %collective-permute-start.3 = (bf16[2,80,1024]{2,1,0:T(8,128)(2,1)S(1)}, bf16[2,80,1024]{2,1,0:T(8,128)(2,1)S(1)}, u32[]{:S(2)}, u32[]{:S(2)}) collective-permute-start(bf16[2,80,1024]{2,1,0:T(8,128)(2,1)S(1)} %get-tuple-element.419), channel_id=1, source_target_pairs={{0,1},{1,0},{2,3},{3,2},{4,5},{5,4},{6,7},{7,6},{8,9},{9,8},{10,11... | collective-permute-start | bytes 983048 | tf_op jit(solution)/shard_map/ppermute | solution.py:536
  14.0 21.8 %collective-permute-start.4 = (bf16[2,80,1024]{2,1,0:T(8,128)(2,1)S(1)}, bf16[2,80,1024]{2,1,0:T(8,128)(2,1)S(1)}, u32[]{:S(2)}, u32[]{:S(2)}) collective-permute-start(bf16[2,80,1024]{2,1,0:T(8,128)(2,1)S(1)} %get-tuple-element.418), channel_id=1, source_target_pairs={{0,2},{1,3},{2,0},{3,1},{4,6},{5,7},{6,4},{7,5},{8,10},{9,11},{10,... | collective-permute-start | bytes 983048 | tf_op jit(solution)/shard_map/ppermute | solution.py:536
  38.7 25.8 %collective-permute-start.5 = (bf16[4,64,2176]{2,1,0:T(8,128)(2,1)}, bf16[4,64,2176]{2,1,0:T(8,128)(2,1)}, u32[]{:S(2)}, u32[]{:S(2)}) collective-permute-start(bf16[4,64,2176]{2,1,0:T(8,128)(2,1)} %all-to-all-done.refs_0_.refs_10_.refs_20_), channel_id=1, source_target_pairs={{0,2},{2,0},{1,3},{3,1},{4,6},{6,4},{5,7},{7,5},{8,10},{10,8},{9,1... | collective-permute-start | bytes 3342344 | tf_op jit(solution)/shard_map/ppermute | solution.py:532
  40.2 25.6 %collective-permute-start.6 = (bf16[4,64,2176]{2,1,0:T(8,128)(2,1)}, bf16[4,64,2176]{2,1,0:T(8,128)(2,1)}, u32[]{:S(2)}, u32[]{:S(2)}) collective-permute-start(bf16[4,64,2176]{2,1,0:T(8,128)(2,1)} %all-to-all-done.refs_0_.refs_10_.refs_20_), channel_id=1, source_target_pairs={{0,4},{4,0},{1,5},{5,1},{2,6},{6,2},{3,7},{7,3},{8,12},{12,8},{9,1... | collective-permute-start | bytes 3342344 | tf_op jit(solution)/shard_map/ppermute | solution.py:532
  41.7 31.8 %all-to-all-start.1 = ((bf16[4,64,2048]{2,1,0:T(8,128)(2,1)}), bf16[4,64,2048]{2,1,0:T(8,128)(2,1)}, u32[]{:S(2)}, u32[]{:S(2)}) async-start(bf16[4,64,2048]{2,1,0:T(8,128)(2,1)} %get-tuple-element.215), calls=%async_computation.1 | async-start | bytes 2097152 | tf_op jit(solution)/shard_map/all_to_all | solution.py:563
  65.8 20.2 %collective-permute-start.10 = (bf16[4,64,2176]{2,1,0:T(8,128)(2,1)}, bf16[4,64,2176]{2,1,0:T(8,128)(2,1)}, u32[]{:S(2)}, u32[]{:S(2)}) collective-permute-start(bf16[4,64,2176]{2,1,0:T(8,128)(2,1)} %collective-permute-done.5.refs_1_.refs_11_.refs_21_), channel_id=1, source_target_pairs={{0,1},{1,0},{2,3},{3,2},{4,5},{5,4},{6,7},{7,6},{8,9},{9,8},{10,11... | collective-permute-start | bytes 3342344 | tf_op jit(solution)/shard_map/ppermute | solution.py:532
  66.9 19.1 %collective-permute-start.11 = (bf16[4,64,2176]{2,1,0:T(8,128)(2,1)}, bf16[4,64,2176]{2,1,0:T(8,128)(2,1)}, u32[]{:S(2)}, u32[]{:S(2)}) collective-permute-start(bf16[4,64,2176]{2,1,0:T(8,128)(2,1)} %collective-permute-done.6.refs_2_.refs_12_.refs_22_), channel_id=1, source_target_pairs={{0,1},{1,0},{2,3},{3,2},{4,5},{5,4},{6,7},{7,6},{8,9},{9,8},{10,11... | collective-permute-start | bytes 3342344 | tf_op jit(solution)/shard_map/ppermute | solution.py:532
  68.5 17.4 %collective-permute-start.9 = (bf16[4,64,2176]{2,1,0:T(8,128)(2,1)}, bf16[4,64,2176]{2,1,0:T(8,128)(2,1)}, u32[]{:S(2)}, u32[]{:S(2)}) collective-permute-start(bf16[4,64,2176]{2,1,0:T(8,128)(2,1)} %all-to-all-done.refs_0_.refs_10_.refs_20_), channel_id=1, source_target_pairs={{0,1},{1,0},{2,3},{3,2},{4,5},{5,4},{6,7},{7,6},{8,9},{9,8},{10,11... | collective-permute-start | bytes 3342344 | tf_op jit(solution)/shard_map/ppermute | solution.py:532
  69.5 15.2 %collective-permute-start.7 = (bf16[2,64,2176]{2,1,0:T(8,128)(2,1)S(1)}, bf16[2,64,2176]{2,1,0:T(8,128)(2,1)}, u32[]{:S(2)}, u32[]{:S(2)}) collective-permute-start(bf16[2,64,2176]{2,1,0:T(8,128)(2,1)S(1)} %slice.90), channel_id=1, source_target_pairs={{0,4},{4,0},{1,5},{5,1},{2,6},{6,2},{3,7},{7,3},{8,12},{12,8},{9,1... | collective-permute-start | bytes 1671176 | tf_op jit(solution)/shard_map/ppermute | solution.py:532
  71.1 14.8 %collective-permute-start.8 = (bf16[2,64,2176]{2,1,0:T(8,128)(2,1)S(1)}, bf16[2,64,2176]{2,1,0:T(8,128)(2,1)}, u32[]{:S(2)}, u32[]{:S(2)}) collective-permute-start(bf16[2,64,2176]{2,1,0:T(8,128)(2,1)S(1)} %slice.91), channel_id=1, source_target_pairs={{0,2},{2,0},{1,3},{3,1},{4,6},{6,4},{5,7},{7,5},{8,10},{10,8},{9,1... | collective-permute-start | bytes 1671176 | tf_op jit(solution)/shard_map/ppermute | solution.py:532
  86.6 25.5 %collective-permute-start.14 = (bf16[4,64,2048]{2,1,0:T(8,128)(2,1)}, bf16[4,64,2048]{2,1,0:T(8,128)(2,1)}, u32[]{:S(2)}, u32[]{:S(2)}) collective-permute-start(bf16[4,64,2048]{2,1,0:T(8,128)(2,1)} %all-to-all-done.1.refs_0_.refs_10_), channel_id=1, source_target_pairs={{0,2},{2,0},{1,3},{3,1},{4,6},{6,4},{5,7},{7,5},{8,10},{10,8},{9,1... | collective-permute-start | bytes 3145736 | tf_op jit(solution)/shard_map/ppermute | solution.py:532
  87.2 25.2 %collective-permute-start.15 = (bf16[4,64,2048]{2,1,0:T(8,128)(2,1)}, bf16[4,64,2048]{2,1,0:T(8,128)(2,1)}, u32[]{:S(2)}, u32[]{:S(2)}) collective-permute-start(bf16[4,64,2048]{2,1,0:T(8,128)(2,1)} %all-to-all-done.1.refs_0_.refs_10_), channel_id=1, source_target_pairs={{0,4},{4,0},{1,5},{5,1},{2,6},{6,2},{3,7},{7,3},{8,12},{12,8},{9,1... | collective-permute-start | bytes 3145736 | tf_op jit(solution)/shard_map/ppermute | solution.py:532
  87.7 24.7 %collective-permute-start.16 = (bf16[4,64,2048]{2,1,0:T(8,128)(2,1)}, bf16[4,64,2048]{2,1,0:T(8,128)(2,1)}, u32[]{:S(2)}, u32[]{:S(2)}) collective-permute-start(bf16[4,64,2048]{2,1,0:T(8,128)(2,1)} %all-to-all-done.1.refs_0_.refs_10_), channel_id=1, source_target_pairs={{0,1},{1,0},{2,3},{3,2},{4,5},{5,4},{6,7},{7,6},{8,9},{9,8},{10,11... | collective-permute-start | bytes 3145736 | tf_op jit(solution)/shard_map/ppermute | solution.py:532
  98.9 36.6 %all-to-all-start.2 = ((bf16[4,64,2048]{2,1,0:T(8,128)(2,1)}), bf16[4,64,2048]{2,1,0:T(8,128)(2,1)}, u32[]{:S(2)}, u32[]{:S(2)}) async-start(bf16[4,64,2048]{2,1,0:T(8,128)(2,1)} %get-tuple-element.242), calls=%async_computation.2 | async-start | bytes 2097152 | tf_op jit(solution)/shard_map/all_to_all | solution.py:563
  113.5 22.0 %collective-permute-start.19 = (bf16[4,64,2048]{2,1,0:T(8,128)(2,1)}, bf16[4,64,2048]{2,1,0:T(8,128)(2,1)}, u32[]{:S(2)}, u32[]{:S(2)}) collective-permute-start(bf16[4,64,2048]{2,1,0:T(8,128)(2,1)} %collective-permute-done.14.refs_1_.refs_11_), channel_id=1, source_target_pairs={{0,1},{1,0},{2,3},{3,2},{4,5},{5,4},{6,7},{7,6},{8,9},{9,8},{10,11... | collective-permute-start | bytes 3145736 | tf_op jit(solution)/shard_map/ppermute | solution.py:532
  114.6 20.8 %collective-permute-start.20 = (bf16[4,64,2048]{2,1,0:T(8,128)(2,1)}, bf16[4,64,2048]{2,1,0:T(8,128)(2,1)}, u32[]{:S(2)}, u32[]{:S(2)}) collective-permute-start(bf16[4,64,2048]{2,1,0:T(8,128)(2,1)} %collective-permute-done.15.refs_2_.refs_12_), channel_id=1, source_target_pairs={{0,1},{1,0},{2,3},{3,2},{4,5},{5,4},{6,7},{7,6},{8,9},{9,8},{10,11... | collective-permute-start | bytes 3145736 | tf_op jit(solution)/shard_map/ppermute | solution.py:532
  115.2 20.3 %collective-permute-start.17 = (bf16[2,64,2048]{2,1,0:T(8,128)(2,1)S(1)}, bf16[2,64,2048]{2,1,0:T(8,128)(2,1)}, u32[]{:S(2)}, u32[]{:S(2)}) collective-permute-start(bf16[2,64,2048]{2,1,0:T(8,128)(2,1)S(1)} %slice.102), channel_id=1, source_target_pairs={{0,4},{4,0},{1,5},{5,1},{2,6},{6,2},{3,7},{7,3},{8,12},{12,8},{9,1... | collective-permute-start | bytes 1572872 | tf_op jit(solution)/shard_map/ppermute | solution.py:532
  115.7 19.8 %collective-permute-start.18 = (bf16[2,64,2048]{2,1,0:T(8,128)(2,1)S(1)}, bf16[2,64,2048]{2,1,0:T(8,128)(2,1)}, u32[]{:S(2)}, u32[]{:S(2)}) collective-permute-start(bf16[2,64,2048]{2,1,0:T(8,128)(2,1)S(1)} %slice.103), channel_id=1, source_target_pairs={{0,2},{2,0},{1,3},{3,1},{4,6},{6,4},{5,7},{7,5},{8,10},{10,8},{9,1... | collective-permute-start | bytes 1572872 | tf_op jit(solution)/shard_map/ppermute | solution.py:532
  117.9 17.5 %collective-permute-start.21 = (bf16[2,80,1024]{2,1,0:T(8,128)(2,1)}, bf16[2,80,1024]{2,1,0:T(8,128)(2,1)S(1)}, u32[]{:S(2)}, u32[]{:S(2)}) collective-permute-start(bf16[2,80,1024]{2,1,0:T(8,128)(2,1)} %dynamic-slice_bitcast_fusion), channel_id=1, source_target_pairs={{0,3},{1,2},{2,1},{3,0},{4,7},{5,6},{6,5},{7,4},{8,11},{9,10},{10,... | collective-permute-start | bytes 983048 | tf_op jit(solution)/shard_map/ppermute | solution.py:536
  136.5 25.7 %collective-permute-start.24 = (bf16[4,64,2048]{2,1,0:T(8,128)(2,1)}, bf16[4,64,2048]{2,1,0:T(8,128)(2,1)S(1)}, u32[]{:S(2)}, u32[]{:S(2)}) collective-permute-start(bf16[4,64,2048]{2,1,0:T(8,128)(2,1)} %all-to-all-done.2.refs_0_), channel_id=1, source_target_pairs={{0,2},{2,0},{1,3},{3,1},{4,6},{6,4},{5,7},{7,5},{8,10},{10,8},{9,1... | collective-permute-start | bytes 3145736 | tf_op jit(solution)/shard_map/ppermute | solution.py:532
  138.0 25.4 %collective-permute-start.25 = (bf16[4,64,2048]{2,1,0:T(8,128)(2,1)}, bf16[4,64,2048]{2,1,0:T(8,128)(2,1)S(1)}, u32[]{:S(2)}, u32[]{:S(2)}) collective-permute-start(bf16[4,64,2048]{2,1,0:T(8,128)(2,1)} %all-to-all-done.2.refs_0_), channel_id=1, source_target_pairs={{0,4},{4,0},{1,5},{5,1},{2,6},{6,2},{3,7},{7,3},{8,12},{12,8},{9,1... | collective-permute-start | bytes 3145736 | tf_op jit(solution)/shard_map/ppermute | solution.py:532
  139.5 23.9 %collective-permute-start.26 = (bf16[4,64,2048]{2,1,0:T(8,128)(2,1)}, bf16[4,64,2048]{2,1,0:T(8,128)(2,1)S(1)}, u32[]{:S(2)}, u32[]{:S(2)}) collective-permute-start(bf16[4,64,2048]{2,1,0:T(8,128)(2,1)} %all-to-all-done.2.refs_0_), channel_id=1, source_target_pairs={{0,1},{1,0},{2,3},{3,2},{4,5},{5,4},{6,7},{7,6},{8,9},{9,8},{10,11... | collective-permute-start | bytes 3145736 | tf_op jit(solution)/shard_map/ppermute | solution.py:532
  140.0 23.5 %collective-permute-start.27 = (bf16[640,1024]{1,0:T(8,128)(2,1)S(1)}, bf16[640,1024]{1,0:T(8,128)(2,1)S(1)}, u32[]{:S(2)}, u32[]{:S(2)}) collective-permute-start(bf16[640,1024]{1,0:T(8,128)(2,1)S(1)} %bitcast_select_fusion.g_ref.refs_30_), channel_id=1, source_target_pairs={{0,1},{1,0},{2,3},{3,2},{4,5},{5,4},{6,7},{7,6},{8,9},{9,8},{10,11... | collective-permute-start | bytes 3932168 | tf_op jit(solution)/shard_map/ppermute | solution.py:532
  165.7 16.9 %collective-permute-start.31 = (bf16[4,64,2048]{2,1,0:T(8,128)(2,1)S(1)}, bf16[4,64,2048]{2,1,0:T(8,128)(2,1)S(1)}, u32[]{:S(2)}, u32[]{:S(2)}) collective-permute-start(bf16[4,64,2048]{2,1,0:T(8,128)(2,1)S(1)} %collective-permute-done.24.refs_1_), channel_id=1, source_target_pairs={{0,1},{1,0},{2,3},{3,2},{4,5},{5,4},{6,7},{7,6},{8,9},{9,8},{10,11... | collective-permute-start | bytes 3145736 | tf_op jit(solution)/shard_map/ppermute | solution.py:532
  167.0 15.6 %collective-permute-start.32 = (bf16[4,64,2048]{2,1,0:T(8,128)(2,1)S(1)}, bf16[4,64,2048]{2,1,0:T(8,128)(2,1)S(1)}, u32[]{:S(2)}, u32[]{:S(2)}) collective-permute-start(bf16[4,64,2048]{2,1,0:T(8,128)(2,1)S(1)} %copy-done.18), channel_id=1, source_target_pairs={{0,1},{1,0},{2,3},{3,2},{4,5},{5,4},{6,7},{7,6},{8,9},{9,8},{10,11... | collective-permute-start | bytes 3145736 | tf_op jit(solution)/shard_map/ppermute | solution.py:532
  167.4 14.5 %collective-permute-start.29 = (bf16[2,64,2048]{2,1,0:T(8,128)(2,1)S(1)}, bf16[2,64,2048]{2,1,0:T(8,128)(2,1)S(1)}, u32[]{:S(2)}, u32[]{:S(2)}) collective-permute-start(bf16[2,64,2048]{2,1,0:T(8,128)(2,1)S(1)} %slice.104), channel_id=1, source_target_pairs={{0,4},{4,0},{1,5},{5,1},{2,6},{6,2},{3,7},{7,3},{8,12},{12,8},{9,1... | collective-permute-start | bytes 1572872 | tf_op jit(solution)/shard_map/ppermute | solution.py:532
  168.9 13.7 %collective-permute-start.30 = (bf16[2,64,2048]{2,1,0:T(8,128)(2,1)S(1)}, bf16[2,64,2048]{2,1,0:T(8,128)(2,1)S(1)}, u32[]{:S(2)}, u32[]{:S(2)}) collective-permute-start(bf16[2,64,2048]{2,1,0:T(8,128)(2,1)S(1)} %slice.105), channel_id=1, source_target_pairs={{0,2},{2,0},{1,3},{3,1},{4,6},{6,4},{5,7},{7,5},{8,10},{10,8},{9,1... | collective-permute-start | bytes 1572872 | tf_op jit(solution)/shard_map/ppermute | solution.py:532
  183.6 29.6 %collective-permute-start.38 = (bf16[640,1024]{1,0:T(8,128)(2,1)S(1)}, bf16[640,1024]{1,0:T(8,128)(2,1)S(1)}, u32[]{:S(2)}, u32[]{:S(2)}) collective-permute-start(bf16[640,1024]{1,0:T(8,128)(2,1)S(1)} %copy-done.21), channel_id=1, source_target_pairs={{0,1},{1,0},{2,3},{3,2},{4,5},{5,4},{6,7},{7,6},{8,9},{9,8},{10,11... | collective-permute-start | bytes 3932168 | tf_op jit(solution)/shard_map/ppermute | solution.py:532
  184.1 29.1 %collective-permute-start.36 = (bf16[640,1024]{1,0:T(8,128)(2,1)S(1)}, bf16[640,1024]{1,0:T(8,128)(2,1)}, u32[]{:S(2)}, u32[]{:S(2)}) collective-permute-start(bf16[640,1024]{1,0:T(8,128)(2,1)S(1)} %bitcast.139), channel_id=1, source_target_pairs={{0,1},{1,0},{2,3},{3,2},{4,5},{5,4},{6,7},{7,6},{8,9},{9,8},{10,11... | collective-permute-start | bytes 3932168 | tf_op jit(solution)/shard_map/ppermute | solution.py:532
  184.2 29.1 %collective-permute-start.37 = (bf16[640,1024]{1,0:T(8,128)(2,1)}, bf16[640,1024]{1,0:T(8,128)(2,1)}, u32[]{:S(2)}, u32[]{:S(2)}) collective-permute-start(bf16[640,1024]{1,0:T(8,128)(2,1)} %get-tuple-element.288.refs_0_), channel_id=1, source_target_pairs={{0,1},{1,0},{2,3},{3,2},{4,5},{5,4},{6,7},{7,6},{8,9},{9,8},{10,11... | collective-permute-start | bytes 3932168 | tf_op jit(solution)/shard_map/ppermute | solution.py:532
  184.7 28.6 %collective-permute-start.35 = (bf16[4,128,1024]{2,1,0:T(8,128)(2,1)}, bf16[4,128,1024]{2,1,0:T(8,128)(2,1)S(1)}, u32[]{:S(2)}, u32[]{:S(2)}) collective-permute-start(bf16[4,128,1024]{2,1,0:T(8,128)(2,1)} %get-tuple-element.285), channel_id=1, source_target_pairs={{0,4},{4,0},{1,5},{5,1},{2,6},{6,2},{3,7},{7,3},{8,12},{12,8},{9,1... | collective-permute-start | bytes 3145736 | tf_op jit(solution)/shard_map/ppermute | solution.py:532
  213.3 13.0 %collective-permute-start.39 = (bf16[640,4096]{1,0:T(8,128)(2,1)}, bf16[640,4096]{1,0:T(8,128)(2,1)}, u32[]{:S(2)}, u32[]{:S(2)}) collective-permute-start(bf16[640,4096]{1,0:T(8,128)(2,1)} %get-tuple-element.292.refs_2_), channel_id=1, source_target_pairs={{0,1},{1,0},{2,3},{3,2},{4,5},{5,4},{6,7},{7,6},{8,9},{9,8},{10,11... | collective-permute-start | bytes 15728648 | tf_op jit(solution)/shard_map/ppermute | solution.py:532
  213.8 36.4 %collective-permute-start.44 = (bf16[4,128,1024]{2,1,0:T(8,128)(2,1)}, bf16[4,128,1024]{2,1,0:T(8,128)(2,1)}, u32[]{:S(2)}, u32[]{:S(2)}) collective-permute-start(bf16[4,128,1024]{2,1,0:T(8,128)(2,1)} %get-tuple-element.316), channel_id=1, source_target_pairs={{0,4},{4,0},{1,5},{5,1},{2,6},{6,2},{3,7},{7,3},{8,12},{12,8},{9,1... | collective-permute-start | bytes 3145736 | tf_op jit(solution)/shard_map/ppermute | solution.py:532
  226.3 36.8 %collective-permute-start.41 = (bf16[640,1536]{1,0:T(8,128)(2,1)}, bf16[640,1536]{1,0:T(8,128)(2,1)}, u32[]{:S(2)}, u32[]{:S(2)}) collective-permute-start(bf16[640,1536]{1,0:T(8,128)(2,1)} %bitcast.131), channel_id=1, source_target_pairs={{0,1},{1,0},{2,3},{3,2},{4,5},{5,4},{6,7},{7,6},{8,9},{9,8},{10,11... | collective-permute-start | bytes 5898248 | tf_op jit(solution)/shard_map/ppermute | solution.py:532
  226.8 25.6 %collective-permute-start.43 = (bf16[4,128,1024]{2,1,0:T(8,128)(2,1)S(1)}, bf16[4,128,1024]{2,1,0:T(8,128)(2,1)S(1)}, u32[]{:S(2)}, u32[]{:S(2)}) collective-permute-start(bf16[4,128,1024]{2,1,0:T(8,128)(2,1)S(1)} %add_convert_fusion.1), channel_id=1, source_target_pairs={{0,2},{2,0},{1,3},{3,1},{4,6},{6,4},{5,7},{7,5},{8,10},{10,8},{9,1... | collective-permute-start | bytes 3145736 | tf_op jit(solution)/shard_map/ppermute | solution.py:532
  235.7 16.7 %collective-permute-start.42 = (bf16[4,64,1024]{2,1,0:T(8,128)(2,1)}, bf16[4,64,1024]{2,1,0:T(8,128)(2,1)}, u32[]{:S(2)}, u32[]{:S(2)}) collective-permute-start(bf16[4,64,1024]{2,1,0:T(8,128)(2,1)} %get-tuple-element.313), channel_id=1, source_target_pairs={{0,4},{4,0},{1,5},{5,1},{2,6},{6,2},{3,7},{7,3},{8,12},{12,8},{9,1... | collective-permute-start | bytes 1572872 | tf_op jit(solution)/shard_map/ppermute | solution.py:532
  236.5 45.2 %collective-permute-start.47 = (bf16[4,64,1024]{2,1,0:T(8,128)(2,1)}, bf16[4,64,1024]{2,1,0:T(8,128)(2,1)}, u32[]{:S(2)}, u32[]{:S(2)}) collective-permute-start(bf16[4,64,1024]{2,1,0:T(8,128)(2,1)} %get-tuple-element.323), channel_id=1, source_target_pairs={{0,4},{4,0},{1,5},{5,1},{2,6},{6,2},{3,7},{7,3},{8,12},{12,8},{9,1... | collective-permute-start | bytes 1572872 | tf_op jit(solution)/shard_map/ppermute | solution.py:532
  255.2 30.3 %all-to-all-start.3 = ((bf16[4,128,1024]{2,1,0:T(8,128)(2,1)}), bf16[4,128,1024]{2,1,0:T(8,128)(2,1)}, u32[]{:S(2)}, u32[]{:S(2)}) async-start(bf16[4,128,1024]{2,1,0:T(8,128)(2,1)} %add_convert_fusion), calls=%async_computation.3 | async-start | bytes 2097152 | tf_op jit(solution)/shard_map/all_to_all | solution.py:563
  261.5 20.1 %collective-permute-start.46 = (bf16[4,64,1024]{2,1,0:T(8,128)(2,1)}, bf16[4,64,1024]{2,1,0:T(8,128)(2,1)}, u32[]{:S(2)}, u32[]{:S(2)}) collective-permute-start(bf16[4,64,1024]{2,1,0:T(8,128)(2,1)} %add_convert_fusion.6), channel_id=1, source_target_pairs={{0,2},{2,0},{1,3},{3,1},{4,6},{6,4},{5,7},{7,5},{8,10},{10,8},{9,1... | collective-permute-start | bytes 1572872 | tf_op jit(solution)/shard_map/ppermute | solution.py:532
  262.3 19.3 %collective-permute-start.48 = (bf16[4,64,1536]{2,1,0:T(8,128)(2,1)}, bf16[4,64,1536]{2,1,0:T(8,128)(2,1)}, u32[]{:S(2)}, u32[]{:S(2)}) collective-permute-start(bf16[4,64,1536]{2,1,0:T(8,128)(2,1)} %get-tuple-element.324), channel_id=1, source_target_pairs={{0,4},{4,0},{1,5},{5,1},{2,6},{6,2},{3,7},{7,3},{8,12},{12,8},{9,1... | collective-permute-start | bytes 2359304 | tf_op jit(solution)/shard_map/ppermute | solution.py:532
  269.4 16.2 %collective-permute-start.45 = (bf16[4,64,768]{2,1,0:T(8,128)(2,1)}, bf16[4,64,768]{2,1,0:T(8,128)(2,1)}, u32[]{:S(2)}, u32[]{:S(2)}) collective-permute-start(bf16[4,64,768]{2,1,0:T(8,128)(2,1)} %get-tuple-element.320), channel_id=1, source_target_pairs={{0,2},{2,0},{1,3},{3,1},{4,6},{6,4},{5,7},{7,5},{8,10},{10,8},{9,1... | collective-permute-start | bytes 1179656 | tf_op jit(solution)/shard_map/ppermute | solution.py:532
  285.5 15.6 %collective-permute-start.49 = (bf16[640,1536]{1,0:T(8,128)(2,1)}, bf16[640,1536]{1,0:T(8,128)(2,1)}, u32[]{:S(2)}, u32[]{:S(2)}) collective-permute-start(bf16[640,1536]{1,0:T(8,128)(2,1)} %bitcast.134), channel_id=1, source_target_pairs={{0,1},{1,0},{2,3},{3,2},{4,5},{5,4},{6,7},{7,6},{8,9},{9,8},{10,11... | collective-permute-start | bytes 5898248 | tf_op jit(solution)/shard_map/ppermute | solution.py:532
  286.4 37.4 %collective-permute-start.54 = (bf16[4,64,1536]{2,1,0:T(8,128)(2,1)}, bf16[4,64,1536]{2,1,0:T(8,128)(2,1)}, u32[]{:S(2)}, u32[]{:S(2)}) collective-permute-start(bf16[4,64,1536]{2,1,0:T(8,128)(2,1)} %get-tuple-element.344), channel_id=1, source_target_pairs={{0,4},{4,0},{1,5},{5,1},{2,6},{6,2},{3,7},{7,3},{8,12},{12,8},{9,1... | collective-permute-start | bytes 2359304 | tf_op jit(solution)/shard_map/ppermute | solution.py:532
  287.2 37.9 %collective-permute-start.51 = (bf16[4,64,768]{2,1,0:T(8,128)(2,1)S(1)}, bf16[4,64,768]{2,1,0:T(8,128)(2,1)}, u32[]{:S(2)}, u32[]{:S(2)}) collective-permute-start(bf16[4,64,768]{2,1,0:T(8,128)(2,1)S(1)} %get-tuple-element.339), channel_id=1, source_target_pairs={{0,2},{2,0},{1,3},{3,1},{4,6},{6,4},{5,7},{7,5},{8,10},{10,8},{9,1... | collective-permute-start | bytes 1179656 | tf_op jit(solution)/shard_map/ppermute | solution.py:532
  290.3 34.8 %all-to-all-start.4 = ((bf16[4,64,1024]{2,1,0:T(8,128)(2,1)}), bf16[4,64,1024]{2,1,0:T(8,128)(2,1)}, u32[]{:S(2)}, u32[]{:S(2)}) async-start(bf16[4,64,1024]{2,1,0:T(8,128)(2,1)} %add_convert_fusion.5), calls=%async_computation.4 | async-start | bytes 1048576 | tf_op jit(solution)/shard_map/all_to_all | solution.py:563
  296.9 28.3 %collective-permute-start.53 = (bf16[4,64,1536]{2,1,0:T(8,128)(2,1)}, bf16[4,64,1536]{2,1,0:T(8,128)(2,1)}, u32[]{:S(2)}, u32[]{:S(2)}) collective-permute-start(bf16[4,64,1536]{2,1,0:T(8,128)(2,1)} %add_convert_fusion.4), channel_id=1, source_target_pairs={{0,2},{2,0},{1,3},{3,1},{4,6},{6,4},{5,7},{7,5},{8,10},{10,8},{9,1... | collective-permute-start | bytes 2359304 | tf_op jit(solution)/shard_map/ppermute | solution.py:532
  299.9 25.2 %collective-permute-start.52 = (bf16[4,64,768]{2,1,0:T(8,128)(2,1)}, bf16[4,64,768]{2,1,0:T(8,128)(2,1)}, u32[]{:S(2)}, u32[]{:S(2)}) collective-permute-start(bf16[4,64,768]{2,1,0:T(8,128)(2,1)} %add_convert_fusion.8), channel_id=1, source_target_pairs={{0,4},{4,0},{1,5},{5,1},{2,6},{6,2},{3,7},{7,3},{8,12},{12,8},{9,1... | collective-permute-start | bytes 1179656 | tf_op jit(solution)/shard_map/ppermute | solution.py:532
  306.7 18.5 %collective-permute-start.50 = (bf16[4,64,768]{2,1,0:T(8,128)(2,1)S(1)}, bf16[4,64,768]{2,1,0:T(8,128)(2,1)}, u32[]{:S(2)}, u32[]{:S(2)}) collective-permute-start(bf16[4,64,768]{2,1,0:T(8,128)(2,1)S(1)} %get-tuple-element.338), channel_id=1, source_target_pairs={{0,4},{4,0},{1,5},{5,1},{2,6},{6,2},{3,7},{7,3},{8,12},{12,8},{9,1... | collective-permute-start | bytes 1179656 | tf_op jit(solution)/shard_map/ppermute | solution.py:532
  323.9 31.5 %collective-permute-start.56 = (bf16[4,64,768]{2,1,0:T(8,128)(2,1)S(1)}, bf16[4,64,768]{2,1,0:T(8,128)(2,1)}, u32[]{:S(2)}, u32[]{:S(2)}) collective-permute-start(bf16[4,64,768]{2,1,0:T(8,128)(2,1)S(1)} %get-tuple-element.358), channel_id=1, source_target_pairs={{0,4},{4,0},{1,5},{5,1},{2,6},{6,2},{3,7},{7,3},{8,12},{12,8},{9,1... | collective-permute-start | bytes 1179656 | tf_op jit(solution)/shard_map/ppermute | solution.py:532
  325.2 14.4 %collective-permute-start.57 = (f32[8,1536]{1,0:T(8,128)}, f32[8,1536]{1,0:T(8,128)S(1)}, u32[]{:S(2)}, u32[]{:S(2)}) collective-permute-start(f32[8,1536]{1,0:T(8,128)} %shard_map.267), channel_id=1, source_target_pairs={{0,1},{1,0},{2,3},{3,2},{4,5},{5,4},{6,7},{7,6},{8,9},{9,8},{10,11... | collective-permute-start | bytes 147464 | tf_op jit(solution)/shard_map/ppermute | solution.py:532
  327.8 27.6 %all-to-all-start.5 = ((bf16[4,64,1536]{2,1,0:T(8,128)(2,1)}), bf16[4,64,1536]{2,1,0:T(8,128)(2,1)S(1)}, u32[]{:S(2)}, u32[]{:S(2)}) async-start(bf16[4,64,1536]{2,1,0:T(8,128)(2,1)} %add_convert_fusion.3), calls=%async_computation.5 | async-start | bytes 1572864 | tf_op jit(solution)/shard_map/all_to_all | solution.py:563
  333.9 21.4 %collective-permute-start.55 = (bf16[4,64,768]{2,1,0:T(8,128)(2,1)S(1)}, bf16[4,64,768]{2,1,0:T(8,128)(2,1)S(1)}, u32[]{:S(2)}, u32[]{:S(2)}) collective-permute-start(bf16[4,64,768]{2,1,0:T(8,128)(2,1)S(1)} %add_convert_fusion.7), channel_id=1, source_target_pairs={{0,2},{2,0},{1,3},{3,1},{4,6},{6,4},{5,7},{7,5},{8,10},{10,8},{9,1... | collective-permute-start | bytes 1179656 | tf_op jit(solution)/shard_map/ppermute | solution.py:532
  336.3 19.1 %collective-permute-start.60 = (bf16[128,1024]{1,0:T(8,128)(2,1)S(1)}, bf16[128,1024]{1,0:T(8,128)(2,1)}, u32[]{:S(2)}, u32[]{:S(2)}) collective-permute-start(bf16[128,1024]{1,0:T(8,128)(2,1)S(1)} %reduce_sum.59.refs_8_), channel_id=1, source_target_pairs={{0,2},{2,0},{1,3},{3,1},{4,6},{6,4},{5,7},{7,5},{8,10},{10,8},{9,1... | collective-permute-start | bytes 786440 | tf_op jit(solution)/shard_map/ppermute | solution.py:532
  338.7 16.7 %collective-permute-start.59 = (bf16[64,1024]{1,0:T(8,128)(2,1)S(1)}, bf16[64,1024]{1,0:T(8,128)(2,1)S(1)}, u32[]{:S(2)}, u32[]{:S(2)}) collective-permute-start(bf16[64,1024]{1,0:T(8,128)(2,1)S(1)} %reduce_sum.58.refs_0_), channel_id=1, source_target_pairs={{0,2},{2,0},{1,3},{3,1},{4,6},{6,4},{5,7},{7,5},{8,10},{10,8},{9,1... | collective-permute-start | bytes 393224 | tf_op jit(solution)/shard_map/ppermute | solution.py:532
  339.6 15.2 %collective-permute-start.58 = (f32[8,1536]{1,0:T(8,128)S(1)}, f32[8,1536]{1,0:T(8,128)S(1)}, u32[]{:S(2)}, u32[]{:S(2)}) collective-permute-start(f32[8,1536]{1,0:T(8,128)S(1)} %add.147), channel_id=1, source_target_pairs={{0,2},{2,0},{1,3},{3,1},{4,6},{6,4},{5,7},{7,5},{8,10},{10,8},{9,1... | collective-permute-start | bytes 147464 | tf_op jit(solution)/shard_map/ppermute | solution.py:532
  358.1 30.5 %all-to-all-start.6 = ((bf16[4,64,1536]{2,1,0:T(8,128)(2,1)}), bf16[4,64,1536]{2,1,0:T(8,128)(2,1)S(1)}, u32[]{:S(2)}, u32[]{:S(2)}) async-start(bf16[4,64,1536]{2,1,0:T(8,128)(2,1)} %add_convert_fusion.2), calls=%async_computation.6 | async-start | bytes 1572864 | tf_op jit(solution)/shard_map/all_to_all | solution.py:563
  366.0 22.0 %collective-permute-start.63 = (bf16[4,80,1024]{2,1,0:T(8,128)(2,1)}, bf16[4,80,1024]{2,1,0:T(8,128)(2,1)S(1)}, u32[]{:S(2)}, u32[]{:S(2)}) collective-permute-start(bf16[4,80,1024]{2,1,0:T(8,128)(2,1)} %get-tuple-element.414), channel_id=1, source_target_pairs={{0,1},{1,0},{2,3},{3,2},{4,5},{5,4},{6,7},{7,6},{8,9},{9,8},{10,11... | collective-permute-start | bytes 1966088 | tf_op jit(solution)/shard_map/ppermute | solution.py:536
  366.0 22.6 %collective-permute-start.64 = (bf16[4,80,1024]{2,1,0:T(8,128)(2,1)}, bf16[4,80,1024]{2,1,0:T(8,128)(2,1)S(1)}, u32[]{:S(2)}, u32[]{:S(2)}) collective-permute-start(bf16[4,80,1024]{2,1,0:T(8,128)(2,1)} %get-tuple-element.415), channel_id=1, source_target_pairs={{0,2},{1,3},{2,0},{3,1},{4,6},{5,7},{6,4},{7,5},{8,10},{9,11},{10,... | collective-permute-start | bytes 1966088 | tf_op jit(solution)/shard_map/ppermute | solution.py:536
  372.0 16.0 %collective-permute-start.61 = (bf16[64,1536]{1,0:T(8,128)(2,1)}, bf16[64,1536]{1,0:T(8,128)(2,1)S(1)}, u32[]{:S(2)}, u32[]{:S(2)}) collective-permute-start(bf16[64,1536]{1,0:T(8,128)(2,1)} %reduce_sum.60.refs_4_), channel_id=1, source_target_pairs={{0,2},{2,0},{1,3},{3,1},{4,6},{6,4},{5,7},{7,5},{8,10},{10,8},{9,1... | collective-permute-start | bytes 589832 | tf_op jit(solution)/shard_map/ppermute | solution.py:532
  373.2 28.0 %collective-permute-start.71 = (bf16[4,80,1024]{2,1,0:T(8,128)(2,1)}, bf16[4,80,1024]{2,1,0:T(8,128)(2,1)S(1)}, u32[]{:S(2)}, u32[]{:S(2)}) collective-permute-start(bf16[4,80,1024]{2,1,0:T(8,128)(2,1)} %get-tuple-element.412), channel_id=1, source_target_pairs={{0,3},{1,2},{2,1},{3,0},{4,7},{5,6},{6,5},{7,4},{8,11},{9,10},{10,... | collective-permute-start | bytes 1966088 | tf_op jit(solution)/shard_map/ppermute | solution.py:536
  392.1 13.7 %collective-permute-start.72 = (bf16[64,1536]{1,0:T(8,128)(2,1)}, bf16[64,1536]{1,0:T(8,128)(2,1)S(1)}, u32[]{:S(2)}, u32[]{:S(2)}) collective-permute-start(bf16[64,1536]{1,0:T(8,128)(2,1)} %reduce_sum.61.refs_0_), channel_id=1, source_target_pairs={{0,2},{2,0},{1,3},{3,1},{4,6},{6,4},{5,7},{7,5},{8,10},{10,8},{9,1... | collective-permute-start | bytes 589832 | tf_op jit(solution)/shard_map/ppermute | solution.py:532
  392.9 24.6 %collective-permute-start.76 = (bf16[64,1536]{1,0:T(8,128)(2,1)}, bf16[64,1536]{1,0:T(8,128)(2,1)S(1)}, u32[]{:S(2)}, u32[]{:S(2)}) collective-permute-start(bf16[64,1536]{1,0:T(8,128)(2,1)} %reduce_sum.61.refs_0_), channel_id=1, source_target_pairs={{0,1},{1,0},{2,3},{3,2},{4,5},{5,4},{6,7},{7,6},{8,9},{9,8},{10,11... | collective-permute-start | bytes 589832 | tf_op jit(solution)/shard_map/ppermute | solution.py:532
  (60 other events, 386.3 us)

commit v3 on v2

--- a/solution.py
+++ b/solution.py
@@ -11,7 +11,7 @@
 HEAD_DIM = 64
 LANES = 128
 GROUPS = 2
-TILES = 2
+TILES = 4
 EPSILON = 1e-06
 BF16 = jnp.bfloat16
 F32 = jnp.float32
@@ -634,16 +634,11 @@
 
 def grad_columns_kernel(ends, cut, place_ref, *refs):
     y, x = place_ref[0], place_ref[1]
-    out_refs, turned_ref = refs[-5:-1], refs[-1]
+    out_refs = refs[-4:]
     j = pl.program_id(0)
 
-    def one(first, a_ref, a_sib_ref, g_ref, g_sib_ref):
-        @pl.when(j == first)
-        def _():
-            turned_ref[0] = a_ref[...].T
-            turned_ref[1] = a_sib_ref[...].T
-
-        total = contract(turned_ref[0], g_ref[...], 1, 0) + contract(turned_ref[1], g_sib_ref[...], 1, 0)
+    def one(a_ref, a_sib_ref, g_ref, g_sib_ref):
+        total = contract(a_ref[...], g_ref[...], 0, 0) + contract(a_sib_ref[...], g_sib_ref[...], 0, 0)
         total = total.reshape(-1, 2, cut.shard_rows, total.shape[1])
         for z in range(total.shape[0]):
             near = jnp.where(y == 0, total[z, 0], total[z, 1]).astype(BF16)
@@ -651,11 +646,11 @@
             part_refs(x, near, far, cut.rows, out_refs, z)
 
     if len(ends) == 1:
-        one(0, *refs[:4])
+        one(*refs[:4])
         return
     for i, end in enumerate(ends):
         first = 0 if i == 0 else ends[i - 1]
-        pl.when((j >= first) & (j < end))(functools.partial(one, first, *refs[4 * i : 4 * i + 4]))
+        pl.when((j >= first) & (j < end))(functools.partial(one, *refs[4 * i : 4 * i + 4]))
 
 
 def grad_rows_kernel(cut, place_ref, a0_ref, a1_ref, a0_sib_ref, a1_sib_ref, g_ref, g_sib_ref, *out_refs):
@@ -714,7 +709,6 @@
             grid=(grid,),
             in_specs=specs,
             out_specs=[out_spec(cut.rows)] * 4,
-            scratch_shapes=[] if cut.by_rows else [pltpu.VMEM((2, jobs[0][0].shape[1], tokens), BF16)],
         ),
         out_shape=[jax.ShapeDtypeStruct((depth, cut.rows, wide), BF16)] * 4,
         compiler_params=pltpu.CompilerParams(vmem_limit_bytes=52 << 20),
@@ -1057,7 +1051,7 @@
         )
         outs = by_slot(input_grad, result)
         early, late = outs[:-1], outs[-1]
-        qkv_b, b_g, packed, a_g, down_g, early = tie(qkv_b, grad_x(b_z), over_rows(packed), a_g, down_g, early)
+        qkv_b, b_g, packed, a_g, down_g, early = tie(qkv_b, grad_x(b_z), over_line(over_rows(packed)), a_g, down_g, early)
         b_g, a_g, down_g = (grad_core(*v) for v in (b_g, a_g, down_g))
         mine, from_x = grad_x(qkv_b)
         half, n_out, n_qkv = cut_up.wide // 2, cut_out.wide, cut_group.wide
@@ -1073,7 +1067,6 @@
         g_up, g_out, g_down, packed, late, from_x = tie(g_up, g_out, g_down, packed, late, from_x)
         outs = early + [late]
         qkv_g = grad_core(mine, from_x)
-        packed = over_line(packed)
         part = width // GROUPS
         qkv_plan = []
         for g in range(GROUPS):

time: 428 us -> 421 us (0.984)
    ppermute x66, waiting for transfers between devices: 67.5 us -> 60.6 us  [swap(): return lax.ppermute(value, axis, [(0, 1), (1, 0)])]
    ppermute x12, waiting for transfers between devices: 28.4 us -> 34.2 us  [send(): lax.ppermute(value, axis, [(i, i ^ step) for i in range(lax.axis_size(axi...]
    unnamed x83 -> x81, local copies, waits for them, and re-layouts: 8.57 us -> 8.61 us
  transfers between devices with their start and end apart: 85 -> 85, of which waited for: 27 -> 28; matrix products, arithmetic and copies ran while one was open for 11% -> 10% of each run, Pallas kernels for 40% -> 40%
where the time goes in v3:
time: 421 us; the launch traced here: 415 us
  Pallas kernels  174 us (41%)
  waiting for transfers between devices  102 us (24%)
  starting transfers between devices  84.3 us (20%)
  other arithmetic  32.4 us (8%)
  local copies, waits for them, and re-layouts  21.4 us (5%)
    pallas_call x5, Pallas kernels, stepped(): pl.pallas_call(functools.partial(kernel, weights), grid_spec=pltpu.Prefet...  83.1 us
    ppermute x66, waiting for transfers between devices, swap(): return lax.ppermute(value, axis, [(0, 1), (1, 0)])  60.6 us
    pallas_call x5, Pallas kernels, grad_parts(): pl.pallas_call(kernel, grid_spec=pltpu.PrefetchScalarGridSpec(num_scalar_...  41.6 us
    ppermute x66, starting transfers between devices, swap(): return lax.ppermute(value, axis, [(0, 1), (1, 0)])  40.8 us
    pallas_call x3, Pallas kernels, attention(): pl.pallas_call(attend_back_kernel if back else attend_kernel, grid=(image...  37.8 us
    all_to_all x7, starting transfers between devices, exchange(): return lax.all_to_all(blocks, axis, split_axis=0, concat_axis=0, tiled=True)  34.4 us
    ppermute x12, waiting for transfers between devices, send(): lax.ppermute(value, axis, [(i, i ^ step) for i in range(lax.axis_size(axi...  34.2 us
    convert_element_type x4, other arithmetic, grad_z(): sum((v.astype(F32) for v in (parts[0], from_x, from_y))).astype(BF16)  10.1 us
  transfers between devices with their start and end apart: 85, of which 28 were waited for; matrix products, arithmetic and copies ran while one was open for 10% of the time, Pallas kernels for 40%

profile of v3, /device:TPU:0, one launch (start us, length us, event | category | flops | bytes accessed | tf_op | source)
XLA Modules:
  0.0 415.4 jit_solution(12385446046185986923)
XLA Ops:
  1.3 3.7 shard_map.254
  5.0 6.4 %all-to-all-start = ((bf16[4,64,2176]{2,1,0:T(8,128)(2,1)}), bf16[4,64,2176]{2,1,0:T(8,128)(2,1)}, u32[]{:S(2)}, u32[]{:S(2)}) async-start(bf16[4,64,2176]{2,1,0:T(8,128)(2,1)} %get-tuple-element.207), calls=%async_computation | async-start | bytes 2228224 | tf_op jit(solution)/shard_map/all_to_all | solution.py:563
  11.6 1.6 collective-permute-start.1
  14.0 1.5 collective-permute-start.4
  15.5 6.7 %collective-permute-done.1 = bf16[2,80,1024]{2,1,0:T(8,128)(2,1)S(1)} collective-permute-done((bf16[2,80,1024]{2,1,0:T(8,128)(2,1)S(1)}, bf16[2,80,1024]{2,1,0:T(8,128)(2,1)S(1)}, u32[]{:S(2)}, u32[]{:S(2)}) %collective-permute-start.1) | collective-permute-done | bytes 327712 | tf_op jit(solution)/shard_map/ppermute | solution.py:536
  22.2 6.1 %collective-permute-done.2 = bf16[2,80,1024]{2,1,0:T(8,128)(2,1)S(1)} collective-permute-done((bf16[2,80,1024]{2,1,0:T(8,128)(2,1)S(1)}, bf16[2,80,1024]{2,1,0:T(8,128)(2,1)S(1)}, u32[]{:S(2)}, u32[]{:S(2)}) %collective-permute-start.2) | collective-permute-done | bytes 327712 | tf_op jit(solution)/shard_map/ppermute | solution.py:536
  29.1 6.8 %collective-permute-done.4 = bf16[2,80,1024]{2,1,0:T(8,128)(2,1)S(1)} collective-permute-done((bf16[2,80,1024]{2,1,0:T(8,128)(2,1)S(1)}, bf16[2,80,1024]{2,1,0:T(8,128)(2,1)S(1)}, u32[]{:S(2)}, u32[]{:S(2)}) %collective-permute-start.4) | collective-permute-done | bytes 327712 | tf_op jit(solution)/shard_map/ppermute | solution.py:536
  35.8 2.9 all-to-all-done.refs_0_.refs_10_.refs_20_
  38.7 1.5 collective-permute-start.5
  40.2 1.5 collective-permute-start.6
  41.7 4.3 %all-to-all-start.1 = ((bf16[4,64,2048]{2,1,0:T(8,128)(2,1)}), bf16[4,64,2048]{2,1,0:T(8,128)(2,1)}, u32[]{:S(2)}, u32[]{:S(2)}) async-start(bf16[4,64,2048]{2,1,0:T(8,128)(2,1)} %get-tuple-element.215), calls=%async_computation.1 | async-start | bytes 2097152 | tf_op jit(solution)/shard_map/all_to_all | solution.py:563
  46.0 2.3 pad_maximum_fusion.2
  48.3 16.3 %collective-permute-done.5.refs_1_.refs_11_.refs_21_ = bf16[4,64,2176]{2,1,0:T(8,128)(2,1)} collective-permute-done((bf16[4,64,2176]{2,1,0:T(8,128)(2,1)}, bf16[4,64,2176]{2,1,0:T(8,128)(2,1)}, u32[]{:S(2)}, u32[]{:S(2)}) %collective-permute-start.5) | collective-permute-done | bytes 1114144 | tf_op jit(solution)/shard_map/ppermute | solution.py:532
  69.5 1.6 collective-permute-start.7
  73.5 11.2 %collective-permute-done.7.refs_3_.refs_13_.refs_23_ = bf16[2,64,2176]{2,1,0:T(8,128)(2,1)} collective-permute-done((bf16[2,64,2176]{2,1,0:T(8,128)(2,1)S(1)}, bf16[2,64,2176]{2,1,0:T(8,128)(2,1)}, u32[]{:S(2)}, u32[]{:S(2)}) %collective-permute-start.7) | collective-permute-done | bytes 557088 | tf_op jit(solution)/shard_map/ppermute | solution.py:532
  89.1 9.8 %shard_map.255 = (bf16[640,1024]{1,0:T(8,128)(2,1)}, bf16[640,3072]{1,0:T(8,128)(2,1)}) custom-call(s32[3]{0:T(128)} %pad_add_fusion.place_ref, bf16[4,64,2176]{2,1,0:T(8,128)(2,1)} %all-to-all-done.refs_0_.refs_10_.refs_20_, bf16[4,64,2176]{2,1,0:T(8,128)(2,1)} %collective-permute-done.5.refs_1_.refs_11_.refs_21_, ...), custom_call_target="tpu_custom_call" | custom-call | flops 11000000512 | tf_op jit(solution)/shard_map/pallas_call | solution.py:260
  98.9 4.8 %all-to-all-start.2 = ((bf16[4,64,2048]{2,1,0:T(8,128)(2,1)}), bf16[4,64,2048]{2,1,0:T(8,128)(2,1)}, u32[]{:S(2)}, u32[]{:S(2)}) async-start(bf16[4,64,2048]{2,1,0:T(8,128)(2,1)} %get-tuple-element.242), calls=%async_computation.2 | async-start | bytes 2097152 | tf_op jit(solution)/shard_map/all_to_all | solution.py:563
  104.5 7.6 %collective-permute-done.14.refs_1_.refs_11_ = bf16[4,64,2048]{2,1,0:T(8,128)(2,1)} collective-permute-done((bf16[4,64,2048]{2,1,0:T(8,128)(2,1)}, bf16[4,64,2048]{2,1,0:T(8,128)(2,1)}, u32[]{:S(2)}, u32[]{:S(2)}) %collective-permute-start.14) | collective-permute-done | bytes 1048608 | tf_op jit(solution)/shard_map/ppermute | solution.py:532
  115.7 1.5 collective-permute-start.18
  117.9 16.2 %shard_map.256 = (bf16[2,320,1024]{2,1,0:T(8,128)(2,1)}, f32[2,320,1024]{2,1,0:T(8,128)}) custom-call(f32[2,320,1]{2,1,0:T(8,128)} %compare_select_fusion.bias_ref, bf16[2,320,3072]{2,1,0:T(8,128)(2,1)} %bitcast.149, bf16[2,320,3072]{2,1,0:T(8,128)(2,1)} %bitcast.150, bf16[2,320,3072]{2,1,0:T(8,128)(2,1)} %bitcast.151), custom_call_target="tpu_custom_call" | custom-call | flops 14080000000 | tf_op jit(solution)/shard_map/pallas_call | solution.py:133
  134.1 1.3 collective-permute-done.21
  136.5 1.5 collective-permute-start.24
  138.0 1.5 collective-permute-start.25
  140.5 18.4 %shard_map.257 = (f32[640,1024]{1,0:T(8,128)}, bf16[640,1024]{1,0:T(8,128)(2,1)}, bf16[640,4096]{1,0:T(8,128)(2,1)}, bf16[640,4096]{1,0:T(8,128)(2,1)}, bf16[640,2048]{1,0:T(8,128)(2,1)}) custom-call(s32[3]{0:T(128)} %pad_add_fusion.place_ref, bf16[4,64,2048]{2,1,0:T(8,128)(2,1)} %all-to-all-done.1.refs_0_.refs_10_, ...), custom_call_target="tpu_custom_call" | custom-call | flops 22000001024 | tf_op jit(solution)/shard_map/pallas_call | solution.py:260
  158.9 3.3 collective-permute-done.24.refs_1_
  167.4 1.5 collective-permute-start.29
  170.4 11.5 %shard_map.258 = (bf16[4,128,1024]{2,1,0:T(8,128)(2,1)S(1)}, bf16[4,128,1024]{2,1,0:T(8,128)(2,1)}, bf16[4,128,1024]{2,1,0:T(8,128)(2,1)}, bf16[4,128,1024]{2,1,0:T(8,128)(2,1)}) custom-call(s32[3]{0:T(128)S(1)} %copy-done.2, bf16[640,4096]{1,0:T(8,128)(2,1)} %get-tuple-element.362.a0_ref.a1_ref.refs_10_, ...), custom_call_target="tpu_custom_call" | custom-call | flops 10150215680 | tf_op jit(solution)/shard_map/pallas_call | solution.py:705
  186.3 26.8 %shard_map.259 = (bf16[640,4096]{1,0:T(8,128)(2,1)}, f32[1,4096]{1,0:T(1,128)}, f32[640,1024]{1,0:T(8,128)}, bf16[640,1024]{1,0:T(8,128)(2,1)}, bf16[640,1024]{1,0:T(8,128)(2,1)}, /*index=5*/f32[8,1024]{1,0:T(8,128)}) custom-call(s32[3]{0:T(128)} %pad_add_fusion.place_ref, bf16[4,64,2048]{2,1,0:T(8,128)(2,1)} %all-to-all-done.2.refs_0_, ...), custom_call_target="tpu_custom_call" | custom-call | flops 25300000768 | tf_op jit(solution)/shard_map/pallas_call | solution.py:260
  215.0 10.8 %shard_map.260 = bf16[2,320,1536]{2,1,0:T(8,128)(2,1)} custom-call(f32[2,320,1]{2,1,0:T(8,128)} %compare_select_fusion.bias_ref, bf16[2,320,3072]{2,1,0:T(8,128)(2,1)} %bitcast.152, bf16[2,320,3072]{2,1,0:T(8,128)(2,1)} %bitcast.153, bf16[2,320,3072]{2,1,0:T(8,128)(2,1)} %bitcast.154, f32[2,320,1024]{2,1,0:T(8,128)} %get-tuple-element.290.lse_ref, ...), custom_call_target="tpu_custom_call" | custom-call | flops 11440000000 | tf_op jit(solution)/shard_map/pallas_call | solution.py:133
  227.2 7.6 %shard_map.263 = (bf16[4,64,1024]{2,1,0:T(8,128)(2,1)S(1)}, bf16[4,64,1024]{2,1,0:T(8,128)(2,1)S(1)}, bf16[4,64,1024]{2,1,0:T(8,128)(2,1)}, bf16[4,64,1024]{2,1,0:T(8,128)(2,1)}) custom-call(s32[3]{0:T(128)S(1)} %copy-done.3, bf16[640,1024]{1,0:T(8,128)(2,1)} %get-tuple-element.288.refs_0_, bf16[640,1024]{1,0:T(8,128)(2,1)} %collective-permute-done.37.refs_1_, ...), custom_call_target="tpu_custom_call" | custom-call | flops 5075107840 | tf_op jit(solution)/shard_map/pallas_call | solution.py:705
  236.8 10.7 %shard_map.262 = (bf16[4,64,1536]{2,1,0:T(8,128)(2,1)S(1)}, bf16[4,64,1536]{2,1,0:T(8,128)(2,1)S(1)}, bf16[4,64,1536]{2,1,0:T(8,128)(2,1)}, bf16[4,64,1536]{2,1,0:T(8,128)(2,1)}) custom-call(s32[3]{0:T(128)S(1)} %copy-done.3, bf16[640,1024]{1,0:T(8,128)(2,1)} %get-tuple-element.288.refs_0_, bf16[640,1024]{1,0:T(8,128)(2,1)} %collective-permute-done.37.refs_1_, ...), custom_call_target="tpu_custom_call" | custom-call | flops 7612661760 | tf_op jit(solution)/shard_map/pallas_call | solution.py:705
  247.5 4.4 %collective-permute-done.43 = bf16[4,128,1024]{2,1,0:T(8,128)(2,1)S(1)} collective-permute-done((bf16[4,128,1024]{2,1,0:T(8,128)(2,1)S(1)}, bf16[4,128,1024]{2,1,0:T(8,128)(2,1)S(1)}, u32[]{:S(2)}, u32[]{:S(2)}) %collective-permute-start.43) | collective-permute-done | bytes 1048608 | tf_op jit(solution)/shard_map/ppermute | solution.py:532
  251.9 2.8 add_convert_fusion
  254.8 4.2 %all-to-all-start.3 = ((bf16[4,128,1024]{2,1,0:T(8,128)(2,1)}), bf16[4,128,1024]{2,1,0:T(8,128)(2,1)}, u32[]{:S(2)}, u32[]{:S(2)}) async-start(bf16[4,128,1024]{2,1,0:T(8,128)(2,1)} %add_convert_fusion), calls=%async_computation.3 | async-start | bytes 2097152 | tf_op jit(solution)/shard_map/all_to_all | solution.py:563
  259.0 2.0 add_convert_fusion.6
  262.7 6.2 %shard_map.261 = (bf16[4,64,768]{2,1,0:T(8,128)(2,1)S(1)}, bf16[4,64,768]{2,1,0:T(8,128)(2,1)S(1)}, bf16[4,64,768]{2,1,0:T(8,128)(2,1)S(1)}, bf16[4,64,768]{2,1,0:T(8,128)(2,1)}) custom-call(s32[3]{0:T(128)S(1)} %copy-done.3, bf16[640,1024]{1,0:T(8,128)(2,1)} %get-tuple-element.236.refs_0_, bf16[640,1024]{1,0:T(8,128)(2,1)} %copy-done.22, ...), custom_call_target="tpu_custom_call" | custom-call | flops 3806330880 | tf_op jit(solution)/shard_map/pallas_call | solution.py:705
  270.1 10.8 %shard_map.264 = bf16[2,320,1536]{2,1,0:T(8,128)(2,1)} custom-call(f32[2,320,1]{2,1,0:T(8,128)} %compare_select_fusion.bias_ref, bf16[2,320,3072]{2,1,0:T(8,128)(2,1)} %bitcast.155, bf16[2,320,3072]{2,1,0:T(8,128)(2,1)} %bitcast.156, bf16[2,320,3072]{2,1,0:T(8,128)(2,1)} %bitcast.157, f32[2,320,1024]{2,1,0:T(8,128)} %get-tuple-element.290.lse_ref, ...), custom_call_target="tpu_custom_call" | custom-call | flops 11440000000 | tf_op jit(solution)/shard_map/pallas_call | solution.py:133
  281.2 3.9 all-to-all-done.3
  287.6 2.3 add_convert_fusion.5
  289.9 4.5 %all-to-all-start.4 = ((bf16[4,64,1024]{2,1,0:T(8,128)(2,1)}), bf16[4,64,1024]{2,1,0:T(8,128)(2,1)}, u32[]{:S(2)}, u32[]{:S(2)}) async-start(bf16[4,64,1024]{2,1,0:T(8,128)(2,1)} %add_convert_fusion.5), calls=%async_computation.4 | async-start | bytes 1048576 | tf_op jit(solution)/shard_map/all_to_all | solution.py:563
  294.4 2.2 add_convert_fusion.4
  297.9 1.8 add_convert_fusion.8
  300.9 5.5 %shard_map.265 = (bf16[4,64,768]{2,1,0:T(8,128)(2,1)S(1)}, bf16[4,64,768]{2,1,0:T(8,128)(2,1)S(1)}, bf16[4,64,768]{2,1,0:T(8,128)(2,1)S(1)}, bf16[4,64,768]{2,1,0:T(8,128)(2,1)S(1)}) custom-call(s32[3]{0:T(128)S(1)} %copy-done.3, bf16[640,1024]{1,0:T(8,128)(2,1)} %get-tuple-element.236.refs_0_, bf16[640,1024]{1,0:T(8,128)(2,1)} %copy-done.22, ...), custom_call_target="tpu_custom_call" | custom-call | flops 3806330880 | tf_op jit(solution)/shard_map/pallas_call | solution.py:705
  307.3 14.9 %shard_map.266 = (bf16[640,1024]{1,0:T(8,128)(2,1)}, f32[1,3072]{1,0:T(1,128)}, f32[8,1024]{1,0:T(8,128)}) custom-call(s32[3]{0:T(128)} %pad_add_fusion.place_ref, bf16[4,64,2176]{2,1,0:T(8,128)(2,1)} %all-to-all-done.refs_0_.refs_10_.refs_20_, bf16[4,64,2176]{2,1,0:T(8,128)(2,1)} %collective-permute-done.5.refs_1_.refs_11_.refs_21_, ...), custom_call_target="tpu_custom_call" | custom-call | flops 14300000256 | tf_op jit(solution)/shard_map/pallas_call | solution.py:260
  322.2 1.5 shard_map.267
  325.0 2.6 add_convert_fusion.3
  327.5 5.1 %all-to-all-start.5 = ((bf16[4,64,1536]{2,1,0:T(8,128)(2,1)}), bf16[4,64,1536]{2,1,0:T(8,128)(2,1)S(1)}, u32[]{:S(2)}, u32[]{:S(2)}) async-start(bf16[4,64,1536]{2,1,0:T(8,128)(2,1)} %add_convert_fusion.3), calls=%async_computation.5 | async-start | bytes 1572864 | tf_op jit(solution)/shard_map/all_to_all | solution.py:563
  334.6 1.4 reduce_sum.59.refs_8_
  336.0 1.3 collective-permute-start.60
  339.3 1.3 collective-permute-start.58
  340.6 13.2 %shard_map.268 = bf16[640,1024]{1,0:T(8,128)(2,1)} custom-call(s32[3]{0:T(128)} %pad_add_fusion.place_ref, bf16[4,64,2048]{2,1,0:T(8,128)(2,1)} %all-to-all-done.2.refs_0_, bf16[4,64,2048]{2,1,0:T(8,128)(2,1)} %copy-done.14, bf16[4,64,2048]{2,1,0:T(8,128)(2,1)} %copy-done.15, bf16[2,64,2048]{2,1,0:T(8,128)(2,1)} %copy-done.28, ...), custom_call_target="tpu_custom_call" | custom-call | flops 12099999744 | tf_op jit(solution)/shard_map/pallas_call | solution.py:260
  355.8 2.4 add_convert_fusion.2
  358.2 5.1 %all-to-all-start.6 = ((bf16[4,64,1536]{2,1,0:T(8,128)(2,1)}), bf16[4,64,1536]{2,1,0:T(8,128)(2,1)S(1)}, u32[]{:S(2)}, u32[]{:S(2)}) async-start(bf16[4,64,1536]{2,1,0:T(8,128)(2,1)} %add_convert_fusion.2), calls=%async_computation.6 | async-start | bytes 1572864 | tf_op jit(solution)/shard_map/all_to_all | solution.py:563
  364.3 2.6 fusion.6
  368.4 2.0 collective-permute-start.63
  370.4 2.4 collective-permute-start.64
  373.6 2.1 collective-permute-done.63
  376.6 6.8 %collective-permute-done.64 = f32[1536]{0:T(1024)} collective-permute-done((f32[1536]{0:T(1024)}, f32[1536]{0:T(1024)}, u32[]{:S(2)}, u32[]{:S(2)}) %collective-permute-start.64) | collective-permute-done | bytes 6176 | tf_op jit(solution)/shard_map/ppermute | solution.py:536
  384.1 4.8 %collective-permute-done.61.refs_5_ = bf16[64,1536]{1,0:T(8,128)(2,1)S(1)} collective-permute-done((bf16[64,1536]{1,0:T(8,128)(2,1)}, bf16[64,1536]{1,0:T(8,128)(2,1)S(1)}, u32[]{:S(2)}, u32[]{:S(2)}) %collective-permute-start.61) | collective-permute-done | bytes 196640 | tf_op jit(solution)/shard_map/ppermute | solution.py:532
  393.9 4.0 shard_map.269
  397.8 4.3 %collective-permute-done.74 = bf16[4,80,1024]{2,1,0:T(8,128)(2,1)S(1)} collective-permute-done((bf16[4,80,1024]{2,1,0:T(8,128)(2,1)}, bf16[4,80,1024]{2,1,0:T(8,128)(2,1)S(1)}, u32[]{:S(2)}, u32[]{:S(2)}) %collective-permute-start.74) | collective-permute-done | bytes 655392 | tf_op jit(solution)/shard_map/ppermute | solution.py:536
  402.2 4.6 %collective-permute-done.75.refs_1_ = bf16[64,1536]{1,0:T(8,128)(2,1)S(1)} collective-permute-done((bf16[64,1536]{1,0:T(8,128)(2,1)}, bf16[64,1536]{1,0:T(8,128)(2,1)S(1)}, u32[]{:S(2)}, u32[]{:S(2)}) %collective-permute-start.75) | collective-permute-done | bytes 196640 | tf_op jit(solution)/shard_map/ppermute | solution.py:532
  409.0 1.7 slice_bitcast_fusion
  412.6 2.6 shard_map.270
  (260 shorter events, 67.3 us)
Async XLA Ops:
  5.0 33.7 %all-to-all-start = ((bf16[4,64,2176]{2,1,0:T(8,128)(2,1)}), bf16[4,64,2176]{2,1,0:T(8,128)(2,1)}, u32[]{:S(2)}, u32[]{:S(2)}) async-start(bf16[4,64,2176]{2,1,0:T(8,128)(2,1)} %get-tuple-element.207), calls=%async_computation | async-start | bytes 2228224 | tf_op jit(solution)/shard_map/all_to_all | solution.py:563
  13.2 15.1 %collective-permute-start.2 = (bf16[2,80,1024]{2,1,0:T(8,128)(2,1)S(1)}, bf16[2,80,1024]{2,1,0:T(8,128)(2,1)S(1)}, u32[]{:S(2)}, u32[]{:S(2)}) collective-permute-start(bf16[2,80,1024]{2,1,0:T(8,128)(2,1)S(1)} %get-tuple-element.421), channel_id=1, source_target_pairs={{0,3},{1,2},{2,1},{3,0},{4,7},{5,6},{6,5},{7,4},{8,11},{9,10},{10,... | collective-permute-start | bytes 983048 | tf_op jit(solution)/shard_map/ppermute | solution.py:536
  13.6 14.8 %collective-permute-start.3 = (bf16[2,80,1024]{2,1,0:T(8,128)(2,1)S(1)}, bf16[2,80,1024]{2,1,0:T(8,128)(2,1)S(1)}, u32[]{:S(2)}, u32[]{:S(2)}) collective-permute-start(bf16[2,80,1024]{2,1,0:T(8,128)(2,1)S(1)} %get-tuple-element.419), channel_id=1, source_target_pairs={{0,1},{1,0},{2,3},{3,2},{4,5},{5,4},{6,7},{7,6},{8,9},{9,8},{10,11... | collective-permute-start | bytes 983048 | tf_op jit(solution)/shard_map/ppermute | solution.py:536
  14.0 21.8 %collective-permute-start.4 = (bf16[2,80,1024]{2,1,0:T(8,128)(2,1)S(1)}, bf16[2,80,1024]{2,1,0:T(8,128)(2,1)S(1)}, u32[]{:S(2)}, u32[]{:S(2)}) collective-permute-start(bf16[2,80,1024]{2,1,0:T(8,128)(2,1)S(1)} %get-tuple-element.418), channel_id=1, source_target_pairs={{0,2},{1,3},{2,0},{3,1},{4,6},{5,7},{6,4},{7,5},{8,10},{9,11},{10,... | collective-permute-start | bytes 983048 | tf_op jit(solution)/shard_map/ppermute | solution.py:536
  38.7 25.8 %collective-permute-start.5 = (bf16[4,64,2176]{2,1,0:T(8,128)(2,1)}, bf16[4,64,2176]{2,1,0:T(8,128)(2,1)}, u32[]{:S(2)}, u32[]{:S(2)}) collective-permute-start(bf16[4,64,2176]{2,1,0:T(8,128)(2,1)} %all-to-all-done.refs_0_.refs_10_.refs_20_), channel_id=1, source_target_pairs={{0,2},{2,0},{1,3},{3,1},{4,6},{6,4},{5,7},{7,5},{8,10},{10,8},{9,1... | collective-permute-start | bytes 3342344 | tf_op jit(solution)/shard_map/ppermute | solution.py:532
  40.2 25.6 %collective-permute-start.6 = (bf16[4,64,2176]{2,1,0:T(8,128)(2,1)}, bf16[4,64,2176]{2,1,0:T(8,128)(2,1)}, u32[]{:S(2)}, u32[]{:S(2)}) collective-permute-start(bf16[4,64,2176]{2,1,0:T(8,128)(2,1)} %all-to-all-done.refs_0_.refs_10_.refs_20_), channel_id=1, source_target_pairs={{0,4},{4,0},{1,5},{5,1},{2,6},{6,2},{3,7},{7,3},{8,12},{12,8},{9,1... | collective-permute-start | bytes 3342344 | tf_op jit(solution)/shard_map/ppermute | solution.py:532
  41.7 31.8 %all-to-all-start.1 = ((bf16[4,64,2048]{2,1,0:T(8,128)(2,1)}), bf16[4,64,2048]{2,1,0:T(8,128)(2,1)}, u32[]{:S(2)}, u32[]{:S(2)}) async-start(bf16[4,64,2048]{2,1,0:T(8,128)(2,1)} %get-tuple-element.215), calls=%async_computation.1 | async-start | bytes 2097152 | tf_op jit(solution)/shard_map/all_to_all | solution.py:563
  65.7 20.2 %collective-permute-start.10 = (bf16[4,64,2176]{2,1,0:T(8,128)(2,1)}, bf16[4,64,2176]{2,1,0:T(8,128)(2,1)}, u32[]{:S(2)}, u32[]{:S(2)}) collective-permute-start(bf16[4,64,2176]{2,1,0:T(8,128)(2,1)} %collective-permute-done.5.refs_1_.refs_11_.refs_21_), channel_id=1, source_target_pairs={{0,1},{1,0},{2,3},{3,2},{4,5},{5,4},{6,7},{7,6},{8,9},{9,8},{10,11... | collective-permute-start | bytes 3342344 | tf_op jit(solution)/shard_map/ppermute | solution.py:532
  66.8 19.1 %collective-permute-start.11 = (bf16[4,64,2176]{2,1,0:T(8,128)(2,1)}, bf16[4,64,2176]{2,1,0:T(8,128)(2,1)}, u32[]{:S(2)}, u32[]{:S(2)}) collective-permute-start(bf16[4,64,2176]{2,1,0:T(8,128)(2,1)} %collective-permute-done.6.refs_2_.refs_12_.refs_22_), channel_id=1, source_target_pairs={{0,1},{1,0},{2,3},{3,2},{4,5},{5,4},{6,7},{7,6},{8,9},{9,8},{10,11... | collective-permute-start | bytes 3342344 | tf_op jit(solution)/shard_map/ppermute | solution.py:532
  68.5 17.4 %collective-permute-start.9 = (bf16[4,64,2176]{2,1,0:T(8,128)(2,1)}, bf16[4,64,2176]{2,1,0:T(8,128)(2,1)}, u32[]{:S(2)}, u32[]{:S(2)}) collective-permute-start(bf16[4,64,2176]{2,1,0:T(8,128)(2,1)} %all-to-all-done.refs_0_.refs_10_.refs_20_), channel_id=1, source_target_pairs={{0,1},{1,0},{2,3},{3,2},{4,5},{5,4},{6,7},{7,6},{8,9},{9,8},{10,11... | collective-permute-start | bytes 3342344 | tf_op jit(solution)/shard_map/ppermute | solution.py:532
  69.5 15.2 %collective-permute-start.7 = (bf16[2,64,2176]{2,1,0:T(8,128)(2,1)S(1)}, bf16[2,64,2176]{2,1,0:T(8,128)(2,1)}, u32[]{:S(2)}, u32[]{:S(2)}) collective-permute-start(bf16[2,64,2176]{2,1,0:T(8,128)(2,1)S(1)} %slice.90), channel_id=1, source_target_pairs={{0,4},{4,0},{1,5},{5,1},{2,6},{6,2},{3,7},{7,3},{8,12},{12,8},{9,1... | collective-permute-start | bytes 1671176 | tf_op jit(solution)/shard_map/ppermute | solution.py:532
  71.1 14.8 %collective-permute-start.8 = (bf16[2,64,2176]{2,1,0:T(8,128)(2,1)S(1)}, bf16[2,64,2176]{2,1,0:T(8,128)(2,1)}, u32[]{:S(2)}, u32[]{:S(2)}) collective-permute-start(bf16[2,64,2176]{2,1,0:T(8,128)(2,1)S(1)} %slice.91), channel_id=1, source_target_pairs={{0,2},{2,0},{1,3},{3,1},{4,6},{6,4},{5,7},{7,5},{8,10},{10,8},{9,1... | collective-permute-start | bytes 1671176 | tf_op jit(solution)/shard_map/ppermute | solution.py:532
  86.6 25.5 %collective-permute-start.14 = (bf16[4,64,2048]{2,1,0:T(8,128)(2,1)}, bf16[4,64,2048]{2,1,0:T(8,128)(2,1)}, u32[]{:S(2)}, u32[]{:S(2)}) collective-permute-start(bf16[4,64,2048]{2,1,0:T(8,128)(2,1)} %all-to-all-done.1.refs_0_.refs_10_), channel_id=1, source_target_pairs={{0,2},{2,0},{1,3},{3,1},{4,6},{6,4},{5,7},{7,5},{8,10},{10,8},{9,1... | collective-permute-start | bytes 3145736 | tf_op jit(solution)/shard_map/ppermute | solution.py:532
  87.2 25.2 %collective-permute-start.15 = (bf16[4,64,2048]{2,1,0:T(8,128)(2,1)}, bf16[4,64,2048]{2,1,0:T(8,128)(2,1)}, u32[]{:S(2)}, u32[]{:S(2)}) collective-permute-start(bf16[4,64,2048]{2,1,0:T(8,128)(2,1)} %all-to-all-done.1.refs_0_.refs_10_), channel_id=1, source_target_pairs={{0,4},{4,0},{1,5},{5,1},{2,6},{6,2},{3,7},{7,3},{8,12},{12,8},{9,1... | collective-permute-start | bytes 3145736 | tf_op jit(solution)/shard_map/ppermute | solution.py:532
  87.7 24.7 %collective-permute-start.16 = (bf16[4,64,2048]{2,1,0:T(8,128)(2,1)}, bf16[4,64,2048]{2,1,0:T(8,128)(2,1)}, u32[]{:S(2)}, u32[]{:S(2)}) collective-permute-start(bf16[4,64,2048]{2,1,0:T(8,128)(2,1)} %all-to-all-done.1.refs_0_.refs_10_), channel_id=1, source_target_pairs={{0,1},{1,0},{2,3},{3,2},{4,5},{5,4},{6,7},{7,6},{8,9},{9,8},{10,11... | collective-permute-start | bytes 3145736 | tf_op jit(solution)/shard_map/ppermute | solution.py:532
  98.9 36.6 %all-to-all-start.2 = ((bf16[4,64,2048]{2,1,0:T(8,128)(2,1)}), bf16[4,64,2048]{2,1,0:T(8,128)(2,1)}, u32[]{:S(2)}, u32[]{:S(2)}) async-start(bf16[4,64,2048]{2,1,0:T(8,128)(2,1)} %get-tuple-element.242), calls=%async_computation.2 | async-start | bytes 2097152 | tf_op jit(solution)/shard_map/all_to_all | solution.py:563
  113.5 22.0 %collective-permute-start.19 = (bf16[4,64,2048]{2,1,0:T(8,128)(2,1)}, bf16[4,64,2048]{2,1,0:T(8,128)(2,1)}, u32[]{:S(2)}, u32[]{:S(2)}) collective-permute-start(bf16[4,64,2048]{2,1,0:T(8,128)(2,1)} %collective-permute-done.14.refs_1_.refs_11_), channel_id=1, source_target_pairs={{0,1},{1,0},{2,3},{3,2},{4,5},{5,4},{6,7},{7,6},{8,9},{9,8},{10,11... | collective-permute-start | bytes 3145736 | tf_op jit(solution)/shard_map/ppermute | solution.py:532
  114.6 20.8 %collective-permute-start.20 = (bf16[4,64,2048]{2,1,0:T(8,128)(2,1)}, bf16[4,64,2048]{2,1,0:T(8,128)(2,1)}, u32[]{:S(2)}, u32[]{:S(2)}) collective-permute-start(bf16[4,64,2048]{2,1,0:T(8,128)(2,1)} %collective-permute-done.15.refs_2_.refs_12_), channel_id=1, source_target_pairs={{0,1},{1,0},{2,3},{3,2},{4,5},{5,4},{6,7},{7,6},{8,9},{9,8},{10,11... | collective-permute-start | bytes 3145736 | tf_op jit(solution)/shard_map/ppermute | solution.py:532
  115.2 20.3 %collective-permute-start.17 = (bf16[2,64,2048]{2,1,0:T(8,128)(2,1)S(1)}, bf16[2,64,2048]{2,1,0:T(8,128)(2,1)}, u32[]{:S(2)}, u32[]{:S(2)}) collective-permute-start(bf16[2,64,2048]{2,1,0:T(8,128)(2,1)S(1)} %slice.102), channel_id=1, source_target_pairs={{0,4},{4,0},{1,5},{5,1},{2,6},{6,2},{3,7},{7,3},{8,12},{12,8},{9,1... | collective-permute-start | bytes 1572872 | tf_op jit(solution)/shard_map/ppermute | solution.py:532
  115.7 19.8 %collective-permute-start.18 = (bf16[2,64,2048]{2,1,0:T(8,128)(2,1)S(1)}, bf16[2,64,2048]{2,1,0:T(8,128)(2,1)}, u32[]{:S(2)}, u32[]{:S(2)}) collective-permute-start(bf16[2,64,2048]{2,1,0:T(8,128)(2,1)S(1)} %slice.103), channel_id=1, source_target_pairs={{0,2},{2,0},{1,3},{3,1},{4,6},{6,4},{5,7},{7,5},{8,10},{10,8},{9,1... | collective-permute-start | bytes 1572872 | tf_op jit(solution)/shard_map/ppermute | solution.py:532
  117.9 17.5 %collective-permute-start.21 = (bf16[2,80,1024]{2,1,0:T(8,128)(2,1)}, bf16[2,80,1024]{2,1,0:T(8,128)(2,1)S(1)}, u32[]{:S(2)}, u32[]{:S(2)}) collective-permute-start(bf16[2,80,1024]{2,1,0:T(8,128)(2,1)} %dynamic-slice_bitcast_fusion), channel_id=1, source_target_pairs={{0,3},{1,2},{2,1},{3,0},{4,7},{5,6},{6,5},{7,4},{8,11},{9,10},{10,... | collective-permute-start | bytes 983048 | tf_op jit(solution)/shard_map/ppermute | solution.py:536
  136.5 25.7 %collective-permute-start.24 = (bf16[4,64,2048]{2,1,0:T(8,128)(2,1)}, bf16[4,64,2048]{2,1,0:T(8,128)(2,1)S(1)}, u32[]{:S(2)}, u32[]{:S(2)}) collective-permute-start(bf16[4,64,2048]{2,1,0:T(8,128)(2,1)} %all-to-all-done.2.refs_0_), channel_id=1, source_target_pairs={{0,2},{2,0},{1,3},{3,1},{4,6},{6,4},{5,7},{7,5},{8,10},{10,8},{9,1... | collective-permute-start | bytes 3145736 | tf_op jit(solution)/shard_map/ppermute | solution.py:532
  138.0 25.4 %collective-permute-start.25 = (bf16[4,64,2048]{2,1,0:T(8,128)(2,1)}, bf16[4,64,2048]{2,1,0:T(8,128)(2,1)S(1)}, u32[]{:S(2)}, u32[]{:S(2)}) collective-permute-start(bf16[4,64,2048]{2,1,0:T(8,128)(2,1)} %all-to-all-done.2.refs_0_), channel_id=1, source_target_pairs={{0,4},{4,0},{1,5},{5,1},{2,6},{6,2},{3,7},{7,3},{8,12},{12,8},{9,1... | collective-permute-start | bytes 3145736 | tf_op jit(solution)/shard_map/ppermute | solution.py:532
  139.5 23.9 %collective-permute-start.26 = (bf16[4,64,2048]{2,1,0:T(8,128)(2,1)}, bf16[4,64,2048]{2,1,0:T(8,128)(2,1)S(1)}, u32[]{:S(2)}, u32[]{:S(2)}) collective-permute-start(bf16[4,64,2048]{2,1,0:T(8,128)(2,1)} %all-to-all-done.2.refs_0_), channel_id=1, source_target_pairs={{0,1},{1,0},{2,3},{3,2},{4,5},{5,4},{6,7},{7,6},{8,9},{9,8},{10,11... | collective-permute-start | bytes 3145736 | tf_op jit(solution)/shard_map/ppermute | solution.py:532
  140.0 23.5 %collective-permute-start.27 = (bf16[640,1024]{1,0:T(8,128)(2,1)S(1)}, bf16[640,1024]{1,0:T(8,128)(2,1)S(1)}, u32[]{:S(2)}, u32[]{:S(2)}) collective-permute-start(bf16[640,1024]{1,0:T(8,128)(2,1)S(1)} %bitcast_select_fusion.g_ref.refs_30_), channel_id=1, source_target_pairs={{0,1},{1,0},{2,3},{3,2},{4,5},{5,4},{6,7},{7,6},{8,9},{9,8},{10,11... | collective-permute-start | bytes 3932168 | tf_op jit(solution)/shard_map/ppermute | solution.py:532
  165.7 16.9 %collective-permute-start.31 = (bf16[4,64,2048]{2,1,0:T(8,128)(2,1)S(1)}, bf16[4,64,2048]{2,1,0:T(8,128)(2,1)S(1)}, u32[]{:S(2)}, u32[]{:S(2)}) collective-permute-start(bf16[4,64,2048]{2,1,0:T(8,128)(2,1)S(1)} %collective-permute-done.24.refs_1_), channel_id=1, source_target_pairs={{0,1},{1,0},{2,3},{3,2},{4,5},{5,4},{6,7},{7,6},{8,9},{9,8},{10,11... | collective-permute-start | bytes 3145736 | tf_op jit(solution)/shard_map/ppermute | solution.py:532
  167.0 15.6 %collective-permute-start.32 = (bf16[4,64,2048]{2,1,0:T(8,128)(2,1)S(1)}, bf16[4,64,2048]{2,1,0:T(8,128)(2,1)S(1)}, u32[]{:S(2)}, u32[]{:S(2)}) collective-permute-start(bf16[4,64,2048]{2,1,0:T(8,128)(2,1)S(1)} %copy-done.16), channel_id=1, source_target_pairs={{0,1},{1,0},{2,3},{3,2},{4,5},{5,4},{6,7},{7,6},{8,9},{9,8},{10,11... | collective-permute-start | bytes 3145736 | tf_op jit(solution)/shard_map/ppermute | solution.py:532
  167.4 14.5 %collective-permute-start.29 = (bf16[2,64,2048]{2,1,0:T(8,128)(2,1)S(1)}, bf16[2,64,2048]{2,1,0:T(8,128)(2,1)S(1)}, u32[]{:S(2)}, u32[]{:S(2)}) collective-permute-start(bf16[2,64,2048]{2,1,0:T(8,128)(2,1)S(1)} %slice.104), channel_id=1, source_target_pairs={{0,4},{4,0},{1,5},{5,1},{2,6},{6,2},{3,7},{7,3},{8,12},{12,8},{9,1... | collective-permute-start | bytes 1572872 | tf_op jit(solution)/shard_map/ppermute | solution.py:532
  168.9 13.7 %collective-permute-start.30 = (bf16[2,64,2048]{2,1,0:T(8,128)(2,1)S(1)}, bf16[2,64,2048]{2,1,0:T(8,128)(2,1)S(1)}, u32[]{:S(2)}, u32[]{:S(2)}) collective-permute-start(bf16[2,64,2048]{2,1,0:T(8,128)(2,1)S(1)} %slice.105), channel_id=1, source_target_pairs={{0,2},{2,0},{1,3},{3,1},{4,6},{6,4},{5,7},{7,5},{8,10},{10,8},{9,1... | collective-permute-start | bytes 1572872 | tf_op jit(solution)/shard_map/ppermute | solution.py:532
  183.6 29.5 %collective-permute-start.38 = (bf16[640,1024]{1,0:T(8,128)(2,1)S(1)}, bf16[640,1024]{1,0:T(8,128)(2,1)S(1)}, u32[]{:S(2)}, u32[]{:S(2)}) collective-permute-start(bf16[640,1024]{1,0:T(8,128)(2,1)S(1)} %copy-done.20), channel_id=1, source_target_pairs={{0,1},{1,0},{2,3},{3,2},{4,5},{5,4},{6,7},{7,6},{8,9},{9,8},{10,11... | collective-permute-start | bytes 3932168 | tf_op jit(solution)/shard_map/ppermute | solution.py:532
  184.1 29.0 %collective-permute-start.36 = (bf16[640,1024]{1,0:T(8,128)(2,1)S(1)}, bf16[640,1024]{1,0:T(8,128)(2,1)}, u32[]{:S(2)}, u32[]{:S(2)}) collective-permute-start(bf16[640,1024]{1,0:T(8,128)(2,1)S(1)} %bitcast.140), channel_id=1, source_target_pairs={{0,1},{1,0},{2,3},{3,2},{4,5},{5,4},{6,7},{7,6},{8,9},{9,8},{10,11... | collective-permute-start | bytes 3932168 | tf_op jit(solution)/shard_map/ppermute | solution.py:532
  184.2 29.0 %collective-permute-start.37 = (bf16[640,1024]{1,0:T(8,128)(2,1)}, bf16[640,1024]{1,0:T(8,128)(2,1)}, u32[]{:S(2)}, u32[]{:S(2)}) collective-permute-start(bf16[640,1024]{1,0:T(8,128)(2,1)} %get-tuple-element.288.refs_0_), channel_id=1, source_target_pairs={{0,1},{1,0},{2,3},{3,2},{4,5},{5,4},{6,7},{7,6},{8,9},{9,8},{10,11... | collective-permute-start | bytes 3932168 | tf_op jit(solution)/shard_map/ppermute | solution.py:532
  184.6 28.5 %collective-permute-start.35 = (bf16[4,128,1024]{2,1,0:T(8,128)(2,1)}, bf16[4,128,1024]{2,1,0:T(8,128)(2,1)S(1)}, u32[]{:S(2)}, u32[]{:S(2)}) collective-permute-start(bf16[4,128,1024]{2,1,0:T(8,128)(2,1)} %get-tuple-element.285), channel_id=1, source_target_pairs={{0,4},{4,0},{1,5},{5,1},{2,6},{6,2},{3,7},{7,3},{8,12},{12,8},{9,1... | collective-permute-start | bytes 3145736 | tf_op jit(solution)/shard_map/ppermute | solution.py:532
  213.8 33.8 %collective-permute-start.44 = (bf16[4,128,1024]{2,1,0:T(8,128)(2,1)}, bf16[4,128,1024]{2,1,0:T(8,128)(2,1)}, u32[]{:S(2)}, u32[]{:S(2)}) collective-permute-start(bf16[4,128,1024]{2,1,0:T(8,128)(2,1)} %get-tuple-element.316), channel_id=1, source_target_pairs={{0,4},{4,0},{1,5},{5,1},{2,6},{6,2},{3,7},{7,3},{8,12},{12,8},{9,1... | collective-permute-start | bytes 3145736 | tf_op jit(solution)/shard_map/ppermute | solution.py:532
  225.8 36.8 %collective-permute-start.41 = (bf16[640,1536]{1,0:T(8,128)(2,1)}, bf16[640,1536]{1,0:T(8,128)(2,1)}, u32[]{:S(2)}, u32[]{:S(2)}) collective-permute-start(bf16[640,1536]{1,0:T(8,128)(2,1)} %bitcast.132), channel_id=1, source_target_pairs={{0,1},{1,0},{2,3},{3,2},{4,5},{5,4},{6,7},{7,6},{8,9},{9,8},{10,11... | collective-permute-start | bytes 5898248 | tf_op jit(solution)/shard_map/ppermute | solution.py:532
  226.3 25.6 %collective-permute-start.43 = (bf16[4,128,1024]{2,1,0:T(8,128)(2,1)S(1)}, bf16[4,128,1024]{2,1,0:T(8,128)(2,1)S(1)}, u32[]{:S(2)}, u32[]{:S(2)}) collective-permute-start(bf16[4,128,1024]{2,1,0:T(8,128)(2,1)S(1)} %add_convert_fusion.1), channel_id=1, source_target_pairs={{0,2},{2,0},{1,3},{3,1},{4,6},{6,4},{5,7},{7,5},{8,10},{10,8},{9,1... | collective-permute-start | bytes 3145736 | tf_op jit(solution)/shard_map/ppermute | solution.py:532
  234.8 17.2 %collective-permute-start.42 = (bf16[4,64,1024]{2,1,0:T(8,128)(2,1)}, bf16[4,64,1024]{2,1,0:T(8,128)(2,1)}, u32[]{:S(2)}, u32[]{:S(2)}) collective-permute-start(bf16[4,64,1024]{2,1,0:T(8,128)(2,1)} %get-tuple-element.313), channel_id=1, source_target_pairs={{0,4},{4,0},{1,5},{5,1},{2,6},{6,2},{3,7},{7,3},{8,12},{12,8},{9,1... | collective-permute-start | bytes 1572872 | tf_op jit(solution)/shard_map/ppermute | solution.py:532
  235.5 45.4 %collective-permute-start.47 = (bf16[4,64,1024]{2,1,0:T(8,128)(2,1)}, bf16[4,64,1024]{2,1,0:T(8,128)(2,1)}, u32[]{:S(2)}, u32[]{:S(2)}) collective-permute-start(bf16[4,64,1024]{2,1,0:T(8,128)(2,1)} %get-tuple-element.323), channel_id=1, source_target_pairs={{0,4},{4,0},{1,5},{5,1},{2,6},{6,2},{3,7},{7,3},{8,12},{12,8},{9,1... | collective-permute-start | bytes 1572872 | tf_op jit(solution)/shard_map/ppermute | solution.py:532
  254.8 30.3 %all-to-all-start.3 = ((bf16[4,128,1024]{2,1,0:T(8,128)(2,1)}), bf16[4,128,1024]{2,1,0:T(8,128)(2,1)}, u32[]{:S(2)}, u32[]{:S(2)}) async-start(bf16[4,128,1024]{2,1,0:T(8,128)(2,1)} %add_convert_fusion), calls=%async_computation.3 | async-start | bytes 2097152 | tf_op jit(solution)/shard_map/all_to_all | solution.py:563
  261.1 19.8 %collective-permute-start.46 = (bf16[4,64,1024]{2,1,0:T(8,128)(2,1)}, bf16[4,64,1024]{2,1,0:T(8,128)(2,1)}, u32[]{:S(2)}, u32[]{:S(2)}) collective-permute-start(bf16[4,64,1024]{2,1,0:T(8,128)(2,1)} %add_convert_fusion.6), channel_id=1, source_target_pairs={{0,2},{2,0},{1,3},{3,1},{4,6},{6,4},{5,7},{7,5},{8,10},{10,8},{9,1... | collective-permute-start | bytes 1572872 | tf_op jit(solution)/shard_map/ppermute | solution.py:532
  261.9 19.3 %collective-permute-start.48 = (bf16[4,64,1536]{2,1,0:T(8,128)(2,1)}, bf16[4,64,1536]{2,1,0:T(8,128)(2,1)}, u32[]{:S(2)}, u32[]{:S(2)}) collective-permute-start(bf16[4,64,1536]{2,1,0:T(8,128)(2,1)} %get-tuple-element.324), channel_id=1, source_target_pairs={{0,4},{4,0},{1,5},{5,1},{2,6},{6,2},{3,7},{7,3},{8,12},{12,8},{9,1... | collective-permute-start | bytes 2359304 | tf_op jit(solution)/shard_map/ppermute | solution.py:532
  268.9 16.2 %collective-permute-start.45 = (bf16[4,64,768]{2,1,0:T(8,128)(2,1)}, bf16[4,64,768]{2,1,0:T(8,128)(2,1)}, u32[]{:S(2)}, u32[]{:S(2)}) collective-permute-start(bf16[4,64,768]{2,1,0:T(8,128)(2,1)} %get-tuple-element.320), channel_id=1, source_target_pairs={{0,2},{2,0},{1,3},{3,1},{4,6},{6,4},{5,7},{7,5},{8,10},{10,8},{9,1... | collective-permute-start | bytes 1179656 | tf_op jit(solution)/shard_map/ppermute | solution.py:532
  285.1 15.9 %collective-permute-start.49 = (bf16[640,1536]{1,0:T(8,128)(2,1)}, bf16[640,1536]{1,0:T(8,128)(2,1)}, u32[]{:S(2)}, u32[]{:S(2)}) collective-permute-start(bf16[640,1536]{1,0:T(8,128)(2,1)} %bitcast.135), channel_id=1, source_target_pairs={{0,1},{1,0},{2,3},{3,2},{4,5},{5,4},{6,7},{7,6},{8,9},{9,8},{10,11... | collective-permute-start | bytes 5898248 | tf_op jit(solution)/shard_map/ppermute | solution.py:532
  286.0 37.7 %collective-permute-start.54 = (bf16[4,64,1536]{2,1,0:T(8,128)(2,1)}, bf16[4,64,1536]{2,1,0:T(8,128)(2,1)}, u32[]{:S(2)}, u32[]{:S(2)}) collective-permute-start(bf16[4,64,1536]{2,1,0:T(8,128)(2,1)} %get-tuple-element.344), channel_id=1, source_target_pairs={{0,4},{4,0},{1,5},{5,1},{2,6},{6,2},{3,7},{7,3},{8,12},{12,8},{9,1... | collective-permute-start | bytes 2359304 | tf_op jit(solution)/shard_map/ppermute | solution.py:532
  286.8 38.1 %collective-permute-start.51 = (bf16[4,64,768]{2,1,0:T(8,128)(2,1)S(1)}, bf16[4,64,768]{2,1,0:T(8,128)(2,1)}, u32[]{:S(2)}, u32[]{:S(2)}) collective-permute-start(bf16[4,64,768]{2,1,0:T(8,128)(2,1)S(1)} %get-tuple-element.339), channel_id=1, source_target_pairs={{0,2},{2,0},{1,3},{3,1},{4,6},{6,4},{5,7},{7,5},{8,10},{10,8},{9,1... | collective-permute-start | bytes 1179656 | tf_op jit(solution)/shard_map/ppermute | solution.py:532
  289.9 35.0 %all-to-all-start.4 = ((bf16[4,64,1024]{2,1,0:T(8,128)(2,1)}), bf16[4,64,1024]{2,1,0:T(8,128)(2,1)}, u32[]{:S(2)}, u32[]{:S(2)}) async-start(bf16[4,64,1024]{2,1,0:T(8,128)(2,1)} %add_convert_fusion.5), calls=%async_computation.4 | async-start | bytes 1048576 | tf_op jit(solution)/shard_map/all_to_all | solution.py:563
  296.6 28.3 %collective-permute-start.53 = (bf16[4,64,1536]{2,1,0:T(8,128)(2,1)}, bf16[4,64,1536]{2,1,0:T(8,128)(2,1)}, u32[]{:S(2)}, u32[]{:S(2)}) collective-permute-start(bf16[4,64,1536]{2,1,0:T(8,128)(2,1)} %add_convert_fusion.4), channel_id=1, source_target_pairs={{0,2},{2,0},{1,3},{3,1},{4,6},{6,4},{5,7},{7,5},{8,10},{10,8},{9,1... | collective-permute-start | bytes 2359304 | tf_op jit(solution)/shard_map/ppermute | solution.py:532
  299.7 25.2 %collective-permute-start.52 = (bf16[4,64,768]{2,1,0:T(8,128)(2,1)}, bf16[4,64,768]{2,1,0:T(8,128)(2,1)}, u32[]{:S(2)}, u32[]{:S(2)}) collective-permute-start(bf16[4,64,768]{2,1,0:T(8,128)(2,1)} %add_convert_fusion.8), channel_id=1, source_target_pairs={{0,4},{4,0},{1,5},{5,1},{2,6},{6,2},{3,7},{7,3},{8,12},{12,8},{9,1... | collective-permute-start | bytes 1179656 | tf_op jit(solution)/shard_map/ppermute | solution.py:532
  306.4 18.5 %collective-permute-start.50 = (bf16[4,64,768]{2,1,0:T(8,128)(2,1)S(1)}, bf16[4,64,768]{2,1,0:T(8,128)(2,1)}, u32[]{:S(2)}, u32[]{:S(2)}) collective-permute-start(bf16[4,64,768]{2,1,0:T(8,128)(2,1)S(1)} %get-tuple-element.338), channel_id=1, source_target_pairs={{0,4},{4,0},{1,5},{5,1},{2,6},{6,2},{3,7},{7,3},{8,12},{12,8},{9,1... | collective-permute-start | bytes 1179656 | tf_op jit(solution)/shard_map/ppermute | solution.py:532
  323.6 31.5 %collective-permute-start.56 = (bf16[4,64,768]{2,1,0:T(8,128)(2,1)S(1)}, bf16[4,64,768]{2,1,0:T(8,128)(2,1)}, u32[]{:S(2)}, u32[]{:S(2)}) collective-permute-start(bf16[4,64,768]{2,1,0:T(8,128)(2,1)S(1)} %get-tuple-element.358), channel_id=1, source_target_pairs={{0,4},{4,0},{1,5},{5,1},{2,6},{6,2},{3,7},{7,3},{8,12},{12,8},{9,1... | collective-permute-start | bytes 1179656 | tf_op jit(solution)/shard_map/ppermute | solution.py:532
  324.9 14.4 %collective-permute-start.57 = (f32[8,1536]{1,0:T(8,128)}, f32[8,1536]{1,0:T(8,128)S(1)}, u32[]{:S(2)}, u32[]{:S(2)}) collective-permute-start(f32[8,1536]{1,0:T(8,128)} %shard_map.267), channel_id=1, source_target_pairs={{0,1},{1,0},{2,3},{3,2},{4,5},{5,4},{6,7},{7,6},{8,9},{9,8},{10,11... | collective-permute-start | bytes 147464 | tf_op jit(solution)/shard_map/ppermute | solution.py:532
  327.5 27.6 %all-to-all-start.5 = ((bf16[4,64,1536]{2,1,0:T(8,128)(2,1)}), bf16[4,64,1536]{2,1,0:T(8,128)(2,1)S(1)}, u32[]{:S(2)}, u32[]{:S(2)}) async-start(bf16[4,64,1536]{2,1,0:T(8,128)(2,1)} %add_convert_fusion.3), calls=%async_computation.5 | async-start | bytes 1572864 | tf_op jit(solution)/shard_map/all_to_all | solution.py:563
  333.7 21.4 %collective-permute-start.55 = (bf16[4,64,768]{2,1,0:T(8,128)(2,1)S(1)}, bf16[4,64,768]{2,1,0:T(8,128)(2,1)S(1)}, u32[]{:S(2)}, u32[]{:S(2)}) collective-permute-start(bf16[4,64,768]{2,1,0:T(8,128)(2,1)S(1)} %add_convert_fusion.7), channel_id=1, source_target_pairs={{0,2},{2,0},{1,3},{3,1},{4,6},{6,4},{5,7},{7,5},{8,10},{10,8},{9,1... | collective-permute-start | bytes 1179656 | tf_op jit(solution)/shard_map/ppermute | solution.py:532
  336.0 19.1 %collective-permute-start.60 = (bf16[128,1024]{1,0:T(8,128)(2,1)S(1)}, bf16[128,1024]{1,0:T(8,128)(2,1)}, u32[]{:S(2)}, u32[]{:S(2)}) collective-permute-start(bf16[128,1024]{1,0:T(8,128)(2,1)S(1)} %reduce_sum.59.refs_8_), channel_id=1, source_target_pairs={{0,2},{2,0},{1,3},{3,1},{4,6},{6,4},{5,7},{7,5},{8,10},{10,8},{9,1... | collective-permute-start | bytes 786440 | tf_op jit(solution)/shard_map/ppermute | solution.py:532
  338.5 16.7 %collective-permute-start.59 = (bf16[64,1024]{1,0:T(8,128)(2,1)S(1)}, bf16[64,1024]{1,0:T(8,128)(2,1)S(1)}, u32[]{:S(2)}, u32[]{:S(2)}) collective-permute-start(bf16[64,1024]{1,0:T(8,128)(2,1)S(1)} %reduce_sum.58.refs_0_), channel_id=1, source_target_pairs={{0,2},{2,0},{1,3},{3,1},{4,6},{6,4},{5,7},{7,5},{8,10},{10,8},{9,1... | collective-permute-start | bytes 393224 | tf_op jit(solution)/shard_map/ppermute | solution.py:532
  339.3 15.2 %collective-permute-start.58 = (f32[8,1536]{1,0:T(8,128)S(1)}, f32[8,1536]{1,0:T(8,128)S(1)}, u32[]{:S(2)}, u32[]{:S(2)}) collective-permute-start(f32[8,1536]{1,0:T(8,128)S(1)} %add.147), channel_id=1, source_target_pairs={{0,2},{2,0},{1,3},{3,1},{4,6},{6,4},{5,7},{7,5},{8,10},{10,8},{9,1... | collective-permute-start | bytes 147464 | tf_op jit(solution)/shard_map/ppermute | solution.py:532
  358.2 31.4 %all-to-all-start.6 = ((bf16[4,64,1536]{2,1,0:T(8,128)(2,1)}), bf16[4,64,1536]{2,1,0:T(8,128)(2,1)S(1)}, u32[]{:S(2)}, u32[]{:S(2)}) async-start(bf16[4,64,1536]{2,1,0:T(8,128)(2,1)} %add_convert_fusion.2), calls=%async_computation.6 | async-start | bytes 1572864 | tf_op jit(solution)/shard_map/all_to_all | solution.py:563
  366.9 22.0 %collective-permute-start.66 = (bf16[4,80,1024]{2,1,0:T(8,128)(2,1)}, bf16[4,80,1024]{2,1,0:T(8,128)(2,1)S(1)}, u32[]{:S(2)}, u32[]{:S(2)}) collective-permute-start(bf16[4,80,1024]{2,1,0:T(8,128)(2,1)} %get-tuple-element.414), channel_id=1, source_target_pairs={{0,1},{1,0},{2,3},{3,2},{4,5},{5,4},{6,7},{7,6},{8,9},{9,8},{10,11... | collective-permute-start | bytes 1966088 | tf_op jit(solution)/shard_map/ppermute | solution.py:536
  366.9 22.6 %collective-permute-start.67 = (bf16[4,80,1024]{2,1,0:T(8,128)(2,1)}, bf16[4,80,1024]{2,1,0:T(8,128)(2,1)S(1)}, u32[]{:S(2)}, u32[]{:S(2)}) collective-permute-start(bf16[4,80,1024]{2,1,0:T(8,128)(2,1)} %get-tuple-element.415), channel_id=1, source_target_pairs={{0,2},{1,3},{2,0},{3,1},{4,6},{5,7},{6,4},{7,5},{8,10},{9,11},{10,... | collective-permute-start | bytes 1966088 | tf_op jit(solution)/shard_map/ppermute | solution.py:536
  370.4 13.0 %collective-permute-start.64 = (f32[1536]{0:T(1024)}, f32[1536]{0:T(1024)}, u32[]{:S(2)}, u32[]{:S(2)}) collective-permute-start(f32[1536]{0:T(1024)} %get-tuple-element.400), channel_id=1, source_target_pairs={{0,16},{8,24},{16,0},{24,8},{1,17},{9,25},{17,1},{25,9},{2,18},{10... | collective-permute-start | bytes 18440 | tf_op jit(solution)/shard_map/ppermute | solution.py:536
  375.8 13.1 %collective-permute-start.61 = (bf16[64,1536]{1,0:T(8,128)(2,1)}, bf16[64,1536]{1,0:T(8,128)(2,1)S(1)}, u32[]{:S(2)}, u32[]{:S(2)}) collective-permute-start(bf16[64,1536]{1,0:T(8,128)(2,1)} %reduce_sum.60.refs_4_), channel_id=1, source_target_pairs={{0,2},{2,0},{1,3},{3,1},{4,6},{6,4},{5,7},{7,5},{8,10},{10,8},{9,1... | collective-permute-start | bytes 589832 | tf_op jit(solution)/shard_map/ppermute | solution.py:532
  383.4 18.8 %collective-permute-start.74 = (bf16[4,80,1024]{2,1,0:T(8,128)(2,1)}, bf16[4,80,1024]{2,1,0:T(8,128)(2,1)S(1)}, u32[]{:S(2)}, u32[]{:S(2)}) collective-permute-start(bf16[4,80,1024]{2,1,0:T(8,128)(2,1)} %get-tuple-element.412), channel_id=1, source_target_pairs={{0,3},{1,2},{2,1},{3,0},{4,7},{5,6},{6,5},{7,4},{8,11},{9,10},{10,... | collective-permute-start | bytes 1966088 | tf_op jit(solution)/shard_map/ppermute | solution.py:536
  393.0 13.7 %collective-permute-start.75 = (bf16[64,1536]{1,0:T(8,128)(2,1)}, bf16[64,1536]{1,0:T(8,128)(2,1)S(1)}, u32[]{:S(2)}, u32[]{:S(2)}) collective-permute-start(bf16[64,1536]{1,0:T(8,128)(2,1)} %reduce_sum.61.refs_0_), channel_id=1, source_target_pairs={{0,2},{2,0},{1,3},{3,1},{4,6},{6,4},{5,7},{7,5},{8,10},{10,8},{9,1... | collective-permute-start | bytes 589832 | tf_op jit(solution)/shard_map/ppermute | solution.py:532
  393.8 17.4 %collective-permute-start.76 = (bf16[64,1536]{1,0:T(8,128)(2,1)}, bf16[64,1536]{1,0:T(8,128)(2,1)S(1)}, u32[]{:S(2)}, u32[]{:S(2)}) collective-permute-start(bf16[64,1536]{1,0:T(8,128)(2,1)} %reduce_sum.61.refs_0_), channel_id=1, source_target_pairs={{0,1},{1,0},{2,3},{3,2},{4,5},{5,4},{6,7},{7,6},{8,9},{9,8},{10,11... | collective-permute-start | bytes 589832 | tf_op jit(solution)/shard_map/ppermute | solution.py:532
  (59 other events, 378.1 us)

commit v4 on v3

--- a/solution.py
+++ b/solution.py
@@ -581,12 +581,12 @@
     lane = 0
     for t in range(3):
         lane = put(first_ref, lane, columns(qkv_ref, t * width + c * part, part))
-    lane = put(first_ref, lane, columns(out_ref, c * part, part))
     packed = jnp.concatenate([ref[...] for ref in vector_refs], axis=0)
     padding = jnp.zeros((rows - packed.shape[0], LANES), packed.dtype)
     put(first_ref, lane, jnp.concatenate([packed, padding], axis=0))
     half = up_ref.shape[1] // 2
-    put(second_ref, 0, columns(up_ref, c * half, half))
+    lane = put(second_ref, 0, columns(up_ref, c * half, half))
+    put(second_ref, lane, columns(out_ref, c * part, part))
     blocks = down_ref.shape[0] // 4 // rows
     lane = 0
     for block in range(blocks):
@@ -598,7 +598,7 @@
     depth, rows = lax.axis_size("z"), qkv.shape[0] // 2
     vectors = [v.reshape(-1, LANES) for v in vectors]
     width = out.shape[1]
-    wide = (2 * width + LANES, up.shape[1] // 2, down.shape[0] // 4 // rows * width)
+    wide = (3 * width // 2 + LANES, (up.shape[1] + width) // 2, down.shape[0] // 4 // rows * width)
     vmem = pl.BlockSpec(memory_space=pltpu.VMEM)
     return pl.pallas_call(
         functools.partial(pieces_kernel, depth, rows),
@@ -918,7 +918,6 @@
         gain_a, shift_a, bias_qv, bias_out, gain_b, shift_b, bias_up, bias_down = vectors
         arrays = (z1, x1, y1, *d1, *c1, *core_swap(*d1))
         qkv_full = Weight(arrays, blocks=GROUPS, step=3 * width // GROUPS)
-        out_full = Weight(arrays, base=cut_qkv.wide, blocks=2, step=cut_out.wide)
         x2, y2 = swap(z2, "x"), swap(z2, "y")
         normed_a, joint = project(place, tokens, gain_a, shift_a, qkv_full, bias_qv)
         joint, third = tie(joint, third)
@@ -932,7 +931,9 @@
         )
         cot = in_images(cot)
         x3, y3 = swap(z3, "x"), swap(z3, "y")
-        up_full = Weight((z2, x2, y2, *d2, *c2, *core_swap(*d2)), blocks=cut_up.columns // STEP)
+        arrays = (z2, x2, y2, *d2, *c2, *core_swap(*d2))
+        up_full = Weight(arrays, blocks=cut_up.columns // STEP)
+        out_full = Weight(arrays, base=cut_up.wide, blocks=2, step=cut_out.wide)
         middle, normed_b, hidden, slope, hidden_other = expand(
             place, tokens, context, out_full, bias_out, gain_b, shift_b, up_full, bias_up
         )

time: 421 us -> 420 us (level)
  waiting for transfers between devices: 102 us -> 95.9 us
    ppermute x66, waiting for transfers between devices: 60.6 us -> 55.8 us  [swap(): return lax.ppermute(value, axis, [(0, 1), (1, 0)])]
    unnamed x81 -> x77, local copies, waits for them, and re-layouts: 8.61 us -> 8.8 us
  transfers between devices with their start and end apart: 85 -> 85, of which waited for: 28 -> 26; matrix products, arithmetic and copies ran while one was open for 10% -> 11% of each run, Pallas kernels for 40% -> 41%
where the time goes in v4:
time: 420 us; the launch traced here: 414 us
  Pallas kernels  174 us (41%)
  waiting for transfers between devices  95.9 us (23%)
  starting transfers between devices  88.3 us (21%)
  other arithmetic  32.3 us (8%)
  local copies, waits for them, and re-layouts  21.8 us (5%)
    pallas_call x5, Pallas kernels, stepped(): pl.pallas_call(functools.partial(kernel, weights), grid_spec=pltpu.Prefet...  83 us
    ppermute x66, waiting for transfers between devices, swap(): return lax.ppermute(value, axis, [(0, 1), (1, 0)])  55.8 us
    pallas_call x5, Pallas kernels, grad_parts(): pl.pallas_call(kernel, grid_spec=pltpu.PrefetchScalarGridSpec(num_scalar_...  41.6 us
    ppermute x66, starting transfers between devices, swap(): return lax.ppermute(value, axis, [(0, 1), (1, 0)])  41.5 us
    pallas_call x3, Pallas kernels, attention(): pl.pallas_call(attend_back_kernel if back else attend_kernel, grid=(image...  37.6 us
    all_to_all x7, starting transfers between devices, exchange(): return lax.all_to_all(blocks, axis, split_axis=0, concat_axis=0, tiled=True)  37 us
    ppermute x12, waiting for transfers between devices, send(): lax.ppermute(value, axis, [(i, i ^ step) for i in range(lax.axis_size(axi...  36.5 us
    convert_element_type x4, other arithmetic, grad_z(): sum((v.astype(F32) for v in (parts[0], from_x, from_y))).astype(BF16)  10 us
  transfers between devices with their start and end apart: 85, of which 26 were waited for; matrix products, arithmetic and copies ran while one was open for 11% of the time, Pallas kernels for 41%

profile of v4, /device:TPU:0, one launch (start us, length us, event | category | flops | bytes accessed | tf_op | source)
XLA Modules:
  0.0 413.8 jit_solution(12669533257524339457)
XLA Ops:
  1.2 3.7 shard_map.254
  4.9 6.4 %all-to-all-start = ((bf16[4,64,1664]{2,1,0:T(8,128)(2,1)}), bf16[4,64,1664]{2,1,0:T(8,128)(2,1)}, u32[]{:S(2)}, u32[]{:S(2)}) async-start(bf16[4,64,1664]{2,1,0:T(8,128)(2,1)} %get-tuple-element.207), calls=%async_computation | async-start | bytes 1703936 | tf_op jit(solution)/shard_map/all_to_all | solution.py:563
  11.6 1.6 collective-permute-start.1
  13.9 1.5 collective-permute-start.4
  15.4 6.7 %collective-permute-done.1 = bf16[2,80,1024]{2,1,0:T(8,128)(2,1)S(1)} collective-permute-done((bf16[2,80,1024]{2,1,0:T(8,128)(2,1)S(1)}, bf16[2,80,1024]{2,1,0:T(8,128)(2,1)S(1)}, u32[]{:S(2)}, u32[]{:S(2)}) %collective-permute-start.1) | collective-permute-done | bytes 327712 | tf_op jit(solution)/shard_map/ppermute | solution.py:536
  22.1 6.1 %collective-permute-done.2 = bf16[2,80,1024]{2,1,0:T(8,128)(2,1)S(1)} collective-permute-done((bf16[2,80,1024]{2,1,0:T(8,128)(2,1)S(1)}, bf16[2,80,1024]{2,1,0:T(8,128)(2,1)S(1)}, u32[]{:S(2)}, u32[]{:S(2)}) %collective-permute-start.2) | collective-permute-done | bytes 327712 | tf_op jit(solution)/shard_map/ppermute | solution.py:536
  28.3 7.6 %collective-permute-done.4 = bf16[2,80,1024]{2,1,0:T(8,128)(2,1)} collective-permute-done((bf16[2,80,1024]{2,1,0:T(8,128)(2,1)S(1)}, bf16[2,80,1024]{2,1,0:T(8,128)(2,1)}, u32[]{:S(2)}, u32[]{:S(2)}) %collective-permute-start.4) | collective-permute-done | bytes 327712 | tf_op jit(solution)/shard_map/ppermute | solution.py:536
  35.8 1.5 collective-permute-start.5
  37.3 1.5 collective-permute-start.6
  38.9 5.1 %all-to-all-start.1 = ((bf16[4,64,2560]{2,1,0:T(8,128)(2,1)}), bf16[4,64,2560]{2,1,0:T(8,128)(2,1)S(1)}, u32[]{:S(2)}, u32[]{:S(2)}) async-start(bf16[4,64,2560]{2,1,0:T(8,128)(2,1)} %get-tuple-element.215), calls=%async_computation.1 | async-start | bytes 2621440 | tf_op jit(solution)/shard_map/all_to_all | solution.py:563
  45.2 11.5 %collective-permute-done.5.refs_1_ = bf16[4,64,1664]{2,1,0:T(8,128)(2,1)} collective-permute-done((bf16[4,64,1664]{2,1,0:T(8,128)(2,1)}, bf16[4,64,1664]{2,1,0:T(8,128)(2,1)}, u32[]{:S(2)}, u32[]{:S(2)}) %collective-permute-start.5) | collective-permute-done | bytes 852000 | tf_op jit(solution)/shard_map/ppermute | solution.py:532
  62.2 1.5 collective-permute-start.7
  65.4 9.0 %collective-permute-done.7.refs_3_ = bf16[2,64,1664]{2,1,0:T(8,128)(2,1)} collective-permute-done((bf16[2,64,1664]{2,1,0:T(8,128)(2,1)S(1)}, bf16[2,64,1664]{2,1,0:T(8,128)(2,1)}, u32[]{:S(2)}, u32[]{:S(2)}) %collective-permute-start.7) | collective-permute-done | bytes 426016 | tf_op jit(solution)/shard_map/ppermute | solution.py:532
  74.5 1.2 collective-permute-done.8.refs_4_
  78.5 9.8 %shard_map.255 = (bf16[640,1024]{1,0:T(8,128)(2,1)}, bf16[640,3072]{1,0:T(8,128)(2,1)}) custom-call(s32[3]{0:T(128)} %pad_add_fusion.place_ref, bf16[4,64,1664]{2,1,0:T(8,128)(2,1)} %all-to-all-done.refs_0_, bf16[4,64,1664]{2,1,0:T(8,128)(2,1)} %collective-permute-done.5.refs_1_, bf16[4,64,1664]{2,1,0:T(8,128)(2,1)} %collective-permute-done.6.refs_2_, ...), custom_call_target="tpu_custom_call" | custom-call | flops 11000000512 | tf_op jit(solution)/shard_map/pallas_call | solution.py:260
  88.3 5.6 %all-to-all-start.2 = ((bf16[4,64,2048]{2,1,0:T(8,128)(2,1)}), bf16[4,64,2048]{2,1,0:T(8,128)(2,1)}, u32[]{:S(2)}, u32[]{:S(2)}) async-start(bf16[4,64,2048]{2,1,0:T(8,128)(2,1)} %get-tuple-element.242), calls=%async_computation.2 | async-start | bytes 2097152 | tf_op jit(solution)/shard_map/all_to_all | solution.py:563
  94.8 12.3 %collective-permute-done.14.refs_1_.refs_11_.refs_21_ = bf16[4,64,2560]{2,1,0:T(8,128)(2,1)S(1)} collective-permute-done((bf16[4,64,2560]{2,1,0:T(8,128)(2,1)S(1)}, bf16[4,64,2560]{2,1,0:T(8,128)(2,1)S(1)}, u32[]{:S(2)}, u32[]{:S(2)}) %collective-permute-start.14) | collective-permute-done | bytes 1310752 | tf_op jit(solution)/shard_map/ppermute | solution.py:532
  113.8 16.1 %shard_map.256 = (bf16[2,320,1024]{2,1,0:T(8,128)(2,1)}, f32[2,320,1024]{2,1,0:T(8,128)}) custom-call(f32[2,320,1]{2,1,0:T(8,128)} %compare_select_fusion.bias_ref, bf16[2,320,3072]{2,1,0:T(8,128)(2,1)} %bitcast.147, bf16[2,320,3072]{2,1,0:T(8,128)(2,1)} %bitcast.148, bf16[2,320,3072]{2,1,0:T(8,128)(2,1)} %bitcast.149), custom_call_target="tpu_custom_call" | custom-call | flops 14080000000 | tf_op jit(solution)/shard_map/pallas_call | solution.py:133
  129.9 3.9 collective-permute-done.21
  136.0 1.5 collective-permute-start.25
  137.5 1.2 pad_maximum_fusion.3
  139.9 18.4 %shard_map.257 = (f32[640,1024]{1,0:T(8,128)}, bf16[640,1024]{1,0:T(8,128)(2,1)}, bf16[640,4096]{1,0:T(8,128)(2,1)}, bf16[640,4096]{1,0:T(8,128)(2,1)}, bf16[640,2048]{1,0:T(8,128)(2,1)}) custom-call(s32[3]{0:T(128)} %pad_add_fusion.place_ref, bf16[4,64,2560]{2,1,0:T(8,128)(2,1)} %copy-done.6, bf16[4,64,2560]{2,1,0:T(8,128)(2,1)} %copy-done.10, ...), custom_call_target="tpu_custom_call" | custom-call | flops 22000001024 | tf_op jit(solution)/shard_map/pallas_call | solution.py:260
  158.3 2.6 collective-permute-done.24.refs_1_
  165.3 1.5 collective-permute-start.29
  168.9 11.6 %shard_map.258 = (bf16[4,128,1024]{2,1,0:T(8,128)(2,1)S(1)}, bf16[4,128,1024]{2,1,0:T(8,128)(2,1)}, bf16[4,128,1024]{2,1,0:T(8,128)(2,1)}, bf16[4,128,1024]{2,1,0:T(8,128)(2,1)}) custom-call(s32[3]{0:T(128)S(1)} %copy-done.2, bf16[640,4096]{1,0:T(8,128)(2,1)} %get-tuple-element.362.a0_ref.a1_ref.refs_10_, ...), custom_call_target="tpu_custom_call" | custom-call | flops 10150215680 | tf_op jit(solution)/shard_map/pallas_call | solution.py:705
  184.3 26.7 %shard_map.259 = (bf16[640,4096]{1,0:T(8,128)(2,1)}, f32[1,4096]{1,0:T(1,128)}, f32[640,1024]{1,0:T(8,128)}, bf16[640,1024]{1,0:T(8,128)(2,1)}, bf16[640,1024]{1,0:T(8,128)(2,1)}, /*index=5*/f32[8,1024]{1,0:T(8,128)}) custom-call(s32[3]{0:T(128)} %pad_add_fusion.place_ref, bf16[4,64,2048]{2,1,0:T(8,128)(2,1)} %all-to-all-done.2.refs_0_, ...), custom_call_target="tpu_custom_call" | custom-call | flops 25300000768 | tf_op jit(solution)/shard_map/pallas_call | solution.py:260
  211.6 1.2 collective-permute-start.44
  212.9 10.8 %shard_map.260 = bf16[2,320,1536]{2,1,0:T(8,128)(2,1)} custom-call(f32[2,320,1]{2,1,0:T(8,128)} %compare_select_fusion.bias_ref, bf16[2,320,3072]{2,1,0:T(8,128)(2,1)} %bitcast.150, bf16[2,320,3072]{2,1,0:T(8,128)(2,1)} %bitcast.151, bf16[2,320,3072]{2,1,0:T(8,128)(2,1)} %bitcast.152, f32[2,320,1024]{2,1,0:T(8,128)} %get-tuple-element.290.lse_ref, ...), custom_call_target="tpu_custom_call" | custom-call | flops 11440000000 | tf_op jit(solution)/shard_map/pallas_call | solution.py:133
  224.2 1.3 collective-permute-start.43
  225.4 7.5 %shard_map.263 = (bf16[4,64,1024]{2,1,0:T(8,128)(2,1)S(1)}, bf16[4,64,1024]{2,1,0:T(8,128)(2,1)S(1)}, bf16[4,64,1024]{2,1,0:T(8,128)(2,1)}, bf16[4,64,1024]{2,1,0:T(8,128)(2,1)}) custom-call(s32[3]{0:T(128)S(1)} %copy-done.3, bf16[640,1024]{1,0:T(8,128)(2,1)} %get-tuple-element.288.refs_0_, bf16[640,1024]{1,0:T(8,128)(2,1)} %collective-permute-done.37.refs_1_, ...), custom_call_target="tpu_custom_call" | custom-call | flops 5075107840 | tf_op jit(solution)/shard_map/pallas_call | solution.py:705
  235.0 10.8 %shard_map.262 = (bf16[4,64,1536]{2,1,0:T(8,128)(2,1)S(1)}, bf16[4,64,1536]{2,1,0:T(8,128)(2,1)S(1)}, bf16[4,64,1536]{2,1,0:T(8,128)(2,1)}, bf16[4,64,1536]{2,1,0:T(8,128)(2,1)}) custom-call(s32[3]{0:T(128)S(1)} %copy-done.3, bf16[640,1024]{1,0:T(8,128)(2,1)} %get-tuple-element.288.refs_0_, bf16[640,1024]{1,0:T(8,128)(2,1)} %collective-permute-done.37.refs_1_, ...), custom_call_target="tpu_custom_call" | custom-call | flops 7612661760 | tf_op jit(solution)/shard_map/pallas_call | solution.py:705
  245.8 4.0 collective-permute-done.43
  249.8 2.8 add_convert_fusion
  252.6 5.1 %all-to-all-start.3 = ((bf16[4,128,1024]{2,1,0:T(8,128)(2,1)}), bf16[4,128,1024]{2,1,0:T(8,128)(2,1)}, u32[]{:S(2)}, u32[]{:S(2)}) async-start(bf16[4,128,1024]{2,1,0:T(8,128)(2,1)} %add_convert_fusion), calls=%async_computation.3 | async-start | bytes 2097152 | tf_op jit(solution)/shard_map/all_to_all | solution.py:563
  257.7 2.0 add_convert_fusion.6
  261.7 6.2 %shard_map.261 = (bf16[4,64,768]{2,1,0:T(8,128)(2,1)S(1)}, bf16[4,64,768]{2,1,0:T(8,128)(2,1)S(1)}, bf16[4,64,768]{2,1,0:T(8,128)(2,1)S(1)}, bf16[4,64,768]{2,1,0:T(8,128)(2,1)}) custom-call(s32[3]{0:T(128)S(1)} %copy-done.3, bf16[640,1024]{1,0:T(8,128)(2,1)} %get-tuple-element.236.refs_0_, bf16[640,1024]{1,0:T(8,128)(2,1)} %copy-done.20, ...), custom_call_target="tpu_custom_call" | custom-call | flops 3806330880 | tf_op jit(solution)/shard_map/pallas_call | solution.py:705
  268.8 10.7 %shard_map.264 = bf16[2,320,1536]{2,1,0:T(8,128)(2,1)} custom-call(f32[2,320,1]{2,1,0:T(8,128)} %compare_select_fusion.bias_ref, bf16[2,320,3072]{2,1,0:T(8,128)(2,1)} %bitcast.153, bf16[2,320,3072]{2,1,0:T(8,128)(2,1)} %bitcast.154, bf16[2,320,3072]{2,1,0:T(8,128)(2,1)} %bitcast.155, f32[2,320,1024]{2,1,0:T(8,128)} %get-tuple-element.290.lse_ref, ...), custom_call_target="tpu_custom_call" | custom-call | flops 11440000000 | tf_op jit(solution)/shard_map/pallas_call | solution.py:133
  280.0 3.6 all-to-all-done.3
  286.4 2.3 add_convert_fusion.5
  288.7 4.5 %all-to-all-start.4 = ((bf16[4,64,1024]{2,1,0:T(8,128)(2,1)}), bf16[4,64,1024]{2,1,0:T(8,128)(2,1)}, u32[]{:S(2)}, u32[]{:S(2)}) async-start(bf16[4,64,1024]{2,1,0:T(8,128)(2,1)} %add_convert_fusion.5), calls=%async_computation.4 | async-start | bytes 1048576 | tf_op jit(solution)/shard_map/all_to_all | solution.py:563
  293.2 2.2 add_convert_fusion.4
  296.3 1.9 add_convert_fusion.8
  299.4 5.5 %shard_map.265 = (bf16[4,64,768]{2,1,0:T(8,128)(2,1)S(1)}, bf16[4,64,768]{2,1,0:T(8,128)(2,1)S(1)}, bf16[4,64,768]{2,1,0:T(8,128)(2,1)S(1)}, bf16[4,64,768]{2,1,0:T(8,128)(2,1)S(1)}) custom-call(s32[3]{0:T(128)S(1)} %copy-done.3, bf16[640,1024]{1,0:T(8,128)(2,1)} %get-tuple-element.236.refs_0_, bf16[640,1024]{1,0:T(8,128)(2,1)} %copy-done.20, ...), custom_call_target="tpu_custom_call" | custom-call | flops 3806330880 | tf_op jit(solution)/shard_map/pallas_call | solution.py:705
  305.7 14.9 %shard_map.266 = (bf16[640,1024]{1,0:T(8,128)(2,1)}, f32[1,3072]{1,0:T(1,128)}, f32[8,1024]{1,0:T(8,128)}) custom-call(s32[3]{0:T(128)} %pad_add_fusion.place_ref, bf16[4,64,1664]{2,1,0:T(8,128)(2,1)} %all-to-all-done.refs_0_, bf16[4,64,1664]{2,1,0:T(8,128)(2,1)} %collective-permute-done.5.refs_1_, bf16[4,64,1664]{2,1,0:T(8,128)(2,1)} %collective-permute-done.6.refs_2_, ...), custom_call_target="tpu_custom_call" | custom-call | flops 14300000256 | tf_op jit(solution)/shard_map/pallas_call | solution.py:260
  320.6 1.5 shard_map.267
  323.4 2.6 add_convert_fusion.3
  326.0 5.1 %all-to-all-start.5 = ((bf16[4,64,1536]{2,1,0:T(8,128)(2,1)}), bf16[4,64,1536]{2,1,0:T(8,128)(2,1)S(1)}, u32[]{:S(2)}, u32[]{:S(2)}) async-start(bf16[4,64,1536]{2,1,0:T(8,128)(2,1)} %add_convert_fusion.3), calls=%async_computation.5 | async-start | bytes 1572864 | tf_op jit(solution)/shard_map/all_to_all | solution.py:563
  332.2 1.3 collective-permute-start.55
  333.4 1.4 reduce_sum.59.refs_8_
  336.9 1.3 collective-permute-start.59
  339.1 13.2 %shard_map.268 = bf16[640,1024]{1,0:T(8,128)(2,1)} custom-call(s32[3]{0:T(128)} %pad_add_fusion.place_ref, bf16[4,64,2048]{2,1,0:T(8,128)(2,1)} %all-to-all-done.2.refs_0_, bf16[4,64,2048]{2,1,0:T(8,128)(2,1)} %copy-done.12, bf16[4,64,2048]{2,1,0:T(8,128)(2,1)} %copy-done.13, bf16[2,64,2048]{2,1,0:T(8,128)(2,1)} %copy-done.26, ...), custom_call_target="tpu_custom_call" | custom-call | flops 12099999744 | tf_op jit(solution)/shard_map/pallas_call | solution.py:260
  354.3 2.4 add_convert_fusion.2
  356.7 5.1 %all-to-all-start.6 = ((bf16[4,64,1536]{2,1,0:T(8,128)(2,1)}), bf16[4,64,1536]{2,1,0:T(8,128)(2,1)S(1)}, u32[]{:S(2)}, u32[]{:S(2)}) async-start(bf16[4,64,1536]{2,1,0:T(8,128)(2,1)} %add_convert_fusion.2), calls=%async_computation.6 | async-start | bytes 1572864 | tf_op jit(solution)/shard_map/all_to_all | solution.py:563
  362.8 2.6 fusion.6
  367.2 2.0 collective-permute-start.63
  369.3 2.4 collective-permute-start.64
  372.5 1.7 collective-permute-done.63
  375.4 6.4 %collective-permute-done.64 = f32[1536]{0:T(1024)} collective-permute-done((f32[1536]{0:T(1024)}, f32[1536]{0:T(1024)}, u32[]{:S(2)}, u32[]{:S(2)}) %collective-permute-start.64) | collective-permute-done | bytes 6176 | tf_op jit(solution)/shard_map/ppermute | solution.py:536
  382.6 4.8 %collective-permute-done.61.refs_5_ = bf16[64,1536]{1,0:T(8,128)(2,1)S(1)} collective-permute-done((bf16[64,1536]{1,0:T(8,128)(2,1)}, bf16[64,1536]{1,0:T(8,128)(2,1)S(1)}, u32[]{:S(2)}, u32[]{:S(2)}) %collective-permute-start.61) | collective-permute-done | bytes 196640 | tf_op jit(solution)/shard_map/ppermute | solution.py:532
  392.7 4.0 shard_map.269
  396.7 3.9 collective-permute-done.74
  400.6 4.6 %collective-permute-done.75.refs_1_ = bf16[64,1536]{1,0:T(8,128)(2,1)S(1)} collective-permute-done((bf16[64,1536]{1,0:T(8,128)(2,1)}, bf16[64,1536]{1,0:T(8,128)(2,1)S(1)}, u32[]{:S(2)}, u32[]{:S(2)}) %collective-permute-start.75) | collective-permute-done | bytes 196640 | tf_op jit(solution)/shard_map/ppermute | solution.py:532
  407.4 1.7 slice_bitcast_fusion
  411.0 2.6 shard_map.270
  (256 shorter events, 68.1 us)
Async XLA Ops:
  4.9 30.9 %all-to-all-start = ((bf16[4,64,1664]{2,1,0:T(8,128)(2,1)}), bf16[4,64,1664]{2,1,0:T(8,128)(2,1)}, u32[]{:S(2)}, u32[]{:S(2)}) async-start(bf16[4,64,1664]{2,1,0:T(8,128)(2,1)} %get-tuple-element.207), calls=%async_computation | async-start | bytes 1703936 | tf_op jit(solution)/shard_map/all_to_all | solution.py:563
  13.1 15.1 %collective-permute-start.2 = (bf16[2,80,1024]{2,1,0:T(8,128)(2,1)S(1)}, bf16[2,80,1024]{2,1,0:T(8,128)(2,1)S(1)}, u32[]{:S(2)}, u32[]{:S(2)}) collective-permute-start(bf16[2,80,1024]{2,1,0:T(8,128)(2,1)S(1)} %get-tuple-element.421), channel_id=1, source_target_pairs={{0,3},{1,2},{2,1},{3,0},{4,7},{5,6},{6,5},{7,4},{8,11},{9,10},{10,... | collective-permute-start | bytes 983048 | tf_op jit(solution)/shard_map/ppermute | solution.py:536
  13.5 14.7 %collective-permute-start.3 = (bf16[2,80,1024]{2,1,0:T(8,128)(2,1)S(1)}, bf16[2,80,1024]{2,1,0:T(8,128)(2,1)}, u32[]{:S(2)}, u32[]{:S(2)}) collective-permute-start(bf16[2,80,1024]{2,1,0:T(8,128)(2,1)S(1)} %get-tuple-element.419), channel_id=1, source_target_pairs={{0,1},{1,0},{2,3},{3,2},{4,5},{5,4},{6,7},{7,6},{8,9},{9,8},{10,11... | collective-permute-start | bytes 983048 | tf_op jit(solution)/shard_map/ppermute | solution.py:536
  13.9 21.9 %collective-permute-start.4 = (bf16[2,80,1024]{2,1,0:T(8,128)(2,1)S(1)}, bf16[2,80,1024]{2,1,0:T(8,128)(2,1)}, u32[]{:S(2)}, u32[]{:S(2)}) collective-permute-start(bf16[2,80,1024]{2,1,0:T(8,128)(2,1)S(1)} %get-tuple-element.418), channel_id=1, source_target_pairs={{0,2},{1,3},{2,0},{3,1},{4,6},{5,7},{6,4},{7,5},{8,10},{9,11},{10,... | collective-permute-start | bytes 983048 | tf_op jit(solution)/shard_map/ppermute | solution.py:536
  35.8 20.8 %collective-permute-start.5 = (bf16[4,64,1664]{2,1,0:T(8,128)(2,1)}, bf16[4,64,1664]{2,1,0:T(8,128)(2,1)}, u32[]{:S(2)}, u32[]{:S(2)}) collective-permute-start(bf16[4,64,1664]{2,1,0:T(8,128)(2,1)} %all-to-all-done.refs_0_), channel_id=1, source_target_pairs={{0,2},{2,0},{1,3},{3,1},{4,6},{6,4},{5,7},{7,5},{8,10},{10,8},{9,1... | collective-permute-start | bytes 2555912 | tf_op jit(solution)/shard_map/ppermute | solution.py:532
  37.3 20.5 %collective-permute-start.6 = (bf16[4,64,1664]{2,1,0:T(8,128)(2,1)}, bf16[4,64,1664]{2,1,0:T(8,128)(2,1)}, u32[]{:S(2)}, u32[]{:S(2)}) collective-permute-start(bf16[4,64,1664]{2,1,0:T(8,128)(2,1)} %all-to-all-done.refs_0_), channel_id=1, source_target_pairs={{0,4},{4,0},{1,5},{5,1},{2,6},{6,2},{3,7},{7,3},{8,12},{12,8},{9,1... | collective-permute-start | bytes 2555912 | tf_op jit(solution)/shard_map/ppermute | solution.py:532
  38.9 36.9 %all-to-all-start.1 = ((bf16[4,64,2560]{2,1,0:T(8,128)(2,1)}), bf16[4,64,2560]{2,1,0:T(8,128)(2,1)S(1)}, u32[]{:S(2)}, u32[]{:S(2)}) async-start(bf16[4,64,2560]{2,1,0:T(8,128)(2,1)} %get-tuple-element.215), calls=%async_computation.1 | async-start | bytes 2621440 | tf_op jit(solution)/shard_map/all_to_all | solution.py:563
  57.9 17.8 %collective-permute-start.10 = (bf16[4,64,1664]{2,1,0:T(8,128)(2,1)}, bf16[4,64,1664]{2,1,0:T(8,128)(2,1)}, u32[]{:S(2)}, u32[]{:S(2)}) collective-permute-start(bf16[4,64,1664]{2,1,0:T(8,128)(2,1)} %collective-permute-done.5.refs_1_), channel_id=1, source_target_pairs={{0,1},{1,0},{2,3},{3,2},{4,5},{5,4},{6,7},{7,6},{8,9},{9,8},{10,11... | collective-permute-start | bytes 2555912 | tf_op jit(solution)/shard_map/ppermute | solution.py:532
  58.9 16.8 %collective-permute-start.11 = (bf16[4,64,1664]{2,1,0:T(8,128)(2,1)}, bf16[4,64,1664]{2,1,0:T(8,128)(2,1)}, u32[]{:S(2)}, u32[]{:S(2)}) collective-permute-start(bf16[4,64,1664]{2,1,0:T(8,128)(2,1)} %collective-permute-done.6.refs_2_), channel_id=1, source_target_pairs={{0,1},{1,0},{2,3},{3,2},{4,5},{5,4},{6,7},{7,6},{8,9},{9,8},{10,11... | collective-permute-start | bytes 2555912 | tf_op jit(solution)/shard_map/ppermute | solution.py:532
  60.5 15.2 %collective-permute-start.9 = (bf16[4,64,1664]{2,1,0:T(8,128)(2,1)}, bf16[4,64,1664]{2,1,0:T(8,128)(2,1)}, u32[]{:S(2)}, u32[]{:S(2)}) collective-permute-start(bf16[4,64,1664]{2,1,0:T(8,128)(2,1)} %all-to-all-done.refs_0_), channel_id=1, source_target_pairs={{0,1},{1,0},{2,3},{3,2},{4,5},{5,4},{6,7},{7,6},{8,9},{9,8},{10,11... | collective-permute-start | bytes 2555912 | tf_op jit(solution)/shard_map/ppermute | solution.py:532
  76.3 30.8 %collective-permute-start.14 = (bf16[4,64,2560]{2,1,0:T(8,128)(2,1)S(1)}, bf16[4,64,2560]{2,1,0:T(8,128)(2,1)S(1)}, u32[]{:S(2)}, u32[]{:S(2)}) collective-permute-start(bf16[4,64,2560]{2,1,0:T(8,128)(2,1)S(1)} %all-to-all-done.1.refs_0_.refs_10_.refs_20_), channel_id=1, source_target_pairs={{0,2},{2,0},{1,3},{3,1},{4,6},{6,4},{5,7},{7,5},{8,10},{10,8},{9,1... | collective-permute-start | bytes 3932168 | tf_op jit(solution)/shard_map/ppermute | solution.py:532
  76.9 30.6 %collective-permute-start.15 = (bf16[4,64,2560]{2,1,0:T(8,128)(2,1)S(1)}, bf16[4,64,2560]{2,1,0:T(8,128)(2,1)}, u32[]{:S(2)}, u32[]{:S(2)}) collective-permute-start(bf16[4,64,2560]{2,1,0:T(8,128)(2,1)S(1)} %all-to-all-done.1.refs_0_.refs_10_.refs_20_), channel_id=1, source_target_pairs={{0,4},{4,0},{1,5},{5,1},{2,6},{6,2},{3,7},{7,3},{8,12},{12,8},{9,1... | collective-permute-start | bytes 3932168 | tf_op jit(solution)/shard_map/ppermute | solution.py:532
  77.4 30.1 %collective-permute-start.16 = (bf16[4,64,2560]{2,1,0:T(8,128)(2,1)S(1)}, bf16[4,64,2560]{2,1,0:T(8,128)(2,1)}, u32[]{:S(2)}, u32[]{:S(2)}) collective-permute-start(bf16[4,64,2560]{2,1,0:T(8,128)(2,1)S(1)} %all-to-all-done.1.refs_0_.refs_10_.refs_20_), channel_id=1, source_target_pairs={{0,1},{1,0},{2,3},{3,2},{4,5},{5,4},{6,7},{7,6},{8,9},{9,8},{10,11... | collective-permute-start | bytes 3932168 | tf_op jit(solution)/shard_map/ppermute | solution.py:532
  88.3 45.5 %all-to-all-start.2 = ((bf16[4,64,2048]{2,1,0:T(8,128)(2,1)}), bf16[4,64,2048]{2,1,0:T(8,128)(2,1)}, u32[]{:S(2)}, u32[]{:S(2)}) async-start(bf16[4,64,2048]{2,1,0:T(8,128)(2,1)} %get-tuple-element.242), calls=%async_computation.2 | async-start | bytes 2097152 | tf_op jit(solution)/shard_map/all_to_all | solution.py:563
  109.3 24.6 %collective-permute-start.19 = (bf16[4,64,2560]{2,1,0:T(8,128)(2,1)}, bf16[4,64,2560]{2,1,0:T(8,128)(2,1)}, u32[]{:S(2)}, u32[]{:S(2)}) collective-permute-start(bf16[4,64,2560]{2,1,0:T(8,128)(2,1)} %copy-done.10), channel_id=1, source_target_pairs={{0,1},{1,0},{2,3},{3,2},{4,5},{5,4},{6,7},{7,6},{8,9},{9,8},{10,11... | collective-permute-start | bytes 3932168 | tf_op jit(solution)/shard_map/ppermute | solution.py:532
  110.5 23.4 %collective-permute-start.20 = (bf16[4,64,2560]{2,1,0:T(8,128)(2,1)}, bf16[4,64,2560]{2,1,0:T(8,128)(2,1)}, u32[]{:S(2)}, u32[]{:S(2)}) collective-permute-start(bf16[4,64,2560]{2,1,0:T(8,128)(2,1)} %collective-permute-done.15.refs_2_.refs_12_.refs_22_), channel_id=1, source_target_pairs={{0,1},{1,0},{2,3},{3,2},{4,5},{5,4},{6,7},{7,6},{8,9},{9,8},{10,11... | collective-permute-start | bytes 3932168 | tf_op jit(solution)/shard_map/ppermute | solution.py:532
  111.0 22.8 %collective-permute-start.17 = (bf16[2,64,2560]{2,1,0:T(8,128)(2,1)S(1)}, bf16[2,64,2560]{2,1,0:T(8,128)(2,1)}, u32[]{:S(2)}, u32[]{:S(2)}) collective-permute-start(bf16[2,64,2560]{2,1,0:T(8,128)(2,1)S(1)} %slice.102), channel_id=1, source_target_pairs={{0,4},{4,0},{1,5},{5,1},{2,6},{6,2},{3,7},{7,3},{8,12},{12,8},{9,1... | collective-permute-start | bytes 1966088 | tf_op jit(solution)/shard_map/ppermute | solution.py:532
  111.6 22.3 %collective-permute-start.18 = (bf16[2,64,2560]{2,1,0:T(8,128)(2,1)S(1)}, bf16[2,64,2560]{2,1,0:T(8,128)(2,1)}, u32[]{:S(2)}, u32[]{:S(2)}) collective-permute-start(bf16[2,64,2560]{2,1,0:T(8,128)(2,1)S(1)} %slice.103), channel_id=1, source_target_pairs={{0,2},{2,0},{1,3},{3,1},{4,6},{6,4},{5,7},{7,5},{8,10},{10,8},{9,1... | collective-permute-start | bytes 1966088 | tf_op jit(solution)/shard_map/ppermute | solution.py:532
  113.4 20.5 %collective-permute-start.21 = (bf16[2,80,1024]{2,1,0:T(8,128)(2,1)S(1)}, bf16[2,80,1024]{2,1,0:T(8,128)(2,1)S(1)}, u32[]{:S(2)}, u32[]{:S(2)}) collective-permute-start(bf16[2,80,1024]{2,1,0:T(8,128)(2,1)S(1)} %dynamic-slice_bitcast_fusion), channel_id=1, source_target_pairs={{0,3},{1,2},{2,1},{3,0},{4,7},{5,6},{6,5},{7,4},{8,11},{9,10},{10,... | collective-permute-start | bytes 983048 | tf_op jit(solution)/shard_map/ppermute | solution.py:536
  135.2 25.7 %collective-permute-start.24 = (bf16[4,64,2048]{2,1,0:T(8,128)(2,1)}, bf16[4,64,2048]{2,1,0:T(8,128)(2,1)S(1)}, u32[]{:S(2)}, u32[]{:S(2)}) collective-permute-start(bf16[4,64,2048]{2,1,0:T(8,128)(2,1)} %all-to-all-done.2.refs_0_), channel_id=1, source_target_pairs={{0,2},{2,0},{1,3},{3,1},{4,6},{6,4},{5,7},{7,5},{8,10},{10,8},{9,1... | collective-permute-start | bytes 3145736 | tf_op jit(solution)/shard_map/ppermute | solution.py:532
  136.0 25.4 %collective-permute-start.25 = (bf16[4,64,2048]{2,1,0:T(8,128)(2,1)}, bf16[4,64,2048]{2,1,0:T(8,128)(2,1)S(1)}, u32[]{:S(2)}, u32[]{:S(2)}) collective-permute-start(bf16[4,64,2048]{2,1,0:T(8,128)(2,1)} %all-to-all-done.2.refs_0_), channel_id=1, source_target_pairs={{0,4},{4,0},{1,5},{5,1},{2,6},{6,2},{3,7},{7,3},{8,12},{12,8},{9,1... | collective-permute-start | bytes 3145736 | tf_op jit(solution)/shard_map/ppermute | solution.py:532
  137.5 23.9 %collective-permute-start.26 = (bf16[4,64,2048]{2,1,0:T(8,128)(2,1)}, bf16[4,64,2048]{2,1,0:T(8,128)(2,1)S(1)}, u32[]{:S(2)}, u32[]{:S(2)}) collective-permute-start(bf16[4,64,2048]{2,1,0:T(8,128)(2,1)} %all-to-all-done.2.refs_0_), channel_id=1, source_target_pairs={{0,1},{1,0},{2,3},{3,2},{4,5},{5,4},{6,7},{7,6},{8,9},{9,8},{10,11... | collective-permute-start | bytes 3145736 | tf_op jit(solution)/shard_map/ppermute | solution.py:532
  139.0 22.4 %collective-permute-start.27 = (bf16[640,1024]{1,0:T(8,128)(2,1)S(1)}, bf16[640,1024]{1,0:T(8,128)(2,1)S(1)}, u32[]{:S(2)}, u32[]{:S(2)}) collective-permute-start(bf16[640,1024]{1,0:T(8,128)(2,1)S(1)} %bitcast_select_fusion.g_ref.refs_30_), channel_id=1, source_target_pairs={{0,1},{1,0},{2,3},{3,2},{4,5},{5,4},{6,7},{7,6},{8,9},{9,8},{10,11... | collective-permute-start | bytes 3932168 | tf_op jit(solution)/shard_map/ppermute | solution.py:532
  163.6 16.9 %collective-permute-start.31 = (bf16[4,64,2048]{2,1,0:T(8,128)(2,1)S(1)}, bf16[4,64,2048]{2,1,0:T(8,128)(2,1)S(1)}, u32[]{:S(2)}, u32[]{:S(2)}) collective-permute-start(bf16[4,64,2048]{2,1,0:T(8,128)(2,1)S(1)} %collective-permute-done.24.refs_1_), channel_id=1, source_target_pairs={{0,1},{1,0},{2,3},{3,2},{4,5},{5,4},{6,7},{7,6},{8,9},{9,8},{10,11... | collective-permute-start | bytes 3145736 | tf_op jit(solution)/shard_map/ppermute | solution.py:532
  164.9 15.6 %collective-permute-start.32 = (bf16[4,64,2048]{2,1,0:T(8,128)(2,1)S(1)}, bf16[4,64,2048]{2,1,0:T(8,128)(2,1)S(1)}, u32[]{:S(2)}, u32[]{:S(2)}) collective-permute-start(bf16[4,64,2048]{2,1,0:T(8,128)(2,1)S(1)} %copy-done.14), channel_id=1, source_target_pairs={{0,1},{1,0},{2,3},{3,2},{4,5},{5,4},{6,7},{7,6},{8,9},{9,8},{10,11... | collective-permute-start | bytes 3145736 | tf_op jit(solution)/shard_map/ppermute | solution.py:532
  165.3 15.2 %collective-permute-start.29 = (bf16[2,64,2048]{2,1,0:T(8,128)(2,1)S(1)}, bf16[2,64,2048]{2,1,0:T(8,128)(2,1)S(1)}, u32[]{:S(2)}, u32[]{:S(2)}) collective-permute-start(bf16[2,64,2048]{2,1,0:T(8,128)(2,1)S(1)} %slice.104), channel_id=1, source_target_pairs={{0,4},{4,0},{1,5},{5,1},{2,6},{6,2},{3,7},{7,3},{8,12},{12,8},{9,1... | collective-permute-start | bytes 1572872 | tf_op jit(solution)/shard_map/ppermute | solution.py:532
  166.8 13.7 %collective-permute-start.30 = (bf16[2,64,2048]{2,1,0:T(8,128)(2,1)S(1)}, bf16[2,64,2048]{2,1,0:T(8,128)(2,1)S(1)}, u32[]{:S(2)}, u32[]{:S(2)}) collective-permute-start(bf16[2,64,2048]{2,1,0:T(8,128)(2,1)S(1)} %slice.105), channel_id=1, source_target_pairs={{0,2},{2,0},{1,3},{3,1},{4,6},{6,4},{5,7},{7,5},{8,10},{10,8},{9,1... | collective-permute-start | bytes 1572872 | tf_op jit(solution)/shard_map/ppermute | solution.py:532
  181.6 29.4 %collective-permute-start.38 = (bf16[640,1024]{1,0:T(8,128)(2,1)S(1)}, bf16[640,1024]{1,0:T(8,128)(2,1)S(1)}, u32[]{:S(2)}, u32[]{:S(2)}) collective-permute-start(bf16[640,1024]{1,0:T(8,128)(2,1)S(1)} %copy-done.18), channel_id=1, source_target_pairs={{0,1},{1,0},{2,3},{3,2},{4,5},{5,4},{6,7},{7,6},{8,9},{9,8},{10,11... | collective-permute-start | bytes 3932168 | tf_op jit(solution)/shard_map/ppermute | solution.py:532
  182.1 29.0 %collective-permute-start.36 = (bf16[640,1024]{1,0:T(8,128)(2,1)S(1)}, bf16[640,1024]{1,0:T(8,128)(2,1)}, u32[]{:S(2)}, u32[]{:S(2)}) collective-permute-start(bf16[640,1024]{1,0:T(8,128)(2,1)S(1)} %bitcast.138), channel_id=1, source_target_pairs={{0,1},{1,0},{2,3},{3,2},{4,5},{5,4},{6,7},{7,6},{8,9},{9,8},{10,11... | collective-permute-start | bytes 3932168 | tf_op jit(solution)/shard_map/ppermute | solution.py:532
  182.1 28.9 %collective-permute-start.37 = (bf16[640,1024]{1,0:T(8,128)(2,1)}, bf16[640,1024]{1,0:T(8,128)(2,1)}, u32[]{:S(2)}, u32[]{:S(2)}) collective-permute-start(bf16[640,1024]{1,0:T(8,128)(2,1)} %get-tuple-element.288.refs_0_), channel_id=1, source_target_pairs={{0,1},{1,0},{2,3},{3,2},{4,5},{5,4},{6,7},{7,6},{8,9},{9,8},{10,11... | collective-permute-start | bytes 3932168 | tf_op jit(solution)/shard_map/ppermute | solution.py:532
  182.6 28.4 %collective-permute-start.35 = (bf16[4,128,1024]{2,1,0:T(8,128)(2,1)}, bf16[4,128,1024]{2,1,0:T(8,128)(2,1)S(1)}, u32[]{:S(2)}, u32[]{:S(2)}) collective-permute-start(bf16[4,128,1024]{2,1,0:T(8,128)(2,1)} %get-tuple-element.285), channel_id=1, source_target_pairs={{0,4},{4,0},{1,5},{5,1},{2,6},{6,2},{3,7},{7,3},{8,12},{12,8},{9,1... | collective-permute-start | bytes 3145736 | tf_op jit(solution)/shard_map/ppermute | solution.py:532
  211.1 12.6 %collective-permute-start.39 = (bf16[640,4096]{1,0:T(8,128)(2,1)}, bf16[640,4096]{1,0:T(8,128)(2,1)}, u32[]{:S(2)}, u32[]{:S(2)}) collective-permute-start(bf16[640,4096]{1,0:T(8,128)(2,1)} %get-tuple-element.292.refs_2_), channel_id=1, source_target_pairs={{0,1},{1,0},{2,3},{3,2},{4,5},{5,4},{6,7},{7,6},{8,9},{9,8},{10,11... | collective-permute-start | bytes 15728648 | tf_op jit(solution)/shard_map/ppermute | solution.py:532
  211.3 12.4 %collective-permute-start.40 = (bf16[640,1024]{1,0:T(8,128)(2,1)}, bf16[640,1024]{1,0:T(8,128)(2,1)}, u32[]{:S(2)}, u32[]{:S(2)}) collective-permute-start(bf16[640,1024]{1,0:T(8,128)(2,1)} %get-tuple-element.293.refs_6_), channel_id=1, source_target_pairs={{0,1},{1,0},{2,3},{3,2},{4,5},{5,4},{6,7},{7,6},{8,9},{9,8},{10,11... | collective-permute-start | bytes 3932168 | tf_op jit(solution)/shard_map/ppermute | solution.py:532
  211.6 34.1 %collective-permute-start.44 = (bf16[4,128,1024]{2,1,0:T(8,128)(2,1)}, bf16[4,128,1024]{2,1,0:T(8,128)(2,1)}, u32[]{:S(2)}, u32[]{:S(2)}) collective-permute-start(bf16[4,128,1024]{2,1,0:T(8,128)(2,1)} %get-tuple-element.316), channel_id=1, source_target_pairs={{0,4},{4,0},{1,5},{5,1},{2,6},{6,2},{3,7},{7,3},{8,12},{12,8},{9,1... | collective-permute-start | bytes 3145736 | tf_op jit(solution)/shard_map/ppermute | solution.py:532
  223.7 38.1 %collective-permute-start.41 = (bf16[640,1536]{1,0:T(8,128)(2,1)}, bf16[640,1536]{1,0:T(8,128)(2,1)}, u32[]{:S(2)}, u32[]{:S(2)}) collective-permute-start(bf16[640,1536]{1,0:T(8,128)(2,1)} %bitcast.130), channel_id=1, source_target_pairs={{0,1},{1,0},{2,3},{3,2},{4,5},{5,4},{6,7},{7,6},{8,9},{9,8},{10,11... | collective-permute-start | bytes 5898248 | tf_op jit(solution)/shard_map/ppermute | solution.py:532
  224.2 25.6 %collective-permute-start.43 = (bf16[4,128,1024]{2,1,0:T(8,128)(2,1)S(1)}, bf16[4,128,1024]{2,1,0:T(8,128)(2,1)S(1)}, u32[]{:S(2)}, u32[]{:S(2)}) collective-permute-start(bf16[4,128,1024]{2,1,0:T(8,128)(2,1)S(1)} %add_convert_fusion.1), channel_id=1, source_target_pairs={{0,2},{2,0},{1,3},{3,1},{4,6},{6,4},{5,7},{7,5},{8,10},{10,8},{9,1... | collective-permute-start | bytes 3145736 | tf_op jit(solution)/shard_map/ppermute | solution.py:532
  233.0 16.8 %collective-permute-start.42 = (bf16[4,64,1024]{2,1,0:T(8,128)(2,1)}, bf16[4,64,1024]{2,1,0:T(8,128)(2,1)}, u32[]{:S(2)}, u32[]{:S(2)}) collective-permute-start(bf16[4,64,1024]{2,1,0:T(8,128)(2,1)} %get-tuple-element.313), channel_id=1, source_target_pairs={{0,4},{4,0},{1,5},{5,1},{2,6},{6,2},{3,7},{7,3},{8,12},{12,8},{9,1... | collective-permute-start | bytes 1572872 | tf_op jit(solution)/shard_map/ppermute | solution.py:532
  233.8 45.7 %collective-permute-start.47 = (bf16[4,64,1024]{2,1,0:T(8,128)(2,1)}, bf16[4,64,1024]{2,1,0:T(8,128)(2,1)}, u32[]{:S(2)}, u32[]{:S(2)}) collective-permute-start(bf16[4,64,1024]{2,1,0:T(8,128)(2,1)} %get-tuple-element.323), channel_id=1, source_target_pairs={{0,4},{4,0},{1,5},{5,1},{2,6},{6,2},{3,7},{7,3},{8,12},{12,8},{9,1... | collective-permute-start | bytes 1572872 | tf_op jit(solution)/shard_map/ppermute | solution.py:532
  252.6 30.9 %all-to-all-start.3 = ((bf16[4,128,1024]{2,1,0:T(8,128)(2,1)}), bf16[4,128,1024]{2,1,0:T(8,128)(2,1)}, u32[]{:S(2)}, u32[]{:S(2)}) async-start(bf16[4,128,1024]{2,1,0:T(8,128)(2,1)} %add_convert_fusion), calls=%async_computation.3 | async-start | bytes 2097152 | tf_op jit(solution)/shard_map/all_to_all | solution.py:563
  259.7 19.8 %collective-permute-start.46 = (bf16[4,64,1024]{2,1,0:T(8,128)(2,1)}, bf16[4,64,1024]{2,1,0:T(8,128)(2,1)}, u32[]{:S(2)}, u32[]{:S(2)}) collective-permute-start(bf16[4,64,1024]{2,1,0:T(8,128)(2,1)} %add_convert_fusion.6), channel_id=1, source_target_pairs={{0,2},{2,0},{1,3},{3,1},{4,6},{6,4},{5,7},{7,5},{8,10},{10,8},{9,1... | collective-permute-start | bytes 1572872 | tf_op jit(solution)/shard_map/ppermute | solution.py:532
  260.9 19.0 %collective-permute-start.48 = (bf16[4,64,1536]{2,1,0:T(8,128)(2,1)}, bf16[4,64,1536]{2,1,0:T(8,128)(2,1)}, u32[]{:S(2)}, u32[]{:S(2)}) collective-permute-start(bf16[4,64,1536]{2,1,0:T(8,128)(2,1)} %get-tuple-element.324), channel_id=1, source_target_pairs={{0,4},{4,0},{1,5},{5,1},{2,6},{6,2},{3,7},{7,3},{8,12},{12,8},{9,1... | collective-permute-start | bytes 2359304 | tf_op jit(solution)/shard_map/ppermute | solution.py:532
  268.0 15.5 %collective-permute-start.45 = (bf16[4,64,768]{2,1,0:T(8,128)(2,1)}, bf16[4,64,768]{2,1,0:T(8,128)(2,1)}, u32[]{:S(2)}, u32[]{:S(2)}) collective-permute-start(bf16[4,64,768]{2,1,0:T(8,128)(2,1)} %get-tuple-element.320), channel_id=1, source_target_pairs={{0,2},{2,0},{1,3},{3,1},{4,6},{6,4},{5,7},{7,5},{8,10},{10,8},{9,1... | collective-permute-start | bytes 1179656 | tf_op jit(solution)/shard_map/ppermute | solution.py:532
  283.5 15.9 %collective-permute-start.49 = (bf16[640,1536]{1,0:T(8,128)(2,1)}, bf16[640,1536]{1,0:T(8,128)(2,1)}, u32[]{:S(2)}, u32[]{:S(2)}) collective-permute-start(bf16[640,1536]{1,0:T(8,128)(2,1)} %bitcast.133), channel_id=1, source_target_pairs={{0,1},{1,0},{2,3},{3,2},{4,5},{5,4},{6,7},{7,6},{8,9},{9,8},{10,11... | collective-permute-start | bytes 5898248 | tf_op jit(solution)/shard_map/ppermute | solution.py:532
  284.4 37.7 %collective-permute-start.54 = (bf16[4,64,1536]{2,1,0:T(8,128)(2,1)}, bf16[4,64,1536]{2,1,0:T(8,128)(2,1)}, u32[]{:S(2)}, u32[]{:S(2)}) collective-permute-start(bf16[4,64,1536]{2,1,0:T(8,128)(2,1)} %get-tuple-element.344), channel_id=1, source_target_pairs={{0,4},{4,0},{1,5},{5,1},{2,6},{6,2},{3,7},{7,3},{8,12},{12,8},{9,1... | collective-permute-start | bytes 2359304 | tf_op jit(solution)/shard_map/ppermute | solution.py:532
  285.2 38.1 %collective-permute-start.51 = (bf16[4,64,768]{2,1,0:T(8,128)(2,1)S(1)}, bf16[4,64,768]{2,1,0:T(8,128)(2,1)}, u32[]{:S(2)}, u32[]{:S(2)}) collective-permute-start(bf16[4,64,768]{2,1,0:T(8,128)(2,1)S(1)} %get-tuple-element.339), channel_id=1, source_target_pairs={{0,2},{2,0},{1,3},{3,1},{4,6},{6,4},{5,7},{7,5},{8,10},{10,8},{9,1... | collective-permute-start | bytes 1179656 | tf_op jit(solution)/shard_map/ppermute | solution.py:532
  288.7 34.7 %all-to-all-start.4 = ((bf16[4,64,1024]{2,1,0:T(8,128)(2,1)}), bf16[4,64,1024]{2,1,0:T(8,128)(2,1)}, u32[]{:S(2)}, u32[]{:S(2)}) async-start(bf16[4,64,1024]{2,1,0:T(8,128)(2,1)} %add_convert_fusion.5), calls=%async_computation.4 | async-start | bytes 1048576 | tf_op jit(solution)/shard_map/all_to_all | solution.py:563
  295.5 27.9 %collective-permute-start.53 = (bf16[4,64,1536]{2,1,0:T(8,128)(2,1)}, bf16[4,64,1536]{2,1,0:T(8,128)(2,1)}, u32[]{:S(2)}, u32[]{:S(2)}) collective-permute-start(bf16[4,64,1536]{2,1,0:T(8,128)(2,1)} %add_convert_fusion.4), channel_id=1, source_target_pairs={{0,2},{2,0},{1,3},{3,1},{4,6},{6,4},{5,7},{7,5},{8,10},{10,8},{9,1... | collective-permute-start | bytes 2359304 | tf_op jit(solution)/shard_map/ppermute | solution.py:532
  298.1 25.2 %collective-permute-start.52 = (bf16[4,64,768]{2,1,0:T(8,128)(2,1)}, bf16[4,64,768]{2,1,0:T(8,128)(2,1)}, u32[]{:S(2)}, u32[]{:S(2)}) collective-permute-start(bf16[4,64,768]{2,1,0:T(8,128)(2,1)} %add_convert_fusion.8), channel_id=1, source_target_pairs={{0,4},{4,0},{1,5},{5,1},{2,6},{6,2},{3,7},{7,3},{8,12},{12,8},{9,1... | collective-permute-start | bytes 1179656 | tf_op jit(solution)/shard_map/ppermute | solution.py:532
  304.9 18.5 %collective-permute-start.50 = (bf16[4,64,768]{2,1,0:T(8,128)(2,1)S(1)}, bf16[4,64,768]{2,1,0:T(8,128)(2,1)}, u32[]{:S(2)}, u32[]{:S(2)}) collective-permute-start(bf16[4,64,768]{2,1,0:T(8,128)(2,1)S(1)} %get-tuple-element.338), channel_id=1, source_target_pairs={{0,4},{4,0},{1,5},{5,1},{2,6},{6,2},{3,7},{7,3},{8,12},{12,8},{9,1... | collective-permute-start | bytes 1179656 | tf_op jit(solution)/shard_map/ppermute | solution.py:532
  322.1 31.5 %collective-permute-start.56 = (bf16[4,64,768]{2,1,0:T(8,128)(2,1)S(1)}, bf16[4,64,768]{2,1,0:T(8,128)(2,1)}, u32[]{:S(2)}, u32[]{:S(2)}) collective-permute-start(bf16[4,64,768]{2,1,0:T(8,128)(2,1)S(1)} %get-tuple-element.358), channel_id=1, source_target_pairs={{0,4},{4,0},{1,5},{5,1},{2,6},{6,2},{3,7},{7,3},{8,12},{12,8},{9,1... | collective-permute-start | bytes 1179656 | tf_op jit(solution)/shard_map/ppermute | solution.py:532
  323.4 14.8 %collective-permute-start.57 = (f32[8,1536]{1,0:T(8,128)}, f32[8,1536]{1,0:T(8,128)S(1)}, u32[]{:S(2)}, u32[]{:S(2)}) collective-permute-start(f32[8,1536]{1,0:T(8,128)} %shard_map.267), channel_id=1, source_target_pairs={{0,1},{1,0},{2,3},{3,2},{4,5},{5,4},{6,7},{7,6},{8,9},{9,8},{10,11... | collective-permute-start | bytes 147464 | tf_op jit(solution)/shard_map/ppermute | solution.py:532
  326.0 27.6 %all-to-all-start.5 = ((bf16[4,64,1536]{2,1,0:T(8,128)(2,1)}), bf16[4,64,1536]{2,1,0:T(8,128)(2,1)S(1)}, u32[]{:S(2)}, u32[]{:S(2)}) async-start(bf16[4,64,1536]{2,1,0:T(8,128)(2,1)} %add_convert_fusion.3), calls=%async_computation.5 | async-start | bytes 1572864 | tf_op jit(solution)/shard_map/all_to_all | solution.py:563
  332.2 21.4 %collective-permute-start.55 = (bf16[4,64,768]{2,1,0:T(8,128)(2,1)S(1)}, bf16[4,64,768]{2,1,0:T(8,128)(2,1)S(1)}, u32[]{:S(2)}, u32[]{:S(2)}) collective-permute-start(bf16[4,64,768]{2,1,0:T(8,128)(2,1)S(1)} %add_convert_fusion.7), channel_id=1, source_target_pairs={{0,2},{2,0},{1,3},{3,1},{4,6},{6,4},{5,7},{7,5},{8,10},{10,8},{9,1... | collective-permute-start | bytes 1179656 | tf_op jit(solution)/shard_map/ppermute | solution.py:532
  334.9 18.7 %collective-permute-start.60 = (bf16[128,1024]{1,0:T(8,128)(2,1)S(1)}, bf16[128,1024]{1,0:T(8,128)(2,1)}, u32[]{:S(2)}, u32[]{:S(2)}) collective-permute-start(bf16[128,1024]{1,0:T(8,128)(2,1)S(1)} %reduce_sum.59.refs_8_), channel_id=1, source_target_pairs={{0,2},{2,0},{1,3},{3,1},{4,6},{6,4},{5,7},{7,5},{8,10},{10,8},{9,1... | collective-permute-start | bytes 786440 | tf_op jit(solution)/shard_map/ppermute | solution.py:532
  336.9 16.7 %collective-permute-start.59 = (bf16[64,1024]{1,0:T(8,128)(2,1)S(1)}, bf16[64,1024]{1,0:T(8,128)(2,1)S(1)}, u32[]{:S(2)}, u32[]{:S(2)}) collective-permute-start(bf16[64,1024]{1,0:T(8,128)(2,1)S(1)} %reduce_sum.58.refs_0_), channel_id=1, source_target_pairs={{0,2},{2,0},{1,3},{3,1},{4,6},{6,4},{5,7},{7,5},{8,10},{10,8},{9,1... | collective-permute-start | bytes 393224 | tf_op jit(solution)/shard_map/ppermute | solution.py:532
  338.2 14.8 %collective-permute-start.58 = (f32[8,1536]{1,0:T(8,128)S(1)}, f32[8,1536]{1,0:T(8,128)S(1)}, u32[]{:S(2)}, u32[]{:S(2)}) collective-permute-start(f32[8,1536]{1,0:T(8,128)S(1)} %add.147), channel_id=1, source_target_pairs={{0,2},{2,0},{1,3},{3,1},{4,6},{6,4},{5,7},{7,5},{8,10},{10,8},{9,1... | collective-permute-start | bytes 147464 | tf_op jit(solution)/shard_map/ppermute | solution.py:532
  356.7 31.3 %all-to-all-start.6 = ((bf16[4,64,1536]{2,1,0:T(8,128)(2,1)}), bf16[4,64,1536]{2,1,0:T(8,128)(2,1)S(1)}, u32[]{:S(2)}, u32[]{:S(2)}) async-start(bf16[4,64,1536]{2,1,0:T(8,128)(2,1)} %add_convert_fusion.2), calls=%async_computation.6 | async-start | bytes 1572864 | tf_op jit(solution)/shard_map/all_to_all | solution.py:563
  365.4 22.0 %collective-permute-start.66 = (bf16[4,80,1024]{2,1,0:T(8,128)(2,1)}, bf16[4,80,1024]{2,1,0:T(8,128)(2,1)S(1)}, u32[]{:S(2)}, u32[]{:S(2)}) collective-permute-start(bf16[4,80,1024]{2,1,0:T(8,128)(2,1)} %get-tuple-element.414), channel_id=1, source_target_pairs={{0,1},{1,0},{2,3},{3,2},{4,5},{5,4},{6,7},{7,6},{8,9},{9,8},{10,11... | collective-permute-start | bytes 1966088 | tf_op jit(solution)/shard_map/ppermute | solution.py:536
  365.4 22.6 %collective-permute-start.67 = (bf16[4,80,1024]{2,1,0:T(8,128)(2,1)}, bf16[4,80,1024]{2,1,0:T(8,128)(2,1)S(1)}, u32[]{:S(2)}, u32[]{:S(2)}) collective-permute-start(bf16[4,80,1024]{2,1,0:T(8,128)(2,1)} %get-tuple-element.415), channel_id=1, source_target_pairs={{0,2},{1,3},{2,0},{3,1},{4,6},{5,7},{6,4},{7,5},{8,10},{9,11},{10,... | collective-permute-start | bytes 1966088 | tf_op jit(solution)/shard_map/ppermute | solution.py:536
  369.3 12.6 %collective-permute-start.64 = (f32[1536]{0:T(1024)}, f32[1536]{0:T(1024)}, u32[]{:S(2)}, u32[]{:S(2)}) collective-permute-start(f32[1536]{0:T(1024)} %get-tuple-element.400), channel_id=1, source_target_pairs={{0,16},{8,24},{16,0},{24,8},{1,17},{9,25},{17,1},{25,9},{2,18},{10... | collective-permute-start | bytes 18440 | tf_op jit(solution)/shard_map/ppermute | solution.py:536
  374.2 13.1 %collective-permute-start.61 = (bf16[64,1536]{1,0:T(8,128)(2,1)}, bf16[64,1536]{1,0:T(8,128)(2,1)S(1)}, u32[]{:S(2)}, u32[]{:S(2)}) collective-permute-start(bf16[64,1536]{1,0:T(8,128)(2,1)} %reduce_sum.60.refs_4_), channel_id=1, source_target_pairs={{0,2},{2,0},{1,3},{3,1},{4,6},{6,4},{5,7},{7,5},{8,10},{10,8},{9,1... | collective-permute-start | bytes 589832 | tf_op jit(solution)/shard_map/ppermute | solution.py:532
  381.8 18.8 %collective-permute-start.74 = (bf16[4,80,1024]{2,1,0:T(8,128)(2,1)}, bf16[4,80,1024]{2,1,0:T(8,128)(2,1)S(1)}, u32[]{:S(2)}, u32[]{:S(2)}) collective-permute-start(bf16[4,80,1024]{2,1,0:T(8,128)(2,1)} %get-tuple-element.412), channel_id=1, source_target_pairs={{0,3},{1,2},{2,1},{3,0},{4,7},{5,6},{6,5},{7,4},{8,11},{9,10},{10,... | collective-permute-start | bytes 1966088 | tf_op jit(solution)/shard_map/ppermute | solution.py:536
  391.5 13.7 %collective-permute-start.75 = (bf16[64,1536]{1,0:T(8,128)(2,1)}, bf16[64,1536]{1,0:T(8,128)(2,1)S(1)}, u32[]{:S(2)}, u32[]{:S(2)}) collective-permute-start(bf16[64,1536]{1,0:T(8,128)(2,1)} %reduce_sum.61.refs_0_), channel_id=1, source_target_pairs={{0,2},{2,0},{1,3},{3,1},{4,6},{6,4},{5,7},{7,5},{8,10},{10,8},{9,1... | collective-permute-start | bytes 589832 | tf_op jit(solution)/shard_map/ppermute | solution.py:532
  392.7 17.0 %collective-permute-start.76 = (bf16[64,1536]{1,0:T(8,128)(2,1)}, bf16[64,1536]{1,0:T(8,128)(2,1)S(1)}, u32[]{:S(2)}, u32[]{:S(2)}) collective-permute-start(bf16[64,1536]{1,0:T(8,128)(2,1)} %reduce_sum.61.refs_0_), channel_id=1, source_target_pairs={{0,1},{1,0},{2,3},{3,2},{4,5},{5,4},{6,7},{7,6},{8,9},{9,8},{10,11... | collective-permute-start | bytes 589832 | tf_op jit(solution)/shard_map/ppermute | solution.py:532
  (57 other events, 344.6 us)

commit v5 on v4

--- a/solution.py
+++ b/solution.py
@@ -11,7 +11,7 @@
 HEAD_DIM = 64
 LANES = 128
 GROUPS = 2
-TILES = 4
+TILES = 2
 EPSILON = 1e-06
 BF16 = jnp.bfloat16
 F32 = jnp.float32

time: 420 us -> 420 us (level)
  no operation moved by 1% of the time
where the time goes in v5:
time: 420 us; the launch traced here: 414 us
  Pallas kernels  174 us (41%)
  waiting for transfers between devices  96.1 us (23%)
  starting transfers between devices  87.7 us (21%)
  other arithmetic  32.3 us (8%)
  local copies, waits for them, and re-layouts  21.8 us (5%)
    pallas_call x5, Pallas kernels, stepped(): pl.pallas_call(functools.partial(kernel, weights), grid_spec=pltpu.Prefet...  83.1 us
    ppermute x66, waiting for transfers between devices, swap(): return lax.ppermute(value, axis, [(0, 1), (1, 0)])  55.5 us
    pallas_call x5, Pallas kernels, grad_parts(): pl.pallas_call(kernel, grid_spec=pltpu.PrefetchScalarGridSpec(num_scalar_...  41.8 us
    ppermute x66, starting transfers between devices, swap(): return lax.ppermute(value, axis, [(0, 1), (1, 0)])  41.4 us
    pallas_call x3, Pallas kernels, attention(): pl.pallas_call(attend_back_kernel if back else attend_kernel, grid=(image...  37.8 us
    ppermute x12, waiting for transfers between devices, send(): lax.ppermute(value, axis, [(i, i ^ step) for i in range(lax.axis_size(axi...  37.1 us
    all_to_all x7, starting transfers between devices, exchange(): return lax.all_to_all(blocks, axis, split_axis=0, concat_axis=0, tiled=True)  36.5 us
    convert_element_type x4, other arithmetic, grad_z(): sum((v.astype(F32) for v in (parts[0], from_x, from_y))).astype(BF16)  10 us
  transfers between devices with their start and end apart: 85, of which 26 were waited for; matrix products, arithmetic and copies ran while one was open for 11% of the time, Pallas kernels for 41%

profile of v5, /device:TPU:0, one launch (start us, length us, event | category | flops | bytes accessed | tf_op | source)
XLA Modules:
  0.0 414.1 jit_solution(4184710309429337834)
XLA Ops:
  1.2 3.7 shard_map.254
  4.9 6.4 %all-to-all-start = ((bf16[4,64,1664]{2,1,0:T(8,128)(2,1)}), bf16[4,64,1664]{2,1,0:T(8,128)(2,1)}, u32[]{:S(2)}, u32[]{:S(2)}) async-start(bf16[4,64,1664]{2,1,0:T(8,128)(2,1)} %get-tuple-element.207), calls=%async_computation | async-start | bytes 1703936 | tf_op jit(solution)/shard_map/all_to_all | solution.py:563
  11.6 1.6 collective-permute-start.1
  13.9 1.5 collective-permute-start.4
  15.4 6.7 %collective-permute-done.1 = bf16[2,80,1024]{2,1,0:T(8,128)(2,1)S(1)} collective-permute-done((bf16[2,80,1024]{2,1,0:T(8,128)(2,1)S(1)}, bf16[2,80,1024]{2,1,0:T(8,128)(2,1)S(1)}, u32[]{:S(2)}, u32[]{:S(2)}) %collective-permute-start.1) | collective-permute-done | bytes 327712 | tf_op jit(solution)/shard_map/ppermute | solution.py:536
  22.1 6.1 %collective-permute-done.2 = bf16[2,80,1024]{2,1,0:T(8,128)(2,1)S(1)} collective-permute-done((bf16[2,80,1024]{2,1,0:T(8,128)(2,1)S(1)}, bf16[2,80,1024]{2,1,0:T(8,128)(2,1)S(1)}, u32[]{:S(2)}, u32[]{:S(2)}) %collective-permute-start.2) | collective-permute-done | bytes 327712 | tf_op jit(solution)/shard_map/ppermute | solution.py:536
  28.3 7.6 %collective-permute-done.4 = bf16[2,80,1024]{2,1,0:T(8,128)(2,1)} collective-permute-done((bf16[2,80,1024]{2,1,0:T(8,128)(2,1)S(1)}, bf16[2,80,1024]{2,1,0:T(8,128)(2,1)}, u32[]{:S(2)}, u32[]{:S(2)}) %collective-permute-start.4) | collective-permute-done | bytes 327712 | tf_op jit(solution)/shard_map/ppermute | solution.py:536
  35.8 1.5 collective-permute-start.5
  37.3 1.5 collective-permute-start.6
  38.9 5.1 %all-to-all-start.1 = ((bf16[4,64,2560]{2,1,0:T(8,128)(2,1)}), bf16[4,64,2560]{2,1,0:T(8,128)(2,1)S(1)}, u32[]{:S(2)}, u32[]{:S(2)}) async-start(bf16[4,64,2560]{2,1,0:T(8,128)(2,1)} %get-tuple-element.215), calls=%async_computation.1 | async-start | bytes 2621440 | tf_op jit(solution)/shard_map/all_to_all | solution.py:563
  45.2 11.5 %collective-permute-done.5.refs_1_ = bf16[4,64,1664]{2,1,0:T(8,128)(2,1)} collective-permute-done((bf16[4,64,1664]{2,1,0:T(8,128)(2,1)}, bf16[4,64,1664]{2,1,0:T(8,128)(2,1)}, u32[]{:S(2)}, u32[]{:S(2)}) %collective-permute-start.5) | collective-permute-done | bytes 852000 | tf_op jit(solution)/shard_map/ppermute | solution.py:532
  62.2 1.5 collective-permute-start.7
  65.4 9.0 %collective-permute-done.7.refs_3_ = bf16[2,64,1664]{2,1,0:T(8,128)(2,1)} collective-permute-done((bf16[2,64,1664]{2,1,0:T(8,128)(2,1)S(1)}, bf16[2,64,1664]{2,1,0:T(8,128)(2,1)}, u32[]{:S(2)}, u32[]{:S(2)}) %collective-permute-start.7) | collective-permute-done | bytes 426016 | tf_op jit(solution)/shard_map/ppermute | solution.py:532
  74.5 1.2 collective-permute-done.8.refs_4_
  78.5 9.8 %shard_map.255 = (bf16[640,1024]{1,0:T(8,128)(2,1)}, bf16[640,3072]{1,0:T(8,128)(2,1)}) custom-call(s32[3]{0:T(128)} %pad_add_fusion.place_ref, bf16[4,64,1664]{2,1,0:T(8,128)(2,1)} %all-to-all-done.refs_0_, bf16[4,64,1664]{2,1,0:T(8,128)(2,1)} %collective-permute-done.5.refs_1_, bf16[4,64,1664]{2,1,0:T(8,128)(2,1)} %collective-permute-done.6.refs_2_, ...), custom_call_target="tpu_custom_call" | custom-call | flops 11000000512 | tf_op jit(solution)/shard_map/pallas_call | solution.py:260
  88.3 5.3 %all-to-all-start.2 = ((bf16[4,64,2048]{2,1,0:T(8,128)(2,1)}), bf16[4,64,2048]{2,1,0:T(8,128)(2,1)}, u32[]{:S(2)}, u32[]{:S(2)}) async-start(bf16[4,64,2048]{2,1,0:T(8,128)(2,1)} %get-tuple-element.242), calls=%async_computation.2 | async-start | bytes 2097152 | tf_op jit(solution)/shard_map/all_to_all | solution.py:563
  94.5 12.6 %collective-permute-done.14.refs_1_.refs_11_.refs_21_ = bf16[4,64,2560]{2,1,0:T(8,128)(2,1)S(1)} collective-permute-done((bf16[4,64,2560]{2,1,0:T(8,128)(2,1)S(1)}, bf16[4,64,2560]{2,1,0:T(8,128)(2,1)S(1)}, u32[]{:S(2)}, u32[]{:S(2)}) %collective-permute-start.14) | collective-permute-done | bytes 1310752 | tf_op jit(solution)/shard_map/ppermute | solution.py:532
  113.8 15.6 %shard_map.256 = (bf16[2,320,1024]{2,1,0:T(8,128)(2,1)}, f32[2,320,1024]{2,1,0:T(8,128)}) custom-call(f32[2,320,1]{2,1,0:T(8,128)} %compare_select_fusion.bias_ref, bf16[2,320,3072]{2,1,0:T(8,128)(2,1)} %bitcast.147, bf16[2,320,3072]{2,1,0:T(8,128)(2,1)} %bitcast.148, bf16[2,320,3072]{2,1,0:T(8,128)(2,1)} %bitcast.149), custom_call_target="tpu_custom_call" | custom-call | flops 14080000000 | tf_op jit(solution)/shard_map/pallas_call | solution.py:133
  129.4 4.5 %collective-permute-done.21 = bf16[2,80,1024]{2,1,0:T(8,128)(2,1)S(1)} collective-permute-done((bf16[2,80,1024]{2,1,0:T(8,128)(2,1)S(1)}, bf16[2,80,1024]{2,1,0:T(8,128)(2,1)S(1)}, u32[]{:S(2)}, u32[]{:S(2)}) %collective-permute-start.21) | collective-permute-done | bytes 327712 | tf_op jit(solution)/shard_map/ppermute | solution.py:536
  136.0 1.5 collective-permute-start.25
  139.9 18.4 %shard_map.257 = (f32[640,1024]{1,0:T(8,128)}, bf16[640,1024]{1,0:T(8,128)(2,1)}, bf16[640,4096]{1,0:T(8,128)(2,1)}, bf16[640,4096]{1,0:T(8,128)(2,1)}, bf16[640,2048]{1,0:T(8,128)(2,1)}) custom-call(s32[3]{0:T(128)} %pad_add_fusion.place_ref, bf16[4,64,2560]{2,1,0:T(8,128)(2,1)} %copy-done.6, bf16[4,64,2560]{2,1,0:T(8,128)(2,1)} %copy-done.10, ...), custom_call_target="tpu_custom_call" | custom-call | flops 22000001024 | tf_op jit(solution)/shard_map/pallas_call | solution.py:260
  158.3 2.6 collective-permute-done.24.refs_1_
  165.3 1.5 collective-permute-start.29
  168.9 11.6 %shard_map.258 = (bf16[4,128,1024]{2,1,0:T(8,128)(2,1)S(1)}, bf16[4,128,1024]{2,1,0:T(8,128)(2,1)}, bf16[4,128,1024]{2,1,0:T(8,128)(2,1)}, bf16[4,128,1024]{2,1,0:T(8,128)(2,1)}) custom-call(s32[3]{0:T(128)S(1)} %copy-done.2, bf16[640,4096]{1,0:T(8,128)(2,1)} %get-tuple-element.362.a0_ref.a1_ref.refs_10_, ...), custom_call_target="tpu_custom_call" | custom-call | flops 10150215680 | tf_op jit(solution)/shard_map/pallas_call | solution.py:705
  184.3 26.8 %shard_map.259 = (bf16[640,4096]{1,0:T(8,128)(2,1)}, f32[1,4096]{1,0:T(1,128)}, f32[640,1024]{1,0:T(8,128)}, bf16[640,1024]{1,0:T(8,128)(2,1)}, bf16[640,1024]{1,0:T(8,128)(2,1)}, /*index=5*/f32[8,1024]{1,0:T(8,128)}) custom-call(s32[3]{0:T(128)} %pad_add_fusion.place_ref, bf16[4,64,2048]{2,1,0:T(8,128)(2,1)} %all-to-all-done.2.refs_0_, ...), custom_call_target="tpu_custom_call" | custom-call | flops 25300000768 | tf_op jit(solution)/shard_map/pallas_call | solution.py:260
  211.7 1.3 collective-permute-start.44
  213.0 11.2 %shard_map.260 = bf16[2,320,1536]{2,1,0:T(8,128)(2,1)} custom-call(f32[2,320,1]{2,1,0:T(8,128)} %compare_select_fusion.bias_ref, bf16[2,320,3072]{2,1,0:T(8,128)(2,1)} %bitcast.150, bf16[2,320,3072]{2,1,0:T(8,128)(2,1)} %bitcast.151, bf16[2,320,3072]{2,1,0:T(8,128)(2,1)} %bitcast.152, f32[2,320,1024]{2,1,0:T(8,128)} %get-tuple-element.290.lse_ref, ...), custom_call_target="tpu_custom_call" | custom-call | flops 11440000000 | tf_op jit(solution)/shard_map/pallas_call | solution.py:133
  225.9 7.3 %shard_map.263 = (bf16[4,64,1024]{2,1,0:T(8,128)(2,1)S(1)}, bf16[4,64,1024]{2,1,0:T(8,128)(2,1)S(1)}, bf16[4,64,1024]{2,1,0:T(8,128)(2,1)}, bf16[4,64,1024]{2,1,0:T(8,128)(2,1)}) custom-call(s32[3]{0:T(128)S(1)} %copy-done.3, bf16[640,1024]{1,0:T(8,128)(2,1)} %get-tuple-element.288.refs_0_, bf16[640,1024]{1,0:T(8,128)(2,1)} %collective-permute-done.37.refs_1_, ...), custom_call_target="tpu_custom_call" | custom-call | flops 5075107840 | tf_op jit(solution)/shard_map/pallas_call | solution.py:705
  235.3 11.2 %shard_map.262 = (bf16[4,64,1536]{2,1,0:T(8,128)(2,1)S(1)}, bf16[4,64,1536]{2,1,0:T(8,128)(2,1)S(1)}, bf16[4,64,1536]{2,1,0:T(8,128)(2,1)}, bf16[4,64,1536]{2,1,0:T(8,128)(2,1)}) custom-call(s32[3]{0:T(128)S(1)} %copy-done.3, bf16[640,1024]{1,0:T(8,128)(2,1)} %get-tuple-element.288.refs_0_, bf16[640,1024]{1,0:T(8,128)(2,1)} %collective-permute-done.37.refs_1_, ...), custom_call_target="tpu_custom_call" | custom-call | flops 7612661760 | tf_op jit(solution)/shard_map/pallas_call | solution.py:705
  246.5 3.8 collective-permute-done.43
  250.3 2.8 add_convert_fusion
  253.1 5.1 %all-to-all-start.3 = ((bf16[4,128,1024]{2,1,0:T(8,128)(2,1)}), bf16[4,128,1024]{2,1,0:T(8,128)(2,1)}, u32[]{:S(2)}, u32[]{:S(2)}) async-start(bf16[4,128,1024]{2,1,0:T(8,128)(2,1)} %add_convert_fusion), calls=%async_computation.3 | async-start | bytes 2097152 | tf_op jit(solution)/shard_map/all_to_all | solution.py:563
  258.2 2.0 add_convert_fusion.6
  262.2 6.2 %shard_map.261 = (bf16[4,64,768]{2,1,0:T(8,128)(2,1)S(1)}, bf16[4,64,768]{2,1,0:T(8,128)(2,1)S(1)}, bf16[4,64,768]{2,1,0:T(8,128)(2,1)S(1)}, bf16[4,64,768]{2,1,0:T(8,128)(2,1)}) custom-call(s32[3]{0:T(128)S(1)} %copy-done.3, bf16[640,1024]{1,0:T(8,128)(2,1)} %get-tuple-element.236.refs_0_, bf16[640,1024]{1,0:T(8,128)(2,1)} %copy-done.20, ...), custom_call_target="tpu_custom_call" | custom-call | flops 3806330880 | tf_op jit(solution)/shard_map/pallas_call | solution.py:705
  269.3 11.1 %shard_map.264 = bf16[2,320,1536]{2,1,0:T(8,128)(2,1)} custom-call(f32[2,320,1]{2,1,0:T(8,128)} %compare_select_fusion.bias_ref, bf16[2,320,3072]{2,1,0:T(8,128)(2,1)} %bitcast.153, bf16[2,320,3072]{2,1,0:T(8,128)(2,1)} %bitcast.154, bf16[2,320,3072]{2,1,0:T(8,128)(2,1)} %bitcast.155, f32[2,320,1024]{2,1,0:T(8,128)} %get-tuple-element.290.lse_ref, ...), custom_call_target="tpu_custom_call" | custom-call | flops 11440000000 | tf_op jit(solution)/shard_map/pallas_call | solution.py:133
  280.4 3.6 all-to-all-done.3
  286.9 2.3 add_convert_fusion.5
  289.1 4.3 %all-to-all-start.4 = ((bf16[4,64,1024]{2,1,0:T(8,128)(2,1)}), bf16[4,64,1024]{2,1,0:T(8,128)(2,1)}, u32[]{:S(2)}, u32[]{:S(2)}) async-start(bf16[4,64,1024]{2,1,0:T(8,128)(2,1)} %add_convert_fusion.5), calls=%async_computation.4 | async-start | bytes 1048576 | tf_op jit(solution)/shard_map/all_to_all | solution.py:563
  293.5 2.2 add_convert_fusion.4
  296.5 1.9 add_convert_fusion.8
  298.4 1.2 collective-permute-start.52
  299.6 5.5 %shard_map.265 = (bf16[4,64,768]{2,1,0:T(8,128)(2,1)S(1)}, bf16[4,64,768]{2,1,0:T(8,128)(2,1)S(1)}, bf16[4,64,768]{2,1,0:T(8,128)(2,1)S(1)}, bf16[4,64,768]{2,1,0:T(8,128)(2,1)S(1)}) custom-call(s32[3]{0:T(128)S(1)} %copy-done.3, bf16[640,1024]{1,0:T(8,128)(2,1)} %get-tuple-element.236.refs_0_, bf16[640,1024]{1,0:T(8,128)(2,1)} %copy-done.20, ...), custom_call_target="tpu_custom_call" | custom-call | flops 3806330880 | tf_op jit(solution)/shard_map/pallas_call | solution.py:705
  306.0 14.9 %shard_map.266 = (bf16[640,1024]{1,0:T(8,128)(2,1)}, f32[1,3072]{1,0:T(1,128)}, f32[8,1024]{1,0:T(8,128)}) custom-call(s32[3]{0:T(128)} %pad_add_fusion.place_ref, bf16[4,64,1664]{2,1,0:T(8,128)(2,1)} %all-to-all-done.refs_0_, bf16[4,64,1664]{2,1,0:T(8,128)(2,1)} %collective-permute-done.5.refs_1_, bf16[4,64,1664]{2,1,0:T(8,128)(2,1)} %collective-permute-done.6.refs_2_, ...), custom_call_target="tpu_custom_call" | custom-call | flops 14300000256 | tf_op jit(solution)/shard_map/pallas_call | solution.py:260
  320.9 1.5 shard_map.267
  322.3 1.3 collective-permute-start.56
  323.7 2.6 add_convert_fusion.3
  326.3 5.0 %all-to-all-start.5 = ((bf16[4,64,1536]{2,1,0:T(8,128)(2,1)}), bf16[4,64,1536]{2,1,0:T(8,128)(2,1)S(1)}, u32[]{:S(2)}, u32[]{:S(2)}) async-start(bf16[4,64,1536]{2,1,0:T(8,128)(2,1)} %add_convert_fusion.3), calls=%async_computation.5 | async-start | bytes 1572864 | tf_op jit(solution)/shard_map/all_to_all | solution.py:563
  332.4 1.2 collective-permute-start.55
  333.7 1.4 reduce_sum.59.refs_8_
  337.2 1.2 collective-permute-start.59
  339.3 13.2 %shard_map.268 = bf16[640,1024]{1,0:T(8,128)(2,1)} custom-call(s32[3]{0:T(128)} %pad_add_fusion.place_ref, bf16[4,64,2048]{2,1,0:T(8,128)(2,1)} %all-to-all-done.2.refs_0_, bf16[4,64,2048]{2,1,0:T(8,128)(2,1)} %copy-done.12, bf16[4,64,2048]{2,1,0:T(8,128)(2,1)} %copy-done.13, bf16[2,64,2048]{2,1,0:T(8,128)(2,1)} %copy-done.26, ...), custom_call_target="tpu_custom_call" | custom-call | flops 12099999744 | tf_op jit(solution)/shard_map/pallas_call | solution.py:260
  354.5 2.4 add_convert_fusion.2
  356.9 5.2 %all-to-all-start.6 = ((bf16[4,64,1536]{2,1,0:T(8,128)(2,1)}), bf16[4,64,1536]{2,1,0:T(8,128)(2,1)S(1)}, u32[]{:S(2)}, u32[]{:S(2)}) async-start(bf16[4,64,1536]{2,1,0:T(8,128)(2,1)} %add_convert_fusion.2), calls=%async_computation.6 | async-start | bytes 1572864 | tf_op jit(solution)/shard_map/all_to_all | solution.py:563
  363.0 2.6 fusion.6
  367.5 2.0 collective-permute-start.63
  369.5 2.4 collective-permute-start.64
  372.7 1.8 collective-permute-done.63
  375.7 6.4 %collective-permute-done.64 = f32[1536]{0:T(1024)} collective-permute-done((f32[1536]{0:T(1024)}, f32[1536]{0:T(1024)}, u32[]{:S(2)}, u32[]{:S(2)}) %collective-permute-start.64) | collective-permute-done | bytes 6176 | tf_op jit(solution)/shard_map/ppermute | solution.py:536
  382.8 4.8 %collective-permute-done.61.refs_5_ = bf16[64,1536]{1,0:T(8,128)(2,1)S(1)} collective-permute-done((bf16[64,1536]{1,0:T(8,128)(2,1)}, bf16[64,1536]{1,0:T(8,128)(2,1)S(1)}, u32[]{:S(2)}, u32[]{:S(2)}) %collective-permute-start.61) | collective-permute-done | bytes 196640 | tf_op jit(solution)/shard_map/ppermute | solution.py:532
  393.0 4.0 shard_map.269
  396.9 3.9 collective-permute-done.74
  400.9 4.6 %collective-permute-done.75.refs_1_ = bf16[64,1536]{1,0:T(8,128)(2,1)S(1)} collective-permute-done((bf16[64,1536]{1,0:T(8,128)(2,1)}, bf16[64,1536]{1,0:T(8,128)(2,1)S(1)}, u32[]{:S(2)}, u32[]{:S(2)}) %collective-permute-start.75) | collective-permute-done | bytes 196640 | tf_op jit(solution)/shard_map/ppermute | solution.py:532
  407.7 1.7 slice_bitcast_fusion
  411.3 2.6 shard_map.270
  (256 shorter events, 67.7 us)
Async XLA Ops:
  4.9 30.9 %all-to-all-start = ((bf16[4,64,1664]{2,1,0:T(8,128)(2,1)}), bf16[4,64,1664]{2,1,0:T(8,128)(2,1)}, u32[]{:S(2)}, u32[]{:S(2)}) async-start(bf16[4,64,1664]{2,1,0:T(8,128)(2,1)} %get-tuple-element.207), calls=%async_computation | async-start | bytes 1703936 | tf_op jit(solution)/shard_map/all_to_all | solution.py:563
  13.1 15.1 %collective-permute-start.2 = (bf16[2,80,1024]{2,1,0:T(8,128)(2,1)S(1)}, bf16[2,80,1024]{2,1,0:T(8,128)(2,1)S(1)}, u32[]{:S(2)}, u32[]{:S(2)}) collective-permute-start(bf16[2,80,1024]{2,1,0:T(8,128)(2,1)S(1)} %get-tuple-element.421), channel_id=1, source_target_pairs={{0,3},{1,2},{2,1},{3,0},{4,7},{5,6},{6,5},{7,4},{8,11},{9,10},{10,... | collective-permute-start | bytes 983048 | tf_op jit(solution)/shard_map/ppermute | solution.py:536
  13.5 14.7 %collective-permute-start.3 = (bf16[2,80,1024]{2,1,0:T(8,128)(2,1)S(1)}, bf16[2,80,1024]{2,1,0:T(8,128)(2,1)}, u32[]{:S(2)}, u32[]{:S(2)}) collective-permute-start(bf16[2,80,1024]{2,1,0:T(8,128)(2,1)S(1)} %get-tuple-element.419), channel_id=1, source_target_pairs={{0,1},{1,0},{2,3},{3,2},{4,5},{5,4},{6,7},{7,6},{8,9},{9,8},{10,11... | collective-permute-start | bytes 983048 | tf_op jit(solution)/shard_map/ppermute | solution.py:536
  13.9 21.9 %collective-permute-start.4 = (bf16[2,80,1024]{2,1,0:T(8,128)(2,1)S(1)}, bf16[2,80,1024]{2,1,0:T(8,128)(2,1)}, u32[]{:S(2)}, u32[]{:S(2)}) collective-permute-start(bf16[2,80,1024]{2,1,0:T(8,128)(2,1)S(1)} %get-tuple-element.418), channel_id=1, source_target_pairs={{0,2},{1,3},{2,0},{3,1},{4,6},{5,7},{6,4},{7,5},{8,10},{9,11},{10,... | collective-permute-start | bytes 983048 | tf_op jit(solution)/shard_map/ppermute | solution.py:536
  35.8 20.8 %collective-permute-start.5 = (bf16[4,64,1664]{2,1,0:T(8,128)(2,1)}, bf16[4,64,1664]{2,1,0:T(8,128)(2,1)}, u32[]{:S(2)}, u32[]{:S(2)}) collective-permute-start(bf16[4,64,1664]{2,1,0:T(8,128)(2,1)} %all-to-all-done.refs_0_), channel_id=1, source_target_pairs={{0,2},{2,0},{1,3},{3,1},{4,6},{6,4},{5,7},{7,5},{8,10},{10,8},{9,1... | collective-permute-start | bytes 2555912 | tf_op jit(solution)/shard_map/ppermute | solution.py:532
  37.3 20.5 %collective-permute-start.6 = (bf16[4,64,1664]{2,1,0:T(8,128)(2,1)}, bf16[4,64,1664]{2,1,0:T(8,128)(2,1)}, u32[]{:S(2)}, u32[]{:S(2)}) collective-permute-start(bf16[4,64,1664]{2,1,0:T(8,128)(2,1)} %all-to-all-done.refs_0_), channel_id=1, source_target_pairs={{0,4},{4,0},{1,5},{5,1},{2,6},{6,2},{3,7},{7,3},{8,12},{12,8},{9,1... | collective-permute-start | bytes 2555912 | tf_op jit(solution)/shard_map/ppermute | solution.py:532
  38.9 36.9 %all-to-all-start.1 = ((bf16[4,64,2560]{2,1,0:T(8,128)(2,1)}), bf16[4,64,2560]{2,1,0:T(8,128)(2,1)S(1)}, u32[]{:S(2)}, u32[]{:S(2)}) async-start(bf16[4,64,2560]{2,1,0:T(8,128)(2,1)} %get-tuple-element.215), calls=%async_computation.1 | async-start | bytes 2621440 | tf_op jit(solution)/shard_map/all_to_all | solution.py:563
  57.9 17.8 %collective-permute-start.10 = (bf16[4,64,1664]{2,1,0:T(8,128)(2,1)}, bf16[4,64,1664]{2,1,0:T(8,128)(2,1)}, u32[]{:S(2)}, u32[]{:S(2)}) collective-permute-start(bf16[4,64,1664]{2,1,0:T(8,128)(2,1)} %collective-permute-done.5.refs_1_), channel_id=1, source_target_pairs={{0,1},{1,0},{2,3},{3,2},{4,5},{5,4},{6,7},{7,6},{8,9},{9,8},{10,11... | collective-permute-start | bytes 2555912 | tf_op jit(solution)/shard_map/ppermute | solution.py:532
  58.9 16.8 %collective-permute-start.11 = (bf16[4,64,1664]{2,1,0:T(8,128)(2,1)}, bf16[4,64,1664]{2,1,0:T(8,128)(2,1)}, u32[]{:S(2)}, u32[]{:S(2)}) collective-permute-start(bf16[4,64,1664]{2,1,0:T(8,128)(2,1)} %collective-permute-done.6.refs_2_), channel_id=1, source_target_pairs={{0,1},{1,0},{2,3},{3,2},{4,5},{5,4},{6,7},{7,6},{8,9},{9,8},{10,11... | collective-permute-start | bytes 2555912 | tf_op jit(solution)/shard_map/ppermute | solution.py:532
  60.5 15.2 %collective-permute-start.9 = (bf16[4,64,1664]{2,1,0:T(8,128)(2,1)}, bf16[4,64,1664]{2,1,0:T(8,128)(2,1)}, u32[]{:S(2)}, u32[]{:S(2)}) collective-permute-start(bf16[4,64,1664]{2,1,0:T(8,128)(2,1)} %all-to-all-done.refs_0_), channel_id=1, source_target_pairs={{0,1},{1,0},{2,3},{3,2},{4,5},{5,4},{6,7},{7,6},{8,9},{9,8},{10,11... | collective-permute-start | bytes 2555912 | tf_op jit(solution)/shard_map/ppermute | solution.py:532
  76.3 30.8 %collective-permute-start.14 = (bf16[4,64,2560]{2,1,0:T(8,128)(2,1)S(1)}, bf16[4,64,2560]{2,1,0:T(8,128)(2,1)S(1)}, u32[]{:S(2)}, u32[]{:S(2)}) collective-permute-start(bf16[4,64,2560]{2,1,0:T(8,128)(2,1)S(1)} %all-to-all-done.1.refs_0_.refs_10_.refs_20_), channel_id=1, source_target_pairs={{0,2},{2,0},{1,3},{3,1},{4,6},{6,4},{5,7},{7,5},{8,10},{10,8},{9,1... | collective-permute-start | bytes 3932168 | tf_op jit(solution)/shard_map/ppermute | solution.py:532
  76.9 30.6 %collective-permute-start.15 = (bf16[4,64,2560]{2,1,0:T(8,128)(2,1)S(1)}, bf16[4,64,2560]{2,1,0:T(8,128)(2,1)}, u32[]{:S(2)}, u32[]{:S(2)}) collective-permute-start(bf16[4,64,2560]{2,1,0:T(8,128)(2,1)S(1)} %all-to-all-done.1.refs_0_.refs_10_.refs_20_), channel_id=1, source_target_pairs={{0,4},{4,0},{1,5},{5,1},{2,6},{6,2},{3,7},{7,3},{8,12},{12,8},{9,1... | collective-permute-start | bytes 3932168 | tf_op jit(solution)/shard_map/ppermute | solution.py:532
  77.4 30.1 %collective-permute-start.16 = (bf16[4,64,2560]{2,1,0:T(8,128)(2,1)S(1)}, bf16[4,64,2560]{2,1,0:T(8,128)(2,1)}, u32[]{:S(2)}, u32[]{:S(2)}) collective-permute-start(bf16[4,64,2560]{2,1,0:T(8,128)(2,1)S(1)} %all-to-all-done.1.refs_0_.refs_10_.refs_20_), channel_id=1, source_target_pairs={{0,1},{1,0},{2,3},{3,2},{4,5},{5,4},{6,7},{7,6},{8,9},{9,8},{10,11... | collective-permute-start | bytes 3932168 | tf_op jit(solution)/shard_map/ppermute | solution.py:532
  88.3 45.5 %all-to-all-start.2 = ((bf16[4,64,2048]{2,1,0:T(8,128)(2,1)}), bf16[4,64,2048]{2,1,0:T(8,128)(2,1)}, u32[]{:S(2)}, u32[]{:S(2)}) async-start(bf16[4,64,2048]{2,1,0:T(8,128)(2,1)} %get-tuple-element.242), calls=%async_computation.2 | async-start | bytes 2097152 | tf_op jit(solution)/shard_map/all_to_all | solution.py:563
  109.3 24.6 %collective-permute-start.19 = (bf16[4,64,2560]{2,1,0:T(8,128)(2,1)}, bf16[4,64,2560]{2,1,0:T(8,128)(2,1)}, u32[]{:S(2)}, u32[]{:S(2)}) collective-permute-start(bf16[4,64,2560]{2,1,0:T(8,128)(2,1)} %copy-done.10), channel_id=1, source_target_pairs={{0,1},{1,0},{2,3},{3,2},{4,5},{5,4},{6,7},{7,6},{8,9},{9,8},{10,11... | collective-permute-start | bytes 3932168 | tf_op jit(solution)/shard_map/ppermute | solution.py:532
  110.5 23.4 %collective-permute-start.20 = (bf16[4,64,2560]{2,1,0:T(8,128)(2,1)}, bf16[4,64,2560]{2,1,0:T(8,128)(2,1)}, u32[]{:S(2)}, u32[]{:S(2)}) collective-permute-start(bf16[4,64,2560]{2,1,0:T(8,128)(2,1)} %collective-permute-done.15.refs_2_.refs_12_.refs_22_), channel_id=1, source_target_pairs={{0,1},{1,0},{2,3},{3,2},{4,5},{5,4},{6,7},{7,6},{8,9},{9,8},{10,11... | collective-permute-start | bytes 3932168 | tf_op jit(solution)/shard_map/ppermute | solution.py:532
  111.0 22.8 %collective-permute-start.17 = (bf16[2,64,2560]{2,1,0:T(8,128)(2,1)S(1)}, bf16[2,64,2560]{2,1,0:T(8,128)(2,1)}, u32[]{:S(2)}, u32[]{:S(2)}) collective-permute-start(bf16[2,64,2560]{2,1,0:T(8,128)(2,1)S(1)} %slice.102), channel_id=1, source_target_pairs={{0,4},{4,0},{1,5},{5,1},{2,6},{6,2},{3,7},{7,3},{8,12},{12,8},{9,1... | collective-permute-start | bytes 1966088 | tf_op jit(solution)/shard_map/ppermute | solution.py:532
  111.6 22.3 %collective-permute-start.18 = (bf16[2,64,2560]{2,1,0:T(8,128)(2,1)S(1)}, bf16[2,64,2560]{2,1,0:T(8,128)(2,1)}, u32[]{:S(2)}, u32[]{:S(2)}) collective-permute-start(bf16[2,64,2560]{2,1,0:T(8,128)(2,1)S(1)} %slice.103), channel_id=1, source_target_pairs={{0,2},{2,0},{1,3},{3,1},{4,6},{6,4},{5,7},{7,5},{8,10},{10,8},{9,1... | collective-permute-start | bytes 1966088 | tf_op jit(solution)/shard_map/ppermute | solution.py:532
  113.4 20.5 %collective-permute-start.21 = (bf16[2,80,1024]{2,1,0:T(8,128)(2,1)S(1)}, bf16[2,80,1024]{2,1,0:T(8,128)(2,1)S(1)}, u32[]{:S(2)}, u32[]{:S(2)}) collective-permute-start(bf16[2,80,1024]{2,1,0:T(8,128)(2,1)S(1)} %dynamic-slice_bitcast_fusion), channel_id=1, source_target_pairs={{0,3},{1,2},{2,1},{3,0},{4,7},{5,6},{6,5},{7,4},{8,11},{9,10},{10,... | collective-permute-start | bytes 983048 | tf_op jit(solution)/shard_map/ppermute | solution.py:536
  135.2 25.7 %collective-permute-start.24 = (bf16[4,64,2048]{2,1,0:T(8,128)(2,1)}, bf16[4,64,2048]{2,1,0:T(8,128)(2,1)S(1)}, u32[]{:S(2)}, u32[]{:S(2)}) collective-permute-start(bf16[4,64,2048]{2,1,0:T(8,128)(2,1)} %all-to-all-done.2.refs_0_), channel_id=1, source_target_pairs={{0,2},{2,0},{1,3},{3,1},{4,6},{6,4},{5,7},{7,5},{8,10},{10,8},{9,1... | collective-permute-start | bytes 3145736 | tf_op jit(solution)/shard_map/ppermute | solution.py:532
  136.0 25.4 %collective-permute-start.25 = (bf16[4,64,2048]{2,1,0:T(8,128)(2,1)}, bf16[4,64,2048]{2,1,0:T(8,128)(2,1)S(1)}, u32[]{:S(2)}, u32[]{:S(2)}) collective-permute-start(bf16[4,64,2048]{2,1,0:T(8,128)(2,1)} %all-to-all-done.2.refs_0_), channel_id=1, source_target_pairs={{0,4},{4,0},{1,5},{5,1},{2,6},{6,2},{3,7},{7,3},{8,12},{12,8},{9,1... | collective-permute-start | bytes 3145736 | tf_op jit(solution)/shard_map/ppermute | solution.py:532
  137.5 23.9 %collective-permute-start.26 = (bf16[4,64,2048]{2,1,0:T(8,128)(2,1)}, bf16[4,64,2048]{2,1,0:T(8,128)(2,1)S(1)}, u32[]{:S(2)}, u32[]{:S(2)}) collective-permute-start(bf16[4,64,2048]{2,1,0:T(8,128)(2,1)} %all-to-all-done.2.refs_0_), channel_id=1, source_target_pairs={{0,1},{1,0},{2,3},{3,2},{4,5},{5,4},{6,7},{7,6},{8,9},{9,8},{10,11... | collective-permute-start | bytes 3145736 | tf_op jit(solution)/shard_map/ppermute | solution.py:532
  139.0 22.4 %collective-permute-start.27 = (bf16[640,1024]{1,0:T(8,128)(2,1)S(1)}, bf16[640,1024]{1,0:T(8,128)(2,1)S(1)}, u32[]{:S(2)}, u32[]{:S(2)}) collective-permute-start(bf16[640,1024]{1,0:T(8,128)(2,1)S(1)} %bitcast_select_fusion.g_ref.refs_30_), channel_id=1, source_target_pairs={{0,1},{1,0},{2,3},{3,2},{4,5},{5,4},{6,7},{7,6},{8,9},{9,8},{10,11... | collective-permute-start | bytes 3932168 | tf_op jit(solution)/shard_map/ppermute | solution.py:532
  163.6 16.9 %collective-permute-start.31 = (bf16[4,64,2048]{2,1,0:T(8,128)(2,1)S(1)}, bf16[4,64,2048]{2,1,0:T(8,128)(2,1)S(1)}, u32[]{:S(2)}, u32[]{:S(2)}) collective-permute-start(bf16[4,64,2048]{2,1,0:T(8,128)(2,1)S(1)} %collective-permute-done.24.refs_1_), channel_id=1, source_target_pairs={{0,1},{1,0},{2,3},{3,2},{4,5},{5,4},{6,7},{7,6},{8,9},{9,8},{10,11... | collective-permute-start | bytes 3145736 | tf_op jit(solution)/shard_map/ppermute | solution.py:532
  164.9 15.6 %collective-permute-start.32 = (bf16[4,64,2048]{2,1,0:T(8,128)(2,1)S(1)}, bf16[4,64,2048]{2,1,0:T(8,128)(2,1)S(1)}, u32[]{:S(2)}, u32[]{:S(2)}) collective-permute-start(bf16[4,64,2048]{2,1,0:T(8,128)(2,1)S(1)} %copy-done.14), channel_id=1, source_target_pairs={{0,1},{1,0},{2,3},{3,2},{4,5},{5,4},{6,7},{7,6},{8,9},{9,8},{10,11... | collective-permute-start | bytes 3145736 | tf_op jit(solution)/shard_map/ppermute | solution.py:532
  165.3 15.2 %collective-permute-start.29 = (bf16[2,64,2048]{2,1,0:T(8,128)(2,1)S(1)}, bf16[2,64,2048]{2,1,0:T(8,128)(2,1)S(1)}, u32[]{:S(2)}, u32[]{:S(2)}) collective-permute-start(bf16[2,64,2048]{2,1,0:T(8,128)(2,1)S(1)} %slice.104), channel_id=1, source_target_pairs={{0,4},{4,0},{1,5},{5,1},{2,6},{6,2},{3,7},{7,3},{8,12},{12,8},{9,1... | collective-permute-start | bytes 1572872 | tf_op jit(solution)/shard_map/ppermute | solution.py:532
  166.8 13.7 %collective-permute-start.30 = (bf16[2,64,2048]{2,1,0:T(8,128)(2,1)S(1)}, bf16[2,64,2048]{2,1,0:T(8,128)(2,1)S(1)}, u32[]{:S(2)}, u32[]{:S(2)}) collective-permute-start(bf16[2,64,2048]{2,1,0:T(8,128)(2,1)S(1)} %slice.105), channel_id=1, source_target_pairs={{0,2},{2,0},{1,3},{3,1},{4,6},{6,4},{5,7},{7,5},{8,10},{10,8},{9,1... | collective-permute-start | bytes 1572872 | tf_op jit(solution)/shard_map/ppermute | solution.py:532
  181.6 29.5 %collective-permute-start.38 = (bf16[640,1024]{1,0:T(8,128)(2,1)S(1)}, bf16[640,1024]{1,0:T(8,128)(2,1)S(1)}, u32[]{:S(2)}, u32[]{:S(2)}) collective-permute-start(bf16[640,1024]{1,0:T(8,128)(2,1)S(1)} %copy-done.18), channel_id=1, source_target_pairs={{0,1},{1,0},{2,3},{3,2},{4,5},{5,4},{6,7},{7,6},{8,9},{9,8},{10,11... | collective-permute-start | bytes 3932168 | tf_op jit(solution)/shard_map/ppermute | solution.py:532
  182.1 29.0 %collective-permute-start.36 = (bf16[640,1024]{1,0:T(8,128)(2,1)S(1)}, bf16[640,1024]{1,0:T(8,128)(2,1)}, u32[]{:S(2)}, u32[]{:S(2)}) collective-permute-start(bf16[640,1024]{1,0:T(8,128)(2,1)S(1)} %bitcast.138), channel_id=1, source_target_pairs={{0,1},{1,0},{2,3},{3,2},{4,5},{5,4},{6,7},{7,6},{8,9},{9,8},{10,11... | collective-permute-start | bytes 3932168 | tf_op jit(solution)/shard_map/ppermute | solution.py:532
  182.2 29.0 %collective-permute-start.37 = (bf16[640,1024]{1,0:T(8,128)(2,1)}, bf16[640,1024]{1,0:T(8,128)(2,1)}, u32[]{:S(2)}, u32[]{:S(2)}) collective-permute-start(bf16[640,1024]{1,0:T(8,128)(2,1)} %get-tuple-element.288.refs_0_), channel_id=1, source_target_pairs={{0,1},{1,0},{2,3},{3,2},{4,5},{5,4},{6,7},{7,6},{8,9},{9,8},{10,11... | collective-permute-start | bytes 3932168 | tf_op jit(solution)/shard_map/ppermute | solution.py:532
  182.6 28.5 %collective-permute-start.35 = (bf16[4,128,1024]{2,1,0:T(8,128)(2,1)}, bf16[4,128,1024]{2,1,0:T(8,128)(2,1)S(1)}, u32[]{:S(2)}, u32[]{:S(2)}) collective-permute-start(bf16[4,128,1024]{2,1,0:T(8,128)(2,1)} %get-tuple-element.285), channel_id=1, source_target_pairs={{0,4},{4,0},{1,5},{5,1},{2,6},{6,2},{3,7},{7,3},{8,12},{12,8},{9,1... | collective-permute-start | bytes 3145736 | tf_op jit(solution)/shard_map/ppermute | solution.py:532
  211.1 13.0 %collective-permute-start.39 = (bf16[640,4096]{1,0:T(8,128)(2,1)}, bf16[640,4096]{1,0:T(8,128)(2,1)}, u32[]{:S(2)}, u32[]{:S(2)}) collective-permute-start(bf16[640,4096]{1,0:T(8,128)(2,1)} %get-tuple-element.292.refs_2_), channel_id=1, source_target_pairs={{0,1},{1,0},{2,3},{3,2},{4,5},{5,4},{6,7},{7,6},{8,9},{9,8},{10,11... | collective-permute-start | bytes 15728648 | tf_op jit(solution)/shard_map/ppermute | solution.py:532
  211.4 12.8 %collective-permute-start.40 = (bf16[640,1024]{1,0:T(8,128)(2,1)}, bf16[640,1024]{1,0:T(8,128)(2,1)}, u32[]{:S(2)}, u32[]{:S(2)}) collective-permute-start(bf16[640,1024]{1,0:T(8,128)(2,1)} %get-tuple-element.293.refs_6_), channel_id=1, source_target_pairs={{0,1},{1,0},{2,3},{3,2},{4,5},{5,4},{6,7},{7,6},{8,9},{9,8},{10,11... | collective-permute-start | bytes 3932168 | tf_op jit(solution)/shard_map/ppermute | solution.py:532
  211.7 34.8 %collective-permute-start.44 = (bf16[4,128,1024]{2,1,0:T(8,128)(2,1)}, bf16[4,128,1024]{2,1,0:T(8,128)(2,1)}, u32[]{:S(2)}, u32[]{:S(2)}) collective-permute-start(bf16[4,128,1024]{2,1,0:T(8,128)(2,1)} %get-tuple-element.316), channel_id=1, source_target_pairs={{0,4},{4,0},{1,5},{5,1},{2,6},{6,2},{3,7},{7,3},{8,12},{12,8},{9,1... | collective-permute-start | bytes 3145736 | tf_op jit(solution)/shard_map/ppermute | solution.py:532
  224.2 38.0 %collective-permute-start.41 = (bf16[640,1536]{1,0:T(8,128)(2,1)}, bf16[640,1536]{1,0:T(8,128)(2,1)}, u32[]{:S(2)}, u32[]{:S(2)}) collective-permute-start(bf16[640,1536]{1,0:T(8,128)(2,1)} %bitcast.130), channel_id=1, source_target_pairs={{0,1},{1,0},{2,3},{3,2},{4,5},{5,4},{6,7},{7,6},{8,9},{9,8},{10,11... | collective-permute-start | bytes 5898248 | tf_op jit(solution)/shard_map/ppermute | solution.py:532
  224.7 25.6 %collective-permute-start.43 = (bf16[4,128,1024]{2,1,0:T(8,128)(2,1)S(1)}, bf16[4,128,1024]{2,1,0:T(8,128)(2,1)S(1)}, u32[]{:S(2)}, u32[]{:S(2)}) collective-permute-start(bf16[4,128,1024]{2,1,0:T(8,128)(2,1)S(1)} %add_convert_fusion.1), channel_id=1, source_target_pairs={{0,2},{2,0},{1,3},{3,1},{4,6},{6,4},{5,7},{7,5},{8,10},{10,8},{9,1... | collective-permute-start | bytes 3145736 | tf_op jit(solution)/shard_map/ppermute | solution.py:532
  233.2 17.1 %collective-permute-start.42 = (bf16[4,64,1024]{2,1,0:T(8,128)(2,1)}, bf16[4,64,1024]{2,1,0:T(8,128)(2,1)}, u32[]{:S(2)}, u32[]{:S(2)}) collective-permute-start(bf16[4,64,1024]{2,1,0:T(8,128)(2,1)} %get-tuple-element.313), channel_id=1, source_target_pairs={{0,4},{4,0},{1,5},{5,1},{2,6},{6,2},{3,7},{7,3},{8,12},{12,8},{9,1... | collective-permute-start | bytes 1572872 | tf_op jit(solution)/shard_map/ppermute | solution.py:532
  234.0 46.3 %collective-permute-start.47 = (bf16[4,64,1024]{2,1,0:T(8,128)(2,1)}, bf16[4,64,1024]{2,1,0:T(8,128)(2,1)}, u32[]{:S(2)}, u32[]{:S(2)}) collective-permute-start(bf16[4,64,1024]{2,1,0:T(8,128)(2,1)} %get-tuple-element.323), channel_id=1, source_target_pairs={{0,4},{4,0},{1,5},{5,1},{2,6},{6,2},{3,7},{7,3},{8,12},{12,8},{9,1... | collective-permute-start | bytes 1572872 | tf_op jit(solution)/shard_map/ppermute | solution.py:532
  253.1 30.9 %all-to-all-start.3 = ((bf16[4,128,1024]{2,1,0:T(8,128)(2,1)}), bf16[4,128,1024]{2,1,0:T(8,128)(2,1)}, u32[]{:S(2)}, u32[]{:S(2)}) async-start(bf16[4,128,1024]{2,1,0:T(8,128)(2,1)} %add_convert_fusion), calls=%async_computation.3 | async-start | bytes 2097152 | tf_op jit(solution)/shard_map/all_to_all | solution.py:563
  260.2 20.1 %collective-permute-start.46 = (bf16[4,64,1024]{2,1,0:T(8,128)(2,1)}, bf16[4,64,1024]{2,1,0:T(8,128)(2,1)}, u32[]{:S(2)}, u32[]{:S(2)}) collective-permute-start(bf16[4,64,1024]{2,1,0:T(8,128)(2,1)} %add_convert_fusion.6), channel_id=1, source_target_pairs={{0,2},{2,0},{1,3},{3,1},{4,6},{6,4},{5,7},{7,5},{8,10},{10,8},{9,1... | collective-permute-start | bytes 1572872 | tf_op jit(solution)/shard_map/ppermute | solution.py:532
  261.4 19.0 %collective-permute-start.48 = (bf16[4,64,1536]{2,1,0:T(8,128)(2,1)}, bf16[4,64,1536]{2,1,0:T(8,128)(2,1)}, u32[]{:S(2)}, u32[]{:S(2)}) collective-permute-start(bf16[4,64,1536]{2,1,0:T(8,128)(2,1)} %get-tuple-element.324), channel_id=1, source_target_pairs={{0,4},{4,0},{1,5},{5,1},{2,6},{6,2},{3,7},{7,3},{8,12},{12,8},{9,1... | collective-permute-start | bytes 2359304 | tf_op jit(solution)/shard_map/ppermute | solution.py:532
  268.4 15.6 %collective-permute-start.45 = (bf16[4,64,768]{2,1,0:T(8,128)(2,1)}, bf16[4,64,768]{2,1,0:T(8,128)(2,1)}, u32[]{:S(2)}, u32[]{:S(2)}) collective-permute-start(bf16[4,64,768]{2,1,0:T(8,128)(2,1)} %get-tuple-element.320), channel_id=1, source_target_pairs={{0,2},{2,0},{1,3},{3,1},{4,6},{6,4},{5,7},{7,5},{8,10},{10,8},{9,1... | collective-permute-start | bytes 1179656 | tf_op jit(solution)/shard_map/ppermute | solution.py:532
  284.0 15.6 %collective-permute-start.49 = (bf16[640,1536]{1,0:T(8,128)(2,1)}, bf16[640,1536]{1,0:T(8,128)(2,1)}, u32[]{:S(2)}, u32[]{:S(2)}) collective-permute-start(bf16[640,1536]{1,0:T(8,128)(2,1)} %bitcast.133), channel_id=1, source_target_pairs={{0,1},{1,0},{2,3},{3,2},{4,5},{5,4},{6,7},{7,6},{8,9},{9,8},{10,11... | collective-permute-start | bytes 5898248 | tf_op jit(solution)/shard_map/ppermute | solution.py:532
  284.9 37.4 %collective-permute-start.54 = (bf16[4,64,1536]{2,1,0:T(8,128)(2,1)}, bf16[4,64,1536]{2,1,0:T(8,128)(2,1)}, u32[]{:S(2)}, u32[]{:S(2)}) collective-permute-start(bf16[4,64,1536]{2,1,0:T(8,128)(2,1)} %get-tuple-element.344), channel_id=1, source_target_pairs={{0,4},{4,0},{1,5},{5,1},{2,6},{6,2},{3,7},{7,3},{8,12},{12,8},{9,1... | collective-permute-start | bytes 2359304 | tf_op jit(solution)/shard_map/ppermute | solution.py:532
  285.7 37.9 %collective-permute-start.51 = (bf16[4,64,768]{2,1,0:T(8,128)(2,1)S(1)}, bf16[4,64,768]{2,1,0:T(8,128)(2,1)}, u32[]{:S(2)}, u32[]{:S(2)}) collective-permute-start(bf16[4,64,768]{2,1,0:T(8,128)(2,1)S(1)} %get-tuple-element.339), channel_id=1, source_target_pairs={{0,2},{2,0},{1,3},{3,1},{4,6},{6,4},{5,7},{7,5},{8,10},{10,8},{9,1... | collective-permute-start | bytes 1179656 | tf_op jit(solution)/shard_map/ppermute | solution.py:532
  289.1 34.5 %all-to-all-start.4 = ((bf16[4,64,1024]{2,1,0:T(8,128)(2,1)}), bf16[4,64,1024]{2,1,0:T(8,128)(2,1)}, u32[]{:S(2)}, u32[]{:S(2)}) async-start(bf16[4,64,1024]{2,1,0:T(8,128)(2,1)} %add_convert_fusion.5), calls=%async_computation.4 | async-start | bytes 1048576 | tf_op jit(solution)/shard_map/all_to_all | solution.py:563
  295.7 27.9 %collective-permute-start.53 = (bf16[4,64,1536]{2,1,0:T(8,128)(2,1)}, bf16[4,64,1536]{2,1,0:T(8,128)(2,1)}, u32[]{:S(2)}, u32[]{:S(2)}) collective-permute-start(bf16[4,64,1536]{2,1,0:T(8,128)(2,1)} %add_convert_fusion.4), channel_id=1, source_target_pairs={{0,2},{2,0},{1,3},{3,1},{4,6},{6,4},{5,7},{7,5},{8,10},{10,8},{9,1... | collective-permute-start | bytes 2359304 | tf_op jit(solution)/shard_map/ppermute | solution.py:532
  298.4 25.2 %collective-permute-start.52 = (bf16[4,64,768]{2,1,0:T(8,128)(2,1)}, bf16[4,64,768]{2,1,0:T(8,128)(2,1)}, u32[]{:S(2)}, u32[]{:S(2)}) collective-permute-start(bf16[4,64,768]{2,1,0:T(8,128)(2,1)} %add_convert_fusion.8), channel_id=1, source_target_pairs={{0,4},{4,0},{1,5},{5,1},{2,6},{6,2},{3,7},{7,3},{8,12},{12,8},{9,1... | collective-permute-start | bytes 1179656 | tf_op jit(solution)/shard_map/ppermute | solution.py:532
  305.1 18.5 %collective-permute-start.50 = (bf16[4,64,768]{2,1,0:T(8,128)(2,1)S(1)}, bf16[4,64,768]{2,1,0:T(8,128)(2,1)}, u32[]{:S(2)}, u32[]{:S(2)}) collective-permute-start(bf16[4,64,768]{2,1,0:T(8,128)(2,1)S(1)} %get-tuple-element.338), channel_id=1, source_target_pairs={{0,4},{4,0},{1,5},{5,1},{2,6},{6,2},{3,7},{7,3},{8,12},{12,8},{9,1... | collective-permute-start | bytes 1179656 | tf_op jit(solution)/shard_map/ppermute | solution.py:532
  322.3 31.5 %collective-permute-start.56 = (bf16[4,64,768]{2,1,0:T(8,128)(2,1)S(1)}, bf16[4,64,768]{2,1,0:T(8,128)(2,1)}, u32[]{:S(2)}, u32[]{:S(2)}) collective-permute-start(bf16[4,64,768]{2,1,0:T(8,128)(2,1)S(1)} %get-tuple-element.358), channel_id=1, source_target_pairs={{0,4},{4,0},{1,5},{5,1},{2,6},{6,2},{3,7},{7,3},{8,12},{12,8},{9,1... | collective-permute-start | bytes 1179656 | tf_op jit(solution)/shard_map/ppermute | solution.py:532
  323.6 14.8 %collective-permute-start.57 = (f32[8,1536]{1,0:T(8,128)}, f32[8,1536]{1,0:T(8,128)S(1)}, u32[]{:S(2)}, u32[]{:S(2)}) collective-permute-start(f32[8,1536]{1,0:T(8,128)} %shard_map.267), channel_id=1, source_target_pairs={{0,1},{1,0},{2,3},{3,2},{4,5},{5,4},{6,7},{7,6},{8,9},{9,8},{10,11... | collective-permute-start | bytes 147464 | tf_op jit(solution)/shard_map/ppermute | solution.py:532
  326.3 27.6 %all-to-all-start.5 = ((bf16[4,64,1536]{2,1,0:T(8,128)(2,1)}), bf16[4,64,1536]{2,1,0:T(8,128)(2,1)S(1)}, u32[]{:S(2)}, u32[]{:S(2)}) async-start(bf16[4,64,1536]{2,1,0:T(8,128)(2,1)} %add_convert_fusion.3), calls=%async_computation.5 | async-start | bytes 1572864 | tf_op jit(solution)/shard_map/all_to_all | solution.py:563
  332.4 21.4 %collective-permute-start.55 = (bf16[4,64,768]{2,1,0:T(8,128)(2,1)S(1)}, bf16[4,64,768]{2,1,0:T(8,128)(2,1)S(1)}, u32[]{:S(2)}, u32[]{:S(2)}) collective-permute-start(bf16[4,64,768]{2,1,0:T(8,128)(2,1)S(1)} %add_convert_fusion.7), channel_id=1, source_target_pairs={{0,2},{2,0},{1,3},{3,1},{4,6},{6,4},{5,7},{7,5},{8,10},{10,8},{9,1... | collective-permute-start | bytes 1179656 | tf_op jit(solution)/shard_map/ppermute | solution.py:532
  335.1 18.7 %collective-permute-start.60 = (bf16[128,1024]{1,0:T(8,128)(2,1)S(1)}, bf16[128,1024]{1,0:T(8,128)(2,1)}, u32[]{:S(2)}, u32[]{:S(2)}) collective-permute-start(bf16[128,1024]{1,0:T(8,128)(2,1)S(1)} %reduce_sum.59.refs_8_), channel_id=1, source_target_pairs={{0,2},{2,0},{1,3},{3,1},{4,6},{6,4},{5,7},{7,5},{8,10},{10,8},{9,1... | collective-permute-start | bytes 786440 | tf_op jit(solution)/shard_map/ppermute | solution.py:532
  337.2 16.7 %collective-permute-start.59 = (bf16[64,1024]{1,0:T(8,128)(2,1)S(1)}, bf16[64,1024]{1,0:T(8,128)(2,1)S(1)}, u32[]{:S(2)}, u32[]{:S(2)}) collective-permute-start(bf16[64,1024]{1,0:T(8,128)(2,1)S(1)} %reduce_sum.58.refs_0_), channel_id=1, source_target_pairs={{0,2},{2,0},{1,3},{3,1},{4,6},{6,4},{5,7},{7,5},{8,10},{10,8},{9,1... | collective-permute-start | bytes 393224 | tf_op jit(solution)/shard_map/ppermute | solution.py:532
  338.4 14.8 %collective-permute-start.58 = (f32[8,1536]{1,0:T(8,128)S(1)}, f32[8,1536]{1,0:T(8,128)S(1)}, u32[]{:S(2)}, u32[]{:S(2)}) collective-permute-start(f32[8,1536]{1,0:T(8,128)S(1)} %add.147), channel_id=1, source_target_pairs={{0,2},{2,0},{1,3},{3,1},{4,6},{6,4},{5,7},{7,5},{8,10},{10,8},{9,1... | collective-permute-start | bytes 147464 | tf_op jit(solution)/shard_map/ppermute | solution.py:532
  356.9 31.4 %all-to-all-start.6 = ((bf16[4,64,1536]{2,1,0:T(8,128)(2,1)}), bf16[4,64,1536]{2,1,0:T(8,128)(2,1)S(1)}, u32[]{:S(2)}, u32[]{:S(2)}) async-start(bf16[4,64,1536]{2,1,0:T(8,128)(2,1)} %add_convert_fusion.2), calls=%async_computation.6 | async-start | bytes 1572864 | tf_op jit(solution)/shard_map/all_to_all | solution.py:563
  365.6 22.0 %collective-permute-start.66 = (bf16[4,80,1024]{2,1,0:T(8,128)(2,1)}, bf16[4,80,1024]{2,1,0:T(8,128)(2,1)S(1)}, u32[]{:S(2)}, u32[]{:S(2)}) collective-permute-start(bf16[4,80,1024]{2,1,0:T(8,128)(2,1)} %get-tuple-element.414), channel_id=1, source_target_pairs={{0,1},{1,0},{2,3},{3,2},{4,5},{5,4},{6,7},{7,6},{8,9},{9,8},{10,11... | collective-permute-start | bytes 1966088 | tf_op jit(solution)/shard_map/ppermute | solution.py:536
  365.6 22.6 %collective-permute-start.67 = (bf16[4,80,1024]{2,1,0:T(8,128)(2,1)}, bf16[4,80,1024]{2,1,0:T(8,128)(2,1)S(1)}, u32[]{:S(2)}, u32[]{:S(2)}) collective-permute-start(bf16[4,80,1024]{2,1,0:T(8,128)(2,1)} %get-tuple-element.415), channel_id=1, source_target_pairs={{0,2},{1,3},{2,0},{3,1},{4,6},{5,7},{6,4},{7,5},{8,10},{9,11},{10,... | collective-permute-start | bytes 1966088 | tf_op jit(solution)/shard_map/ppermute | solution.py:536
  369.5 12.6 %collective-permute-start.64 = (f32[1536]{0:T(1024)}, f32[1536]{0:T(1024)}, u32[]{:S(2)}, u32[]{:S(2)}) collective-permute-start(f32[1536]{0:T(1024)} %get-tuple-element.400), channel_id=1, source_target_pairs={{0,16},{8,24},{16,0},{24,8},{1,17},{9,25},{17,1},{25,9},{2,18},{10... | collective-permute-start | bytes 18440 | tf_op jit(solution)/shard_map/ppermute | solution.py:536
  374.5 13.1 %collective-permute-start.61 = (bf16[64,1536]{1,0:T(8,128)(2,1)}, bf16[64,1536]{1,0:T(8,128)(2,1)S(1)}, u32[]{:S(2)}, u32[]{:S(2)}) collective-permute-start(bf16[64,1536]{1,0:T(8,128)(2,1)} %reduce_sum.60.refs_4_), channel_id=1, source_target_pairs={{0,2},{2,0},{1,3},{3,1},{4,6},{6,4},{5,7},{7,5},{8,10},{10,8},{9,1... | collective-permute-start | bytes 589832 | tf_op jit(solution)/shard_map/ppermute | solution.py:532
  382.1 18.8 %collective-permute-start.74 = (bf16[4,80,1024]{2,1,0:T(8,128)(2,1)}, bf16[4,80,1024]{2,1,0:T(8,128)(2,1)S(1)}, u32[]{:S(2)}, u32[]{:S(2)}) collective-permute-start(bf16[4,80,1024]{2,1,0:T(8,128)(2,1)} %get-tuple-element.412), channel_id=1, source_target_pairs={{0,3},{1,2},{2,1},{3,0},{4,7},{5,6},{6,5},{7,4},{8,11},{9,10},{10,... | collective-permute-start | bytes 1966088 | tf_op jit(solution)/shard_map/ppermute | solution.py:536
  391.8 13.7 %collective-permute-start.75 = (bf16[64,1536]{1,0:T(8,128)(2,1)}, bf16[64,1536]{1,0:T(8,128)(2,1)S(1)}, u32[]{:S(2)}, u32[]{:S(2)}) collective-permute-start(bf16[64,1536]{1,0:T(8,128)(2,1)} %reduce_sum.61.refs_0_), channel_id=1, source_target_pairs={{0,2},{2,0},{1,3},{3,1},{4,6},{6,4},{5,7},{7,5},{8,10},{10,8},{9,1... | collective-permute-start | bytes 589832 | tf_op jit(solution)/shard_map/ppermute | solution.py:532
  392.9 17.0 %collective-permute-start.76 = (bf16[64,1536]{1,0:T(8,128)(2,1)}, bf16[64,1536]{1,0:T(8,128)(2,1)S(1)}, u32[]{:S(2)}, u32[]{:S(2)}) collective-permute-start(bf16[64,1536]{1,0:T(8,128)(2,1)} %reduce_sum.61.refs_0_), channel_id=1, source_target_pairs={{0,1},{1,0},{2,3},{3,2},{4,5},{5,4},{6,7},{7,6},{8,9},{9,8},{10,11... | collective-permute-start | bytes 589832 | tf_op jit(solution)/shard_map/ppermute | solution.py:532
  (57 other events, 345.5 us)
